TPU v7x, 32 devices: a whole 2x2x4 slice. The times are simulated.
32 devices in a mesh: dp: 8 (over y, x, core), tensor: 4 (over z).
Axes of the slice: x: 2, y: 2, z: 4, core: 2. Of those that a mesh axis runs over, the one named last changes fastest.
Arguments:
- clip_rows: bfloat16 [12544, 1024], P(('dp', 'tensor')), may hold values from -6 to 6
- out_grad: bfloat16 [12544, 1024], P(('dp', 'tensor')), may hold values from -6 to 6
- clip_valid: int32 [8], P('dp'), may hold values from 0 to 1, as said below
- gain_rows: bfloat16 [2, 1024], P(None, ('dp', 'tensor')), may hold values from 0.099609375 to 1.8984375
- bias_rows: bfloat16 [4, 1024], P(None, ('dp', 'tensor')), may hold values from -1.796875 to 1.796875
- qkv_weight: bfloat16 [3, 1024, 1024], P(None, 'dp', 'tensor'), may hold values from -0.1875 to 0.1875
- qv_bias: bfloat16 [2, 16, 64], P(None, 'tensor', 'dp'), may hold values from -3 to 3
- proj_weight: bfloat16 [1024, 1024], P('tensor', 'dp'), may hold values from -4 to 4
- fc1_weight: bfloat16 [1024, 4096], P('dp', 'tensor'), may hold values from -0.1875 to 0.1875
- fc1_bias: bfloat16 [4, 1024], P('tensor', 'dp'), may hold values from -1.796875 to 1.796875
- fc2_weight: bfloat16 [4096, 1024], P('tensor', 'dp'), may hold values from -0.125 to 0.125
Outputs:
- layer_out: bfloat16 [12544, 1024], P(('dp', 'tensor'))
- input_grad: float32 [12544, 1024], P(('dp', 'tensor'))
- grad_gains: float32 [2, 1024], P(None, ('dp', 'tensor'))
- grad_biases: float32 [4, 1024], P(None, ('dp', 'tensor'))
- grad_qkv: float32 [3, 1024, 1024], P(None, 'dp', 'tensor')
- grad_qv_bias: float32 [2, 16, 64], P(None, 'tensor', 'dp')
- grad_proj: float32 [1024, 1024], P('tensor', 'dp')
- grad_fc1: float32 [1024, 4096], P('dp', 'tensor')
- grad_fc1_bias: float32 [4, 1024], P('tensor', 'dp')
- grad_fc2: float32 [4096, 1024], P('tensor', 'dp')
- grad_fc2_bias: float32 [1024], P(('dp', 'tensor'))
Inputs may be any that keep to these rules, and one draw needn't show every extreme that they name: `clip_valid`: exactly 2 of the 8 slots hold a clip; which ones is drawn from the seed.
All inputs are finite; a program needn't handle non-finite values.
Results may differ from a plain program's by a relative error of at most 0.012.
Values may be sent and summed in bfloat16 or wider, within the bound.
No kernel may reach another device: no remote copies, remote signals or barrier semaphores. Data moves between devices by JAX's collectives and lax.ppermute only.
A program may use at most 256 MiB of HBM per device.

v0:
```python
import math

import jax
import jax.numpy as jnp
from jax import lax
from jax.sharding import PartitionSpec as P

HD = 64


norm_eps = 1e-06
root_half = 0.7071067811865476
inv_root_tau = 0.3989422804014327


def normalize(values, gain_row, shift_row):
    centre = jnp.mean(values, axis=1, keepdims=True)
    offsets = values - centre
    inverse = lax.rsqrt(jnp.mean(offsets * offsets, axis=1, keepdims=True) + norm_eps)
    scaled = offsets * inverse
    return (scaled * gain_row + shift_row, scaled, inverse)


def normalize_back(upstream, scaled, inverse, gain_row):
    grad_hat = upstream * gain_row
    return (
        grad_hat
        - jnp.mean(grad_hat, axis=1, keepdims=True)
        - scaled * jnp.mean(grad_hat * scaled, axis=1, keepdims=True)
    ) * inverse


def gelu_value(inputs):
    return 0.5 * inputs * (1.0 + lax.erf(inputs * root_half))


def gelu_slope(inputs):
    return (
        0.5 * (1.0 + lax.erf(inputs * root_half))
        + inputs * jnp.exp(-0.5 * inputs * inputs) * inv_root_tau
    )


def fetch(qkv_weight, proj_weight, fc1_weight, fc2_weight, qv_bias, fc1_bias, gain_rows, bias_rows):
    matrices = (
        lax.all_gather(qkv_weight, "dp", axis=1, tiled=True),
        lax.all_gather(proj_weight, "dp", axis=1, tiled=True),
        lax.all_gather(fc1_weight, "dp", axis=0, tiled=True),
        lax.all_gather(fc2_weight, "dp", axis=1, tiled=True),
        lax.all_gather(qv_bias, "dp", axis=2, tiled=True),
        lax.all_gather(fc1_bias, "dp", axis=1, tiled=True),
    )
    vectors = (
        lax.all_gather(gain_rows, ("dp", "tensor"), axis=1, tiled=True),
        lax.all_gather(bias_rows, ("dp", "tensor"), axis=1, tiled=True),
    )
    return (matrices, (vectors[0].astype(jnp.float32), vectors[1].astype(jnp.float32)))


def spread_rows(local_rows):
    return lax.all_gather(local_rows, "tensor", axis=0, tiled=True)


def reduce_rows(term_fn, row_count):
    return lax.psum_scatter(
        term_fn(jnp.int32(0), lax.axis_size("tensor") * row_count),
        "tensor",
        scatter_dimension=0,
        tiled=True,
    )


def spread_grads(local_rows):
    return lax.all_gather(local_rows, "tensor", axis=0, tiled=True)


def reduce_grads(term_fn, row_count):
    return lax.psum_scatter(
        term_fn(jnp.int32(0), lax.axis_size("tensor") * row_count),
        "tensor",
        scatter_dimension=0,
        tiled=True,
    )


def forward(clip_rows, matrices, vectors):
    w_qkv, w_proj, w_fc1, w_fc2, b_qv, b_fc1 = matrices
    gain_rows, bias_rows = vectors
    row_count = clip_rows.shape[0]
    head_cols = w_qkv.shape[2]
    heads_here = head_cols // HD
    score_scale = 1.0 / math.sqrt(HD)
    inputs = clip_rows.astype(jnp.float32)
    normed_one, scaled_one, inverse_one = normalize(inputs, gain_rows[0], bias_rows[0])
    whole_one = spread_rows(normed_one.astype(jnp.bfloat16))
    seq_len = whole_one.shape[0]
    projected = jnp.einsum("sd,jde->jse", whole_one, w_qkv, preferred_element_type=jnp.float32)
    bias_cols = b_qv.reshape(2, head_cols).astype(jnp.float32)
    queries = (projected[0] + bias_cols[0]).astype(jnp.bfloat16).reshape(seq_len, heads_here, HD)
    keys_all = projected[1].astype(jnp.bfloat16).reshape(seq_len, heads_here, HD)
    values_all = (projected[2] + bias_cols[1]).astype(jnp.bfloat16).reshape(seq_len, heads_here, HD)
    scores = (
        jnp.einsum("qhd,khd->hqk", queries, keys_all, preferred_element_type=jnp.float32)
        * score_scale
    )
    top_score = jnp.max(scores, axis=2, keepdims=True)
    weights_exp = jnp.exp(scores - top_score)
    totals = jnp.sum(weights_exp, axis=2, keepdims=True)
    attn_probs = (weights_exp / totals).astype(jnp.bfloat16)
    log_total = top_score + jnp.log(totals)
    attended = (
        jnp.einsum("hqk,khd->qhd", attn_probs, values_all, preferred_element_type=jnp.float32)
        .reshape(seq_len, head_cols)
        .astype(jnp.bfloat16)
    )

    def proj_term(offset, length):
        return jnp.dot(attended, w_proj, preferred_element_type=jnp.float32)

    residual_one = inputs + (reduce_rows(proj_term, row_count) + bias_rows[2])
    normed_two, scaled_two, inverse_two = normalize(residual_one, gain_rows[1], bias_rows[1])
    whole_two = spread_rows(normed_two.astype(jnp.bfloat16))
    pre_act = jnp.dot(whole_two, w_fc1, preferred_element_type=jnp.float32) + b_fc1.reshape(
        -1
    ).astype(jnp.float32)
    hidden = gelu_value(pre_act).astype(jnp.bfloat16)

    def fc2_term(offset, length):
        return jnp.dot(hidden, w_fc2, preferred_element_type=jnp.float32)

    layer_out = residual_one + (reduce_rows(fc2_term, row_count) + bias_rows[3])
    stored = (
        scaled_one,
        inverse_one,
        whole_one,
        queries,
        keys_all,
        values_all,
        log_total,
        attended,
        scaled_two,
        inverse_two,
        whole_two,
        pre_act,
        hidden,
    )
    return (layer_out, stored)


def backward(upstream, matrices, vectors, stored):
    w_qkv, w_proj, w_fc1, w_fc2, b_qv, b_fc1 = matrices
    gain_rows, bias_rows = vectors
    (
        scaled_one,
        inverse_one,
        whole_one,
        queries,
        keys_all,
        values_all,
        log_total,
        attended,
        scaled_two,
        inverse_two,
        whole_two,
        pre_act,
        hidden,
    ) = stored
    row_count = upstream.shape[0]
    seq_len = queries.shape[0]
    heads_here = queries.shape[1]
    head_cols = heads_here * HD
    score_scale = 1.0 / math.sqrt(HD)
    grad_mlp = upstream.astype(jnp.bfloat16)
    grad_fc2_bias = jnp.sum(grad_mlp.astype(jnp.float32), axis=0)
    whole_mlp = spread_grads(grad_mlp)
    grad_fc2 = jnp.einsum("sf,sd->fd", hidden, whole_mlp, preferred_element_type=jnp.float32)
    grad_hidden = jnp.einsum("sd,fd->sf", whole_mlp, w_fc2, preferred_element_type=jnp.float32)
    grad_pre = (grad_hidden * gelu_slope(pre_act)).astype(jnp.bfloat16)
    grad_fc1_bias = jnp.sum(grad_pre.astype(jnp.float32), axis=0)
    grad_fc1 = jnp.einsum("sd,sf->df", whole_two, grad_pre, preferred_element_type=jnp.float32)

    def fc1_back(offset, length):
        return jnp.einsum("sf,df->sd", grad_pre, w_fc1, preferred_element_type=jnp.float32)

    grad_normed_two = reduce_grads(fc1_back, row_count)
    grad_residual = upstream + normalize_back(
        grad_normed_two, scaled_two, inverse_two, gain_rows[1]
    )
    grad_branch = grad_residual.astype(jnp.bfloat16)
    grad_proj_bias = jnp.sum(grad_branch.astype(jnp.float32), axis=0)
    whole_branch = spread_grads(grad_branch)
    grad_proj = jnp.einsum("se,sd->ed", attended, whole_branch, preferred_element_type=jnp.float32)
    grad_att = (
        jnp.einsum("sd,ed->se", whole_branch, w_proj, preferred_element_type=jnp.float32)
        .astype(jnp.bfloat16)
        .reshape(seq_len, heads_here, HD)
    )
    scores = (
        jnp.einsum("qhd,khd->hqk", queries, keys_all, preferred_element_type=jnp.float32)
        * score_scale
    )
    attn_probs = jnp.exp(scores - log_total)
    grad_probs = jnp.einsum(
        "qhd,khd->hqk", grad_att, values_all, preferred_element_type=jnp.float32
    )
    row_dot = jnp.sum(attn_probs * grad_probs, axis=2, keepdims=True)
    grad_scores = (attn_probs * (grad_probs - row_dot)).astype(jnp.bfloat16)
    grad_query = (
        jnp.einsum("hqk,khd->qhd", grad_scores, keys_all, preferred_element_type=jnp.float32)
        * score_scale
    ).astype(jnp.bfloat16)
    grad_key = (
        jnp.einsum("hqk,qhd->khd", grad_scores, queries, preferred_element_type=jnp.float32)
        * score_scale
    ).astype(jnp.bfloat16)
    grad_value = jnp.einsum(
        "hqk,qhd->khd",
        attn_probs.astype(jnp.bfloat16),
        grad_att,
        preferred_element_type=jnp.float32,
    ).astype(jnp.bfloat16)
    grad_qkv = jnp.stack([grad_query, grad_key, grad_value]).reshape(3, seq_len, head_cols)
    grad_qv = jnp.stack(
        [
            jnp.sum(grad_query.astype(jnp.float32), axis=0),
            jnp.sum(grad_value.astype(jnp.float32), axis=0),
        ]
    )
    grad_qkv_weight = jnp.einsum(
        "sd,jse->jde", whole_one, grad_qkv, preferred_element_type=jnp.float32
    )

    def qkv_back(offset, length):
        return jnp.einsum("jse,jde->sd", grad_qkv, w_qkv, preferred_element_type=jnp.float32)

    grad_normed_one = reduce_grads(qkv_back, row_count)
    grad_input = grad_residual + normalize_back(
        grad_normed_one, scaled_one, inverse_one, gain_rows[0]
    )
    grad_gain = jnp.stack(
        [
            jnp.sum(grad_normed_one * scaled_one, axis=0),
            jnp.sum(grad_normed_two * scaled_two, axis=0),
        ]
    )
    grad_bias = jnp.stack(
        [
            jnp.sum(grad_normed_one, axis=0),
            jnp.sum(grad_normed_two, axis=0),
            grad_proj_bias,
            grad_fc2_bias,
        ]
    )
    weight_part = (
        lax.psum_scatter(grad_qkv_weight, "dp", scatter_dimension=1, tiled=True),
        lax.psum_scatter(grad_proj, "dp", scatter_dimension=1, tiled=True),
        lax.psum_scatter(grad_fc1, "dp", scatter_dimension=0, tiled=True),
        lax.psum_scatter(grad_fc2, "dp", scatter_dimension=1, tiled=True),
        lax.psum_scatter(grad_qv, "dp", scatter_dimension=2, tiled=True),
        lax.psum_scatter(grad_fc1_bias.reshape(1, -1), "dp", scatter_dimension=1, tiled=True),
    )
    vector_part = (
        lax.psum_scatter(grad_gain, ("dp", "tensor"), scatter_dimension=1, tiled=True),
        lax.psum_scatter(grad_bias, ("dp", "tensor"), scatter_dimension=1, tiled=True),
    )
    return (grad_input, weight_part, vector_part)


def on_device(
    clip_rows,
    out_grad,
    clip_valid,
    gain_rows,
    bias_rows,
    qkv_weight,
    qv_bias,
    proj_weight,
    fc1_weight,
    fc1_bias,
    fc2_weight,
):
    clip_weight = clip_valid[0].astype(jnp.float32)
    upstream = out_grad.astype(jnp.float32) * clip_weight
    matrices, vectors = fetch(
        qkv_weight, proj_weight, fc1_weight, fc2_weight, qv_bias, fc1_bias, gain_rows, bias_rows
    )
    layer_out, stored = forward(clip_rows, matrices, vectors)
    matrices, vectors = fetch(
        qkv_weight, proj_weight, fc1_weight, fc2_weight, qv_bias, fc1_bias, gain_rows, bias_rows
    )
    unused_out, stored = forward(clip_rows, matrices, vectors)
    grad_input, weight_part, vector_part = backward(upstream, matrices, vectors, stored)
    return (
        (layer_out * clip_weight).astype(jnp.bfloat16),
        grad_input,
        vector_part[0],
        vector_part[1],
        weight_part[0],
        weight_part[4],
        weight_part[1],
        weight_part[2],
        weight_part[5],
        weight_part[3],
        vector_part[1][3],
    )


def solution(mesh):
    in_specs = (
        P(("dp", "tensor"), None),
        P(("dp", "tensor"), None),
        P("dp"),
        P(None, ("dp", "tensor")),
        P(None, ("dp", "tensor")),
        P(None, "dp", "tensor"),
        P(None, "tensor", "dp"),
        P("tensor", "dp"),
        P("dp", "tensor"),
        P("tensor", "dp"),
        P("tensor", "dp"),
    )
    out_specs = (
        P(("dp", "tensor"), None),
        P(("dp", "tensor"), None),
        P(None, ("dp", "tensor")),
        P(None, ("dp", "tensor")),
        P(None, "dp", "tensor"),
        P(None, "tensor", "dp"),
        P("tensor", "dp"),
        P("dp", "tensor"),
        P("tensor", "dp"),
        P("tensor", "dp"),
        P(("dp", "tensor")),
    )
    return jax.shard_map(
        on_device, mesh=mesh, in_specs=in_specs, out_specs=out_specs, check_vma=False
    )
```

profile of v0, /device:TPU:0, one launch (start us, length us, event | category | flops | bytes accessed | tf_op | source)
XLA Modules:
  0.0 1630.0 jit_solution(12553502785783311040)
XLA Ops:
  8.0 69.5 %all-gather = bf16[32,32,2]{1,2,0:T(2,128)(2,1)S(1)} all-gather(bf16[1,32,2]{1,2,0:T(2,128)(2,1)} %bitcast.144), channel_id=1, replica_groups=mesh['dp'=8,'tensor'=4] {'dp','tensor'}, dimensions={0}, use_global_device_ids=true | all-gather | bytes 4224 | tf_op jit(solution)/shard_map/all_gather | solution.py:54
  77.5 63.8 %all-gather.1 = bf16[32,32,4]{1,2,0:T(4,128)(2,1)S(1)} all-gather(bf16[1,32,4]{1,2,0:T(4,128)(2,1)} %bitcast.143), channel_id=1, replica_groups=mesh['dp'=8,'tensor'=4] {'dp','tensor'}, dimensions={0}, use_global_device_ids=true | all-gather | bytes 8448 | tf_op jit(solution)/shard_map/all_gather | solution.py:55
  141.4 1.4 convert_reduce_fusion.1
  142.8 1.5 fusion.37
  144.9 1.2 fusion.31
  146.4 8.1 all_gather.50
  154.6 11.0 all_gather.51
  165.6 43.3 %all-gather.10.cloned.1.call-done = bf16[1568,1024]{1,0:T(8,128)(2,1)} async-done(((bf16[392,1024]{1,0:T(8,128)(2,1)}), bf16[1568,1024]{1,0:T(8,128)(2,1)}) %all-gather.10.cloned.1.call-update) | async-done | bytes 3211280 | tf_op jit(solution)/shard_map/all_gather | solution.py:61
  208.9 5.1 convolution_bitcast_fusion.1
  215.0 1.4 fusion.44
  216.3 1.5 copy.74
  217.9 1.7 copy.69
  219.5 1.8 copy.72
  221.3 16.1 fusion.48
  237.5 16.4 %fusion = f32[4,1568]{1,0:T(4,128)S(1)} fusion(f32[4,1568,1568]{1,2,0:T(8,128)} %get-tuple-element.82, f32[4,1568]{1,0:T(4,128)S(1)} %get-tuple-element.81), kind=kLoop, calls=%fused_computation.6 | loop fusion | flops 19662720 | bytes 39388160 | tf_op jit(solution)/shard_map/reduce_sum | solution.py:108
  253.8 17.4 %fusion.20 = bf16[4,64,1568]{2,1,0:T(8,128)(2,1)} fusion(f32[4,1568,1568]{1,2,0:T(8,128)} %get-tuple-element.82, f32[4,1568]{1,0:T(4,128)S(1)} %fusion, f32[4,1568]{1,0:T(4,128)S(1)} %get-tuple-element.81, f32[1568,4,64]{0,2,1:T(8,128)S(1)} %bitcast.106, f32[4,64]{1,0:T(4,128)S(1)} %copy.71), kind=kOutput, calls=%fused_computation.32 | convolution fusion | flops 1289523200 | bytes 41797632 | tf_op jit(solution)/shard_map/hqk,khd->qhd/dot_general | solution.py:112
  271.3 4.9 fusion.49
  277.2 110.7 %reduce-scatter.19.cloned.1.call-done = f32[392,1024]{1,0:T(8,128)} async-done(((f32[1568,1024]{1,0:T(8,128)}), f32[392,1024]{1,0:T(8,128)}) %reduce-scatter.19.cloned.1.call-update) | async-done | bytes 1605648 | tf_op jit(solution)/shard_map/reduce_scatter | solution.py:65
  387.9 1.7 fusion.43
  389.9 1.2 add_convert_fusion.2
  392.5 1.1 convert_reduce_fusion.4
  393.6 8.7 all_gather.54
  402.4 15.7 all-gather.16.cloned.1.call-done
  418.1 66.6 %all-gather.14.cloned.1.call-done = bf16[1568,1024]{1,0:T(8,128)(2,1)} async-done(((bf16[392,1024]{1,0:T(8,128)(2,1)}), bf16[1568,1024]{1,0:T(8,128)(2,1)}) %all-gather.14.cloned.1.call-update) | async-done | bytes 3211280 | tf_op jit(solution)/shard_map/all_gather | solution.py:61
  484.7 8.5 multiply_convert_fusion.1
  493.2 20.1 %all-gather.18.cloned.1.call-done = bf16[1024,1024]{1,0:T(8,128)(2,1)} async-done(((bf16[1024,128]{1,0:T(8,128)(2,1)}), bf16[1024,1024]{1,0:T(8,128)(2,1)}) %all-gather.18.cloned.1.call-update) | async-done | bytes 2097168 | tf_op jit(solution)/shard_map/all_gather | solution.py:49
  513.3 66.8 %all-gather.20.cloned.1.call-done = bf16[1568,1024]{1,0:T(8,128)(2,1)} async-done(((bf16[392,1024]{1,0:T(8,128)(2,1)}), bf16[1568,1024]{1,0:T(8,128)(2,1)}) %all-gather.20.cloned.1.call-update) | async-done | bytes 3211280 | tf_op jit(solution)/shard_map/all_gather | solution.py:74
  580.0 9.5 convert_reduce_fusion
  589.6 1.7 copy-done.30
  591.3 5.7 fusion.51
  597.0 8.8 fusion.50
  605.9 102.8 %reduce-scatter.23.cloned.1.call-done = f32[392,1024]{1,0:T(8,128)} async-done(((f32[1568,1024]{1,0:T(8,128)}), f32[392,1024]{1,0:T(8,128)}) %reduce-scatter.23.cloned.1.call-update) | async-done | bytes 1605648 | tf_op jit(solution)/shard_map/reduce_scatter | solution.py:78
  708.6 2.1 multiply_reduce_fusion.1
  710.8 113.6 %reduce-scatter.21.cloned.1.call-done = f32[392,1024]{1,0:T(8,128)} async-done(((f32[1568,1024]{1,0:T(8,128)}), f32[392,1024]{1,0:T(8,128)}) %reduce-scatter.21.cloned.1.call-update) | async-done | bytes 1605648 | tf_op jit(solution)/shard_map/reduce_scatter | solution.py:65
  824.4 4.4 convert_reduce_fusion.5
  828.9 65.2 %all-gather.22.cloned.1.call-done = bf16[1568,1024]{1,0:T(8,128)(2,1)} async-done(((bf16[392,1024]{1,0:T(8,128)(2,1)}), bf16[1568,1024]{1,0:T(8,128)(2,1)}) %all-gather.22.cloned.1.call-update) | async-done | bytes 3211280 | tf_op jit(solution)/shard_map/all_gather | solution.py:74
  894.1 3.0 convolution_convert_fusion
  898.0 16.9 %convert_reduce_fusion.2 = (f32[4,64]{1,0:T(4,128)S(1)}, bf16[4,64,1568]{2,1,0:T(8,128)(2,1)}) fusion(bf16[1568,4,64]{0,2,1:T(8,128)(2,1)S(1)} %bitcast.104, f32[4,1568,1568]{1,2,0:T(8,128)} %get-tuple-element.82, f32[4,1568]{1,0:T(4,128)S(1)} %log_add_fusion), kind=kOutput, calls=%fused_computation.44 | convolution fusion | flops 1279688448 | bytes 40969728 | tf_op jit(solution)/shard_map/hqk,qhd->khd/dot_general | solution.py:216
  914.9 26.3 %multiply_reduce_fusion = (f32[4,1568]{1,0:T(4,128)S(1)}, f32[4,1568,1568]{1,2,0:T(8,128)}) fusion(f32[4,1568,1568]{1,2,0:T(8,128)} %get-tuple-element.82, f32[4,1568]{1,0:T(4,128)S(1)} %log_add_fusion, bf16[1568,4,64]{0,2,1:T(8,128)(2,1)S(1)} %bitcast.105, f32[1568,4,64]{0,2,1:T(8,128)S(1)} %bitcast.107, f32[4,64]{1,0:T(4,128)S(1)} %copy.71), kind=kOutput, calls=%fused_computation.1 | convolution fusion | flops 1289115520 | bytes 81135616 | tf_op jit(solution)/shard_map/qhd,khd->hqk/dot_general | solution.py:203
  941.2 33.6 %multiply_convert_fusion = bf16[4,1568,1568]{1,2,0:T(8,128)(2,1)} fusion(f32[4,1568,1568]{1,2,0:T(8,128)} %get-tuple-element.86, f32[4,1568,1568]{1,2,0:T(8,128)} %get-tuple-element.82, f32[4,1568]{1,0:T(4,128)S(1)} %get-tuple-element.85, f32[4,1568]{1,0:T(4,128)S(1)} %log_add_fusion), kind=kLoop, calls=%fused_computation | loop fusion | flops 39337984 | bytes 98395136 | tf_op jit(solution)/shard_map/convert_element_type | solution.py:207
  974.8 11.4 fusion.16
  986.2 10.4 convert_reduce_fusion.3
  996.7 1.2 copy.82
  997.9 1.2 copy.80
  999.9 7.3 convolution_bitcast_fusion
  1008.8 6.7 fusion.27
  1015.6 103.3 %reduce-scatter.25.cloned.1.call-done = f32[392,1024]{1,0:T(8,128)} async-done(((f32[1568,1024]{1,0:T(8,128)}), f32[392,1024]{1,0:T(8,128)}) %reduce-scatter.25.cloned.1.call-update) | async-done | bytes 1605648 | tf_op jit(solution)/shard_map/reduce_scatter | solution.py:78
  1119.0 2.2 fusion.36
  1123.4 8.8 fusion.53
  1132.6 8.9 fusion.54
  1141.6 1.1 copy-done.11
  1142.7 4.0 fusion.52
  1148.0 8.6 reduce-scatter.39.cloned.1.call-done
  1156.6 1.4 copy.95
  1158.0 12.2 all-reduce
  1170.9 35.7 %reduce-scatter.27.cloned.1.call-done = f32[3,128,256]{1,2,0:T(8,128)} async-done(((f32[3,1024,256]{1,2,0:T(8,128)}), f32[3,128,256]{1,2,0:T(8,128)}) %reduce-scatter.27.cloned.1.call-update) | async-done | bytes 393232 | tf_op jit(solution)/shard_map/reduce_scatter | solution.py:255
  1206.6 1.9 copy.83
  1208.5 3.1 fusion.35
  1211.7 131.5 %reduce-scatter.35.cloned.1.call-done = f32[32,2]{1,0:T(8,128)} async-done(((f32[1024,2]{1,0:T(8,128)}), f32[32,2]{1,0:T(8,128)}) %reduce-scatter.35.cloned.1.call-update) | async-done | bytes 272
  1343.2 1.4 copy.89
  1344.6 131.6 %reduce-scatter.37.cloned.1.call-done = f32[32,4]{1,0:T(8,128)} async-done(((f32[1024,4]{1,0:T(8,128)}), f32[32,4]{1,0:T(8,128)}) %reduce-scatter.37.cloned.1.call-update) | async-done | bytes 528
  1477.5 50.1 %reduce-scatter.31.cloned.1.call-done = f32[128,1024]{1,0:T(8,128)} async-done(((f32[1024,1024]{1,0:T(8,128)}), f32[128,1024]{1,0:T(8,128)}) %reduce-scatter.31.cloned.1.call-update) | async-done | bytes 524304 | tf_op jit(solution)/shard_map/reduce_scatter | solution.py:257
  1527.6 55.5 %reduce-scatter.33.cloned.1.call-done = f32[1024,128]{1,0:T(8,128)} async-done(((f32[1024,1024]{1,0:T(8,128)}), f32[1024,128]{1,0:T(8,128)}) %reduce-scatter.33.cloned.1.call-update) | async-done | bytes 524304 | tf_op jit(solution)/shard_map/reduce_scatter | solution.py:258
  1583.1 39.6 %reduce-scatter.29.cloned.1.call-done = f32[256,128]{1,0:T(8,128)} async-done(((f32[256,1024]{1,0:T(8,128)}), f32[256,128]{1,0:T(8,128)}) %reduce-scatter.29.cloned.1.call-update) | async-done | bytes 131088 | tf_op jit(solution)/shard_map/reduce_scatter | solution.py:256
  (130 shorter events, 13.5 us)
Async XLA Ops:
  7.2 137.8 %copy-start.2 = (bf16[392,1024]{1,0:T(8,128)(2,1)S(1)}, bf16[392,1024]{1,0:T(8,128)(2,1)}, u32[]{:S(2)}) copy-start(bf16[392,1024]{1,0:T(8,128)(2,1)} %param.11) | copy-start | bytes 2408452
  7.2 158.4 %all-gather.12.cloned.1.call-start = ((), (), s32[]{:S(2)}) async-start(), calls=%async_computation.12 | async-start | bytes 1769472 | tf_op jit(solution)/shard_map/all_gather | solution.py:46
  7.9 201.0 %all-gather.10.cloned.1.call-start = ((), (), s32[]{:S(2)}) async-start(), calls=%async_computation.11 | async-start | bytes 4014080 | tf_op jit(solution)/shard_map/all_gather | solution.py:61
  141.3 4.9 copy-start.25
  141.4 13.2 copy-start.20
  142.8 71.2 %copy-start.21 = (f32[392]{0:T(512)}, f32[392]{0:T(512)S(1)}, u32[]{:S(2)}) copy-start(f32[392]{0:T(512)S(1)} %broadcast_multiply_fusion.5) | copy-start | bytes 4708
  144.3 69.7 %copy-start.23 = (f32[392]{0:T(512)}, f32[392]{0:T(512)S(1)}, u32[]{:S(2)}) copy-start(f32[392]{0:T(512)S(1)} %add_rsqrt_fusion.1) | copy-start | bytes 4708
  144.3 0.6 copy-start.18
  146.2 241.7 %reduce-scatter.19.cloned.1.call-start = ((), (), s32[]{:S(2)}) async-start(), calls=%async_computation.13 | async-start | bytes 8028160 | tf_op jit(solution)/shard_map/reduce_scatter | solution.py:65
  154.6 66.7 %copy-start.16 = (f32[4,64]{1,0:T(4,128)}, f32[4,64]{1,0:T(4,128)S(1)}, u32[]{:S(2)}) copy-start(f32[4,64]{1,0:T(4,128)S(1)} %copy.73) | copy-start | bytes 3076
  217.9 3.4 copy-start
  221.3 16.2 copy-start.3
  237.4 16.4 %copy-start.5 = (f32[1,1568,256]{1,2,0:T(8,128)S(1)}, f32[1,1568,256]{1,2,0:T(8,128)}, u32[]{:S(2)}) copy-start(f32[1,1568,256]{1,2,0:T(8,128)} %copy.69) | copy-start | bytes 4816900
  253.8 17.4 %copy-start.10 = (bf16[256,1024]{1,0:T(8,128)(2,1)S(1)}, bf16[256,1024]{1,0:T(8,128)(2,1)}, u32[]{:S(2)}) copy-start(bf16[256,1024]{1,0:T(8,128)(2,1)} %all_gather.51) | copy-start | bytes 1572868
  276.2 141.9 %all-gather.16.cloned.1.call-start = ((), (), s32[]{:S(2)}) async-start(), calls=%async_computation.15 | async-start | bytes 2359296 | tf_op jit(solution)/shard_map/all_gather | solution.py:48
  276.8 207.9 %all-gather.14.cloned.1.call-start = ((), (), s32[]{:S(2)}) async-start(), calls=%async_computation.14 | async-start | bytes 4014080 | tf_op jit(solution)/shard_map/all_gather | solution.py:61
  389.9 2.5 copy-start.9
  391.2 2.5 copy-start.27
  391.2 122.1 %all-gather.18.cloned.1.call-start = ((), (), s32[]{:S(2)}) async-start(), calls=%async_computation.16 | async-start | bytes 2359296 | tf_op jit(solution)/shard_map/all_gather | solution.py:49
  391.8 188.3 %all-gather.20.cloned.1.call-start = ((), (), s32[]{:S(2)}) async-start(), calls=%async_computation.18 | async-start | bytes 4014080 | tf_op jit(solution)/shard_map/all_gather | solution.py:74
  393.6 315.1 %reduce-scatter.23.cloned.1.call-start = ((), (), s32[]{:S(2)}) async-start(), calls=%async_computation.19 | async-start | bytes 8028160 | tf_op jit(solution)/shard_map/reduce_scatter | solution.py:78
  580.0 11.2 copy-start.28
  589.6 1.7 copy-start.30
  597.0 227.4 %reduce-scatter.21.cloned.1.call-start = ((), (), s32[]{:S(2)}) async-start(), calls=%async_computation.17 | async-start | bytes 8028160 | tf_op jit(solution)/shard_map/reduce_scatter | solution.py:65
  605.8 288.3 %all-gather.22.cloned.1.call-start = ((), (), s32[]{:S(2)}) async-start(), calls=%async_computation.20 | async-start | bytes 4014080 | tf_op jit(solution)/shard_map/all_gather | solution.py:74
  828.8 290.1 %reduce-scatter.25.cloned.1.call-start = ((), (), s32[]{:S(2)}) async-start(), calls=%async_computation.21 | async-start | bytes 8028160 | tf_op jit(solution)/shard_map/reduce_scatter | solution.py:78
  898.0 16.9 %copy-start.6 = (f32[1,1568,256]{1,2,0:T(8,128)S(1)}, f32[1,1568,256]{1,2,0:T(8,128)}, u32[]{:S(2)}) copy-start(f32[1,1568,256]{1,2,0:T(8,128)} %copy.69) | copy-start | bytes 4816900
  941.2 33.6 %copy-start.4 = (f32[1,1568,256]{1,2,0:T(8,128)S(1)}, f32[1,1568,256]{1,2,0:T(8,128)}, u32[]{:S(2)}) copy-start(f32[1,1568,256]{1,2,0:T(8,128)} %copy-done.3) | copy-start | bytes 4816900
  941.2 33.6 %copy-start.17 = (f32[4,64]{1,0:T(4,128)S(1)}, f32[4,64]{1,0:T(4,128)}, u32[]{:S(2)}) copy-start(f32[4,64]{1,0:T(4,128)} %copy-done.16) | copy-start | bytes 3076
  974.8 11.4 copy-start.1
  986.2 10.4 copy-start.8
  997.9 2.0 copy-start.12
  999.9 7.3 copy-start.14
  1007.2 1.2 copy-start.13
  1007.3 1.6 copy-start.15
  1007.3 149.3 %reduce-scatter.39.cloned.1.call-start = ((), (), s32[]{:S(2)}) async-start(), calls=%async_computation.28 | async-start | bytes 589824
  1008.4 198.2 %reduce-scatter.27.cloned.1.call-start = ((), (), s32[]{:S(2)}) async-start(), calls=%async_computation.22 | async-start | bytes 3538944 | tf_op jit(solution)/shard_map/reduce_scatter | solution.py:255
  1015.5 103.4 %copy-start.19 = (f32[1,1024]{1,0:T(1,128)S(1)}, f32[1,1024]{1,0:T(1,128)}, u32[]{:S(2)}) copy-start(f32[1,1024]{1,0:T(1,128)} %copy-done.18) | copy-start | bytes 12292
  1015.5 103.4 %copy-start.22 = (f32[392]{0:T(512)S(1)}, f32[392]{0:T(512)}, u32[]{:S(2)}) copy-start(f32[392]{0:T(512)} %copy-done.21) | copy-start | bytes 4708
  1015.5 103.4 %copy-start.24 = (f32[392]{0:T(512)S(1)}, f32[392]{0:T(512)}, u32[]{:S(2)}) copy-start(f32[392]{0:T(512)} %copy-done.23) | copy-start | bytes 4708
  1015.6 327.6 %reduce-scatter.35.cloned.1.call-start = ((), (), s32[]{:S(2)}) async-start(), calls=%async_computation.26 | async-start | bytes 540672
  1122.2 353.9 %reduce-scatter.37.cloned.1.call-start = ((), (), s32[]{:S(2)}) async-start(), calls=%async_computation.27 | async-start | bytes 540672
  1123.4 404.2 %reduce-scatter.31.cloned.1.call-start = ((), (), s32[]{:S(2)}) async-start(), calls=%async_computation.24 | async-start | bytes 4718592 | tf_op jit(solution)/shard_map/reduce_scatter | solution.py:257
  1132.3 450.8 %reduce-scatter.33.cloned.1.call-start = ((), (), s32[]{:S(2)}) async-start(), calls=%async_computation.25 | async-start | bytes 4718592 | tf_op jit(solution)/shard_map/reduce_scatter | solution.py:258
  1141.5 1.2 copy-start.11
  1141.5 5.2 copy-start.29
  1141.5 481.2 %reduce-scatter.29.cloned.1.call-start = ((), (), s32[]{:S(2)}) async-start(), calls=%async_computation.23 | async-start | bytes 1179648 | tf_op jit(solution)/shard_map/reduce_scatter | solution.py:256
  1146.7 61.8 %copy-start.7 = (f32[392,1024]{1,0:T(8,128)S(1)}, f32[392,1024]{1,0:T(8,128)}, u32[]{:S(2)}) copy-start(f32[392,1024]{1,0:T(8,128)} %reduce-scatter.25.cloned.1.call-done) | copy-start | bytes 4816900
  1476.9 145.8 %copy-start.26 = (f32[4,32]{1,0:T(4,128)}, f32[4,32]{1,0:T(4,128)S(1)}, u32[]{:S(2)}) copy-start(f32[4,32]{1,0:T(4,128)S(1)} %copy.91) | copy-start | bytes 1540
Sparse Core Ops, SparseCore 0:
  9.9 28.3 all-gather.11
  146.3 62.5 all-gather.9
  276.3 111.5 reduce-scatter.18
  389.6 28.3 all-gather.15
  420.1 64.5 all-gather.13
  486.4 26.8 all-gather.17
  515.4 64.5 all-gather.19
  597.1 111.5 reduce-scatter.22
  711.0 113.3 reduce-scatter.20
  829.0 65.0 all-gather.21
  1007.4 111.5 reduce-scatter.24
  1121.9 34.6 reduce-scatter.38
  1160.3 46.2 reduce-scatter.26
  1208.7 134.4 reduce-scatter.34
  1345.4 130.7 reduce-scatter.36
  1479.9 47.6 reduce-scatter.30
  1531.7 51.3 reduce-scatter.32
  1586.7 35.9 reduce-scatter.28
where the time goes:
time: 1640 us; the launch traced here: 1630 us
  waiting for transfers between devices  1160 us (71%)
  matrix products  180 us (11%)
  blocking collectives  173 us (11%)
  other arithmetic  70.3 us (4%)
  local copies, waits for them, and re-layouts  26 us (2%)
  between operations  16.5 us (1%)
    unnamed x21, waiting for transfers between devices  274 us
    reduce_scatter x2, waiting for transfers between devices, reduce_rows(): lax.psum_scatter(term_fn(jnp.int32(0), lax.axis_size('tensor') * row_coun...  224 us
    reduce_scatter x2, waiting for transfers between devices, reduce_grads(): lax.psum_scatter(term_fn(jnp.int32(0), lax.axis_size('tensor') * row_coun...  206 us
    all_gather x2, waiting for transfers between devices, spread_grads(): return lax.all_gather(local_rows, 'tensor', axis=0, tiled=True)  132 us
    all_gather x2, waiting for transfers between devices, spread_rows(): return lax.all_gather(local_rows, 'tensor', axis=0, tiled=True)  110 us
    all_gather x1, blocking collectives, fetch(): lax.all_gather(gain_rows, ('dp', 'tensor'), axis=1, tiled=True)  69.5 us
    all_gather x1, blocking collectives, fetch(): lax.all_gather(bias_rows, ('dp', 'tensor'), axis=1, tiled=True)  63.8 us
    reduce_scatter x1, waiting for transfers between devices, backward(): lax.psum_scatter(grad_fc2, 'dp', scatter_dimension=1, tiled=True)  55.5 us
  transfers between devices with their start and end apart: 18, of which 17 were waited for; matrix products, arithmetic and copies ran while one was open for 4% of the time, Pallas kernels for 0%

commit v1 on v0

--- a/solution.py
+++ b/solution.py
@@ -3,6 +3,8 @@
 import jax
 import jax.numpy as jnp
 from jax import lax
+from jax.experimental import pallas as pl
+from jax.experimental.pallas import tpu as pltpu
 from jax.sharding import PartitionSpec as P
 
 HD = 64
@@ -305,7 +307,391 @@
     )
 
 
+VALID_CLIPS = 2
+AXES = ("dp", "tensor")
+Z_LOW, Z_HIGH, CORE, X, Y = 1, 2, 4, 8, 16
+CHIP_MASKS = (0, X, Y, X | Y)
+BF16, F32 = jnp.bfloat16, jnp.float32
+
+
+def swap(value, mask):
+    return lax.ppermute(value, AXES, [(i, i ^ mask) for i in range(32)])
+
+
+def dot(left, right, dims):
+    return lax.dot_general(left, right, (dims, ((), ())), preferred_element_type=F32)
+
+
+NN = ((1,), (0,))
+NT = ((1,), (1,))
+TN = ((0,), (0,))
+
+
+def call(body, outs, scalar, *args):
+    return pl.pallas_call(
+        body,
+        out_shape=[jax.ShapeDtypeStruct(s, t) for s, t in outs],
+        in_specs=[pl.BlockSpec(memory_space=pltpu.SMEM)]
+        + [pl.BlockSpec(memory_space=pltpu.VMEM)] * len(args),
+        out_specs=[pl.BlockSpec(memory_space=pltpu.VMEM)] * len(outs),
+    )(scalar, *args)
+
+
+def qkv_kernel(chip, rows, w0, w1, w2, w3, bias, out):
+    weights = (w0, w1, w2, w3)
+    for j in range(3):
+        cols = slice(256 * j, 256 * j + 256)
+        total = bias[j : j + 1, :]
+        for m in range(4):
+            total = total + dot(rows[:, 256 * m : 256 * m + 256], weights[m][:, cols], NN)
+        total = total.astype(BF16)
+        for h in range(4):
+            out[h ^ chip[0], :, 64 * j : 64 * j + 64] = total[:, 64 * h : 64 * h + 64]
+
+
+def attention_kernel(chip, qkv, out, lse):
+    keys = qkv[:, 64:128]
+    values = qkv[:, 128:192]
+    step = 224
+
+    def body(i, carry):
+        start = pl.multiple_of(i * step, 32)
+        queries = qkv[pl.ds(start, step), 0:64] * 0.125
+        scores = dot(queries, keys, NT)
+        top = jnp.max(scores, axis=1, keepdims=True)
+        weights = jnp.exp(scores - top)
+        total = jnp.sum(weights, axis=1, keepdims=True)
+        mixed = dot(weights.astype(BF16), values, NN)
+        out[pl.ds(start, step), :] = (mixed / total).astype(BF16)
+        spread = jnp.broadcast_to(top + jnp.log(total), (step, 128))
+        lse[i, :, :] = jnp.transpose(spread)[0:8, :]
+        return carry
+
+    lax.fori_loop(0, qkv.shape[0] // step, body, 0)
+
+
+def attention_back_kernel(chip, qkv, grads, lse, out, grad_k, grad_v):
+    keys = qkv[:, 64:128]
+    values = qkv[:, 128:192]
+    keys_t = jnp.transpose(keys)
+    step = 224
+    grad_k[...] = jnp.zeros_like(grad_k)
+    grad_v[...] = jnp.zeros_like(grad_v)
+
+    def body(i, carry):
+        start = pl.multiple_of(i * step, 32)
+        queries = qkv[pl.ds(start, step), 0:64] * 0.125
+        grad = grads[pl.ds(start, step), :]
+        probs = jnp.exp(dot(keys, queries, NT) - lse[i, 0:1, :])
+        grad_probs = dot(values, grad, NT)
+        row_dot = jnp.sum(probs * grad_probs, axis=0, keepdims=True)
+        grad_scores = (probs * (grad_probs - row_dot)).astype(BF16)
+        grad_v[...] += dot(probs.astype(BF16), grad, NN)
+        grad_k[...] += dot(grad_scores, queries, NN)
+        grad_q = jnp.transpose(dot(keys_t, grad_scores, NN)) * 0.125
+        out[pl.ds(start, step), 0:64] = grad_q.astype(BF16)
+        return carry
+
+    lax.fori_loop(0, qkv.shape[0] // step, body, 0)
+    out[:, 64:128] = grad_k[...].astype(BF16)
+    out[:, 128:192] = grad_v[...].astype(BF16)
+
+
+def proj_kernel(chip, mixed, w0, w1, w2, w3, joined, keep, send):
+    weights = (w0, w1, w2, w3)
+    half = keep.shape[0]
+    for h in range(4):
+        joined[:, 64 * h : 64 * h + 64] = mixed[h ^ chip[0], :, :]
+    rows = joined[...]
+    for m in range(4):
+        cols = slice(256 * m, 256 * m + 256)
+        total = dot(rows, weights[m][...], NT)
+        keep[:, cols] = total[:half]
+        send[:, cols] = total[half:].astype(BF16)
+
+
+def grad_att_kernel(chip, grads, w0, w1, w2, w3, out):
+    weights = (w0, w1, w2, w3)
+    total = dot(grads[:, 0:256], w0[...], NN)
+    for m in range(1, 4):
+        total = total + dot(grads[:, 256 * m : 256 * m + 256], weights[m][...], NN)
+    total = total.astype(BF16)
+    for h in range(4):
+        out[h ^ chip[0], :, :] = total[:, 64 * h : 64 * h + 64]
+
+
+def qkv_back_kernel(chip, grads, w0, w1, w2, w3, joined, keep, send, sums):
+    weights = (w0, w1, w2, w3)
+    half = keep.shape[0]
+    for h in range(4):
+        for j in range(3):
+            joined[:, 256 * j + 64 * h : 256 * j + 64 * h + 64] = grads[
+                h ^ chip[0], :, 64 * j : 64 * j + 64
+            ]
+    rows = joined[...]
+    for m in range(4):
+        cols = slice(256 * m, 256 * m + 256)
+        total = dot(rows, weights[m][...], NT)
+        keep[:, cols] = total[:half]
+        send[:, cols] = total[half:].astype(BF16)
+    sums[...] = jnp.sum(rows.astype(F32), axis=0, keepdims=True)
+
+
+def back_rows(total, upstream, scaled, inverse, gain):
+    return upstream + normalize_back(total, scaled, inverse, gain)
+
+
+def sum_grad(parts, x_first):
+    first, second, near, far = (X, Y, 1, 2) if x_first else (Y, X, 2, 1)
+    got = swap(jnp.stack([parts[near], parts[3]]).astype(BF16), first).astype(F32)
+    whole = parts[0] + got[0]
+    other = parts[far] + got[1]
+    return whole + swap(other.astype(BF16), second).astype(F32)
+
+
+def settle_grad(part, core):
+    pairs = [(i, i ^ Z_HIGH) for i in range(32) if i & CORE]
+    moved = lax.ppermute(part.astype(BF16), AXES, pairs).astype(F32)
+    part = jnp.where(core == 0, part, moved)
+    low, high = part[:128], part[128:]
+    send = jnp.where(core == 0, high, low)
+    keep = jnp.where(core == 0, low, high)
+    return keep + swap(send.astype(BF16), CORE).astype(F32)
+
+
+def on_device_spread(
+    clip_rows,
+    out_grad,
+    clip_valid,
+    gain_rows,
+    bias_rows,
+    qkv_weight,
+    qv_bias,
+    proj_weight,
+    fc1_weight,
+    fc1_bias,
+    fc2_weight,
+):
+    d, t = lax.axis_index("dp"), lax.axis_index("tensor")
+    z_high = t >> 1
+    core = d & 1
+    chip = d >> 1
+    x_bit, y_bit = chip & 1, chip >> 1
+    chip_ref = chip.reshape(1).astype(jnp.int32)
+    quarter = jnp.where(core == 0, t, t ^ 2)
+    share = clip_rows.shape[0] // 8
+
+    def turn(value, axis):
+        size = value.shape
+        value = value.reshape(*size[:axis], 2, 2, size[axis] // 4, *size[axis + 1 :])
+        value = jnp.where(x_bit == 1, jnp.flip(value, axis + 1), value)
+        value = jnp.where(y_bit == 1, jnp.flip(value, axis), value)
+        return value.reshape(size)
+
+    def home(shard):
+        far = swap(shard, Z_HIGH)
+        keep = jnp.where(core == 0, shard, far)
+        got = swap(jnp.where(core == 0, far, shard), CORE)
+        return jnp.concatenate(
+            [jnp.where(core == 0, keep, got), jnp.where(core == 0, got, keep)], axis=0
+        )
+
+    def around(block, by_y):
+        w1, w2 = swap(block, X), swap(block, Y)
+        w3 = swap(w1, Y) if by_y else swap(w2, X)
+        return block, w1, w2, w3
+
+    flag = jnp.broadcast_to(clip_valid.astype(BF16).reshape(1, 1, 1), (8, 1, clip_rows.shape[1]))
+    sent = jnp.concatenate([clip_rows.reshape(8, share, -1), flag], axis=1)
+    got = lax.all_to_all(sent, "dp", 0, 0)
+    valid = got[:, share, 0] > 0.5
+    numbers = jnp.arange(8)
+    first = jnp.min(jnp.where(valid, numbers, 8))
+    second = jnp.max(jnp.where(valid, numbers, -1))
+    mine = jnp.where(z_high == 0, first, second)
+    other = jnp.where(z_high == 0, second, first)
+
+    def settle(blocks):
+        here = lax.dynamic_index_in_dim(blocks, mine, 0, keepdims=False)[:share]
+        there = lax.dynamic_index_in_dim(blocks, other, 0, keepdims=False)[:share]
+        pair = jnp.concatenate([here, swap(there, Z_HIGH)])
+        pair = turn(pair, 1)
+        return jnp.concatenate([pair, swap(pair, Z_LOW)])
+
+    rows = settle(got)
+    small = jnp.concatenate(
+        [v.reshape(-1) for v in (gain_rows, bias_rows, qv_bias, fc1_bias)]
+    )
+    small = lax.all_gather(small, AXES, axis=0)
+    vectors = turn(small[:, :192].astype(F32), 0).reshape(32, 6, 32)
+    vectors = jnp.transpose(vectors, (1, 0, 2)).reshape(6, -1)
+    gains, biases = vectors[:2], vectors[2:]
+    mine_small = lax.dynamic_index_in_dim(small.reshape(8, 4, -1), quarter, 1, keepdims=False)
+    mine_small = mine_small.astype(F32)
+    qv = jnp.transpose(mine_small[:, 192:256].reshape(8, 2, 4, 8), (1, 2, 0, 3)).reshape(2, 256)
+    b_fc1 = mine_small[:, 256:].reshape(-1)
+    qkv_bias = jnp.stack([qv[0], jnp.zeros_like(qv[0]), qv[1]])
+
+    w_qkv = around(home(jnp.transpose(qkv_weight, (1, 0, 2)).reshape(128, -1)), True)
+    w_proj = around(home(jnp.transpose(proj_weight)), False)
+    w_fc1 = around(home(fc1_weight), False)
+    w_fc2 = around(home(jnp.transpose(fc2_weight)), True)
+
+    own = rows.shape[0] // 2
+    inputs = rows.astype(F32)
+    normed_one, scaled_one, inverse_one = normalize(inputs, gains[0:1], biases[0:1])
+    normed_one = normed_one.astype(BF16)
+    whole_one = jnp.concatenate([normed_one, swap(normed_one, CORE)])
+    tokens = whole_one.shape[0]
+    (qkv,) = call(qkv_kernel, [((4, tokens, 192), BF16)], chip_ref, whole_one, *w_qkv, qkv_bias)
+
+    def trade(blocks):
+        return jnp.stack([blocks[0]] + [swap(blocks[m], CHIP_MASKS[m]) for m in range(1, 4)])
+
+    qkv = trade(qkv).reshape(4 * tokens, 192)
+    steps = qkv.shape[0] // 224
+    mixed, lse = call(
+        attention_kernel,
+        [((4 * tokens, 64), BF16), ((steps, 8, 224), F32)],
+        chip_ref,
+        qkv,
+    )
+    mixed = trade(mixed.reshape(4, tokens, 64))
+    half = tokens // 2
+    attended, keep, send = call(
+        proj_kernel,
+        [((tokens, 256), BF16), ((half, 1024), F32), ((half, 1024), BF16)],
+        chip_ref,
+        mixed,
+        *w_proj,
+    )
+
+    def all_z(keep, send):
+        part = keep + swap(send, CORE).astype(F32)
+        turned = jnp.concatenate([part[own:], part[:own]]).astype(BF16)
+        return part + swap(turned, Z_LOW).astype(F32)
+
+    def one_z(keep, send):
+        part = keep + swap(send, CORE).astype(F32)
+        return part[:own] + swap(part[own:].astype(BF16), Z_LOW).astype(F32)
+
+    residual_one = inputs + (all_z(keep, send) + biases[2:3])
+    normed_two, scaled_two, inverse_two = normalize(residual_one, gains[1:2], biases[1:2])
+    normed_two = normed_two.astype(BF16)
+    whole_two = jnp.concatenate([normed_two, swap(normed_two, CORE)])
+
+    grad_rows = settle(lax.all_to_all(out_grad.reshape(8, share, -1), "dp", 0, 0))
+    upstream = grad_rows.astype(F32)
+    whole_mlp = jnp.concatenate([grad_rows, swap(grad_rows, CORE)])
+
+    m_fc1 = jnp.concatenate(w_fc1)
+    m_fc2 = jnp.concatenate(w_fc2)
+    pre_act = dot(whole_two, m_fc1, NN) + b_fc1
+    hidden = gelu_value(pre_act).astype(BF16)
+    grad_hidden = dot(whole_mlp, m_fc2, NN)
+    grad_pre = (grad_hidden * gelu_slope(pre_act)).astype(BF16)
+    grad_fc1_bias = jnp.sum(grad_pre.astype(F32), axis=0)
+    back = dot(grad_pre, m_fc1, NT)
+    grad_normed_two = all_z(back[:half], back[half:].astype(BF16))
+    grad_residual = back_rows(grad_normed_two, upstream, scaled_two, inverse_two, gains[1:2])
+    grad_branch = grad_residual.astype(BF16)
+    whole_branch = jnp.concatenate([grad_branch, swap(grad_branch, CORE)])
+
+    (grad_att,) = call(
+        grad_att_kernel, [((4, tokens, 64), BF16)], chip_ref, whole_branch, *w_proj
+    )
+    grad_att = trade(grad_att).reshape(4 * tokens, 64)
+    (grad_qkv,) = pl.pallas_call(
+        attention_back_kernel,
+        out_shape=[jax.ShapeDtypeStruct(qkv.shape, BF16)],
+        in_specs=[pl.BlockSpec(memory_space=pltpu.SMEM)]
+        + [pl.BlockSpec(memory_space=pltpu.VMEM)] * 3,
+        out_specs=[pl.BlockSpec(memory_space=pltpu.VMEM)],
+        scratch_shapes=[pltpu.VMEM((4 * tokens, 64), F32)] * 2,
+    )(chip_ref, qkv, grad_att, lse)
+    grad_qkv = trade(grad_qkv.reshape(4, tokens, 192))
+    joined, keep, send, qkv_sums = call(
+        qkv_back_kernel,
+        [((tokens, 768), BF16), ((half, 1024), F32), ((half, 1024), BF16), ((1, 768), F32)],
+        chip_ref,
+        grad_qkv,
+        *w_qkv,
+    )
+    grad_normed_one = one_z(keep, send)
+    grad_input = back_rows(
+        grad_normed_one, grad_residual[:own], scaled_one[:own], inverse_one[:own], gains[0:1]
+    )
+
+    def give_back(value):
+        value = turn(value.astype(BF16), 1)
+        away = swap(value[share:], Z_HIGH)
+        goal = numbers.reshape(8, 1, 1)
+        blank = jnp.zeros((), BF16)
+        sent = jnp.where(
+            goal == mine, value[:share], jnp.where(goal == other, away, blank)
+        )
+        return lax.all_to_all(sent, "dp", 0, 0).reshape(clip_rows.shape)
+
+    grad_input = give_back(grad_input).astype(F32)
+    out = dot(hidden, m_fc2, NT)
+    out = one_z(out[:half], out[half:].astype(BF16))
+    layer_out = give_back(residual_one[:own] + (out + biases[3:4]))
+
+    def blocks(value):
+        return value.reshape(4, 256, -1)
+
+    grad_fc2 = settle_grad(sum_grad(blocks(dot(whole_mlp, hidden, TN)), True), core)
+    grad_fc1 = settle_grad(sum_grad(blocks(dot(whole_two, grad_pre, TN)), False), core)
+    grad_proj = settle_grad(sum_grad(blocks(dot(whole_branch, attended, TN)), True), core)
+    grad_w = settle_grad(sum_grad(blocks(dot(whole_one, joined, TN)), False), core)
+
+    sums = jnp.stack(
+        [
+            jnp.sum(grad_normed_one * scaled_one[:own], axis=0),
+            jnp.sum(grad_normed_two[:own] * scaled_two[:own], axis=0),
+            jnp.sum(grad_normed_one, axis=0),
+            jnp.sum(grad_normed_two[:own], axis=0),
+            jnp.sum(grad_branch[:own].astype(F32), axis=0),
+            jnp.sum(upstream[:own], axis=0),
+        ]
+    )
+    sums = jnp.transpose(sums.reshape(6, 32, 32), (1, 0, 2)).reshape(32, 192)
+    sums = turn(sums, 0)
+    here = jnp.arange(4).reshape(1, 4, 1) == quarter
+    by_part = jnp.concatenate(
+        [
+            jnp.transpose(
+                jnp.stack([qkv_sums[0, :256], qkv_sums[0, 512:]]).reshape(2, 4, 8, 8), (2, 0, 1, 3)
+            ).reshape(8, 64),
+            grad_fc1_bias.reshape(8, 128),
+        ],
+        axis=1,
+    )
+    by_part = jnp.where(here, by_part[:, None, :], 0.0).reshape(32, 192)
+    vector = jnp.concatenate([sums, by_part], axis=1)
+    for mask, bit in ((Y, y_bit), (X, x_bit), (CORE, core), (Z_HIGH, z_high), (Z_LOW, t & 1)):
+        low, high = vector[: vector.shape[0] // 2], vector[vector.shape[0] // 2 :]
+        send = jnp.where(bit == 1, low, high)
+        vector = jnp.where(bit == 1, high, low) + swap(send, mask)
+    vector = vector[0]
+    grad_biases = vector[64:192].reshape(4, 32)
+    return (
+        layer_out,
+        grad_input,
+        vector[:64].reshape(2, 32),
+        grad_biases,
+        jnp.transpose(grad_w.reshape(128, 3, 256), (1, 0, 2)),
+        vector[192:256].reshape(2, 4, 8),
+        jnp.transpose(grad_proj),
+        grad_fc1,
+        vector[256:].reshape(1, 128),
+        jnp.transpose(grad_fc2),
+        grad_biases[3],
+    )
+
+
 def solution(mesh):
+    spread = (mesh.shape["dp"], mesh.shape["tensor"]) == (8, 4)
     in_specs = (
         P(("dp", "tensor"), None),
         P(("dp", "tensor"), None),
@@ -333,5 +719,5 @@
         P(("dp", "tensor")),
     )
     return jax.shard_map(
-        on_device, mesh=mesh, in_specs=in_specs, out_specs=out_specs, check_vma=False
-    )
+        on_device_spread if spread else on_device, mesh=mesh, in_specs=in_specs, out_specs=out_specs, check_vma=False
+    )

time: 1640 us -> 467 us (0.28)
  waiting for transfers between devices: 1160 us -> 109 us
  matrix products: 180 us -> 22.3 us
  blocking collectives: 173 us -> 79.3 us
  starting transfers between devices: 1.33 us -> 83.1 us
  Pallas kernels: 0 us -> 35.1 us
  local copies, waits for them, and re-layouts: 26 us -> 57.7 us
    reduce_scatter x8 -> x0, waiting for transfers between devices: 611 us -> none  [the longest x2 224 us: reduce_rows(): lax.psum_scatter(term_fn(jnp.int32(0), lax.axis_size('tensor') * row_coun...]
    all_gather x7 -> x0, waiting for transfers between devices: 278 us -> none  [the longest x2 132 us: spread_grads(): return lax.all_gather(local_rows, 'tensor', axis=0, tiled=True)]
    unnamed x21 -> x0, waiting for transfers between devices: 274 us -> none
    dot_general x18 -> x8, matrix products: 180 us -> 22.3 us  [dot(): lax.dot_general(left, right, (dims, ((), ())), preferred_element_type=F32)]
    ppermute x0 -> x71, waiting for transfers between devices: none -> 95.9 us  [the longest x67 95.9 us: swap(): return lax.ppermute(value, AXES, [(i, i ^ mask) for i in range(32)])]
    all_gather x5 -> x1, blocking collectives: 161 us -> 79.3 us  [on_device_spread(): small = lax.all_gather(small, AXES, axis=0)]
    ppermute x0 -> x71, starting transfers between devices: none -> 65.9 us  [the longest x67 60.6 us: swap(): return lax.ppermute(value, AXES, [(i, i ^ mask) for i in range(32)])]
    pallas_call x0 -> x6, Pallas kernels: none -> 35.1 us  [the longest x5 21.4 us: call(): pl.pallas_call(body, out_shape=[jax.ShapeDtypeStruct(s, t) for s, t in ou...]
  transfers between devices with their start and end apart: 18 -> 75, of which waited for: 17 -> 30; matrix products, arithmetic and copies ran while one was open for 4% -> 30% of each run, Pallas kernels for 0% -> 8%
where the time goes in v1:
time: 467 us; the launch traced here: 461 us
  waiting for transfers between devices  109 us (23%)
  starting transfers between devices  83.1 us (18%)
  blocking collectives  79.3 us (17%)
  other arithmetic  69.4 us (15%)
  local copies, waits for them, and re-layouts  57.7 us (12%)
  Pallas kernels  35.1 us (8%)
  matrix products  22.3 us (5%)
  between operations  5.77 us (1%)
    ppermute x67, waiting for transfers between devices, swap(): return lax.ppermute(value, AXES, [(i, i ^ mask) for i in range(32)])  95.9 us
    all_gather x1, blocking collectives, on_device_spread(): small = lax.all_gather(small, AXES, axis=0)  79.3 us
    ppermute x67, starting transfers between devices, swap(): return lax.ppermute(value, AXES, [(i, i ^ mask) for i in range(32)])  60.6 us
    dot_general x8, matrix products, dot(): lax.dot_general(left, right, (dims, ((), ())), preferred_element_type=F32)  22.3 us
    pallas_call x5, Pallas kernels, call(): pl.pallas_call(body, out_shape=[jax.ShapeDtypeStruct(s, t) for s, t in ou...  21.4 us
    unnamed x125, local copies, waits for them, and re-layouts  16.9 us
    pallas_call x1, Pallas kernels, on_device_spread(): pl.pallas_call(attention_back_kernel, out_shape=[jax.ShapeDtypeStruct(qkv...  13.6 us
    all_to_all x2, waiting for transfers between devices, give_back(): return lax.all_to_all(sent, 'dp', 0, 0).reshape(clip_rows.shape)  12.8 us
  transfers between devices with their start and end apart: 75, of which 30 were waited for; matrix products, arithmetic and copies ran while one was open for 30% of the time, Pallas kernels for 8%

profile of v1, /device:TPU:0, one launch (start us, length us, event | category | flops | bytes accessed | tf_op | source)
XLA Modules:
  0.0 461.3 jit_solution(22209861872160379)
XLA Ops:
  1.6 4.1 collective-permute-start.14
  8.1 3.0 collective-permute-start.27
  14.3 4.4 all-to-all-start
  19.0 79.3 %all-gather.1 = bf16[32,1,384]{2,1,0:T(2,128)(2,1)S(1)} all-gather(bf16[1,1,384]{2,1,0:T(2,128)(2,1)S(1)} %reshape.335), channel_id=2, replica_groups=mesh['dp'=8,'tensor'=4] {'dp','tensor'}, dimensions={0}, use_global_device_ids=true | all-gather | bytes 25344 | tf_op jit(solution)/shard_map/all_gather | solution.py:525
  113.0 4.4 all-to-all-start.2
  122.8 7.3 %collective-permute-done = bf16[49,1024]{1,0:T(8,128)(2,1)S(1)} collective-permute-done((bf16[49,1024]{1,0:T(8,128)(2,1)S(1)}, bf16[49,1024]{1,0:T(8,128)(2,1)S(1)}, u32[]{:S(2)}, u32[]{:S(2)}) %collective-permute-start) | collective-permute-done | bytes 100384 | tf_op jit(solution)/shard_map/ppermute | solution.py:318
  132.9 6.4 %collective-permute-done.1 = bf16[98,1024]{1,0:T(8,128)(2,1)S(1)} collective-permute-done((bf16[98,1024]{1,0:T(8,128)(2,1)S(1)}, bf16[98,1024]{1,0:T(8,128)(2,1)S(1)}, u32[]{:S(2)}, u32[]{:S(2)}) %collective-permute-start.1) | collective-permute-done | bytes 200736 | tf_op jit(solution)/shard_map/ppermute | solution.py:318
  146.4 2.0 pad_maximum_fusion.2.rows
  148.4 5.1 %collective-permute-done.7.w3 = bf16[256,768]{1,0:T(8,128)(2,1)S(1)} collective-permute-done((bf16[256,768]{1,0:T(8,128)(2,1)S(1)}, bf16[256,768]{1,0:T(8,128)(2,1)S(1)}, u32[]{:S(2)}, u32[]{:S(2)}) %collective-permute-start.7) | collective-permute-done | bytes 393248 | tf_op jit(solution)/shard_map/ppermute | solution.py:318
  154.3 3.6 shard_map.194
  159.1 2.5 collective-permute-start.10
  165.1 4.8 %collective-permute-done.35 = bf16[49,1024]{1,0:T(8,128)(2,1)S(1)} collective-permute-done((bf16[49,1024]{1,0:T(8,128)(2,1)S(1)}, bf16[49,1024]{1,0:T(8,128)(2,1)S(1)}, u32[]{:S(2)}, u32[]{:S(2)}) %collective-permute-start.35) | collective-permute-done | bytes 100384 | tf_op jit(solution)/shard_map/ppermute | solution.py:318
  173.6 9.1 %shard_map.195 = (bf16[1568,64]{1,0:T(8,128)(2,1)}, f32[7,8,224]{2,1,0:T(8,128)}) custom-call(s32[1]{0:T(128)} %bitcast.2.chip, bf16[1568,192]{1,0:T(8,128)(2,1)} %bitcast.176), custom_call_target="tpu_custom_call" | custom-call | tf_op jit(solution)/shard_map/pallas_call | solution.py:331
  195.9 2.7 shard_map.196
  203.0 4.8 %collective-permute-done.36 = bf16[98,1024]{1,0:T(8,128)(2,1)S(1)} collective-permute-done((bf16[98,1024]{1,0:T(8,128)(2,1)S(1)}, bf16[98,1024]{1,0:T(8,128)(2,1)S(1)}, u32[]{:S(2)}, u32[]{:S(2)}) %collective-permute-start.36) | collective-permute-done | bytes 200736 | tf_op jit(solution)/shard_map/ppermute | solution.py:318
  211.3 3.0 collective-permute-done.29
  214.3 4.1 collective-permute-start.31
  218.4 1.9 constant_dynamic-update-slice_fusion.4
  220.3 1.9 constant_dynamic-update-slice_fusion.3
  228.2 2.8 multiply_convert_fusion
  232.0 2.8 convert_reduce_fusion
  234.9 2.6 fusion.62
  238.3 3.4 fusion.60
  242.8 3.3 fusion.59
  247.4 2.0 collective-permute-start.39
  251.0 3.4 collective-permute-done.33
  254.7 2.0 rev.44
  256.6 5.8 %collective-permute-done.39 = bf16[196,1024]{1,0:T(8,128)(2,1)} collective-permute-done((bf16[196,1024]{1,0:T(8,128)(2,1)}, bf16[196,1024]{1,0:T(8,128)(2,1)}, u32[]{:S(2)}, u32[]{:S(2)}) %collective-permute-start.39) | collective-permute-done | bytes 401440 | tf_op jit(solution)/shard_map/ppermute | solution.py:318
  263.9 2.2 fusion.46
  269.8 2.9 fusion.7
  272.9 2.5 collective-permute-done.63
  276.9 2.1 fusion.11
  279.0 1.7 collective-permute-start.64
  280.8 2.0 pad_maximum_fusion.6.grads
  282.8 2.6 shard_map.197
  288.3 1.7 collective-permute-start.41
  290.0 2.6 fusion.58
  292.6 2.6 collective-permute-done.43
  296.8 13.6 %shard_map.198 = bf16[1568,192]{1,0:T(8,128)(2,1)} custom-call(s32[1]{0:T(128)} %bitcast.2.chip, bf16[1568,192]{1,0:T(8,128)(2,1)} %bitcast.177, bf16[1568,64]{1,0:T(8,128)(2,1)} %bitcast.179, f32[7,8,224]{2,1,0:T(8,128)} %get-tuple-element.23.lse), custom_call_target="tpu_custom_call" | custom-call | tf_op jit(solution)/shard_map/pallas_call | solution.py:604
  311.8 2.1 collective-permute-start.46
  316.1 4.5 collective-permute-done.46
  321.6 2.5 collective-permute-done.44
  325.3 3.5 shard_map.199
  329.9 3.8 fusion.57
  338.5 2.5 fusion.36
  342.4 15.2 %collective-permute-done.60 = bf16[256,256]{1,0:T(8,128)(2,1)S(1)} collective-permute-done((bf16[256,256]{1,0:T(8,128)(2,1)S(1)}, bf16[256,256]{1,0:T(8,128)(2,1)S(1)}, u32[]{:S(2)}, u32[]{:S(2)}) %collective-permute-start.60) | collective-permute-done | bytes 131104 | tf_op jit(solution)/shard_map/ppermute | solution.py:318
  358.5 2.5 fusion.35
  362.7 3.8 collective-permute-start.62
  368.2 11.2 %collective-permute-done.48 = bf16[98,1024]{1,0:T(8,128)(2,1)S(1)} collective-permute-done((bf16[98,1024]{1,0:T(8,128)(2,1)S(1)}, bf16[98,1024]{1,0:T(8,128)(2,1)S(1)}, u32[]{:S(2)}, u32[]{:S(2)}) %collective-permute-start.48) | collective-permute-done | bytes 200736 | tf_op jit(solution)/shard_map/ppermute | solution.py:318
  388.1 2.0 collective-permute-start.51
  393.4 4.3 collective-permute-done.53
  401.4 2.3 collective-permute-start.49
  406.8 2.2 convert_select_fusion
  412.3 1.9 fusion.18
  414.3 2.0 collective-permute-start.56
  418.1 2.6 select_select_fusion
  420.6 4.2 all-to-all-start.1
  426.2 2.0 fusion.37
  433.1 5.8 %all-to-all-done.1 = bf16[8,49,1024]{2,1,0:T(8,128)(2,1)} async-done(((bf16[8,49,1024]{2,1,0:T(8,128)(2,1)}), bf16[8,49,1024]{2,1,0:T(8,128)(2,1)}, u32[]{:S(2)}, u32[]{:S(2)}) %all-to-all-start.1) | async-done | bytes 802848 | tf_op jit(solution)/shard_map/all_to_all | solution.py:633
  438.9 4.2 all-to-all-start.3
  445.9 1.8 convert_add_fusion.4
  447.8 2.4 reshape.316
  450.1 7.0 %all-to-all-done.3 = bf16[8,49,1024]{2,1,0:T(8,128)(2,1)} async-done(((bf16[8,49,1024]{2,1,0:T(8,128)(2,1)}), bf16[8,49,1024]{2,1,0:T(8,128)(2,1)}, u32[]{:S(2)}, u32[]{:S(2)}) %all-to-all-start.3) | async-done | bytes 802848 | tf_op jit(solution)/shard_map/all_to_all | solution.py:633
  457.1 2.5 reshape.332
  (427 shorter events, 137.4 us)
Async XLA Ops:
  1.6 99.0 %collective-permute-start.14 = (bf16[128,256]{1,0:T(8,128)(2,1)S(1)}, bf16[128,256]{1,0:T(8,128)(2,1)S(1)}, u32[]{:S(2)}, u32[]{:S(2)}) collective-permute-start(bf16[128,256]{1,0:T(8,128)(2,1)S(1)} %bitcast.182), channel_id=1, source_target_pairs={{0,2},{1,3},{2,0},{3,1},{4,6},{5,7},{6,4},{7,5},{8,10},{9,11},{10,... | collective-permute-start | bytes 196616 | tf_op jit(solution)/shard_map/ppermute | solution.py:318
  6.9 101.2 %collective-permute-start.3 = (bf16[128,768]{1,0:T(8,128)(2,1)S(1)}, bf16[128,768]{1,0:T(8,128)(2,1)S(1)}, u32[]{:S(2)}, u32[]{:S(2)}) collective-permute-start(bf16[128,768]{1,0:T(8,128)(2,1)S(1)} %copy.82), channel_id=1, source_target_pairs={{0,2},{1,3},{2,0},{3,1},{4,6},{5,7},{6,4},{7,5},{8,10},{9,11},{10,... | collective-permute-start | bytes 589832 | tf_op jit(solution)/shard_map/ppermute | solution.py:318
  8.1 100.3 %collective-permute-start.27 = (bf16[128,1024]{1,0:T(8,128)(2,1)S(1)}, bf16[128,1024]{1,0:T(8,128)(2,1)S(1)}, u32[]{:S(2)}, u32[]{:S(2)}) collective-permute-start(bf16[128,1024]{1,0:T(8,128)(2,1)S(1)} %bitcast.178), channel_id=1, source_target_pairs={{0,2},{1,3},{2,0},{3,1},{4,6},{5,7},{6,4},{7,5},{8,10},{9,11},{10,... | collective-permute-start | bytes 786440 | tf_op jit(solution)/shard_map/ppermute | solution.py:318
  11.1 98.4 %collective-permute-start.22 = (bf16[128,1024]{1,0:T(8,128)(2,1)}, bf16[128,1024]{1,0:T(8,128)(2,1)S(1)}, u32[]{:S(2)}, u32[]{:S(2)}) collective-permute-start(bf16[128,1024]{1,0:T(8,128)(2,1)} %param.19), channel_id=1, source_target_pairs={{0,2},{1,3},{2,0},{3,1},{4,6},{5,7},{6,4},{7,5},{8,10},{9,11},{10,... | collective-permute-start | bytes 786440 | tf_op jit(solution)/shard_map/ppermute | solution.py:318
  14.3 98.7 %all-to-all-start = ((bf16[8,50,1024]{2,1,0:T(8,128)(2,1)}), bf16[8,50,1024]{2,1,0:T(8,128)(2,1)}, u32[]{:S(2)}, u32[]{:S(2)}) async-start(bf16[8,50,1024]{2,1,0:T(8,128)(2,1)} %concatenate.76), calls=%async_computation | async-start | bytes 1835008 | tf_op jit(solution)/shard_map/all_to_all | solution.py:506
  100.6 5.9 %collective-permute-start.15 = (bf16[128,256]{1,0:T(8,128)(2,1)S(1)}, bf16[128,256]{1,0:T(8,128)(2,1)S(1)}, u32[]{:S(2)}, u32[]{:S(2)}) collective-permute-start(bf16[128,256]{1,0:T(8,128)(2,1)S(1)} %broadcast_select_fusion.22), channel_id=1, source_target_pairs={{0,4},{1,5},{2,6},{3,7},{4,0},{5,1},{6,2},{7,3},{8,12},{9,13},{10,... | collective-permute-start | bytes 196616 | tf_op jit(solution)/shard_map/ppermute | solution.py:318
  106.5 56.9 %collective-permute-start.17 = (bf16[256,256]{1,0:T(8,128)(2,1)S(1)}, bf16[256,256]{1,0:T(8,128)(2,1)S(1)}, u32[]{:S(2)}, u32[]{:S(2)}) collective-permute-start(bf16[256,256]{1,0:T(8,128)(2,1)S(1)} %pad_maximum_fusion.23.w0), channel_id=1, source_target_pairs={{0,16},{1,17},{2,18},{3,19},{4,20},{5,21},{6,22},{7,23},{8,24},{9,... | collective-permute-start | bytes 393224 | tf_op jit(solution)/shard_map/ppermute | solution.py:318
  109.2 22.8 %collective-permute-start.28 = (bf16[128,1024]{1,0:T(8,128)(2,1)}, bf16[128,1024]{1,0:T(8,128)(2,1)S(1)}, u32[]{:S(2)}, u32[]{:S(2)}) collective-permute-start(bf16[128,1024]{1,0:T(8,128)(2,1)} %broadcast_select_fusion.10), channel_id=1, source_target_pairs={{0,4},{1,5},{2,6},{3,7},{4,0},{5,1},{6,2},{7,3},{8,12},{9,13},{10,... | collective-permute-start | bytes 786440 | tf_op jit(solution)/shard_map/ppermute | solution.py:318
  109.9 38.6 %collective-permute-start.6 = (bf16[256,768]{1,0:T(8,128)(2,1)S(1)}, bf16[256,768]{1,0:T(8,128)(2,1)S(1)}, u32[]{:S(2)}, u32[]{:S(2)}) collective-permute-start(bf16[256,768]{1,0:T(8,128)(2,1)S(1)} %pad_maximum_fusion.19.w0), channel_id=1, source_target_pairs={{0,16},{1,17},{2,18},{3,19},{4,20},{5,21},{6,22},{7,23},{8,24},{9,... | collective-permute-start | bytes 1179656 | tf_op jit(solution)/shard_map/ppermute | solution.py:318
  110.4 31.5 %collective-permute-start.5 = (bf16[256,768]{1,0:T(8,128)(2,1)S(1)}, bf16[256,768]{1,0:T(8,128)(2,1)S(1)}, u32[]{:S(2)}, u32[]{:S(2)}) collective-permute-start(bf16[256,768]{1,0:T(8,128)(2,1)S(1)} %pad_maximum_fusion.19.w0), channel_id=1, source_target_pairs={{0,8},{1,9},{2,10},{3,11},{4,12},{5,13},{6,14},{7,15},{8,0},{9,1},... | collective-permute-start | bytes 1179656 | tf_op jit(solution)/shard_map/ppermute | solution.py:318
  113.0 32.4 %all-to-all-start.2 = ((bf16[8,49,1024]{2,1,0:T(8,128)(2,1)}), bf16[8,49,1024]{2,1,0:T(8,128)(2,1)}, u32[]{:S(2)}, u32[]{:S(2)}) async-start(bf16[8,49,1024]{2,1,0:T(8,128)(2,1)} %reshape.317), calls=%async_computation.2 | async-start | bytes 1835008 | tf_op jit(solution)/shard_map/all_to_all | solution.py:583
  122.6 7.4 %collective-permute-start = (bf16[49,1024]{1,0:T(8,128)(2,1)S(1)}, bf16[49,1024]{1,0:T(8,128)(2,1)S(1)}, u32[]{:S(2)}, u32[]{:S(2)}) collective-permute-start(bf16[49,1024]{1,0:T(8,128)(2,1)S(1)} %get-tuple-element.127), channel_id=1, source_target_pairs={{0,2},{1,3},{2,0},{3,1},{4,6},{5,7},{6,4},{7,5},{8,10},{9,11},{10,... | collective-permute-start | bytes 301064 | tf_op jit(solution)/shard_map/ppermute | solution.py:318
  131.9 7.4 %collective-permute-start.1 = (bf16[98,1024]{1,0:T(8,128)(2,1)S(1)}, bf16[98,1024]{1,0:T(8,128)(2,1)S(1)}, u32[]{:S(2)}, u32[]{:S(2)}) collective-permute-start(bf16[98,1024]{1,0:T(8,128)(2,1)S(1)} %reshape.303), channel_id=1, source_target_pairs={{0,1},{1,0},{2,3},{3,2},{4,5},{5,4},{6,7},{7,6},{8,9},{9,8},{10,11... | collective-permute-start | bytes 602120 | tf_op jit(solution)/shard_map/ppermute | solution.py:318
  141.1 5.3 %collective-permute-start.2 = (bf16[196,1024]{1,0:T(8,128)(2,1)S(1)}, bf16[196,1024]{1,0:T(8,128)(2,1)}, u32[]{:S(2)}, u32[]{:S(2)}) collective-permute-start(bf16[196,1024]{1,0:T(8,128)(2,1)S(1)} %get-tuple-element.142), channel_id=1, source_target_pairs={{0,4},{1,5},{2,6},{3,7},{4,0},{5,1},{6,2},{7,3},{8,12},{9,13},{10,... | collective-permute-start | bytes 1204232 | tf_op jit(solution)/shard_map/ppermute | solution.py:318
  142.0 11.6 %collective-permute-start.7 = (bf16[256,768]{1,0:T(8,128)(2,1)S(1)}, bf16[256,768]{1,0:T(8,128)(2,1)S(1)}, u32[]{:S(2)}, u32[]{:S(2)}) collective-permute-start(bf16[256,768]{1,0:T(8,128)(2,1)S(1)} %collective-permute-done.5.w1), channel_id=1, source_target_pairs={{0,16},{1,17},{2,18},{3,19},{4,20},{5,21},{6,22},{7,23},{8,24},{9,... | collective-permute-start | bytes 1179656 | tf_op jit(solution)/shard_map/ppermute | solution.py:318
  159.1 12.3 %collective-permute-start.10 = (bf16[392,192]{1,0:T(8,128)(2,1)S(1)}, bf16[392,192]{1,0:T(8,128)(2,1)S(1)}, u32[]{:S(2)}, u32[]{:S(2)}) collective-permute-start(bf16[392,192]{1,0:T(8,128)(2,1)S(1)} %get-tuple-element.134), channel_id=1, source_target_pairs={{0,24},{1,25},{2,26},{3,27},{4,28},{5,29},{6,30},{7,31},{8,16},{9,... | collective-permute-start | bytes 451592 | tf_op jit(solution)/shard_map/ppermute | solution.py:318
  161.7 9.8 %collective-permute-start.9 = (bf16[392,192]{1,0:T(8,128)(2,1)S(1)}, bf16[392,192]{1,0:T(8,128)(2,1)S(1)}, u32[]{:S(2)}, u32[]{:S(2)}) collective-permute-start(bf16[392,192]{1,0:T(8,128)(2,1)S(1)} %get-tuple-element.135), channel_id=1, source_target_pairs={{0,16},{1,17},{2,18},{3,19},{4,20},{5,21},{6,22},{7,23},{8,24},{9,... | collective-permute-start | bytes 451592 | tf_op jit(solution)/shard_map/ppermute | solution.py:318
  162.2 10.3 %collective-permute-start.8 = (bf16[392,192]{1,0:T(8,128)(2,1)S(1)}, bf16[392,192]{1,0:T(8,128)(2,1)S(1)}, u32[]{:S(2)}, u32[]{:S(2)}) collective-permute-start(bf16[392,192]{1,0:T(8,128)(2,1)S(1)} %get-tuple-element.136), channel_id=1, source_target_pairs={{0,8},{1,9},{2,10},{3,11},{4,12},{5,13},{6,14},{7,15},{8,0},{9,1},... | collective-permute-start | bytes 451592 | tf_op jit(solution)/shard_map/ppermute | solution.py:318
  162.8 7.1 %collective-permute-start.35 = (bf16[49,1024]{1,0:T(8,128)(2,1)S(1)}, bf16[49,1024]{1,0:T(8,128)(2,1)S(1)}, u32[]{:S(2)}, u32[]{:S(2)}) collective-permute-start(bf16[49,1024]{1,0:T(8,128)(2,1)S(1)} %get-tuple-element.125), channel_id=1, source_target_pairs={{0,2},{1,3},{2,0},{3,1},{4,6},{5,7},{6,4},{7,5},{8,10},{9,11},{10,... | collective-permute-start | bytes 301064 | tf_op jit(solution)/shard_map/ppermute | solution.py:318
  163.5 31.0 %collective-permute-start.16 = (bf16[256,256]{1,0:T(8,128)(2,1)S(1)}, bf16[256,256]{1,0:T(8,128)(2,1)S(1)}, u32[]{:S(2)}, u32[]{:S(2)}) collective-permute-start(bf16[256,256]{1,0:T(8,128)(2,1)S(1)} %pad_maximum_fusion.23.w0), channel_id=1, source_target_pairs={{0,8},{1,9},{2,10},{3,11},{4,12},{5,13},{6,14},{7,15},{8,0},{9,1},... | collective-permute-start | bytes 393224 | tf_op jit(solution)/shard_map/ppermute | solution.py:318
  169.8 25.4 %collective-permute-start.18 = (bf16[256,256]{1,0:T(8,128)(2,1)S(1)}, bf16[256,256]{1,0:T(8,128)(2,1)S(1)}, u32[]{:S(2)}, u32[]{:S(2)}) collective-permute-start(bf16[256,256]{1,0:T(8,128)(2,1)S(1)} %collective-permute-done.17.w2), channel_id=1, source_target_pairs={{0,8},{1,9},{2,10},{3,11},{4,12},{5,13},{6,14},{7,15},{8,0},{9,1},... | collective-permute-start | bytes 393224 | tf_op jit(solution)/shard_map/ppermute | solution.py:318
  183.8 5.7 %collective-permute-start.13 = (bf16[392,64]{1,0:T(8,128)(2,1)S(1)}, bf16[392,64]{1,0:T(8,128)(2,1)S(1)}, u32[]{:S(2)}, u32[]{:S(2)}) collective-permute-start(bf16[392,64]{1,0:T(8,128)(2,1)S(1)} %get-tuple-element.152), channel_id=1, source_target_pairs={{0,24},{1,25},{2,26},{3,27},{4,28},{5,29},{6,30},{7,31},{8,16},{9,... | collective-permute-start | bytes 150536 | tf_op jit(solution)/shard_map/ppermute | solution.py:318
  185.2 6.0 %collective-permute-start.12 = (bf16[392,64]{1,0:T(8,128)(2,1)S(1)}, bf16[392,64]{1,0:T(8,128)(2,1)S(1)}, u32[]{:S(2)}, u32[]{:S(2)}) collective-permute-start(bf16[392,64]{1,0:T(8,128)(2,1)S(1)} %get-tuple-element.153), channel_id=1, source_target_pairs={{0,16},{1,17},{2,18},{3,19},{4,20},{5,21},{6,22},{7,23},{8,24},{9,... | collective-permute-start | bytes 150536 | tf_op jit(solution)/shard_map/ppermute | solution.py:318
  186.6 5.5 %collective-permute-start.11 = (bf16[392,64]{1,0:T(8,128)(2,1)S(1)}, bf16[392,64]{1,0:T(8,128)(2,1)S(1)}, u32[]{:S(2)}, u32[]{:S(2)}) collective-permute-start(bf16[392,64]{1,0:T(8,128)(2,1)S(1)} %get-tuple-element.154), channel_id=1, source_target_pairs={{0,8},{1,9},{2,10},{3,11},{4,12},{5,13},{6,14},{7,15},{8,0},{9,1},... | collective-permute-start | bytes 150536 | tf_op jit(solution)/shard_map/ppermute | solution.py:318
  189.4 20.5 %collective-permute-start.25 = (bf16[256,1024]{1,0:T(8,128)(2,1)}, bf16[256,1024]{1,0:T(8,128)(2,1)}, u32[]{:S(2)}, u32[]{:S(2)}) collective-permute-start(bf16[256,1024]{1,0:T(8,128)(2,1)} %pad_maximum_fusion.9), channel_id=1, source_target_pairs={{0,16},{1,17},{2,18},{3,19},{4,20},{5,21},{6,22},{7,23},{8,24},{9,... | collective-permute-start | bytes 1572872 | tf_op jit(solution)/shard_map/ppermute | solution.py:318
  191.2 18.7 %collective-permute-start.24 = (bf16[256,1024]{1,0:T(8,128)(2,1)}, bf16[256,1024]{1,0:T(8,128)(2,1)}, u32[]{:S(2)}, u32[]{:S(2)}) collective-permute-start(bf16[256,1024]{1,0:T(8,128)(2,1)} %pad_maximum_fusion.9), channel_id=1, source_target_pairs={{0,8},{1,9},{2,10},{3,11},{4,12},{5,13},{6,14},{7,15},{8,0},{9,1},... | collective-permute-start | bytes 1572872 | tf_op jit(solution)/shard_map/ppermute | solution.py:318
  192.1 34.0 %collective-permute-start.30 = (bf16[256,1024]{1,0:T(8,128)(2,1)}, bf16[256,1024]{1,0:T(8,128)(2,1)}, u32[]{:S(2)}, u32[]{:S(2)}) collective-permute-start(bf16[256,1024]{1,0:T(8,128)(2,1)} %pad_maximum_fusion.10), channel_id=1, source_target_pairs={{0,16},{1,17},{2,18},{3,19},{4,20},{5,21},{6,22},{7,23},{8,24},{9,... | collective-permute-start | bytes 1572872 | tf_op jit(solution)/shard_map/ppermute | solution.py:318
  194.5 19.8 %collective-permute-start.29 = (bf16[256,1024]{1,0:T(8,128)(2,1)}, bf16[256,1024]{1,0:T(8,128)(2,1)}, u32[]{:S(2)}, u32[]{:S(2)}) collective-permute-start(bf16[256,1024]{1,0:T(8,128)(2,1)} %pad_maximum_fusion.10), channel_id=1, source_target_pairs={{0,8},{1,9},{2,10},{3,11},{4,12},{5,13},{6,14},{7,15},{8,0},{9,1},... | collective-permute-start | bytes 1572872 | tf_op jit(solution)/shard_map/ppermute | solution.py:318
  200.5 7.3 %collective-permute-start.36 = (bf16[98,1024]{1,0:T(8,128)(2,1)S(1)}, bf16[98,1024]{1,0:T(8,128)(2,1)S(1)}, u32[]{:S(2)}, u32[]{:S(2)}) collective-permute-start(bf16[98,1024]{1,0:T(8,128)(2,1)S(1)} %reshape.318), channel_id=1, source_target_pairs={{0,1},{1,0},{2,3},{3,2},{4,5},{5,4},{6,7},{7,6},{8,9},{9,8},{10,11... | collective-permute-start | bytes 602120 | tf_op jit(solution)/shard_map/ppermute | solution.py:318
  207.8 14.3 %collective-permute-start.20 = (bf16[196,1024]{1,0:T(8,128)(2,1)}, bf16[196,1024]{1,0:T(8,128)(2,1)}, u32[]{:S(2)}, u32[]{:S(2)}) collective-permute-start(bf16[196,1024]{1,0:T(8,128)(2,1)} %pad_maximum_fusion.14), channel_id=1, source_target_pairs={{0,1},{1,0},{2,3},{3,2},{4,5},{5,4},{6,7},{7,6},{8,9},{9,8},{10,11... | collective-permute-start | bytes 1204232 | tf_op jit(solution)/shard_map/ppermute | solution.py:318
  209.9 22.1 %collective-permute-start.37 = (bf16[196,1024]{1,0:T(8,128)(2,1)S(1)}, bf16[196,1024]{1,0:T(8,128)(2,1)S(1)}, u32[]{:S(2)}, u32[]{:S(2)}) collective-permute-start(bf16[196,1024]{1,0:T(8,128)(2,1)S(1)} %get-tuple-element.103), channel_id=1, source_target_pairs={{0,4},{1,5},{2,6},{3,7},{4,0},{5,1},{6,2},{7,3},{8,12},{9,13},{10,... | collective-permute-start | bytes 1204232 | tf_op jit(solution)/shard_map/ppermute | solution.py:318
  209.9 17.3 %collective-permute-start.26 = (bf16[256,1024]{1,0:T(8,128)(2,1)}, bf16[256,1024]{1,0:T(8,128)(2,1)S(1)}, u32[]{:S(2)}, u32[]{:S(2)}) collective-permute-start(bf16[256,1024]{1,0:T(8,128)(2,1)} %collective-permute-done.25), channel_id=1, source_target_pairs={{0,8},{1,9},{2,10},{3,11},{4,12},{5,13},{6,14},{7,15},{8,0},{9,1},... | collective-permute-start | bytes 1572872 | tf_op jit(solution)/shard_map/ppermute | solution.py:318
  214.3 13.9 %collective-permute-start.31 = (bf16[256,1024]{1,0:T(8,128)(2,1)}, bf16[256,1024]{1,0:T(8,128)(2,1)S(1)}, u32[]{:S(2)}, u32[]{:S(2)}) collective-permute-start(bf16[256,1024]{1,0:T(8,128)(2,1)} %collective-permute-done.29), channel_id=1, source_target_pairs={{0,16},{1,17},{2,18},{3,19},{4,20},{5,21},{6,22},{7,23},{8,24},{9,... | collective-permute-start | bytes 1572872 | tf_op jit(solution)/shard_map/ppermute | solution.py:318
  237.7 8.4 %collective-permute-start.32 = (bf16[196,1024]{1,0:T(8,128)(2,1)S(1)}, bf16[196,1024]{1,0:T(8,128)(2,1)S(1)}, u32[]{:S(2)}, u32[]{:S(2)}) collective-permute-start(bf16[196,1024]{1,0:T(8,128)(2,1)S(1)} %slice.829), channel_id=1, source_target_pairs={{0,4},{1,5},{2,6},{3,7},{4,0},{5,1},{6,2},{7,3},{8,12},{9,13},{10,... | collective-permute-start | bytes 1204232 | tf_op jit(solution)/shard_map/ppermute | solution.py:318
  237.8 8.6 %collective-permute-start.38 = (bf16[196,1024]{1,0:T(8,128)(2,1)S(1)}, bf16[196,1024]{1,0:T(8,128)(2,1)S(1)}, u32[]{:S(2)}, u32[]{:S(2)}) collective-permute-start(bf16[196,1024]{1,0:T(8,128)(2,1)S(1)} %slice.828), channel_id=1, source_target_pairs={{0,4},{1,5},{2,6},{3,7},{4,0},{5,1},{6,2},{7,3},{8,12},{9,13},{10,... | collective-permute-start | bytes 1204232 | tf_op jit(solution)/shard_map/ppermute | solution.py:318
  242.8 25.5 %collective-permute-start.67 = (bf16[2,256,1024]{2,1,0:T(8,128)(2,1)}, bf16[2,256,1024]{2,1,0:T(8,128)(2,1)}, u32[]{:S(2)}, u32[]{:S(2)}) collective-permute-start(bf16[2,256,1024]{2,1,0:T(8,128)(2,1)} %pad_maximum_fusion.1), channel_id=1, source_target_pairs={{0,8},{1,9},{2,10},{3,11},{4,12},{5,13},{6,14},{7,15},{8,0},{9,1},... | collective-permute-start | bytes 3145736 | tf_op jit(solution)/shard_map/ppermute | solution.py:318
  246.3 8.2 %collective-permute-start.33 = (bf16[98,1024]{1,0:T(8,128)(2,1)S(1)}, bf16[98,1024]{1,0:T(8,128)(2,1)S(1)}, u32[]{:S(2)}, u32[]{:S(2)}) collective-permute-start(bf16[98,1024]{1,0:T(8,128)(2,1)S(1)} %slice.831), channel_id=1, source_target_pairs={{0,1},{1,0},{2,3},{3,2},{4,5},{5,4},{6,7},{7,6},{8,9},{9,8},{10,11... | collective-permute-start | bytes 602120 | tf_op jit(solution)/shard_map/ppermute | solution.py:318
  247.4 15.1 %collective-permute-start.39 = (bf16[196,1024]{1,0:T(8,128)(2,1)}, bf16[196,1024]{1,0:T(8,128)(2,1)}, u32[]{:S(2)}, u32[]{:S(2)}) collective-permute-start(bf16[196,1024]{1,0:T(8,128)(2,1)} %pad_maximum_fusion.16), channel_id=1, source_target_pairs={{0,1},{1,0},{2,3},{3,2},{4,5},{5,4},{6,7},{7,6},{8,9},{9,8},{10,11... | collective-permute-start | bytes 1204232 | tf_op jit(solution)/shard_map/ppermute | solution.py:318
  250.5 24.9 %collective-permute-start.63 = (bf16[2,256,1024]{2,1,0:T(8,128)(2,1)}, bf16[2,256,1024]{2,1,0:T(8,128)(2,1)}, u32[]{:S(2)}, u32[]{:S(2)}) collective-permute-start(bf16[2,256,1024]{2,1,0:T(8,128)(2,1)} %pad_maximum_fusion), channel_id=1, source_target_pairs={{0,16},{1,17},{2,18},{3,19},{4,20},{5,21},{6,22},{7,23},{8,24},{9,... | collective-permute-start | bytes 3145736 | tf_op jit(solution)/shard_map/ppermute | solution.py:318
  266.1 14.7 %collective-permute-start.40 = (bf16[196,1024]{1,0:T(8,128)(2,1)S(1)}, bf16[196,1024]{1,0:T(8,128)(2,1)}, u32[]{:S(2)}, u32[]{:S(2)}) collective-permute-start(bf16[196,1024]{1,0:T(8,128)(2,1)S(1)} %get-tuple-element.104), channel_id=1, source_target_pairs={{0,4},{1,5},{2,6},{3,7},{4,0},{5,1},{6,2},{7,3},{8,12},{9,13},{10,... | collective-permute-start | bytes 1204232 | tf_op jit(solution)/shard_map/ppermute | solution.py:318
  272.7 65.8 %collective-permute-start.68 = (bf16[256,1024]{1,0:T(8,128)(2,1)}, bf16[256,1024]{1,0:T(8,128)(2,1)}, u32[]{:S(2)}, u32[]{:S(2)}) collective-permute-start(bf16[256,1024]{1,0:T(8,128)(2,1)} %fusion.7), channel_id=1, source_target_pairs={{0,16},{1,17},{2,18},{3,19},{4,20},{5,21},{6,22},{7,23},{8,24},{9,... | collective-permute-start | bytes 1572872 | tf_op jit(solution)/shard_map/ppermute | solution.py:318
  279.0 79.5 %collective-permute-start.64 = (bf16[256,1024]{1,0:T(8,128)(2,1)}, bf16[256,1024]{1,0:T(8,128)(2,1)S(1)}, u32[]{:S(2)}, u32[]{:S(2)}) collective-permute-start(bf16[256,1024]{1,0:T(8,128)(2,1)} %fusion.11), channel_id=1, source_target_pairs={{0,8},{1,9},{2,10},{3,11},{4,12},{5,13},{6,14},{7,15},{8,0},{9,1},... | collective-permute-start | bytes 1572872 | tf_op jit(solution)/shard_map/ppermute | solution.py:318
  286.5 8.7 %collective-permute-start.43 = (bf16[392,64]{1,0:T(8,128)(2,1)S(1)}, bf16[392,64]{1,0:T(8,128)(2,1)S(1)}, u32[]{:S(2)}, u32[]{:S(2)}) collective-permute-start(bf16[392,64]{1,0:T(8,128)(2,1)S(1)} %get-tuple-element.148), channel_id=1, source_target_pairs={{0,24},{1,25},{2,26},{3,27},{4,28},{5,29},{6,30},{7,31},{8,16},{9,... | collective-permute-start | bytes 150536 | tf_op jit(solution)/shard_map/ppermute | solution.py:318
  286.6 8.7 %collective-permute-start.42 = (bf16[392,64]{1,0:T(8,128)(2,1)S(1)}, bf16[392,64]{1,0:T(8,128)(2,1)S(1)}, u32[]{:S(2)}, u32[]{:S(2)}) collective-permute-start(bf16[392,64]{1,0:T(8,128)(2,1)S(1)} %get-tuple-element.149), channel_id=1, source_target_pairs={{0,16},{1,17},{2,18},{3,19},{4,20},{5,21},{6,22},{7,23},{8,24},{9,... | collective-permute-start | bytes 150536 | tf_op jit(solution)/shard_map/ppermute | solution.py:318
  288.3 7.7 %collective-permute-start.41 = (bf16[392,64]{1,0:T(8,128)(2,1)S(1)}, bf16[392,64]{1,0:T(8,128)(2,1)S(1)}, u32[]{:S(2)}, u32[]{:S(2)}) collective-permute-start(bf16[392,64]{1,0:T(8,128)(2,1)S(1)} %get-tuple-element.150), channel_id=1, source_target_pairs={{0,8},{1,9},{2,10},{3,11},{4,12},{5,13},{6,14},{7,15},{8,0},{9,1},... | collective-permute-start | bytes 150536 | tf_op jit(solution)/shard_map/ppermute | solution.py:318
  311.8 8.8 %collective-permute-start.46 = (bf16[392,192]{1,0:T(8,128)(2,1)S(1)}, bf16[392,192]{1,0:T(8,128)(2,1)S(1)}, u32[]{:S(2)}, u32[]{:S(2)}) collective-permute-start(bf16[392,192]{1,0:T(8,128)(2,1)S(1)} %get-tuple-element.130), channel_id=1, source_target_pairs={{0,24},{1,25},{2,26},{3,27},{4,28},{5,29},{6,30},{7,31},{8,16},{9,... | collective-permute-start | bytes 451592 | tf_op jit(solution)/shard_map/ppermute | solution.py:318
  313.9 7.7 %collective-permute-start.45 = (bf16[392,192]{1,0:T(8,128)(2,1)S(1)}, bf16[392,192]{1,0:T(8,128)(2,1)S(1)}, u32[]{:S(2)}, u32[]{:S(2)}) collective-permute-start(bf16[392,192]{1,0:T(8,128)(2,1)S(1)} %get-tuple-element.131), channel_id=1, source_target_pairs={{0,16},{1,17},{2,18},{3,19},{4,20},{5,21},{6,22},{7,23},{8,24},{9,... | collective-permute-start | bytes 451592 | tf_op jit(solution)/shard_map/ppermute | solution.py:318
  314.7 9.4 %collective-permute-start.44 = (bf16[392,192]{1,0:T(8,128)(2,1)S(1)}, bf16[392,192]{1,0:T(8,128)(2,1)S(1)}, u32[]{:S(2)}, u32[]{:S(2)}) collective-permute-start(bf16[392,192]{1,0:T(8,128)(2,1)S(1)} %get-tuple-element.132), channel_id=1, source_target_pairs={{0,8},{1,9},{2,10},{3,11},{4,12},{5,13},{6,14},{7,15},{8,0},{9,1},... | collective-permute-start | bytes 451592 | tf_op jit(solution)/shard_map/ppermute | solution.py:318
  320.5 16.1 %collective-permute-start.59 = (bf16[2,256,256]{2,1,0:T(8,128)(2,1)}, bf16[2,256,256]{2,1,0:T(8,128)(2,1)}, u32[]{:S(2)}, u32[]{:S(2)}) collective-permute-start(bf16[2,256,256]{2,1,0:T(8,128)(2,1)} %pad_maximum_fusion.22), channel_id=1, source_target_pairs={{0,8},{1,9},{2,10},{3,11},{4,12},{5,13},{6,14},{7,15},{8,0},{9,1},... | collective-permute-start | bytes 786440 | tf_op jit(solution)/shard_map/ppermute | solution.py:318
  329.8 36.7 %collective-permute-start.47 = (bf16[196,1024]{1,0:T(8,128)(2,1)}, bf16[196,1024]{1,0:T(8,128)(2,1)S(1)}, u32[]{:S(2)}, u32[]{:S(2)}) collective-permute-start(bf16[196,1024]{1,0:T(8,128)(2,1)} %get-tuple-element.25), channel_id=1, source_target_pairs={{0,4},{1,5},{2,6},{3,7},{4,0},{5,1},{6,2},{7,3},{8,12},{9,13},{10,... | collective-permute-start | bytes 1204232 | tf_op jit(solution)/shard_map/ppermute | solution.py:318
  334.7 75.2 %collective-permute-start.55 = (bf16[2,256,768]{2,1,0:T(8,128)(2,1)}, bf16[2,256,768]{2,1,0:T(8,128)(2,1)}, u32[]{:S(2)}, u32[]{:S(2)}) collective-permute-start(bf16[2,256,768]{2,1,0:T(8,128)(2,1)} %pad_maximum_fusion.8), channel_id=1, source_target_pairs={{0,16},{1,17},{2,18},{3,19},{4,20},{5,21},{6,22},{7,23},{8,24},{9,... | collective-permute-start | bytes 2359304 | tf_op jit(solution)/shard_map/ppermute | solution.py:318
  337.6 20.0 %collective-permute-start.60 = (bf16[256,256]{1,0:T(8,128)(2,1)S(1)}, bf16[256,256]{1,0:T(8,128)(2,1)S(1)}, u32[]{:S(2)}, u32[]{:S(2)}) collective-permute-start(bf16[256,256]{1,0:T(8,128)(2,1)S(1)} %fusion.31), channel_id=1, source_target_pairs={{0,16},{1,17},{2,18},{3,19},{4,20},{5,21},{6,22},{7,23},{8,24},{9,... | collective-permute-start | bytes 393224 | tf_op jit(solution)/shard_map/ppermute | solution.py:318
  341.0 65.9 %collective-permute-start.69 = (bf16[256,1024]{1,0:T(8,128)(2,1)}, bf16[256,1024]{1,0:T(8,128)(2,1)}, u32[]{:S(2)}, u32[]{:S(2)}) collective-permute-start(bf16[256,1024]{1,0:T(8,128)(2,1)} %fusion.36), channel_id=1, source_target_pairs={{4,6},{5,7},{6,4},{7,5},{12,14},{13,15},{14,12},{15,13},{20,22},{2... | collective-permute-start | bytes 1572872 | tf_op jit(solution)/shard_map/ppermute | solution.py:454
  361.0 55.3 %collective-permute-start.65 = (bf16[256,1024]{1,0:T(8,128)(2,1)}, bf16[256,1024]{1,0:T(8,128)(2,1)}, u32[]{:S(2)}, u32[]{:S(2)}) collective-permute-start(bf16[256,1024]{1,0:T(8,128)(2,1)} %fusion.35), channel_id=1, source_target_pairs={{4,6},{5,7},{6,4},{7,5},{12,14},{13,15},{14,12},{15,13},{20,22},{2... | collective-permute-start | bytes 1572872 | tf_op jit(solution)/shard_map/ppermute | solution.py:454
  366.7 12.8 %collective-permute-start.48 = (bf16[98,1024]{1,0:T(8,128)(2,1)S(1)}, bf16[98,1024]{1,0:T(8,128)(2,1)S(1)}, u32[]{:S(2)}, u32[]{:S(2)}) collective-permute-start(bf16[98,1024]{1,0:T(8,128)(2,1)S(1)} %slice.830), channel_id=1, source_target_pairs={{0,1},{1,0},{2,3},{3,2},{4,5},{5,4},{6,7},{7,6},{8,9},{9,8},{10,11... | collective-permute-start | bytes 602120 | tf_op jit(solution)/shard_map/ppermute | solution.py:318
  400.7 17.3 %collective-permute-start.34 = (bf16[49,1024]{1,0:T(8,128)(2,1)}, bf16[49,1024]{1,0:T(8,128)(2,1)}, u32[]{:S(2)}, u32[]{:S(2)}) collective-permute-start(bf16[49,1024]{1,0:T(8,128)(2,1)} %slice.454), channel_id=1, source_target_pairs={{0,2},{1,3},{2,0},{3,1},{4,6},{5,7},{6,4},{7,5},{8,10},{9,11},{10,... | collective-permute-start | bytes 301064 | tf_op jit(solution)/shard_map/ppermute | solution.py:318
  401.4 16.6 %collective-permute-start.49 = (bf16[49,1024]{1,0:T(8,128)(2,1)}, bf16[49,1024]{1,0:T(8,128)(2,1)}, u32[]{:S(2)}, u32[]{:S(2)}) collective-permute-start(bf16[49,1024]{1,0:T(8,128)(2,1)} %slice.476), channel_id=1, source_target_pairs={{0,2},{1,3},{2,0},{3,1},{4,6},{5,7},{6,4},{7,5},{8,10},{9,11},{10,... | collective-permute-start | bytes 301064 | tf_op jit(solution)/shard_map/ppermute | solution.py:318
  409.8 21.2 %collective-permute-start.70 = (bf16[128,1024]{1,0:T(8,128)(2,1)}, bf16[128,1024]{1,0:T(8,128)(2,1)}, u32[]{:S(2)}, u32[]{:S(2)}) collective-permute-start(bf16[128,1024]{1,0:T(8,128)(2,1)} %select_convert_fusion), channel_id=1, source_target_pairs={{0,4},{1,5},{2,6},{3,7},{4,0},{5,1},{6,2},{7,3},{8,12},{9,13},{10,... | collective-permute-start | bytes 786440 | tf_op jit(solution)/shard_map/ppermute | solution.py:318
  414.3 12.0 %collective-permute-start.56 = (bf16[256,768]{1,0:T(8,128)(2,1)}, bf16[256,768]{1,0:T(8,128)(2,1)S(1)}, u32[]{:S(2)}, u32[]{:S(2)}) collective-permute-start(bf16[256,768]{1,0:T(8,128)(2,1)} %fusion.18), channel_id=1, source_target_pairs={{0,8},{1,9},{2,10},{3,11},{4,12},{5,13},{6,14},{7,15},{8,0},{9,1},... | collective-permute-start | bytes 1179656 | tf_op jit(solution)/shard_map/ppermute | solution.py:318
  420.6 18.3 %all-to-all-start.1 = ((bf16[8,49,1024]{2,1,0:T(8,128)(2,1)}), bf16[8,49,1024]{2,1,0:T(8,128)(2,1)}, u32[]{:S(2)}, u32[]{:S(2)}) async-start(bf16[8,49,1024]{2,1,0:T(8,128)(2,1)} %get-tuple-element.168), calls=%async_computation.1 | async-start | bytes 1835008 | tf_op jit(solution)/shard_map/all_to_all | solution.py:633
  428.2 14.9 %collective-permute-start.57 = (bf16[256,768]{1,0:T(8,128)(2,1)}, bf16[256,768]{1,0:T(8,128)(2,1)}, u32[]{:S(2)}, u32[]{:S(2)}) collective-permute-start(bf16[256,768]{1,0:T(8,128)(2,1)} %fusion.37), channel_id=1, source_target_pairs={{4,6},{5,7},{6,4},{7,5},{12,14},{13,15},{14,12},{15,13},{20,22},{2... | collective-permute-start | bytes 1179656 | tf_op jit(solution)/shard_map/ppermute | solution.py:454
  430.4 15.5 %collective-permute-start.66 = (bf16[128,1024]{1,0:T(8,128)(2,1)}, bf16[128,1024]{1,0:T(8,128)(2,1)}, u32[]{:S(2)}, u32[]{:S(2)}) collective-permute-start(bf16[128,1024]{1,0:T(8,128)(2,1)} %select_convert_fusion.1), channel_id=1, source_target_pairs={{0,4},{1,5},{2,6},{3,7},{4,0},{5,1},{6,2},{7,3},{8,12},{9,13},{10,... | collective-permute-start | bytes 786440 | tf_op jit(solution)/shard_map/ppermute | solution.py:318
  438.9 18.3 %all-to-all-start.3 = ((bf16[8,49,1024]{2,1,0:T(8,128)(2,1)}), bf16[8,49,1024]{2,1,0:T(8,128)(2,1)}, u32[]{:S(2)}, u32[]{:S(2)}) async-start(bf16[8,49,1024]{2,1,0:T(8,128)(2,1)} %get-tuple-element.167), calls=%async_computation.3 | async-start | bytes 1835008 | tf_op jit(solution)/shard_map/all_to_all | solution.py:633
  445.5 14.2 %collective-permute-start.58 = (bf16[128,768]{1,0:T(8,128)(2,1)S(1)}, bf16[128,768]{1,0:T(8,128)(2,1)S(1)}, u32[]{:S(2)}, u32[]{:S(2)}) collective-permute-start(bf16[128,768]{1,0:T(8,128)(2,1)S(1)} %select_convert_fusion.2), channel_id=1, source_target_pairs={{0,4},{1,5},{2,6},{3,7},{4,0},{5,1},{6,2},{7,3},{8,12},{9,13},{10,... | collective-permute-start | bytes 589832 | tf_op jit(solution)/shard_map/ppermute | solution.py:318
  (66 other events, 543.3 us)

commit v2 on v0

--- a/solution.py
+++ b/solution.py
@@ -3,6 +3,8 @@
 import jax
 import jax.numpy as jnp
 from jax import lax
+from jax.experimental import pallas as pl
+from jax.experimental.pallas import tpu as pltpu
 from jax.sharding import PartitionSpec as P
 
 HD = 64
@@ -305,7 +307,883 @@
     )
 
 
+AXES = ("dp", "tensor")
+Z_LOW, Z_HIGH, CORE, X, Y = 1, 2, 4, 8, 16
+CHIP_MASKS = (0, X, Y, X | Y)
+BF16, F32 = jnp.bfloat16, jnp.float32
+NN, NT, TN = ((1,), (0,)), ((1,), (1,)), ((0,), (0,))
+SHARE = 49
+PAD = 56
+CHIP_ID, CORE_ID, D_ID, T_ID = range(4)
+
+
+def swap(value, mask):
+    return lax.ppermute(value, AXES, [(i, i ^ mask) for i in range(32)])
+
+
+def dot(left, right, dims):
+    return lax.dot_general(left, right, (dims, ((), ())), preferred_element_type=F32)
+
+
+def call(body, outs, scalars, *args, scratch=(), flops=0):
+    moved = sum(math.prod(a.shape) * a.dtype.itemsize for a in args)
+    moved += sum(math.prod(s) * jnp.dtype(t).itemsize for s, t in outs)
+    held = sum(math.prod(s[:-1]) * max(s[-1], 128) * jnp.dtype(t).itemsize for s, t in scratch)
+    return pl.pallas_call(
+        body,
+        out_shape=[jax.ShapeDtypeStruct(s, t) for s, t in outs],
+        in_specs=[pl.BlockSpec(memory_space=pltpu.SMEM)]
+        + [pl.BlockSpec(memory_space=pltpu.VMEM)] * len(args),
+        out_specs=[pl.BlockSpec(memory_space=pltpu.VMEM)] * len(outs),
+        scratch_shapes=[pltpu.VMEM(s, t) for s, t in scratch],
+        compiler_params=pltpu.CompilerParams(vmem_limit_bytes=moved + held + (4 << 20)),
+        cost_estimate=pl.CostEstimate(flops=flops, bytes_accessed=moved, transcendentals=0),
+    )(scalars, *args)
+
+
+def chip_lanes(ids, m):
+    return pl.ds(pl.multiple_of((ids[CHIP_ID] ^ m) * 256, 256), 256)
+
+
+def lanes(m):
+    return slice(256 * m, 256 * m + 256)
+
+
+def row_ids(shape):
+    return lax.broadcasted_iota(jnp.int32, shape, 0)
+
+
+def pick(condition, left, right):
+    return jnp.where(jnp.full(left.shape, condition, jnp.int32) != 0, left, right)
+
+
+def is_zero(number):
+    return jnp.where(number == 0, 1, 0)
+
+
+def z_low(ids):
+    return ids[T_ID] & 1
+
+
+def z_high(ids):
+    return ids[T_ID] >> 1
+
+
+def pack_kernel(ids, rows, gains, biases, qv, b_fc1, out, wide):
+    lane32 = lax.broadcasted_iota(jnp.int32, (32, 128), 1)
+    spot = (lane32 == row_ids((32, 128)) + 32 * ids[T_ID]).astype(F32).astype(BF16)
+    lane8 = lax.broadcasted_iota(jnp.int32, (8, 128), 1)
+    spot8 = (lane8 == row_ids((8, 128)) + 8 * ids[D_ID]).astype(F32).astype(BF16)
+    g = dot(gains[...], spot, NN)
+    b = dot(biases[...], spot, NN)
+    qv_rows = dot(qv[...], spot8, NN)
+    row_a = jnp.concatenate(
+        [g[k : k + 1] for k in range(2)]
+        + [b[k : k + 1] for k in range(4)]
+        + [b_fc1[...].astype(F32), jnp.zeros((1, 128), F32)],
+        axis=1,
+    )
+    row_b = jnp.concatenate([qv_rows[k : k + 1] for k in range(8)], axis=1)
+    flag = jnp.full((PAD, 1024), ids[4], jnp.int32).astype(F32)
+    row = row_ids((PAD, 1024))
+    tail = jnp.where(row == SHARE, row_a, jnp.where(row == SHARE + 1, row_b, flag))
+    wide[0 : rows.shape[0], :] = rows[...].astype(F32)
+    for j in range(8):
+        block = wide[SHARE * j : SHARE * j + PAD, :]
+        out[j, :, :] = jnp.where(row < SHARE, block, tail).astype(BF16)
+
+
+def pack_grad_kernel(ids, rows, out, wide):
+    wide[0 : rows.shape[0], :] = rows[...].astype(F32)
+    for j in range(8):
+        out[j, :, :] = wide[SHARE * j : SHARE * j + PAD, :].astype(BF16)
+
+
+def pick_kernel(ids, got, here, there, slots):
+    row8 = row_ids((8, 1024))
+    row = row_ids((PAD, 1024))
+    seen = jnp.zeros((1, 1024), F32)
+    mine = jnp.zeros((PAD, 1024), F32)
+    other = jnp.zeros((PAD, 1024), F32)
+    params = jnp.zeros((8, 1024), F32)
+    qv = jnp.zeros((1, 1024), F32)
+    high = jnp.full((1, 1024), z_high(ids), jnp.int32).astype(F32)
+    for c in range(8):
+        block = got[c, :, :].astype(F32)
+        flag = block[SHARE + 2 : SHARE + 3]
+        is_mine = jnp.where(seen == high, flag, 0.0)
+        is_other = flag - is_mine
+        seen = seen + flag
+        mine = jnp.where(is_mine > 0.5, block, mine)
+        other = jnp.where(is_other > 0.5, block, other)
+        params = jnp.where(row8 == c, block[SHARE : SHARE + 1], params)
+        qv = qv + block[SHARE + 1 : SHARE + 2]
+        slots[c : c + 1, :] = is_mine[:, 0:128]
+        slots[8 + c : 9 + c, :] = is_other[:, 0:128]
+    for value, out in ((mine, here), (other, there)):
+        out[0:PAD, :] = jnp.where(row == PAD - 1, qv, value).astype(BF16)
+        out[PAD : PAD + 8, :] = params.astype(BF16)
+
+
+def pick_grad_kernel(ids, slots, got, here, there):
+    mine = jnp.zeros((PAD, 1024), F32)
+    other = jnp.zeros((PAD, 1024), F32)
+    for c in range(8):
+        block = got[c, :, :].astype(F32)
+        mine = jnp.where(slots[c : c + 1, 0:1] > 0.5, block, mine)
+        other = jnp.where(slots[8 + c : 9 + c, 0:1] > 0.5, block, other)
+    here[...] = mine.astype(BF16)
+    there[...] = other.astype(BF16)
+
+
+def lay_rows(ids, here, r1, r2, r3, wide):
+    low = is_zero(z_low(ids))
+    for m in range(4):
+        cols = chip_lanes(ids, m)
+        blocks = [ref[0:PAD, cols].astype(F32) for ref in (here, r1, r2, r3)]
+        order = (
+            pick(low, blocks[0], blocks[1]),
+            pick(low, blocks[2], blocks[3]),
+            pick(low, blocks[1], blocks[0]),
+            pick(low, blocks[3], blocks[2]),
+        )
+        for i, block in enumerate(order):
+            wide[SHARE * i : SHARE * i + SHARE, lanes(m)] = block[0:SHARE]
+
+
+def norm_parts(values):
+    centre = jnp.mean(values, axis=1, keepdims=True)
+    offsets = values - centre
+    inverse = lax.rsqrt(jnp.mean(offsets * offsets, axis=1, keepdims=True) + norm_eps)
+    return offsets * inverse, inverse
+
+
+def norm_one_kernel(ids, here, r1, r2, r3, rows, normed, vec, qv_bias, b_fc1, wide, small):
+    lay_rows(ids, here, r1, r2, r3, wide)
+    own = here[PAD - 8 : PAD + 8, :].astype(F32)
+    far = r2[PAD - 8 : PAD + 8, :].astype(F32)
+    tails = [own[8:], far[8:]] + [r[PAD : PAD + 8, :].astype(F32) for r in (r1, r3)]
+    params = tails[0] + tails[1] + tails[2] + tails[3]
+    small[...] = jnp.zeros_like(small)
+    for d in range(8):
+        for k in range(6):
+            small[k : k + 1, 128 * d : 128 * d + 128] = params[
+                d : d + 1, 128 * k : 128 * k + 128
+            ]
+    for m in range(4):
+        vec[:, lanes(m)] = small[:, chip_lanes(ids, m)]
+    home = pick(is_zero(ids[CORE_ID]), own, far)
+    for k in range(8):
+        qv_bias[k : k + 1, :] = home[7:8, 128 * k : 128 * k + 128]
+        b_fc1[0:1, 128 * k : 128 * k + 128] = home[8 + k : 9 + k, 768:896]
+    values = wide[...]
+    scaled, _ = norm_parts(values)
+    rows[...] = values.astype(BF16)
+    normed[...] = (scaled * vec[0:1, :] + vec[2:3, :]).astype(BF16)
+
+
+def lay_grad_kernel(ids, here, r1, r2, r3, out, wide):
+    lay_rows(ids, here, r1, r2, r3, wide)
+    out[...] = wide[...].astype(BF16)
+
+
+def join_rows(wide, own, got):
+    half = own.shape[0]
+    wide[0:half, :] = own[...].astype(F32)
+    wide[half : 2 * half, :] = got[...].astype(F32)
+
+
+def qkv_kernel(ids, own, got, qv_bias, w0, w1, w2, w3, whole, o0, o1, o2, o3, wide, heads):
+    weights = (w0, w1, w2, w3)
+    join_rows(wide, own, got)
+    whole[...] = wide[...].astype(BF16)
+    for j in range(3):
+        total = dot(whole[:, lanes(0)], w0[:, lanes(j)], NN)
+        for m in range(1, 4):
+            total = total + dot(whole[:, lanes(m)], weights[m][:, lanes(j)], NN)
+        for h in range(4):
+            part = total[:, 64 * h : 64 * h + 64]
+            if j != 1:
+                k = (j // 2) * 4 + h
+                part = part + qv_bias[k : k + 1, 0:64]
+            heads[h, :, 64 * j : 64 * j + 64] = part.astype(BF16)
+    for m, out in enumerate((o0, o1, o2, o3)):
+        out[...] = heads[ids[CHIP_ID] ^ m, :, :]
+
+
+STEP = 224
+
+
+def attention_kernel(ids, a0, a1, a2, a3, o0, o1, o2, o3, lse, stage, q, k, v):
+    tokens = a0.shape[0]
+    for m, part in enumerate((a0, a1, a2, a3)):
+        stage[tokens * m : tokens * m + tokens, :] = part[...].astype(F32)
+    q[...] = (stage[:, 0:64] * 0.125).astype(BF16)
+    k[...] = stage[:, 64:128].astype(BF16)
+    v[...] = stage[:, 128:192].astype(BF16)
+
+    def body(i, carry):
+        rows = pl.ds(pl.multiple_of(i * STEP, 32), STEP)
+        scores = dot(q[rows, :], k[...], NT)
+        top = jnp.max(scores, axis=1, keepdims=True)
+        weights = jnp.exp(scores - top)
+        total = jnp.sum(weights, axis=1, keepdims=True)
+        mixed = dot(weights.astype(BF16), v[...], NN)
+        stage[rows, 0:64] = mixed / total
+        spread = jnp.broadcast_to(top + jnp.log(total), (STEP, 128))
+        lse[i, :, :] = jnp.transpose(spread)[0:8, :]
+        return carry
+
+    lax.fori_loop(0, stage.shape[0] // STEP, body, 0)
+    for m, out in enumerate((o0, o1, o2, o3)):
+        out[...] = stage[tokens * m : tokens * m + tokens, 0:64].astype(BF16)
+
+
+def attention_back_kernel(
+    ids, a0, a1, a2, a3, g0, g1, g2, g3, lse, o0, o1, o2, o3, stage, q, k, v, g, grad_k, grad_v
+):
+    tokens = a0.shape[0]
+    for m, part in enumerate((a0, a1, a2, a3)):
+        stage[tokens * m : tokens * m + tokens, :] = part[...].astype(F32)
+    q[...] = (stage[:, 0:64] * 0.125).astype(BF16)
+    k[...] = stage[:, 64:128].astype(BF16)
+    v[...] = stage[:, 128:192].astype(BF16)
+    for m, part in enumerate((g0, g1, g2, g3)):
+        stage[tokens * m : tokens * m + tokens, 0:64] = part[...].astype(F32)
+    g[...] = stage[:, 0:64].astype(BF16)
+    keys_t = jnp.transpose(k[...])
+    grad_k[...] = jnp.zeros_like(grad_k)
+    grad_v[...] = jnp.zeros_like(grad_v)
+
+    def body(i, carry):
+        rows = pl.ds(pl.multiple_of(i * STEP, 32), STEP)
+        queries, grad = q[rows, :], g[rows, :]
+        probs = jnp.exp(dot(k[...], queries, NT) - lse[i, 0:1, :])
+        grad_probs = dot(v[...], grad, NT)
+        row_dot = jnp.sum(probs * grad_probs, axis=0, keepdims=True)
+        grad_scores = (probs * (grad_probs - row_dot)).astype(BF16)
+        grad_v[...] += dot(probs.astype(BF16), grad, NN)
+        grad_k[...] += dot(grad_scores, queries, NN)
+        stage[rows, 0:64] = jnp.transpose(dot(keys_t, grad_scores, NN)) * 0.125
+        return carry
+
+    lax.fori_loop(0, stage.shape[0] // STEP, body, 0)
+    for m, out in enumerate((o0, o1, o2, o3)):
+        rows = slice(tokens * m, tokens * m + tokens)
+        out[:, 0:64] = stage[rows, 0:64].astype(BF16)
+        out[:, 64:128] = grad_k[rows, :].astype(BF16)
+        out[:, 128:192] = grad_v[rows, :].astype(BF16)
+
+
+def split_rows(total, keep, send, cols):
+    half = keep.shape[0]
+    keep[:, cols] = total[:half]
+    send[:, cols] = total[half:].astype(BF16)
+
+
+def proj_kernel(ids, a0, a1, a2, a3, w0, w1, w2, w3, joined, keep, send, heads):
+    for m, part in enumerate((a0, a1, a2, a3)):
+        heads[m, :, :] = part[...]
+    for h in range(4):
+        joined[:, 64 * h : 64 * h + 64] = heads[h ^ ids[CHIP_ID], :, :]
+    for m, weight in enumerate((w0, w1, w2, w3)):
+        split_rows(dot(joined[...], weight[:, 0:256], NT), keep, send, lanes(m))
+
+
+def pair_kernel(ids, keep, got, part, send):
+    total = keep[...] + got[...].astype(F32)
+    part[...] = total
+    send[...] = total.astype(BF16)
+
+
+def half_kernel(ids, keep, got, part, send):
+    own = part.shape[0]
+    total = keep[...] + got[...].astype(F32)
+    low = is_zero(z_low(ids))
+    part[...] = pick(low, total[:own], total[own:])
+    send[...] = pick(low, total[own:], total[:own]).astype(BF16)
+
+
+def norm_two_kernel(ids, rows, part, got, vec, residual, normed):
+    total = rows[...].astype(F32) + (part[...] + got[...].astype(F32) + vec[4:5, :])
+    residual[...] = total
+    scaled, _ = norm_parts(total)
+    normed[...] = (scaled * vec[1:2, :] + vec[3:4, :]).astype(BF16)
+
+
+def grad_hidden_kernel(ids, own, got, w0, w1, w2, w3, whole, out, wide):
+    join_rows(wide, own, got)
+    whole[...] = wide[...].astype(BF16)
+    for c in range(4):
+        total = dot(whole[:, lanes(0)], w0[:, lanes(c)], NN)
+        for m, weight in enumerate((w1, w2, w3)):
+            total = total + dot(whole[:, lanes(m + 1)], weight[:, lanes(c)], NN)
+        out[:, lanes(c)] = total
+
+
+def fc_kernel(
+    ids, own, got, grad_hidden, b_fc1, w0, w1, w2, w3, whole, hidden, grad_pre, sums, keep, send, wide
+):
+    weights = (w0, w1, w2, w3)
+    join_rows(wide, own, got)
+    whole[...] = wide[...].astype(BF16)
+    wide[...] = jnp.zeros_like(wide)
+
+    def body(c, carry):
+        cols = pl.ds(pl.multiple_of(c * 256, 256), 256)
+        fc1 = pl.ds(pl.multiple_of(c * 256 + 256, 256), 256)
+        pre = b_fc1[:, cols] + dot(whole[:, lanes(0)], w0[:, fc1], NN)
+        for m in range(1, 4):
+            pre = pre + dot(whole[:, lanes(m)], weights[m][:, fc1], NN)
+        half_erf = 0.5 * (1.0 + lax.erf(pre * root_half))
+        hidden[:, cols] = (pre * half_erf).astype(BF16)
+        slope = half_erf + pre * jnp.exp(-0.5 * pre * pre) * inv_root_tau
+        grad = (grad_hidden[:, cols] * slope).astype(BF16)
+        grad_pre[:, cols] = grad
+        sums[:, cols] = jnp.sum(grad.astype(F32), axis=0, keepdims=True)
+        for m in range(4):
+            wide[:, lanes(m)] += dot(grad, weights[m][:, fc1], NT)
+        return carry
+
+    lax.fori_loop(0, 4, body, 0)
+    for m in range(4):
+        split_rows(wide[:, lanes(m)], keep, send, lanes(m))
+
+
+def norm_back(total, scaled, inverse, gain):
+    hat = total * gain
+    return (
+        hat
+        - jnp.mean(hat, axis=1, keepdims=True)
+        - scaled * jnp.mean(hat * scaled, axis=1, keepdims=True)
+    ) * inverse
+
+
+def norm_two_back_kernel(ids, residual, part, got, grads, vec, grad_residual, grad_branch, sums):
+    scaled, inverse = norm_parts(residual[...])
+    total = part[...] + got[...].astype(F32)
+    upstream = grads[...].astype(F32)
+    result = upstream + norm_back(total, scaled, inverse, vec[1:2, :])
+    branch = result.astype(BF16)
+    grad_residual[...] = result
+    grad_branch[...] = branch
+    own = total.shape[0] // 2
+    row = row_ids(total.shape)
+    low = jnp.full(total.shape, z_low(ids), jnp.int32)
+    mine = jnp.where(row < own, 1 - low, low) != 0
+
+    def column_sum(value):
+        return jnp.sum(jnp.where(mine, value, 0.0), axis=0, keepdims=True)
+
+    sums[0:1, :] = column_sum(total * scaled)
+    sums[1:2, :] = column_sum(total)
+    sums[2:3, :] = column_sum(branch.astype(F32))
+    sums[3:4, :] = column_sum(upstream)
+    sums[4:8, :] = jnp.zeros((4, sums.shape[1]), F32)
+
+
+def grad_att_kernel(ids, own, got, w0, w1, w2, w3, whole, o0, o1, o2, o3, wide, heads):
+    join_rows(wide, own, got)
+    whole[...] = wide[...].astype(BF16)
+    total = dot(whole[:, lanes(0)], w0[:, 0:256], NN)
+    for m, weight in enumerate((w1, w2, w3)):
+        total = total + dot(whole[:, lanes(m + 1)], weight[:, 0:256], NN)
+    for h in range(4):
+        heads[h, :, :] = total[:, 64 * h : 64 * h + 64].astype(BF16)
+    for m, out in enumerate((o0, o1, o2, o3)):
+        out[...] = heads[ids[CHIP_ID] ^ m, :, :]
+
+
+def qkv_back_kernel(ids, g0, g1, g2, g3, w0, w1, w2, w3, joined, keep, send, sums, heads):
+    for m, part in enumerate((g0, g1, g2, g3)):
+        heads[m, :, :] = part[...]
+    for h in range(4):
+        part = heads[h ^ ids[CHIP_ID], :, :]
+        for j in range(3):
+            piece = part[:, 64 * j : 64 * j + 64]
+            joined[:, 256 * j + 64 * h : 256 * j + 64 * h + 64] = piece
+            if j != 1:
+                k = (j // 2) * 4 + h
+                total = jnp.sum(piece.astype(F32), axis=0, keepdims=True)
+                sums[0:1, 128 * k : 128 * k + 128] = jnp.concatenate(
+                    [total, jnp.zeros((1, 64), F32)], axis=1
+                )
+    for m, weight in enumerate((w0, w1, w2, w3)):
+        split_rows(dot(joined[...], weight[...], NT), keep, send, lanes(m))
+
+
+def to_owners(ids, value, wide, here, there):
+    wide[0 : 2 * SHARE, :] = value
+    wide[2 * SHARE :, :] = jnp.zeros((wide.shape[0] - 2 * SHARE, wide.shape[1]), F32)
+    for m in range(4):
+        cols = chip_lanes(ids, m)
+        here[0:PAD, cols] = wide[0:PAD, lanes(m)].astype(BF16)
+        there[0:PAD, cols] = wide[SHARE : SHARE + PAD, lanes(m)].astype(BF16)
+
+
+def own_half(ids, ref):
+    own = ref.shape[0] // 2
+    value = ref[...].astype(F32)
+    return pick(is_zero(z_low(ids)), value[:own], value[own:])
+
+
+def norm_one_back_kernel(
+    ids, rows, part, got, grad_residual, vec, sums_two, sums_fc1, sums_qv, here, there, small_out, wide
+):
+    scaled, inverse = norm_parts(own_half(ids, rows))
+    total = part[...] + got[...].astype(F32)
+    result = own_half(ids, grad_residual) + norm_back(total, scaled, inverse, vec[0:1, :])
+    to_owners(ids, result, wide, here, there)
+    small = jnp.concatenate(
+        [
+            jnp.sum(total * scaled, axis=0, keepdims=True),
+            sums_two[0:1, :],
+            jnp.sum(total, axis=0, keepdims=True),
+            sums_two[1:4, :],
+            sums_qv[...],
+            sums_fc1[...],
+        ],
+        axis=0,
+    )
+    small_out[...] = small.astype(BF16)
+    here[PAD : PAD + 8, :] = small.astype(BF16)
+    there[PAD : PAD + 8, :] = small.astype(BF16)
+
+
+def layer_out_kernel(ids, residual, part, got, vec, here, there, wide):
+    result = own_half(ids, residual) + (part[...] + got[...].astype(F32) + vec[5:6, :])
+    to_owners(ids, result, wide, here, there)
+
+
+def fc2_kernel(ids, hidden, w0, w1, w2, w3, keep, send):
+    for m, weight in enumerate((w0, w1, w2, w3)):
+        split_rows(dot(hidden[...], weight[...], NT), keep, send, lanes(m))
+
+
+def give_kernel(ids, slots, here, away, out):
+    left = here[0:PAD, :].astype(F32)
+    right = away[0:PAD, :].astype(F32)
+    for c in range(8):
+        value = jnp.where(slots[8 + c : 9 + c, 0:1] > 0.5, right, 0.0)
+        out[c, :, :] = jnp.where(slots[c : c + 1, 0:1] > 0.5, left, value).astype(BF16)
+
+
+def give_grad_kernel(ids, slots, here, s1, away, s3, out, rel, flat, tail):
+    left = here[0:PAD, :].astype(F32)
+    right = away[0:PAD, :].astype(F32)
+    own = here[PAD : PAD + 8, :].astype(F32)
+    far = away[PAD : PAD + 8, :].astype(F32)
+    rel[...] = own + far + s1[...].astype(F32) + s3[...].astype(F32)
+    home = pick(is_zero(ids[CORE_ID]), own, far)
+    for m in range(4):
+        flat[:, chip_lanes(ids, m)] = rel[:, lanes(m)]
+    tail[...] = jnp.zeros_like(tail)
+    for k in range(8):
+        row, lane = (SHARE + k, 128) if k < 7 else (SHARE, 256)
+        tail[row : row + 1, lane : lane + 128] = home[6:7, 128 * k : 128 * k + 128]
+    row = row_ids((PAD, 1024))
+    for c in range(8):
+        cols = slice(128 * c, 128 * c + 128)
+        tail[SHARE : SHARE + 6, 0:128] = flat[0:6, cols]
+        tail[SHARE + 6 : PAD, 0:128] = home[7:8, cols]
+        value = jnp.where(slots[8 + c : 9 + c, 0:1] > 0.5, right, 0.0)
+        value = jnp.where(slots[c : c + 1, 0:1] > 0.5, left, value)
+        out[c, :, :] = jnp.where(row < SHARE, value, tail[...]).astype(BF16)
+
+
+def take_kernel(ids, got, out, wide):
+    for c in range(8):
+        wide[SHARE * c : SHARE * c + SHARE, :] = got[c, :, :].astype(F32)[0:SHARE]
+    out[...] = wide[...].astype(out.dtype)
+
+
+def take_grad_kernel(ids, got, out, gains, biases, last, qv, b_fc1):
+    total = jnp.zeros((8, 384), F32)
+    for c in range(8):
+        out[SHARE * c : SHARE * c + SHARE, :] = got[c, :, :].astype(F32)[0:SHARE]
+        total = total + got[c, PAD - 8 : PAD, 0:384].astype(F32)
+    rows = pltpu.roll(total[:, 0:128], (128 - 32 * ids[T_ID]) & 127, 1)
+    gains[...] = rows[1:3, 0:32]
+    biases[...] = rows[3:7, 0:32]
+    last[...] = rows[6:7, 0:32]
+    b_fc1[...] = total[7:8, 0:128]
+    parts = jnp.concatenate([total[1:8, 128:256], total[1:2, 256:384]], axis=0)
+    qv[...] = pltpu.roll(parts, (128 - 8 * ids[D_ID]) & 127, 1)[:, 0:8]
+
+
+def shards_kernel(ids, qkv, proj, fc1, fc2, first, second, third):
+    for j in range(3):
+        first[:, lanes(j)] = qkv[j, :, :]
+    second[:, 0:256] = jnp.transpose(proj[...])
+    second[:, 256:1280] = fc1[...]
+    third[...] = jnp.transpose(fc2[...])
+
+
+def offer_kernel(ids, own, far, send):
+    @pl.when(ids[CORE_ID] == 0)
+    def _():
+        send[...] = far[...]
+
+    @pl.when(ids[CORE_ID] != 0)
+    def _():
+        send[...] = own[...]
+
+
+def merge_kernel(ids, own, far, got, out):
+    half = own.shape[0]
+
+    @pl.when(ids[CORE_ID] == 0)
+    def _():
+        out[0:half, :] = own[...]
+        out[half:, :] = got[...]
+
+    @pl.when(ids[CORE_ID] != 0)
+    def _():
+        out[0:half, :] = got[...]
+        out[half:, :] = far[...]
+
+
+def grads_of(near, far, first_col=0):
+    def grads_kernel(ids, left, right, send, here, there):
+        for slot, m in ((0, near), (1, 3)):
+            send[slot, :, :] = dot(left[:, lanes(m)], right[...], TN).astype(BF16)
+        here[...] = dot(left[:, lanes(0)], right[...], TN)
+        there[...] = dot(left[:, lanes(far)], right[...], TN)
+
+    return grads_kernel
+
+
+def sum_grad(ids, left, right, x_first):
+    first, second, near, far = (X, Y, 1, 2) if x_first else (Y, X, 2, 1)
+    n = right.shape[1]
+    send, here, there = call(
+        grads_of(near, far),
+        [((2, 256, n), BF16), ((256, n), F32), ((256, n), F32)],
+        ids,
+        left,
+        right,
+        flops=2 * left.shape[0] * 1024 * n,
+    )
+    got = swap(send, first)
+    other = (there + got[1].astype(F32)).astype(BF16)
+    whole = here + got[0].astype(F32)
+    return whole + swap(other, second).astype(F32)
+
+
+def settle_grad(part, core):
+    pairs = [(i, i ^ Z_HIGH) for i in range(32) if i & CORE]
+    moved = lax.ppermute(part.astype(BF16), AXES, pairs).astype(F32)
+    part = jnp.where(core == 0, part, moved)
+    low, high = part[:128], part[128:]
+    send = jnp.where(core == 0, high, low)
+    keep = jnp.where(core == 0, low, high)
+    return keep + swap(send.astype(BF16), CORE).astype(F32)
+
+
+def on_device_spread(
+    clip_rows,
+    out_grad,
+    clip_valid,
+    gain_rows,
+    bias_rows,
+    qkv_weight,
+    qv_bias,
+    proj_weight,
+    fc1_weight,
+    fc1_bias,
+    fc2_weight,
+):
+    d, t = lax.axis_index("dp"), lax.axis_index("tensor")
+    core = d & 1
+    ids = jnp.stack([d >> 1, core, d, t, clip_valid[0]]).astype(jnp.int32)
+    count = clip_rows.shape[0]
+    half, own = count // 2, count // 4
+    block = (8, PAD, 1024)
+    behind = (PAD + 8, 1024)
+
+    (sent,) = call(
+        pack_kernel,
+        [(block, BF16)],
+        ids,
+        clip_rows,
+        gain_rows,
+        bias_rows,
+        qv_bias.reshape(8, 8),
+        fc1_bias,
+        scratch=[((400, 1024), F32)],
+    )
+    shards = call(
+        shards_kernel,
+        [((128, 768), BF16), ((128, 1280), BF16), ((128, 1024), BF16)],
+        ids,
+        qkv_weight,
+        proj_weight,
+        fc1_weight,
+        fc2_weight,
+    )
+
+    def gather(shard, by_y):
+        far = swap(shard, Z_HIGH)
+        (send,) = call(offer_kernel, [(shard.shape, BF16)], ids, shard, far)
+        (w0,) = call(
+            merge_kernel, [((256, shard.shape[1]), BF16)], ids, shard, far, swap(send, CORE)
+        )
+        w1, w2 = swap(w0, X), swap(w0, Y)
+        return w0, w1, w2, (swap(w1, Y) if by_y else swap(w2, X))
+
+    got = lax.all_to_all(sent, "dp", 0, 0)
+    w_qkv = gather(shards[0], True)
+    here, there, slots = call(
+        pick_kernel, [(behind, BF16), (behind, BF16), ((16, 128), F32)], ids, got
+    )
+    r1, r2, r3 = swap(here, Z_LOW), swap(there, Z_HIGH), swap(there, Z_LOW | Z_HIGH)
+    rows, normed, vec, qkv_bias, b_fc1 = call(
+        norm_one_kernel,
+        [
+            ((half, 1024), BF16),
+            ((half, 1024), BF16),
+            ((8, 1024), F32),
+            ((8, 128), F32),
+            ((1, 1024), F32),
+        ],
+        ids,
+        here,
+        r1,
+        r2,
+        r3,
+        scratch=[((half, 1024), F32), ((8, 1024), F32)],
+    )
+    late = lax.optimization_barrier((shards[1], shards[2], out_grad, here))
+    w_mid = gather(late[0], False)
+    w_fc2 = gather(late[1], True)
+
+    wide = ((count, 1024), F32)
+    whole_one, *qkv = call(
+        qkv_kernel,
+        [((count, 1024), BF16)] + [((count, 192), BF16)] * 4,
+        ids,
+        normed,
+        swap(normed, CORE),
+        qkv_bias,
+        *w_qkv,
+        scratch=[wide, ((4, count, 192), BF16)],
+        flops=2 * count * 1024 * 768,
+    )
+
+    def trade(parts):
+        return [parts[0]] + [swap(parts[m], CHIP_MASKS[m]) for m in range(1, 4)]
+
+    qkv = trade(qkv)
+    tokens = 4 * count
+    *mixed, lse = call(
+        attention_kernel,
+        [((count, 64), BF16)] * 4 + [((tokens // STEP, 8, STEP), F32)],
+        ids,
+        *qkv,
+        scratch=[((tokens, 192), F32)] + [((tokens, 64), BF16)] * 3,
+        flops=4 * tokens * tokens * 64,
+    )
+    attended, keep, send = call(
+        proj_kernel,
+        [((count, 256), BF16), ((half, 1024), F32), ((half, 1024), BF16)],
+        ids,
+        *trade(mixed),
+        *w_mid,
+        scratch=[((4, count, 64), BF16)],
+        flops=2 * count * 1024 * 256,
+    )
+
+    def all_z(keep, send):
+        part, send = call(
+            pair_kernel,
+            [((half, 1024), F32), ((half, 1024), BF16)],
+            ids,
+            keep,
+            swap(send, CORE),
+        )
+        return part, swap(send, Z_LOW)
+
+    def one_z(keep, send):
+        part, send = call(
+            half_kernel, [((own, 1024), F32), ((own, 1024), BF16)], ids, keep, swap(send, CORE)
+        )
+        return part, swap(send, Z_LOW)
+
+    residual, normed_two = call(
+        norm_two_kernel,
+        [((half, 1024), F32), ((half, 1024), BF16)],
+        ids,
+        rows,
+        *all_z(keep, send),
+        vec,
+    )
+
+    (sent,) = call(
+        pack_grad_kernel, [(block, BF16)], ids, late[2], scratch=[((400, 1024), F32)]
+    )
+    got = lax.all_to_all(sent, "dp", 0, 0)
+    here, there = call(pick_grad_kernel, [((PAD, 1024), BF16)] * 2, ids, slots, got)
+    r1, r2, r3 = swap(here, Z_LOW), swap(there, Z_HIGH), swap(there, Z_LOW | Z_HIGH)
+    (grads,) = call(
+        lay_grad_kernel,
+        [((half, 1024), BF16)],
+        ids,
+        here,
+        r1,
+        r2,
+        r3,
+        scratch=[((half, 1024), F32)],
+    )
+    whole_mlp, grad_hidden = call(
+        grad_hidden_kernel,
+        [((count, 1024), BF16), ((count, 1024), F32)],
+        ids,
+        grads,
+        swap(grads, CORE),
+        *w_fc2,
+        scratch=[wide],
+        flops=2 * count * 1024 * 1024,
+    )
+
+    whole_two, hidden, grad_pre, sums_fc1, keep, send = call(
+        fc_kernel,
+        [((count, 1024), BF16)] * 3
+        + [((1, 1024), F32), ((half, 1024), F32), ((half, 1024), BF16)],
+        ids,
+        normed_two,
+        swap(normed_two, CORE),
+        grad_hidden,
+        b_fc1,
+        *w_mid,
+        scratch=[wide],
+        flops=4 * count * 1024 * 1024,
+    )
+    grad_residual, grad_branch, sums_two = call(
+        norm_two_back_kernel,
+        [((half, 1024), F32), ((half, 1024), BF16), ((8, 1024), F32)],
+        ids,
+        residual,
+        *all_z(keep, send),
+        grads,
+        vec,
+    )
+
+    whole_branch, *grad_att = call(
+        grad_att_kernel,
+        [((count, 1024), BF16)] + [((count, 64), BF16)] * 4,
+        ids,
+        grad_branch,
+        swap(grad_branch, CORE),
+        *w_mid,
+        scratch=[wide, ((4, count, 64), BF16)],
+        flops=2 * count * 1024 * 256,
+    )
+    grad_qkv = call(
+        attention_back_kernel,
+        [((count, 192), BF16)] * 4,
+        ids,
+        *qkv,
+        *trade(grad_att),
+        lse,
+        scratch=[((tokens, 192), F32)] + [((tokens, 64), BF16)] * 4 + [((tokens, 64), F32)] * 2,
+        flops=10 * tokens * tokens * 64,
+    )
+    joined, keep, send, sums_qv = call(
+        qkv_back_kernel,
+        [((count, 768), BF16), ((half, 1024), F32), ((half, 1024), BF16), ((1, 1024), F32)],
+        ids,
+        *trade(grad_qkv),
+        *w_qkv,
+        scratch=[((4, count, 192), BF16)],
+        flops=2 * count * 1024 * 768,
+    )
+    here, there, small = call(
+        norm_one_back_kernel,
+        [(behind, BF16), (behind, BF16), ((8, 1024), BF16)],
+        ids,
+        rows,
+        *one_z(keep, send),
+        grad_residual,
+        vec,
+        sums_two,
+        sums_fc1,
+        sums_qv,
+        scratch=[((2 * PAD, 1024), F32)],
+    )
+    (sent,) = call(
+        give_grad_kernel,
+        [(block, BF16)],
+        ids,
+        slots,
+        here,
+        swap(small, Z_LOW),
+        swap(there, Z_HIGH),
+        swap(small, Z_LOW | Z_HIGH),
+        scratch=[((8, 1024), F32), ((8, 1024), F32), ((PAD, 1024), F32)],
+    )
+    input_grad, grad_gains, grad_biases, grad_last, grad_qv, grad_b_fc1 = call(
+        take_grad_kernel,
+        [
+            ((count, 1024), F32),
+            ((2, 32), F32),
+            ((4, 32), F32),
+            ((1, 32), F32),
+            ((8, 8), F32),
+            ((1, 128), F32),
+        ],
+        ids,
+        lax.all_to_all(sent, "dp", 0, 0),
+    )
+
+    keep, send = call(
+        fc2_kernel,
+        [((half, 1024), F32), ((half, 1024), BF16)],
+        ids,
+        hidden,
+        *w_fc2,
+        flops=2 * count * 1024 * 1024,
+    )
+    here, there = call(
+        layer_out_kernel,
+        [((PAD, 1024), BF16)] * 2,
+        ids,
+        residual,
+        *one_z(keep, send),
+        vec,
+        scratch=[((2 * PAD, 1024), F32)],
+    )
+    (sent,) = call(
+        give_kernel, [(block, BF16)], ids, slots, here, swap(there, Z_HIGH)
+    )
+    (layer_out,) = call(
+        take_kernel,
+        [((count, 1024), BF16)],
+        ids,
+        lax.all_to_all(sent, "dp", 0, 0),
+        scratch=[((count, 1024), F32)],
+    )
+
+    grad_fc2 = settle_grad(sum_grad(ids, whole_mlp, hidden, True), core)
+    grad_fc1 = settle_grad(sum_grad(ids, whole_two, grad_pre, False), core)
+    grad_proj = settle_grad(sum_grad(ids, whole_branch, attended, True), core)
+    grad_w = settle_grad(sum_grad(ids, whole_one, joined, False), core)
+    return (
+        layer_out,
+        input_grad,
+        grad_gains,
+        grad_biases,
+        jnp.transpose(grad_w.reshape(128, 3, 256), (1, 0, 2)),
+        grad_qv.reshape(2, 4, 8),
+        jnp.transpose(grad_proj),
+        grad_fc1,
+        grad_b_fc1,
+        jnp.transpose(grad_fc2),
+        grad_last[0],
+    )
+
+
 def solution(mesh):
+    spread = (mesh.shape["dp"], mesh.shape["tensor"]) == (8, 4)
     in_specs = (
         P(("dp", "tensor"), None),
         P(("dp", "tensor"), None),
@@ -333,5 +1211,5 @@
         P(("dp", "tensor")),
     )
     return jax.shard_map(
-        on_device, mesh=mesh, in_specs=in_specs, out_specs=out_specs, check_vma=False
-    )
+        on_device_spread if spread else on_device, mesh=mesh, in_specs=in_specs, out_specs=out_specs, check_vma=False
+    )

time: 1640 us -> 371 us (0.23)
  waiting for transfers between devices: 1160 us -> 156 us
  matrix products: 180 us -> 0 us
  blocking collectives: 173 us -> 0 us
  starting transfers between devices: 1.33 us -> 82.2 us
  Pallas kernels: 0 us -> 79.1 us
  other arithmetic: 70.3 us -> 24.4 us
    reduce_scatter x8 -> x0, waiting for transfers between devices: 611 us -> none  [the longest x2 224 us: reduce_rows(): lax.psum_scatter(term_fn(jnp.int32(0), lax.axis_size('tensor') * row_coun...]
    all_gather x7 -> x0, waiting for transfers between devices: 278 us -> none  [the longest x2 132 us: spread_grads(): return lax.all_gather(local_rows, 'tensor', axis=0, tiled=True)]
    unnamed x21 -> x0, waiting for transfers between devices: 274 us -> none
    dot_general x18 -> x0, matrix products: 180 us -> none  [the longest x1 26.3 us: backward(): jnp.einsum('qhd,khd->hqk', grad_att, values_all, preferred_element_type=j...]
    all_gather x5 -> x0, blocking collectives: 161 us -> none  [the longest x1 69.5 us: fetch(): lax.all_gather(gain_rows, ('dp', 'tensor'), axis=1, tiled=True)]
    ppermute x0 -> x65, waiting for transfers between devices: none -> 137 us  [the longest x61 137 us: swap(): return lax.ppermute(value, AXES, [(i, i ^ mask) for i in range(32)])]
    pallas_call x0 -> x38, Pallas kernels: none -> 79.1 us  [call(): pl.pallas_call(body, out_shape=[jax.ShapeDtypeStruct(s, t) for s, t in ou...]
    ppermute x0 -> x65, starting transfers between devices: none -> 65.4 us  [the longest x61 60.2 us: swap(): return lax.ppermute(value, AXES, [(i, i ^ mask) for i in range(32)])]
  transfers between devices with their start and end apart: 18 -> 69, of which waited for: 17 -> 27; matrix products, arithmetic and copies ran while one was open for 4% -> 7% of each run, Pallas kernels for 0% -> 19%
where the time goes in v2:
time: 371 us; the launch traced here: 369 us
  waiting for transfers between devices  156 us (42%)
  starting transfers between devices  82.2 us (22%)
  Pallas kernels  79.1 us (21%)
  local copies, waits for them, and re-layouts  25.3 us (7%)
  other arithmetic  24.4 us (7%)
    ppermute x61, waiting for transfers between devices, swap(): return lax.ppermute(value, AXES, [(i, i ^ mask) for i in range(32)])  137 us
    pallas_call x38, Pallas kernels, call(): pl.pallas_call(body, out_shape=[jax.ShapeDtypeStruct(s, t) for s, t in ou...  79.1 us
    ppermute x61, starting transfers between devices, swap(): return lax.ppermute(value, AXES, [(i, i ^ mask) for i in range(32)])  60.2 us
    unnamed x131, local copies, waits for them, and re-layouts  25.1 us
    all_to_all x2, waiting for transfers between devices, on_device_spread(): got = lax.all_to_all(sent, 'dp', 0, 0)  13.3 us
    all_to_all x2, starting transfers between devices, on_device_spread(): got = lax.all_to_all(sent, 'dp', 0, 0)  8.72 us
    all_to_all x2, starting transfers between devices, on_device_spread(): lax.all_to_all(sent, 'dp', 0, 0)  8 us
    convert_element_type x4, other arithmetic, settle_grad(): moved = lax.ppermute(part.astype(BF16), AXES, pairs).astype(F32)  7.45 us
  transfers between devices with their start and end apart: 69, of which 27 were waited for; matrix products, arithmetic and copies ran while one was open for 7% of the time, Pallas kernels for 19%

profile of v2, /device:TPU:0, one launch (start us, length us, event | category | flops | bytes accessed | tf_op | source)
XLA Modules:
  0.0 369.1 jit_solution(8042083627948160611)
XLA Ops:
  5.2 1.8 shard_map.194
  7.0 5.2 %all-to-all-start = ((bf16[8,56,1024]{2,1,0:T(8,128)(2,1)}), bf16[8,56,1024]{2,1,0:T(8,128)(2,1)S(1)}, u32[]{:S(2)}, u32[]{:S(2)}) async-start(bf16[8,56,1024]{2,1,0:T(8,128)(2,1)} %shard_map.194), calls=%async_computation | async-start | bytes 1835008 | tf_op jit(solution)/shard_map/all_to_all | solution.py:934
  12.9 13.3 %all-to-all-done.got = bf16[8,56,1024]{2,1,0:T(8,128)(2,1)S(1)} async-done(((bf16[8,56,1024]{2,1,0:T(8,128)(2,1)}), bf16[8,56,1024]{2,1,0:T(8,128)(2,1)S(1)}, u32[]{:S(2)}, u32[]{:S(2)}) %all-to-all-start) | async-done | bytes 917536 | tf_op jit(solution)/shard_map/all_to_all | solution.py:934
  27.2 2.7 collective-permute-start.15
  29.8 12.0 %collective-permute-done.15.far = bf16[128,1280]{1,0:T(8,128)(2,1)S(1)} collective-permute-done((bf16[128,1280]{1,0:T(8,128)(2,1)S(1)}, bf16[128,1280]{1,0:T(8,128)(2,1)S(1)}, u32[]{:S(2)}, u32[]{:S(2)}) %collective-permute-start.15) | collective-permute-done | bytes 327712 | tf_op jit(solution)/shard_map/ppermute | solution.py:321
  42.6 12.4 %collective-permute-done.4.far = bf16[128,768]{1,0:T(8,128)(2,1)S(1)} collective-permute-done((bf16[128,768]{1,0:T(8,128)(2,1)S(1)}, bf16[128,768]{1,0:T(8,128)(2,1)S(1)}, u32[]{:S(2)}, u32[]{:S(2)}) %collective-permute-start.4) | collective-permute-done | bytes 196640 | tf_op jit(solution)/shard_map/ppermute | solution.py:321
  58.2 3.0 collective-permute-start.6
  63.7 5.8 %collective-permute-done.2.r3 = bf16[64,1024]{1,0:T(8,128)(2,1)S(1)} collective-permute-done((bf16[64,1024]{1,0:T(8,128)(2,1)S(1)}, bf16[64,1024]{1,0:T(8,128)(2,1)S(1)}, u32[]{:S(2)}, u32[]{:S(2)}) %collective-permute-start.2) | collective-permute-done | bytes 131104 | tf_op jit(solution)/shard_map/ppermute | solution.py:321
  69.5 4.5 %collective-permute-done.1.r2 = bf16[64,1024]{1,0:T(8,128)(2,1)S(1)} collective-permute-done((bf16[64,1024]{1,0:T(8,128)(2,1)S(1)}, bf16[64,1024]{1,0:T(8,128)(2,1)S(1)}, u32[]{:S(2)}, u32[]{:S(2)}) %collective-permute-start.1) | collective-permute-done | bytes 131104 | tf_op jit(solution)/shard_map/ppermute | solution.py:321
  80.0 2.2 collective-permute-done.7.w2
  82.2 8.0 %collective-permute-done.8.w3 = bf16[256,768]{1,0:T(8,128)(2,1)S(1)} collective-permute-done((bf16[256,768]{1,0:T(8,128)(2,1)S(1)}, bf16[256,768]{1,0:T(8,128)(2,1)S(1)}, u32[]{:S(2)}, u32[]{:S(2)}) %collective-permute-start.8) | collective-permute-done | bytes 393248 | tf_op jit(solution)/shard_map/ppermute | solution.py:321
  90.2 2.4 shard_map.200
  94.3 3.5 collective-permute-start.9
  99.3 1.7 shard_map.207
  101.0 3.6 all-to-all-start.1
  107.1 6.9 %collective-permute-done.9.a1 = bf16[392,192]{1,0:T(8,128)(2,1)} collective-permute-done((bf16[392,192]{1,0:T(8,128)(2,1)}, bf16[392,192]{1,0:T(8,128)(2,1)}, u32[]{:S(2)}, u32[]{:S(2)}) %collective-permute-start.9) | collective-permute-done | bytes 150560 | tf_op jit(solution)/shard_map/ppermute | solution.py:321
  114.0 4.3 %collective-permute-done.11.a3 = bf16[392,192]{1,0:T(8,128)(2,1)} collective-permute-done((bf16[392,192]{1,0:T(8,128)(2,1)}, bf16[392,192]{1,0:T(8,128)(2,1)}, u32[]{:S(2)}, u32[]{:S(2)}) %collective-permute-start.11) | collective-permute-done | bytes 150560 | tf_op jit(solution)/shard_map/ppermute | solution.py:321
  119.2 8.2 %shard_map.201 = (bf16[392,64]{1,0:T(8,128)(2,1)S(1)}, bf16[392,64]{1,0:T(8,128)(2,1)S(1)}, bf16[392,64]{1,0:T(8,128)(2,1)S(1)}, bf16[392,64]{1,0:T(8,128)(2,1)S(1)}, f32[7,8,224]{2,1,0:T(8,128)S(1)}) custom-call(s32[5]{0:T(128)S(1)} %stack.19.ids, bf16[392,192]{1,0:T(8,128)(2,1)S(1)} %copy-done.53, bf16[392,192]{1,0:T(8,128)(2,1)} %collective-permute-done.9.a1, ...), custom_call_target="tpu_custom_call" | custom-call | flops 629407744 | bytes 852992 | tf_op jit(solution)/shard_map/pallas_call | solution.py:332
  129.7 2.5 collective-permute-done.12.a1
  133.8 4.0 %collective-permute-done.14.a3 = bf16[392,64]{1,0:T(8,128)(2,1)S(1)} collective-permute-done((bf16[392,64]{1,0:T(8,128)(2,1)S(1)}, bf16[392,64]{1,0:T(8,128)(2,1)S(1)}, u32[]{:S(2)}, u32[]{:S(2)}) %collective-permute-start.14) | collective-permute-done | bytes 50208 | tf_op jit(solution)/shard_map/ppermute | solution.py:321
  137.7 1.8 shard_map.204
  145.3 2.1 collective-permute-start.23
  148.7 7.2 %collective-permute-done.29.w1 = bf16[256,1024]{1,0:T(8,128)(2,1)} collective-permute-done((bf16[256,1024]{1,0:T(8,128)(2,1)}, bf16[256,1024]{1,0:T(8,128)(2,1)}, u32[]{:S(2)}, u32[]{:S(2)}) %collective-permute-start.29) | collective-permute-done | bytes 524320 | tf_op jit(solution)/shard_map/ppermute | solution.py:321
  159.5 5.4 %collective-permute-done.25.r3 = bf16[56,1024]{1,0:T(8,128)(2,1)S(1)} collective-permute-done((bf16[56,1024]{1,0:T(8,128)(2,1)S(1)}, bf16[56,1024]{1,0:T(8,128)(2,1)S(1)}, u32[]{:S(2)}, u32[]{:S(2)}) %collective-permute-start.25) | collective-permute-done | bytes 114720 | tf_op jit(solution)/shard_map/ppermute | solution.py:321
  164.9 3.8 %collective-permute-done.24.r2 = bf16[56,1024]{1,0:T(8,128)(2,1)S(1)} collective-permute-done((bf16[56,1024]{1,0:T(8,128)(2,1)S(1)}, bf16[56,1024]{1,0:T(8,128)(2,1)S(1)}, u32[]{:S(2)}, u32[]{:S(2)}) %collective-permute-start.24) | collective-permute-done | bytes 114720 | tf_op jit(solution)/shard_map/ppermute | solution.py:321
  172.2 2.2 shard_map.212
  174.5 6.4 %shard_map.213 = (bf16[392,1024]{1,0:T(8,128)(2,1)S(1)}, bf16[392,1024]{1,0:T(8,128)(2,1)S(1)}, bf16[392,1024]{1,0:T(8,128)(2,1)S(1)}, f32[1,1024]{1,0:T(1,128)S...) custom-call(s32[5]{0:T(128)S(1)} %stack.19.ids, bf16[196,1024]{1,0:T(8,128)(2,1)S(1)} %get-tuple-element.123.own, ...), custom_call_target="tpu_custom_call" | custom-call | flops 1644167168 | bytes 8650752 | tf_op jit(solution)/shard_map/pallas_call | solution.py:332
  181.0 2.6 shard_map.231
  186.8 2.3 shard_map.214
  189.2 8.9 %collective-permute-done.36.got = bf16[196,1024]{1,0:T(8,128)(2,1)S(1)} collective-permute-done((bf16[196,1024]{1,0:T(8,128)(2,1)S(1)}, bf16[196,1024]{1,0:T(8,128)(2,1)S(1)}, u32[]{:S(2)}, u32[]{:S(2)}) %collective-permute-start.36) | collective-permute-done | bytes 401440 | tf_op jit(solution)/shard_map/ppermute | solution.py:321
  198.0 2.2 shard_map.220
  201.7 2.5 shard_map.230
  206.9 7.0 %collective-permute-done.33.got = bf16[98,1024]{1,0:T(8,128)(2,1)S(1)} collective-permute-done((bf16[98,1024]{1,0:T(8,128)(2,1)S(1)}, bf16[98,1024]{1,0:T(8,128)(2,1)S(1)}, u32[]{:S(2)}, u32[]{:S(2)}) %collective-permute-start.33) | collective-permute-done | bytes 200736 | tf_op jit(solution)/shard_map/ppermute | solution.py:321
  217.2 6.8 %collective-permute-done.34.away = bf16[56,1024]{1,0:T(8,128)(2,1)} collective-permute-done((bf16[56,1024]{1,0:T(8,128)(2,1)}, bf16[56,1024]{1,0:T(8,128)(2,1)}, u32[]{:S(2)}, u32[]{:S(2)}) %collective-permute-start.34) | collective-permute-done | bytes 114720 | tf_op jit(solution)/shard_map/ppermute | solution.py:321
  227.0 4.4 %all-to-all-start.2 = ((bf16[8,56,1024]{2,1,0:T(8,128)(2,1)}), bf16[8,56,1024]{2,1,0:T(8,128)(2,1)}, u32[]{:S(2)}, u32[]{:S(2)}) async-start(bf16[8,56,1024]{2,1,0:T(8,128)(2,1)} %copy-done), calls=%async_computation.2 | async-start | bytes 1835008 | tf_op jit(solution)/shard_map/all_to_all | solution.py:1162
  232.6 2.2 shard_map.221
  234.8 1.7 collective-permute-start.38
  239.4 1.7 collective-permute-start.53
  241.2 2.0 fusion
  243.1 3.8 %collective-permute-done.38.g1 = bf16[392,64]{1,0:T(8,128)(2,1)S(1)} collective-permute-done((bf16[392,64]{1,0:T(8,128)(2,1)S(1)}, bf16[392,64]{1,0:T(8,128)(2,1)S(1)}, u32[]{:S(2)}, u32[]{:S(2)}) %collective-permute-start.38) | collective-permute-done | bytes 50208 | tf_op jit(solution)/shard_map/ppermute | solution.py:321
  250.0 12.7 %shard_map.222 = (bf16[392,192]{1,0:T(8,128)(2,1)S(1)}, bf16[392,192]{1,0:T(8,128)(2,1)S(1)}, bf16[392,192]{1,0:T(8,128)(2,1)S(1)}, bf16[392,192]{1,0:T(8,128)(2,1)S(1)}) custom-call(s32[5]{0:T(128)S(1)} %stack.19.ids, bf16[392,192]{1,0:T(8,128)(2,1)S(1)} %copy-done.54, bf16[392,192]{1,0:T(8,128)(2,1)} %collective-permute-done.9.a1, ...), custom_call_target="tpu_custom_call" | custom-call | flops 1573519360 | bytes 1455104 | tf_op jit(solution)/shard_map/pallas_call | solution.py:332
  263.6 2.7 collective-permute-start.43
  267.5 2.0 fusion.2
  271.3 3.5 collective-permute-done.42.g2
  274.9 2.3 shard_map.223
  278.1 2.4 shard_map.228
  282.9 2.3 shard_map.218
  286.9 2.2 fusion.7
  291.6 4.3 %collective-permute-start.56 = (bf16[128,256]{1,0:T(8,128)(2,1)S(1)}, bf16[128,256]{1,0:T(8,128)(2,1)S(1)}, u32[]{:S(2)}, u32[]{:S(2)}) collective-permute-start(bf16[128,256]{1,0:T(8,128)(2,1)S(1)} %select_convert_fusion.3), channel_id=1, source_target_pairs={{0,4},{1,5},{2,6},{3,7},{4,0},{5,1},{6,2},{7,3},{8,12},{9,13},{10,... | collective-permute-start | bytes 196616 | tf_op jit(solution)/shard_map/ppermute | solution.py:321
  296.0 2.2 fusion.6
  299.8 1.8 shard_map.224
  303.1 1.7 copy.27
  304.7 15.5 %collective-permute-done.45.got = bf16[98,1024]{1,0:T(8,128)(2,1)S(1)} collective-permute-done((bf16[98,1024]{1,0:T(8,128)(2,1)}, bf16[98,1024]{1,0:T(8,128)(2,1)S(1)}, u32[]{:S(2)}, u32[]{:S(2)}) %collective-permute-start.45) | collective-permute-done | bytes 200736 | tf_op jit(solution)/shard_map/ppermute | solution.py:321
  325.8 3.7 collective-permute-start.47
  329.4 1.7 convert_select_fusion
  333.8 1.7 convert_select_fusion.1
  335.5 7.0 %collective-permute-done.50 = bf16[256,768]{1,0:T(8,128)(2,1)S(1)} collective-permute-done((bf16[256,768]{1,0:T(8,128)(2,1)S(1)}, bf16[256,768]{1,0:T(8,128)(2,1)S(1)}, u32[]{:S(2)}, u32[]{:S(2)}) %collective-permute-start.50) | collective-permute-done | bytes 393248 | tf_op jit(solution)/shard_map/ppermute | solution.py:321
  342.5 2.0 fusion.10
  346.8 1.8 shard_map.226
  348.6 3.6 all-to-all-start.3
  355.7 2.3 collective-permute-start.52
  358.0 1.8 convert_add_fusion.6
  359.8 6.2 %all-to-all-done.3.got = bf16[8,56,1024]{2,1,0:T(8,128)(2,1)S(1)} async-done(((bf16[8,56,1024]{2,1,0:T(8,128)(2,1)}), bf16[8,56,1024]{2,1,0:T(8,128)(2,1)S(1)}, u32[]{:S(2)}, u32[]{:S(2)}) %all-to-all-start.3) | async-done | bytes 917536 | tf_op jit(solution)/shard_map/all_to_all | solution.py:1135
  366.1 1.9 shard_map.227
  (265 shorter events, 93.0 us)
Async XLA Ops:
  7.0 19.2 %all-to-all-start = ((bf16[8,56,1024]{2,1,0:T(8,128)(2,1)}), bf16[8,56,1024]{2,1,0:T(8,128)(2,1)S(1)}, u32[]{:S(2)}, u32[]{:S(2)}) async-start(bf16[8,56,1024]{2,1,0:T(8,128)(2,1)} %shard_map.194), calls=%async_computation | async-start | bytes 1835008 | tf_op jit(solution)/shard_map/all_to_all | solution.py:934
  27.2 14.7 %collective-permute-start.15 = (bf16[128,1280]{1,0:T(8,128)(2,1)S(1)}, bf16[128,1280]{1,0:T(8,128)(2,1)S(1)}, u32[]{:S(2)}, u32[]{:S(2)}) collective-permute-start(bf16[128,1280]{1,0:T(8,128)(2,1)S(1)} %get-tuple-element.116.own), channel_id=1, source_target_pairs={{0,2},{1,3},{2,0},{3,1},{4,6},{5,7},{6,4},{7,5},{8,10},{9,11},{10,... | collective-permute-start | bytes 983048 | tf_op jit(solution)/shard_map/ppermute | solution.py:321
  42.4 13.2 %collective-permute-start.16 = (bf16[128,1280]{1,0:T(8,128)(2,1)S(1)}, bf16[128,1280]{1,0:T(8,128)(2,1)S(1)}, u32[]{:S(2)}, u32[]{:S(2)}) collective-permute-start(bf16[128,1280]{1,0:T(8,128)(2,1)S(1)} %shard_map.202), channel_id=1, source_target_pairs={{0,4},{1,5},{2,6},{3,7},{4,0},{5,1},{6,2},{7,3},{8,12},{9,13},{10,... | collective-permute-start | bytes 983048 | tf_op jit(solution)/shard_map/ppermute | solution.py:321
  42.5 12.4 %collective-permute-start.4 = (bf16[128,768]{1,0:T(8,128)(2,1)S(1)}, bf16[128,768]{1,0:T(8,128)(2,1)S(1)}, u32[]{:S(2)}, u32[]{:S(2)}) collective-permute-start(bf16[128,768]{1,0:T(8,128)(2,1)S(1)} %get-tuple-element.105.own), channel_id=1, source_target_pairs={{0,2},{1,3},{2,0},{3,1},{4,6},{5,7},{6,4},{7,5},{8,10},{9,11},{10,... | collective-permute-start | bytes 589832 | tf_op jit(solution)/shard_map/ppermute | solution.py:321
  56.2 22.5 %collective-permute-start.18 = (bf16[256,1280]{1,0:T(8,128)(2,1)S(1)}, bf16[256,1280]{1,0:T(8,128)(2,1)S(1)}, u32[]{:S(2)}, u32[]{:S(2)}) collective-permute-start(bf16[256,1280]{1,0:T(8,128)(2,1)S(1)} %shard_map.203.w0), channel_id=1, source_target_pairs={{0,16},{1,17},{2,18},{3,19},{4,20},{5,21},{6,22},{7,23},{8,24},{9,... | collective-permute-start | bytes 1966088 | tf_op jit(solution)/shard_map/ppermute | solution.py:321
  58.2 18.2 %collective-permute-start.6 = (bf16[256,768]{1,0:T(8,128)(2,1)S(1)}, bf16[256,768]{1,0:T(8,128)(2,1)S(1)}, u32[]{:S(2)}, u32[]{:S(2)}) collective-permute-start(bf16[256,768]{1,0:T(8,128)(2,1)S(1)} %shard_map.199.w0), channel_id=1, source_target_pairs={{0,8},{1,9},{2,10},{3,11},{4,12},{5,13},{6,14},{7,15},{8,0},{9,1},... | collective-permute-start | bytes 1179656 | tf_op jit(solution)/shard_map/ppermute | solution.py:321
  61.2 8.3 %collective-permute-start.2 = (bf16[64,1024]{1,0:T(8,128)(2,1)S(1)}, bf16[64,1024]{1,0:T(8,128)(2,1)S(1)}, u32[]{:S(2)}, u32[]{:S(2)}) collective-permute-start(bf16[64,1024]{1,0:T(8,128)(2,1)S(1)} %get-tuple-element.101), channel_id=1, source_target_pairs={{0,3},{1,2},{2,1},{3,0},{4,7},{5,6},{6,5},{7,4},{8,11},{9,10},{10,... | collective-permute-start | bytes 393224 | tf_op jit(solution)/shard_map/ppermute | solution.py:321
  62.3 19.8 %collective-permute-start.7 = (bf16[256,768]{1,0:T(8,128)(2,1)S(1)}, bf16[256,768]{1,0:T(8,128)(2,1)S(1)}, u32[]{:S(2)}, u32[]{:S(2)}) collective-permute-start(bf16[256,768]{1,0:T(8,128)(2,1)S(1)} %shard_map.199.w0), channel_id=1, source_target_pairs={{0,16},{1,17},{2,18},{3,19},{4,20},{5,21},{6,22},{7,23},{8,24},{9,... | collective-permute-start | bytes 1179656 | tf_op jit(solution)/shard_map/ppermute | solution.py:321
  63.7 10.3 %collective-permute-start.1 = (bf16[64,1024]{1,0:T(8,128)(2,1)S(1)}, bf16[64,1024]{1,0:T(8,128)(2,1)S(1)}, u32[]{:S(2)}, u32[]{:S(2)}) collective-permute-start(bf16[64,1024]{1,0:T(8,128)(2,1)S(1)} %get-tuple-element.101), channel_id=1, source_target_pairs={{0,2},{1,3},{2,0},{3,1},{4,6},{5,7},{6,4},{7,5},{8,10},{9,11},{10,... | collective-permute-start | bytes 393224 | tf_op jit(solution)/shard_map/ppermute | solution.py:321
  69.5 5.9 %collective-permute-start = (bf16[64,1024]{1,0:T(8,128)(2,1)S(1)}, bf16[64,1024]{1,0:T(8,128)(2,1)S(1)}, u32[]{:S(2)}, u32[]{:S(2)}) collective-permute-start(bf16[64,1024]{1,0:T(8,128)(2,1)S(1)} %get-tuple-element.100.here), channel_id=1, source_target_pairs={{0,1},{1,0},{2,3},{3,2},{4,5},{5,4},{6,7},{7,6},{8,9},{9,8},{10,11... | collective-permute-start | bytes 393224 | tf_op jit(solution)/shard_map/ppermute | solution.py:321
  76.3 13.9 %collective-permute-start.3 = (bf16[196,1024]{1,0:T(8,128)(2,1)S(1)}, bf16[196,1024]{1,0:T(8,128)(2,1)S(1)}, u32[]{:S(2)}, u32[]{:S(2)}) collective-permute-start(bf16[196,1024]{1,0:T(8,128)(2,1)S(1)} %get-tuple-element.103.own), channel_id=1, source_target_pairs={{0,4},{1,5},{2,6},{3,7},{4,0},{5,1},{6,2},{7,3},{8,12},{9,13},{10,... | collective-permute-start | bytes 1204232 | tf_op jit(solution)/shard_map/ppermute | solution.py:321
  76.4 13.8 %collective-permute-start.8 = (bf16[256,768]{1,0:T(8,128)(2,1)S(1)}, bf16[256,768]{1,0:T(8,128)(2,1)S(1)}, u32[]{:S(2)}, u32[]{:S(2)}) collective-permute-start(bf16[256,768]{1,0:T(8,128)(2,1)S(1)} %collective-permute-done.6.w1), channel_id=1, source_target_pairs={{0,16},{1,17},{2,18},{3,19},{4,20},{5,21},{6,22},{7,23},{8,24},{9,... | collective-permute-start | bytes 1179656 | tf_op jit(solution)/shard_map/ppermute | solution.py:321
  77.9 59.8 %collective-permute-start.17 = (bf16[256,1280]{1,0:T(8,128)(2,1)S(1)}, bf16[256,1280]{1,0:T(8,128)(2,1)}, u32[]{:S(2)}, u32[]{:S(2)}) collective-permute-start(bf16[256,1280]{1,0:T(8,128)(2,1)S(1)} %shard_map.203.w0), channel_id=1, source_target_pairs={{0,8},{1,9},{2,10},{3,11},{4,12},{5,13},{6,14},{7,15},{8,0},{9,1},... | collective-permute-start | bytes 1966088 | tf_op jit(solution)/shard_map/ppermute | solution.py:321
  78.6 59.1 %collective-permute-start.19 = (bf16[256,1280]{1,0:T(8,128)(2,1)S(1)}, bf16[256,1280]{1,0:T(8,128)(2,1)}, u32[]{:S(2)}, u32[]{:S(2)}) collective-permute-start(bf16[256,1280]{1,0:T(8,128)(2,1)S(1)} %collective-permute-done.18.w2), channel_id=1, source_target_pairs={{0,8},{1,9},{2,10},{3,11},{4,12},{5,13},{6,14},{7,15},{8,0},{9,1},... | collective-permute-start | bytes 1966088 | tf_op jit(solution)/shard_map/ppermute | solution.py:321
  82.2 16.0 %collective-permute-start.27 = (bf16[128,1024]{1,0:T(8,128)(2,1)S(1)}, bf16[128,1024]{1,0:T(8,128)(2,1)S(1)}, u32[]{:S(2)}, u32[]{:S(2)}) collective-permute-start(bf16[128,1024]{1,0:T(8,128)(2,1)S(1)} %get-tuple-element.127.own), channel_id=1, source_target_pairs={{0,2},{1,3},{2,0},{3,1},{4,6},{5,7},{6,4},{7,5},{8,10},{9,11},{10,... | collective-permute-start | bytes 786440 | tf_op jit(solution)/shard_map/ppermute | solution.py:321
  94.3 19.7 %collective-permute-start.9 = (bf16[392,192]{1,0:T(8,128)(2,1)}, bf16[392,192]{1,0:T(8,128)(2,1)}, u32[]{:S(2)}, u32[]{:S(2)}) collective-permute-start(bf16[392,192]{1,0:T(8,128)(2,1)} %get-tuple-element.107), channel_id=1, source_target_pairs={{0,8},{1,9},{2,10},{3,11},{4,12},{5,13},{6,14},{7,15},{8,0},{9,1},... | collective-permute-start | bytes 451592 | tf_op jit(solution)/shard_map/ppermute | solution.py:321
  97.8 16.1 %collective-permute-start.10 = (bf16[392,192]{1,0:T(8,128)(2,1)}, bf16[392,192]{1,0:T(8,128)(2,1)}, u32[]{:S(2)}, u32[]{:S(2)}) collective-permute-start(bf16[392,192]{1,0:T(8,128)(2,1)} %get-tuple-element.108), channel_id=1, source_target_pairs={{0,16},{1,17},{2,18},{3,19},{4,20},{5,21},{6,22},{7,23},{8,24},{9,... | collective-permute-start | bytes 451592 | tf_op jit(solution)/shard_map/ppermute | solution.py:321
  98.2 20.1 %collective-permute-start.11 = (bf16[392,192]{1,0:T(8,128)(2,1)}, bf16[392,192]{1,0:T(8,128)(2,1)}, u32[]{:S(2)}, u32[]{:S(2)}) collective-permute-start(bf16[392,192]{1,0:T(8,128)(2,1)} %get-tuple-element.109), channel_id=1, source_target_pairs={{0,24},{1,25},{2,26},{3,27},{4,28},{5,29},{6,30},{7,31},{8,16},{9,... | collective-permute-start | bytes 451592 | tf_op jit(solution)/shard_map/ppermute | solution.py:321
  101.0 43.3 %all-to-all-start.1 = ((bf16[8,56,1024]{2,1,0:T(8,128)(2,1)}), bf16[8,56,1024]{2,1,0:T(8,128)(2,1)S(1)}, u32[]{:S(2)}, u32[]{:S(2)}) async-start(bf16[8,56,1024]{2,1,0:T(8,128)(2,1)} %shard_map.207), calls=%async_computation.1 | async-start | bytes 1835008 | tf_op jit(solution)/shard_map/all_to_all | solution.py:1024
  114.0 25.7 %collective-permute-start.28 = (bf16[128,1024]{1,0:T(8,128)(2,1)S(1)}, bf16[128,1024]{1,0:T(8,128)(2,1)S(1)}, u32[]{:S(2)}, u32[]{:S(2)}) collective-permute-start(bf16[128,1024]{1,0:T(8,128)(2,1)S(1)} %shard_map.210), channel_id=1, source_target_pairs={{0,4},{1,5},{2,6},{3,7},{4,0},{5,1},{6,2},{7,3},{8,12},{9,13},{10,... | collective-permute-start | bytes 786440 | tf_op jit(solution)/shard_map/ppermute | solution.py:321
  127.5 4.7 %collective-permute-start.12 = (bf16[392,64]{1,0:T(8,128)(2,1)S(1)}, bf16[392,64]{1,0:T(8,128)(2,1)S(1)}, u32[]{:S(2)}, u32[]{:S(2)}) collective-permute-start(bf16[392,64]{1,0:T(8,128)(2,1)S(1)} %get-tuple-element.111), channel_id=1, source_target_pairs={{0,8},{1,9},{2,10},{3,11},{4,12},{5,13},{6,14},{7,15},{8,0},{9,1},... | collective-permute-start | bytes 150536 | tf_op jit(solution)/shard_map/ppermute | solution.py:321
  128.3 5.4 %collective-permute-start.13 = (bf16[392,64]{1,0:T(8,128)(2,1)S(1)}, bf16[392,64]{1,0:T(8,128)(2,1)S(1)}, u32[]{:S(2)}, u32[]{:S(2)}) collective-permute-start(bf16[392,64]{1,0:T(8,128)(2,1)S(1)} %get-tuple-element.112), channel_id=1, source_target_pairs={{0,16},{1,17},{2,18},{3,19},{4,20},{5,21},{6,22},{7,23},{8,24},{9,... | collective-permute-start | bytes 150536 | tf_op jit(solution)/shard_map/ppermute | solution.py:321
  132.2 5.5 %collective-permute-start.14 = (bf16[392,64]{1,0:T(8,128)(2,1)S(1)}, bf16[392,64]{1,0:T(8,128)(2,1)S(1)}, u32[]{:S(2)}, u32[]{:S(2)}) collective-permute-start(bf16[392,64]{1,0:T(8,128)(2,1)S(1)} %get-tuple-element.113), channel_id=1, source_target_pairs={{0,24},{1,25},{2,26},{3,27},{4,28},{5,29},{6,30},{7,31},{8,16},{9,... | collective-permute-start | bytes 150536 | tf_op jit(solution)/shard_map/ppermute | solution.py:321
  141.3 14.6 %collective-permute-start.29 = (bf16[256,1024]{1,0:T(8,128)(2,1)}, bf16[256,1024]{1,0:T(8,128)(2,1)}, u32[]{:S(2)}, u32[]{:S(2)}) collective-permute-start(bf16[256,1024]{1,0:T(8,128)(2,1)} %shard_map.211.w0), channel_id=1, source_target_pairs={{0,8},{1,9},{2,10},{3,11},{4,12},{5,13},{6,14},{7,15},{8,0},{9,1},... | collective-permute-start | bytes 1572872 | tf_op jit(solution)/shard_map/ppermute | solution.py:321
  144.3 25.2 %collective-permute-start.21 = (bf16[196,1024]{1,0:T(8,128)(2,1)}, bf16[196,1024]{1,0:T(8,128)(2,1)}, u32[]{:S(2)}, u32[]{:S(2)}) collective-permute-start(bf16[196,1024]{1,0:T(8,128)(2,1)} %get-tuple-element.120), channel_id=1, source_target_pairs={{0,1},{1,0},{2,3},{3,2},{4,5},{5,4},{6,7},{7,6},{8,9},{9,8},{10,11... | collective-permute-start | bytes 1204232 | tf_op jit(solution)/shard_map/ppermute | solution.py:321
  145.3 13.4 %collective-permute-start.23 = (bf16[56,1024]{1,0:T(8,128)(2,1)S(1)}, bf16[56,1024]{1,0:T(8,128)(2,1)S(1)}, u32[]{:S(2)}, u32[]{:S(2)}) collective-permute-start(bf16[56,1024]{1,0:T(8,128)(2,1)S(1)} %get-tuple-element.125.here), channel_id=1, source_target_pairs={{0,1},{1,0},{2,3},{3,2},{4,5},{5,4},{6,7},{7,6},{8,9},{9,8},{10,11... | collective-permute-start | bytes 344072 | tf_op jit(solution)/shard_map/ppermute | solution.py:321
  147.3 24.2 %collective-permute-start.30 = (bf16[256,1024]{1,0:T(8,128)(2,1)}, bf16[256,1024]{1,0:T(8,128)(2,1)S(1)}, u32[]{:S(2)}, u32[]{:S(2)}) collective-permute-start(bf16[256,1024]{1,0:T(8,128)(2,1)} %shard_map.211.w0), channel_id=1, source_target_pairs={{0,16},{1,17},{2,18},{3,19},{4,20},{5,21},{6,22},{7,23},{8,24},{9,... | collective-permute-start | bytes 1572872 | tf_op jit(solution)/shard_map/ppermute | solution.py:321
  155.9 16.4 %collective-permute-start.31 = (bf16[256,1024]{1,0:T(8,128)(2,1)}, bf16[256,1024]{1,0:T(8,128)(2,1)S(1)}, u32[]{:S(2)}, u32[]{:S(2)}) collective-permute-start(bf16[256,1024]{1,0:T(8,128)(2,1)} %collective-permute-done.29.w1), channel_id=1, source_target_pairs={{0,16},{1,17},{2,18},{3,19},{4,20},{5,21},{6,22},{7,23},{8,24},{9,... | collective-permute-start | bytes 1572872 | tf_op jit(solution)/shard_map/ppermute | solution.py:321
  157.3 7.6 %collective-permute-start.25 = (bf16[56,1024]{1,0:T(8,128)(2,1)S(1)}, bf16[56,1024]{1,0:T(8,128)(2,1)S(1)}, u32[]{:S(2)}, u32[]{:S(2)}) collective-permute-start(bf16[56,1024]{1,0:T(8,128)(2,1)S(1)} %get-tuple-element.126), channel_id=1, source_target_pairs={{0,3},{1,2},{2,1},{3,0},{4,7},{5,6},{6,5},{7,4},{8,11},{9,10},{10,... | collective-permute-start | bytes 344072 | tf_op jit(solution)/shard_map/ppermute | solution.py:321
  158.6 10.1 %collective-permute-start.24 = (bf16[56,1024]{1,0:T(8,128)(2,1)S(1)}, bf16[56,1024]{1,0:T(8,128)(2,1)S(1)}, u32[]{:S(2)}, u32[]{:S(2)}) collective-permute-start(bf16[56,1024]{1,0:T(8,128)(2,1)S(1)} %get-tuple-element.126), channel_id=1, source_target_pairs={{0,2},{1,3},{2,0},{3,1},{4,6},{5,7},{6,4},{7,5},{8,10},{9,11},{10,... | collective-permute-start | bytes 344072 | tf_op jit(solution)/shard_map/ppermute | solution.py:321
  180.9 4.8 %collective-permute-start.35 = (bf16[196,1024]{1,0:T(8,128)(2,1)S(1)}, bf16[196,1024]{1,0:T(8,128)(2,1)S(1)}, u32[]{:S(2)}, u32[]{:S(2)}) collective-permute-start(bf16[196,1024]{1,0:T(8,128)(2,1)S(1)} %get-tuple-element.138), channel_id=1, source_target_pairs={{0,4},{1,5},{2,6},{3,7},{4,0},{5,1},{6,2},{7,3},{8,12},{9,13},{10,... | collective-permute-start | bytes 1204232 | tf_op jit(solution)/shard_map/ppermute | solution.py:321
  184.5 54.9 %collective-permute-start.61 = (bf16[2,256,1024]{2,1,0:T(8,128)(2,1)}, bf16[2,256,1024]{2,1,0:T(8,128)(2,1)}, u32[]{:S(2)}, u32[]{:S(2)}) collective-permute-start(bf16[2,256,1024]{2,1,0:T(8,128)(2,1)} %get-tuple-element.184), channel_id=1, source_target_pairs={{0,8},{1,9},{2,10},{3,11},{4,12},{5,13},{6,14},{7,15},{8,0},{9,1},... | collective-permute-start | bytes 3145736 | tf_op jit(solution)/shard_map/ppermute | solution.py:321
  186.4 11.7 %collective-permute-start.36 = (bf16[196,1024]{1,0:T(8,128)(2,1)S(1)}, bf16[196,1024]{1,0:T(8,128)(2,1)S(1)}, u32[]{:S(2)}, u32[]{:S(2)}) collective-permute-start(bf16[196,1024]{1,0:T(8,128)(2,1)S(1)} %get-tuple-element.140), channel_id=1, source_target_pairs={{0,1},{1,0},{2,3},{3,2},{4,5},{5,4},{6,7},{7,6},{8,9},{9,8},{10,11... | collective-permute-start | bytes 1204232 | tf_op jit(solution)/shard_map/ppermute | solution.py:321
  189.1 16.6 %collective-permute-start.32 = (bf16[196,1024]{1,0:T(8,128)(2,1)S(1)}, bf16[196,1024]{1,0:T(8,128)(2,1)S(1)}, u32[]{:S(2)}, u32[]{:S(2)}) collective-permute-start(bf16[196,1024]{1,0:T(8,128)(2,1)S(1)} %get-tuple-element.132), channel_id=1, source_target_pairs={{0,4},{1,5},{2,6},{3,7},{4,0},{5,1},{6,2},{7,3},{8,12},{9,13},{10,... | collective-permute-start | bytes 1204232 | tf_op jit(solution)/shard_map/ppermute | solution.py:321
  201.7 29.8 %collective-permute-start.37 = (bf16[196,1024]{1,0:T(8,128)(2,1)}, bf16[196,1024]{1,0:T(8,128)(2,1)}, u32[]{:S(2)}, u32[]{:S(2)}) collective-permute-start(bf16[196,1024]{1,0:T(8,128)(2,1)} %get-tuple-element.141.own), channel_id=1, source_target_pairs={{0,4},{1,5},{2,6},{3,7},{4,0},{5,1},{6,2},{7,3},{8,12},{9,13},{10,... | collective-permute-start | bytes 1204232 | tf_op jit(solution)/shard_map/ppermute | solution.py:321
  204.3 62.7 %collective-permute-start.57 = (bf16[2,256,1024]{2,1,0:T(8,128)(2,1)}, bf16[2,256,1024]{2,1,0:T(8,128)(2,1)}, u32[]{:S(2)}, u32[]{:S(2)}) collective-permute-start(bf16[2,256,1024]{2,1,0:T(8,128)(2,1)} %get-tuple-element.179), channel_id=1, source_target_pairs={{0,16},{1,17},{2,18},{3,19},{4,20},{5,21},{6,22},{7,23},{8,24},{9,... | collective-permute-start | bytes 3145736 | tf_op jit(solution)/shard_map/ppermute | solution.py:321
  206.4 7.4 %collective-permute-start.33 = (bf16[98,1024]{1,0:T(8,128)(2,1)S(1)}, bf16[98,1024]{1,0:T(8,128)(2,1)S(1)}, u32[]{:S(2)}, u32[]{:S(2)}) collective-permute-start(bf16[98,1024]{1,0:T(8,128)(2,1)S(1)} %get-tuple-element.134), channel_id=1, source_target_pairs={{0,1},{1,0},{2,3},{3,2},{4,5},{5,4},{6,7},{7,6},{8,9},{9,8},{10,11... | collective-permute-start | bytes 602120 | tf_op jit(solution)/shard_map/ppermute | solution.py:321
  215.9 8.0 %collective-permute-start.34 = (bf16[56,1024]{1,0:T(8,128)(2,1)}, bf16[56,1024]{1,0:T(8,128)(2,1)}, u32[]{:S(2)}, u32[]{:S(2)}) collective-permute-start(bf16[56,1024]{1,0:T(8,128)(2,1)} %get-tuple-element.136), channel_id=1, source_target_pairs={{0,2},{1,3},{2,0},{3,1},{4,6},{5,7},{6,4},{7,5},{8,10},{9,11},{10,... | collective-permute-start | bytes 344072 | tf_op jit(solution)/shard_map/ppermute | solution.py:321
  227.0 55.9 %all-to-all-start.2 = ((bf16[8,56,1024]{2,1,0:T(8,128)(2,1)}), bf16[8,56,1024]{2,1,0:T(8,128)(2,1)}, u32[]{:S(2)}, u32[]{:S(2)}) async-start(bf16[8,56,1024]{2,1,0:T(8,128)(2,1)} %copy-done), calls=%async_computation.2 | async-start | bytes 1835008 | tf_op jit(solution)/shard_map/all_to_all | solution.py:1162
  234.8 12.1 %collective-permute-start.38 = (bf16[392,64]{1,0:T(8,128)(2,1)S(1)}, bf16[392,64]{1,0:T(8,128)(2,1)S(1)}, u32[]{:S(2)}, u32[]{:S(2)}) collective-permute-start(bf16[392,64]{1,0:T(8,128)(2,1)S(1)} %get-tuple-element.143), channel_id=1, source_target_pairs={{0,8},{1,9},{2,10},{3,11},{4,12},{5,13},{6,14},{7,15},{8,0},{9,1},... | collective-permute-start | bytes 150536 | tf_op jit(solution)/shard_map/ppermute | solution.py:321
  236.5 11.9 %collective-permute-start.39 = (bf16[392,64]{1,0:T(8,128)(2,1)S(1)}, bf16[392,64]{1,0:T(8,128)(2,1)S(1)}, u32[]{:S(2)}, u32[]{:S(2)}) collective-permute-start(bf16[392,64]{1,0:T(8,128)(2,1)S(1)} %get-tuple-element.144), channel_id=1, source_target_pairs={{0,16},{1,17},{2,18},{3,19},{4,20},{5,21},{6,22},{7,23},{8,24},{9,... | collective-permute-start | bytes 150536 | tf_op jit(solution)/shard_map/ppermute | solution.py:321
  238.0 12.0 %collective-permute-start.40 = (bf16[392,64]{1,0:T(8,128)(2,1)S(1)}, bf16[392,64]{1,0:T(8,128)(2,1)S(1)}, u32[]{:S(2)}, u32[]{:S(2)}) collective-permute-start(bf16[392,64]{1,0:T(8,128)(2,1)S(1)} %get-tuple-element.145), channel_id=1, source_target_pairs={{0,24},{1,25},{2,26},{3,27},{4,28},{5,29},{6,30},{7,31},{8,16},{9,... | collective-permute-start | bytes 150536 | tf_op jit(solution)/shard_map/ppermute | solution.py:321
  239.4 24.2 %collective-permute-start.53 = (bf16[2,256,256]{2,1,0:T(8,128)(2,1)S(1)}, bf16[2,256,256]{2,1,0:T(8,128)(2,1)S(1)}, u32[]{:S(2)}, u32[]{:S(2)}) collective-permute-start(bf16[2,256,256]{2,1,0:T(8,128)(2,1)S(1)} %get-tuple-element.174), channel_id=1, source_target_pairs={{0,8},{1,9},{2,10},{3,11},{4,12},{5,13},{6,14},{7,15},{8,0},{9,1},... | collective-permute-start | bytes 786440 | tf_op jit(solution)/shard_map/ppermute | solution.py:321
  246.9 40.0 %collective-permute-start.62 = (bf16[256,1024]{1,0:T(8,128)(2,1)}, bf16[256,1024]{1,0:T(8,128)(2,1)}, u32[]{:S(2)}, u32[]{:S(2)}) collective-permute-start(bf16[256,1024]{1,0:T(8,128)(2,1)} %fusion), channel_id=1, source_target_pairs={{0,16},{1,17},{2,18},{3,19},{4,20},{5,21},{6,22},{7,23},{8,24},{9,... | collective-permute-start | bytes 1572872 | tf_op jit(solution)/shard_map/ppermute | solution.py:321
  262.7 8.0 %collective-permute-start.41 = (bf16[392,192]{1,0:T(8,128)(2,1)S(1)}, bf16[392,192]{1,0:T(8,128)(2,1)S(1)}, u32[]{:S(2)}, u32[]{:S(2)}) collective-permute-start(bf16[392,192]{1,0:T(8,128)(2,1)S(1)} %get-tuple-element.148), channel_id=1, source_target_pairs={{0,8},{1,9},{2,10},{3,11},{4,12},{5,13},{6,14},{7,15},{8,0},{9,1},... | collective-permute-start | bytes 451592 | tf_op jit(solution)/shard_map/ppermute | solution.py:321
  263.3 11.4 %collective-permute-start.42 = (bf16[392,192]{1,0:T(8,128)(2,1)S(1)}, bf16[392,192]{1,0:T(8,128)(2,1)S(1)}, u32[]{:S(2)}, u32[]{:S(2)}) collective-permute-start(bf16[392,192]{1,0:T(8,128)(2,1)S(1)} %get-tuple-element.149), channel_id=1, source_target_pairs={{0,16},{1,17},{2,18},{3,19},{4,20},{5,21},{6,22},{7,23},{8,24},{9,... | collective-permute-start | bytes 451592 | tf_op jit(solution)/shard_map/ppermute | solution.py:321
  263.6 11.3 %collective-permute-start.43 = (bf16[392,192]{1,0:T(8,128)(2,1)S(1)}, bf16[392,192]{1,0:T(8,128)(2,1)S(1)}, u32[]{:S(2)}, u32[]{:S(2)}) collective-permute-start(bf16[392,192]{1,0:T(8,128)(2,1)S(1)} %get-tuple-element.150), channel_id=1, source_target_pairs={{0,24},{1,25},{2,26},{3,27},{4,28},{5,29},{6,30},{7,31},{8,16},{9,... | collective-permute-start | bytes 451592 | tf_op jit(solution)/shard_map/ppermute | solution.py:321
  267.0 18.3 %collective-permute-start.54 = (bf16[256,256]{1,0:T(8,128)(2,1)}, bf16[256,256]{1,0:T(8,128)(2,1)}, u32[]{:S(2)}, u32[]{:S(2)}) collective-permute-start(bf16[256,256]{1,0:T(8,128)(2,1)} %fusion.8), channel_id=1, source_target_pairs={{0,16},{1,17},{2,18},{3,19},{4,20},{5,21},{6,22},{7,23},{8,24},{9,... | collective-permute-start | bytes 393224 | tf_op jit(solution)/shard_map/ppermute | solution.py:321
  270.7 25.3 %collective-permute-start.58 = (bf16[256,1024]{1,0:T(8,128)(2,1)}, bf16[256,1024]{1,0:T(8,128)(2,1)}, u32[]{:S(2)}, u32[]{:S(2)}) collective-permute-start(bf16[256,1024]{1,0:T(8,128)(2,1)} %fusion.2), channel_id=1, source_target_pairs={{0,8},{1,9},{2,10},{3,11},{4,12},{5,13},{6,14},{7,15},{8,0},{9,1},... | collective-permute-start | bytes 1572872 | tf_op jit(solution)/shard_map/ppermute | solution.py:321
  278.1 21.7 %collective-permute-start.44 = (bf16[196,1024]{1,0:T(8,128)(2,1)}, bf16[196,1024]{1,0:T(8,128)(2,1)}, u32[]{:S(2)}, u32[]{:S(2)}) collective-permute-start(bf16[196,1024]{1,0:T(8,128)(2,1)} %get-tuple-element.152), channel_id=1, source_target_pairs={{0,4},{1,5},{2,6},{3,7},{4,0},{5,1},{6,2},{7,3},{8,12},{9,13},{10,... | collective-permute-start | bytes 1204232 | tf_op jit(solution)/shard_map/ppermute | solution.py:321
  281.4 49.7 %collective-permute-start.49 = (bf16[2,256,768]{2,1,0:T(8,128)(2,1)}, bf16[2,256,768]{2,1,0:T(8,128)(2,1)}, u32[]{:S(2)}, u32[]{:S(2)}) collective-permute-start(bf16[2,256,768]{2,1,0:T(8,128)(2,1)} %get-tuple-element.168), channel_id=1, source_target_pairs={{0,16},{1,17},{2,18},{3,19},{4,20},{5,21},{6,22},{7,23},{8,24},{9,... | collective-permute-start | bytes 2359304 | tf_op jit(solution)/shard_map/ppermute | solution.py:321
  289.1 36.6 %collective-permute-start.63 = (bf16[256,1024]{1,0:T(8,128)(2,1)}, bf16[256,1024]{1,0:T(8,128)(2,1)}, u32[]{:S(2)}, u32[]{:S(2)}) collective-permute-start(bf16[256,1024]{1,0:T(8,128)(2,1)} %fusion.7), channel_id=1, source_target_pairs={{4,6},{5,7},{6,4},{7,5},{12,14},{13,15},{14,12},{15,13},{20,22},{2... | collective-permute-start | bytes 1572872 | tf_op jit(solution)/shard_map/ppermute | solution.py:875
  291.6 10.8 %collective-permute-start.56 = (bf16[128,256]{1,0:T(8,128)(2,1)S(1)}, bf16[128,256]{1,0:T(8,128)(2,1)S(1)}, u32[]{:S(2)}, u32[]{:S(2)}) collective-permute-start(bf16[128,256]{1,0:T(8,128)(2,1)S(1)} %select_convert_fusion.3), channel_id=1, source_target_pairs={{0,4},{1,5},{2,6},{3,7},{4,0},{5,1},{6,2},{7,3},{8,12},{9,13},{10,... | collective-permute-start | bytes 196616 | tf_op jit(solution)/shard_map/ppermute | solution.py:321
  298.2 35.6 %collective-permute-start.59 = (bf16[256,1024]{1,0:T(8,128)(2,1)}, bf16[256,1024]{1,0:T(8,128)(2,1)}, u32[]{:S(2)}, u32[]{:S(2)}) collective-permute-start(bf16[256,1024]{1,0:T(8,128)(2,1)} %fusion.6), channel_id=1, source_target_pairs={{4,6},{5,7},{6,4},{7,5},{12,14},{13,15},{14,12},{15,13},{20,22},{2... | collective-permute-start | bytes 1572872 | tf_op jit(solution)/shard_map/ppermute | solution.py:875
  302.4 17.9 %collective-permute-start.45 = (bf16[98,1024]{1,0:T(8,128)(2,1)}, bf16[98,1024]{1,0:T(8,128)(2,1)S(1)}, u32[]{:S(2)}, u32[]{:S(2)}) collective-permute-start(bf16[98,1024]{1,0:T(8,128)(2,1)} %get-tuple-element.154), channel_id=1, source_target_pairs={{0,1},{1,0},{2,3},{3,2},{4,5},{5,4},{6,7},{7,6},{8,9},{9,8},{10,11... | collective-permute-start | bytes 602120 | tf_op jit(solution)/shard_map/ppermute | solution.py:321
  325.0 21.8 %collective-permute-start.48 = (bf16[8,1024]{1,0:T(8,128)(2,1)S(1)}, bf16[8,1024]{1,0:T(8,128)(2,1)S(1)}, u32[]{:S(2)}, u32[]{:S(2)}) collective-permute-start(bf16[8,1024]{1,0:T(8,128)(2,1)S(1)} %get-tuple-element.160), channel_id=1, source_target_pairs={{0,3},{1,2},{2,1},{3,0},{4,7},{5,6},{6,5},{7,4},{8,11},{9,10},{10,... | collective-permute-start | bytes 49160 | tf_op jit(solution)/shard_map/ppermute | solution.py:321
  325.8 21.0 %collective-permute-start.46 = (bf16[8,1024]{1,0:T(8,128)(2,1)S(1)}, bf16[8,1024]{1,0:T(8,128)(2,1)S(1)}, u32[]{:S(2)}, u32[]{:S(2)}) collective-permute-start(bf16[8,1024]{1,0:T(8,128)(2,1)S(1)} %get-tuple-element.160), channel_id=1, source_target_pairs={{0,1},{1,0},{2,3},{3,2},{4,5},{5,4},{6,7},{7,6},{8,9},{9,8},{10,11... | collective-permute-start | bytes 49160 | tf_op jit(solution)/shard_map/ppermute | solution.py:321
  325.8 21.0 %collective-permute-start.47 = (bf16[64,1024]{1,0:T(8,128)(2,1)S(1)}, bf16[64,1024]{1,0:T(8,128)(2,1)S(1)}, u32[]{:S(2)}, u32[]{:S(2)}) collective-permute-start(bf16[64,1024]{1,0:T(8,128)(2,1)S(1)} %get-tuple-element.161), channel_id=1, source_target_pairs={{0,2},{1,3},{2,0},{3,1},{4,6},{5,7},{6,4},{7,5},{8,10},{9,11},{10,... | collective-permute-start | bytes 393224 | tf_op jit(solution)/shard_map/ppermute | solution.py:321
  332.5 10.0 %collective-permute-start.50 = (bf16[256,768]{1,0:T(8,128)(2,1)S(1)}, bf16[256,768]{1,0:T(8,128)(2,1)S(1)}, u32[]{:S(2)}, u32[]{:S(2)}) collective-permute-start(bf16[256,768]{1,0:T(8,128)(2,1)S(1)} %fusion.4), channel_id=1, source_target_pairs={{0,8},{1,9},{2,10},{3,11},{4,12},{5,13},{6,14},{7,15},{8,0},{9,1},... | collective-permute-start | bytes 1179656 | tf_op jit(solution)/shard_map/ppermute | solution.py:321
  333.8 18.3 %collective-permute-start.64 = (bf16[128,1024]{1,0:T(8,128)(2,1)}, bf16[128,1024]{1,0:T(8,128)(2,1)}, u32[]{:S(2)}, u32[]{:S(2)}) collective-permute-start(bf16[128,1024]{1,0:T(8,128)(2,1)} %select_convert_fusion), channel_id=1, source_target_pairs={{0,4},{1,5},{2,6},{3,7},{4,0},{5,1},{6,2},{7,3},{8,12},{9,13},{10,... | collective-permute-start | bytes 786440 | tf_op jit(solution)/shard_map/ppermute | solution.py:321
  344.6 9.7 %collective-permute-start.51 = (bf16[256,768]{1,0:T(8,128)(2,1)}, bf16[256,768]{1,0:T(8,128)(2,1)}, u32[]{:S(2)}, u32[]{:S(2)}) collective-permute-start(bf16[256,768]{1,0:T(8,128)(2,1)} %fusion.10), channel_id=1, source_target_pairs={{4,6},{5,7},{6,4},{7,5},{12,14},{13,15},{14,12},{15,13},{20,22},{2... | collective-permute-start | bytes 1179656 | tf_op jit(solution)/shard_map/ppermute | solution.py:875
  346.8 11.2 %collective-permute-start.60 = (bf16[128,1024]{1,0:T(8,128)(2,1)}, bf16[128,1024]{1,0:T(8,128)(2,1)}, u32[]{:S(2)}, u32[]{:S(2)}) collective-permute-start(bf16[128,1024]{1,0:T(8,128)(2,1)} %select_convert_fusion.1), channel_id=1, source_target_pairs={{0,4},{1,5},{2,6},{3,7},{4,0},{5,1},{6,2},{7,3},{8,12},{9,13},{10,... | collective-permute-start | bytes 786440 | tf_op jit(solution)/shard_map/ppermute | solution.py:321
  348.6 17.5 %all-to-all-start.3 = ((bf16[8,56,1024]{2,1,0:T(8,128)(2,1)}), bf16[8,56,1024]{2,1,0:T(8,128)(2,1)S(1)}, u32[]{:S(2)}, u32[]{:S(2)}) async-start(bf16[8,56,1024]{2,1,0:T(8,128)(2,1)} %shard_map.226), calls=%async_computation.3 | async-start | bytes 1835008 | tf_op jit(solution)/shard_map/all_to_all | solution.py:1135
  355.7 12.2 %collective-permute-start.52 = (bf16[128,768]{1,0:T(8,128)(2,1)S(1)}, bf16[128,768]{1,0:T(8,128)(2,1)S(1)}, u32[]{:S(2)}, u32[]{:S(2)}) collective-permute-start(bf16[128,768]{1,0:T(8,128)(2,1)S(1)} %select_convert_fusion.2), channel_id=1, source_target_pairs={{0,4},{1,5},{2,6},{3,7},{4,0},{5,1},{6,2},{7,3},{8,12},{9,13},{10,... | collective-permute-start | bytes 589832 | tf_op jit(solution)/shard_map/ppermute | solution.py:321
  (69 other events, 798.5 us)

commit v3 on v2

--- a/solution.py
+++ b/solution.py
@@ -369,18 +369,20 @@
     return ids[T_ID] >> 1
 
 
-def pack_kernel(ids, rows, gains, biases, qv, b_fc1, out, wide):
+def far_chips(ids, core_flip):
+    return [(ids[CHIP_ID] ^ m) * 2 + (ids[CORE_ID] ^ core_flip) for m in range(4)]
+
+
+def pack_kernel(ids, rows, grads, params, keep, send, wide, stage):
     lane32 = lax.broadcasted_iota(jnp.int32, (32, 128), 1)
     spot = (lane32 == row_ids((32, 128)) + 32 * ids[T_ID]).astype(F32).astype(BF16)
     lane8 = lax.broadcasted_iota(jnp.int32, (8, 128), 1)
     spot8 = (lane8 == row_ids((8, 128)) + 8 * ids[D_ID]).astype(F32).astype(BF16)
-    g = dot(gains[...], spot, NN)
-    b = dot(biases[...], spot, NN)
-    qv_rows = dot(qv[...], spot8, NN)
+    placed = dot(params[0:8, 0:32], spot, NN)
+    qv_rows = dot(params[8:16, 0:8], spot8, NN)
     row_a = jnp.concatenate(
-        [g[k : k + 1] for k in range(2)]
-        + [b[k : k + 1] for k in range(4)]
-        + [b_fc1[...].astype(F32), jnp.zeros((1, 128), F32)],
+        [placed[k : k + 1] for k in range(6)]
+        + [params[...].astype(F32)[16:17], jnp.zeros((1, 128), F32)],
         axis=1,
     )
     row_b = jnp.concatenate([qv_rows[k : k + 1] for k in range(8)], axis=1)
@@ -390,50 +392,64 @@
     wide[0 : rows.shape[0], :] = rows[...].astype(F32)
     for j in range(8):
         block = wide[SHARE * j : SHARE * j + PAD, :]
-        out[j, :, :] = jnp.where(row < SHARE, block, tail).astype(BF16)
-
-
-def pack_grad_kernel(ids, rows, out, wide):
-    wide[0 : rows.shape[0], :] = rows[...].astype(F32)
+        stage[j, 0:PAD, :] = jnp.where(row < SHARE, block, tail).astype(BF16)
+    wide[0 : rows.shape[0], :] = grads[...].astype(F32)
     for j in range(8):
-        out[j, :, :] = wide[SHARE * j : SHARE * j + PAD, :].astype(BF16)
-
-
-def pick_kernel(ids, got, here, there, slots):
+        stage[j, PAD : 2 * PAD, :] = wide[SHARE * j : SHARE * j + PAD, :].astype(BF16)
+    for m, (d0, d1) in enumerate(zip(far_chips(ids, 0), far_chips(ids, 1))):
+        keep[m, :, :] = stage[d0, :, :]
+        send[m, :, :] = stage[d1, :, :]
+
+
+def pair_up_kernel(ids, keep, got, o1, o2, o3):
+    for m, out in enumerate((o1, o2, o3)):
+        out[0, :, :] = keep[m + 1, :, :]
+        out[1, :, :] = got[m + 1, :, :]
+
+
+def arrived(ids, keep, got, d1, d2, d3):
+    parts = []
+    for m, (a0, a1) in enumerate(zip(far_chips(ids, 0), far_chips(ids, 1))):
+        first, second = ((keep, 0), (got, 0)) if m == 0 else (((d1, d2, d3)[m - 1], k) for k in range(2))
+        parts += [(a0, *first), (a1, *second)]
+    return parts
+
+
+def pick_kernel(ids, keep, got, d1, d2, d3, here, there, here_grad, there_grad, slots):
     row8 = row_ids((8, 1024))
     row = row_ids((PAD, 1024))
-    seen = jnp.zeros((1, 1024), F32)
     mine = jnp.zeros((PAD, 1024), F32)
-    other = jnp.zeros((PAD, 1024), F32)
+    other, mine_grad, other_grad = mine, mine, mine
     params = jnp.zeros((8, 1024), F32)
     qv = jnp.zeros((1, 1024), F32)
     high = jnp.full((1, 1024), z_high(ids), jnp.int32).astype(F32)
-    for c in range(8):
-        block = got[c, :, :].astype(F32)
-        flag = block[SHARE + 2 : SHARE + 3]
-        is_mine = jnp.where(seen == high, flag, 0.0)
-        is_other = flag - is_mine
-        seen = seen + flag
+    parts = arrived(ids, keep, got, d1, d2, d3)
+    flags = [
+        ref[k, PAD - 8 : PAD, :].astype(F32)[SHARE + 10 - PAD : SHARE + 11 - PAD]
+        for _, ref, k in parts
+    ]
+    for i, (a, ref, k) in enumerate(parts):
+        seen = jnp.zeros((1, 1024), F32)
+        for (c, _, _), flag in zip(parts, flags):
+            earlier = jnp.full((1, 1024), jnp.where(c < a, 1, 0), jnp.int32).astype(F32)
+            seen = seen + flag * earlier
+        block = ref[k, 0:PAD, :].astype(F32)
+        grad = ref[k, PAD : 2 * PAD, :].astype(F32)
+        is_mine = jnp.where(seen == high, flags[i], 0.0)
+        is_other = flags[i] - is_mine
         mine = jnp.where(is_mine > 0.5, block, mine)
         other = jnp.where(is_other > 0.5, block, other)
-        params = jnp.where(row8 == c, block[SHARE : SHARE + 1], params)
+        mine_grad = jnp.where(is_mine > 0.5, grad, mine_grad)
+        other_grad = jnp.where(is_other > 0.5, grad, other_grad)
+        params = jnp.where(row8 == a, block[SHARE : SHARE + 1], params)
         qv = qv + block[SHARE + 1 : SHARE + 2]
-        slots[c : c + 1, :] = is_mine[:, 0:128]
-        slots[8 + c : 9 + c, :] = is_other[:, 0:128]
+        slots[a, :, :] = jnp.broadcast_to(is_mine[:, 0:128], (8, 128))
+        slots[8 + a, :, :] = jnp.broadcast_to(is_other[:, 0:128], (8, 128))
     for value, out in ((mine, here), (other, there)):
         out[0:PAD, :] = jnp.where(row == PAD - 1, qv, value).astype(BF16)
         out[PAD : PAD + 8, :] = params.astype(BF16)
-
-
-def pick_grad_kernel(ids, slots, got, here, there):
-    mine = jnp.zeros((PAD, 1024), F32)
-    other = jnp.zeros((PAD, 1024), F32)
-    for c in range(8):
-        block = got[c, :, :].astype(F32)
-        mine = jnp.where(slots[c : c + 1, 0:1] > 0.5, block, mine)
-        other = jnp.where(slots[8 + c : 9 + c, 0:1] > 0.5, block, other)
-    here[...] = mine.astype(BF16)
-    there[...] = other.astype(BF16)
+    here_grad[...] = mine_grad.astype(BF16)
+    there_grad[...] = other_grad.astype(BF16)
 
 
 def lay_rows(ids, here, r1, r2, r3, wide):
@@ -493,6 +509,9 @@
     wide[half : 2 * half, :] = got[...].astype(F32)
 
 
+PROJ = 3
+
+
 def qkv_kernel(ids, own, got, qv_bias, w0, w1, w2, w3, whole, o0, o1, o2, o3, wide, heads):
     weights = (w0, w1, w2, w3)
     join_rows(wide, own, got)
@@ -586,8 +605,9 @@
         heads[m, :, :] = part[...]
     for h in range(4):
         joined[:, 64 * h : 64 * h + 64] = heads[h ^ ids[CHIP_ID], :, :]
-    for m, weight in enumerate((w0, w1, w2, w3)):
-        split_rows(dot(joined[...], weight[:, 0:256], NT), keep, send, lanes(m))
+    for m in range(4):
+        weight = (w0, w1, w2, w3)[m]
+        split_rows(dot(joined[...], weight[:, lanes(PROJ)], NT), keep, send, lanes(m))
 
 
 def pair_kernel(ids, keep, got, part, send):
@@ -631,10 +651,9 @@
 
     def body(c, carry):
         cols = pl.ds(pl.multiple_of(c * 256, 256), 256)
-        fc1 = pl.ds(pl.multiple_of(c * 256 + 256, 256), 256)
-        pre = b_fc1[:, cols] + dot(whole[:, lanes(0)], w0[:, fc1], NN)
+        pre = b_fc1[:, cols] + dot(whole[:, lanes(0)], w0[:, cols], NN)
         for m in range(1, 4):
-            pre = pre + dot(whole[:, lanes(m)], weights[m][:, fc1], NN)
+            pre = pre + dot(whole[:, lanes(m)], weights[m][:, cols], NN)
         half_erf = 0.5 * (1.0 + lax.erf(pre * root_half))
         hidden[:, cols] = (pre * half_erf).astype(BF16)
         slope = half_erf + pre * jnp.exp(-0.5 * pre * pre) * inv_root_tau
@@ -642,7 +661,7 @@
         grad_pre[:, cols] = grad
         sums[:, cols] = jnp.sum(grad.astype(F32), axis=0, keepdims=True)
         for m in range(4):
-            wide[:, lanes(m)] += dot(grad, weights[m][:, fc1], NT)
+            wide[:, lanes(m)] += dot(grad, weights[m][:, cols], NT)
         return carry
 
     lax.fori_loop(0, 4, body, 0)
@@ -685,9 +704,10 @@
 def grad_att_kernel(ids, own, got, w0, w1, w2, w3, whole, o0, o1, o2, o3, wide, heads):
     join_rows(wide, own, got)
     whole[...] = wide[...].astype(BF16)
-    total = dot(whole[:, lanes(0)], w0[:, 0:256], NN)
-    for m, weight in enumerate((w1, w2, w3)):
-        total = total + dot(whole[:, lanes(m + 1)], weight[:, 0:256], NN)
+    weights = (w0, w1, w2, w3)
+    total = dot(whole[:, lanes(0)], w0[:, lanes(PROJ)], NN)
+    for m in range(1, 4):
+        total = total + dot(whole[:, lanes(m)], weights[m][:, lanes(PROJ)], NN)
     for h in range(4):
         heads[h, :, :] = total[:, 64 * h : 64 * h + 64].astype(BF16)
     for m, out in enumerate((o0, o1, o2, o3)):
@@ -708,8 +728,10 @@
                 sums[0:1, 128 * k : 128 * k + 128] = jnp.concatenate(
                     [total, jnp.zeros((1, 64), F32)], axis=1
                 )
-    for m, weight in enumerate((w0, w1, w2, w3)):
-        split_rows(dot(joined[...], weight[...], NT), keep, send, lanes(m))
+    for m in range(4):
+        weight = (w0, w1, w2, w3)[m]
+        total = dot(joined[...], weight[:, 0:768], NT)
+        split_rows(total, keep, send, lanes(m))
 
 
 def to_owners(ids, value, wide, here, there):
@@ -760,15 +782,20 @@
         split_rows(dot(hidden[...], weight[...], NT), keep, send, lanes(m))
 
 
-def give_kernel(ids, slots, here, away, out):
+def for_slot(slots, d, left, right):
+    value = jnp.where(slots[8 + d, 0:1, 0:1] > 0.5, right, 0.0)
+    return jnp.where(slots[d, 0:1, 0:1] > 0.5, left, value)
+
+
+def give_kernel(ids, slots, here, away, keep, send):
     left = here[0:PAD, :].astype(F32)
     right = away[0:PAD, :].astype(F32)
-    for c in range(8):
-        value = jnp.where(slots[8 + c : 9 + c, 0:1] > 0.5, right, 0.0)
-        out[c, :, :] = jnp.where(slots[c : c + 1, 0:1] > 0.5, left, value).astype(BF16)
-
-
-def give_grad_kernel(ids, slots, here, s1, away, s3, out, rel, flat, tail):
+    for out, flip in ((keep, 0), (send, 1)):
+        for m, d in enumerate(far_chips(ids, flip)):
+            out[m, :, :] = for_slot(slots, d, left, right).astype(BF16)
+
+
+def give_grad_kernel(ids, slots, here, s1, away, s3, keep, send, rel, flat, tail):
     left = here[0:PAD, :].astype(F32)
     right = away[0:PAD, :].astype(F32)
     own = here[PAD : PAD + 8, :].astype(F32)
@@ -777,31 +804,41 @@
     home = pick(is_zero(ids[CORE_ID]), own, far)
     for m in range(4):
         flat[:, chip_lanes(ids, m)] = rel[:, lanes(m)]
+    rel[0:1, :] = home[7:8]
     tail[...] = jnp.zeros_like(tail)
     for k in range(8):
         row, lane = (SHARE + k, 128) if k < 7 else (SHARE, 256)
         tail[row : row + 1, lane : lane + 128] = home[6:7, 128 * k : 128 * k + 128]
     row = row_ids((PAD, 1024))
-    for c in range(8):
-        cols = slice(128 * c, 128 * c + 128)
-        tail[SHARE : SHARE + 6, 0:128] = flat[0:6, cols]
-        tail[SHARE + 6 : PAD, 0:128] = home[7:8, cols]
-        value = jnp.where(slots[8 + c : 9 + c, 0:1] > 0.5, right, 0.0)
-        value = jnp.where(slots[c : c + 1, 0:1] > 0.5, left, value)
-        out[c, :, :] = jnp.where(row < SHARE, value, tail[...]).astype(BF16)
-
-
-def take_kernel(ids, got, out, wide):
-    for c in range(8):
-        wide[SHARE * c : SHARE * c + SHARE, :] = got[c, :, :].astype(F32)[0:SHARE]
+    for out, flip in ((keep, 0), (send, 1)):
+        for m, d in enumerate(far_chips(ids, flip)):
+            cols = pl.ds(pl.multiple_of(d * 128, 128), 128)
+            tail[SHARE : SHARE + 6, 0:128] = flat[0:6, cols]
+            tail[SHARE + 6 : PAD, 0:128] = rel[0:1, cols]
+            value = for_slot(slots, d, left, right)
+            out[m, :, :] = jnp.where(row < SHARE, value, tail[...]).astype(BF16)
+
+
+def settle_rows(parts, stage, out):
+    for a, ref, k in parts:
+        stage[a, :, :] = ref[k, :, :].astype(F32)
+    for j in range(8):
+        out[SHARE * j : SHARE * j + SHARE, :] = stage[j, 0:SHARE, :]
+
+
+def take_kernel(ids, keep, got, d1, d2, d3, out, stage, wide):
+    settle_rows(arrived(ids, keep, got, d1, d2, d3), stage, wide)
     out[...] = wide[...].astype(out.dtype)
 
 
-def take_grad_kernel(ids, got, out, gains, biases, last, qv, b_fc1):
+def take_grad_kernel(
+    ids, keep, got, d1, d2, d3, out, gains, biases, last, qv, b_fc1, stage
+):
+    parts = arrived(ids, keep, got, d1, d2, d3)
+    settle_rows(parts, stage, out)
     total = jnp.zeros((8, 384), F32)
-    for c in range(8):
-        out[SHARE * c : SHARE * c + SHARE, :] = got[c, :, :].astype(F32)[0:SHARE]
-        total = total + got[c, PAD - 8 : PAD, 0:384].astype(F32)
+    for _, ref, k in parts:
+        total = total + ref[k, PAD - 8 : PAD, 0:384].astype(F32)
     rows = pltpu.roll(total[:, 0:128], (128 - 32 * ids[T_ID]) & 127, 1)
     gains[...] = rows[1:3, 0:32]
     biases[...] = rows[3:7, 0:32]
@@ -811,12 +848,11 @@
     qv[...] = pltpu.roll(parts, (128 - 8 * ids[D_ID]) & 127, 1)[:, 0:8]
 
 
-def shards_kernel(ids, qkv, proj, fc1, fc2, first, second, third):
+def shards_kernel(ids, qkv, proj, fc2, first, second):
     for j in range(3):
         first[:, lanes(j)] = qkv[j, :, :]
-    second[:, 0:256] = jnp.transpose(proj[...])
-    second[:, 256:1280] = fc1[...]
-    third[...] = jnp.transpose(fc2[...])
+    first[:, lanes(PROJ)] = jnp.transpose(proj[...])
+    second[...] = jnp.transpose(fc2[...])
 
 
 def offer_kernel(ids, own, far, send):
@@ -843,41 +879,102 @@
         out[half:, :] = far[...]
 
 
-def grads_of(near, far, first_col=0):
-    def grads_kernel(ids, left, right, send, here, there):
-        for slot, m in ((0, near), (1, 3)):
-            send[slot, :, :] = dot(left[:, lanes(m)], right[...], TN).astype(BF16)
-        here[...] = dot(left[:, lanes(0)], right[...], TN)
-        there[...] = dot(left[:, lanes(far)], right[...], TN)
-
-    return grads_kernel
-
-
-def sum_grad(ids, left, right, x_first):
-    first, second, near, far = (X, Y, 1, 2) if x_first else (Y, X, 2, 1)
-    n = right.shape[1]
-    send, here, there = call(
-        grads_of(near, far),
-        [((2, 256, n), BF16), ((256, n), F32), ((256, n), F32)],
-        ids,
-        left,
-        right,
-        flops=2 * left.shape[0] * 1024 * n,
-    )
-    got = swap(send, first)
-    other = (there + got[1].astype(F32)).astype(BF16)
-    whole = here + got[0].astype(F32)
-    return whole + swap(other, second).astype(F32)
-
-
-def settle_grad(part, core):
+X_FIRST, Y_FIRST = (1, 2), (2, 1)
+
+
+def blocks_of(order, left, right, cols, send, here, there, out_cols):
+    near, far = order
+    for slot, m in ((0, near), (1, 3)):
+        send[slot, :, out_cols] = dot(left[:, lanes(m)], right[:, cols], TN).astype(BF16)
+    here[:, out_cols] = dot(left[:, lanes(0)], right[:, cols], TN)
+    there[:, out_cols] = dot(left[:, lanes(far)], right[:, cols], TN)
+
+
+def grads_fc1_kernel(ids, left, right, send, here, there):
+    for c in range(2):
+        cols = slice(512 * c, 512 * c + 512)
+        blocks_of(X_FIRST, left, right, cols, send, here, there, cols)
+
+
+def grads_fc2_kernel(ids, left, right, send, here, there):
+    for c in range(2):
+        cols = slice(512 * c, 512 * c + 512)
+        blocks_of(Y_FIRST, left, right, cols, send, here, there, cols)
+
+
+def grads_att_kernel(
+    ids, rows, joined, branch, mixed, send_x, here_x, there_x, send_y, here_y, there_y
+):
+    blocks_of(X_FIRST, rows, joined, slice(0, 512), send_x, here_x, there_x, slice(0, 512))
+    blocks_of(Y_FIRST, rows, joined, slice(512, 768), send_y, here_y, there_y, slice(0, 256))
+    blocks_of(Y_FIRST, branch, mixed, slice(0, 256), send_y, here_y, there_y, slice(256, 512))
+
+
+def fold_kernel(ids, here, there, got, other, whole):
+    other[...] = (there[...] + got[1, :, :].astype(F32)).astype(BF16)
+    whole[...] = here[...] + got[0, :, :].astype(F32)
+
+
+def gather_kernel(ids, whole_x, got_x, whole_y, got_y, part, send):
+    for k, (whole, got) in enumerate(((whole_x, got_x), (whole_y, got_y))):
+        total = whole[...] + got[...].astype(F32)
+        part[k, :, :] = total
+        send[k, :, :] = total.astype(BF16)
+
+
+def divide_kernel(ids, part, moved, keep, send):
+    @pl.when(ids[CORE_ID] == 0)
+    def _():
+        keep[...] = part[:, 0:128, :]
+        send[...] = part[:, 128:256, :].astype(BF16)
+
+    @pl.when(ids[CORE_ID] != 0)
+    def _():
+        keep[...] = moved[:, 128:256, :].astype(F32)
+        send[...] = moved[:, 0:128, :]
+
+
+def finish_mlp_kernel(ids, keep, got, fc1, fc2):
+    fc1[...] = keep[0, :, :] + got[0, :, :].astype(F32)
+    fc2[...] = jnp.transpose(keep[1, :, :] + got[1, :, :].astype(F32))
+
+
+def finish_att_kernel(ids, keep, got, qkv, proj):
+    first = keep[0, :, :] + got[0, :, :].astype(F32)
+    second = keep[1, :, :] + got[1, :, :].astype(F32)
+    qkv[0, :, :] = first[:, 0:256]
+    qkv[1, :, :] = first[:, 256:512]
+    qkv[2, :, :] = second[:, 0:256]
+    proj[...] = jnp.transpose(second[:, 256:512])
+
+
+def tie(*values):
+    return lax.optimization_barrier(values)
+
+
+def sum_second(ids, first, second):
+    n = first[1].shape[1]
+    outs = [((256, n), BF16), ((256, n), F32)]
+    other_x, whole_x = call(fold_kernel, outs, ids, *first)
+    other_y, whole_y = call(fold_kernel, outs, ids, *second)
+    return whole_x, swap(other_x, Y), whole_y, swap(other_y, X)
+
+
+def sum_third(ids, parts):
+    n = parts[0].shape[1]
+    part, send = call(
+        gather_kernel, [((2, 256, n), F32), ((2, 256, n), BF16)], ids, *parts
+    )
     pairs = [(i, i ^ Z_HIGH) for i in range(32) if i & CORE]
-    moved = lax.ppermute(part.astype(BF16), AXES, pairs).astype(F32)
-    part = jnp.where(core == 0, part, moved)
-    low, high = part[:128], part[128:]
-    send = jnp.where(core == 0, high, low)
-    keep = jnp.where(core == 0, low, high)
-    return keep + swap(send.astype(BF16), CORE).astype(F32)
+    return part, lax.ppermute(send, AXES, pairs)
+
+
+def sum_last(ids, body, outs, part, moved):
+    n = part.shape[2]
+    keep, send = call(
+        divide_kernel, [((2, 128, n), F32), ((2, 128, n), BF16)], ids, part, moved
+    )
+    return call(body, outs, ids, keep, swap(send, CORE))
 
 
 def on_device_spread(
@@ -898,45 +995,70 @@
     ids = jnp.stack([d >> 1, core, d, t, clip_valid[0]]).astype(jnp.int32)
     count = clip_rows.shape[0]
     half, own = count // 2, count // 4
-    block = (8, PAD, 1024)
     behind = (PAD + 8, 1024)
-
-    (sent,) = call(
-        pack_kernel,
-        [(block, BF16)],
-        ids,
-        clip_rows,
-        gain_rows,
-        bias_rows,
-        qv_bias.reshape(8, 8),
-        fc1_bias,
-        scratch=[((400, 1024), F32)],
-    )
-    shards = call(
+    plain = (PAD, 1024)
+    wide = ((count, 1024), F32)
+
+    def to_devices(keep, send):
+        got = swap(send, CORE)
+        shape = (2, *keep.shape[1:])
+        outs = call(pair_up_kernel, [(shape, BF16)] * 3, ids, keep, got)
+        return keep, got, *(swap(outs[m], CHIP_MASKS[m + 1]) for m in range(3))
+
+    def offer(shard, far):
+        (send,) = call(offer_kernel, [(shard.shape, BF16)], ids, shard, far)
+        return send
+
+    def merge(shard, far, send):
+        (out,) = call(
+            merge_kernel, [((256, shard.shape[1]), BF16)], ids, shard, far, swap(send, CORE)
+        )
+        return out
+
+    def trade(parts):
+        return [parts[0]] + [swap(parts[m], CHIP_MASKS[m]) for m in range(1, 4)]
+
+    params = jnp.concatenate(
+        [
+            jnp.pad(v, ((0, n - v.shape[0]), (0, 128 - v.shape[1])))
+            for v, n in (
+                (jnp.concatenate([gain_rows, bias_rows]), 8),
+                (qv_bias.reshape(8, 8), 8),
+                (fc1_bias, 8),
+            )
+        ]
+    )
+    shard_a, shard_g = call(
         shards_kernel,
-        [((128, 768), BF16), ((128, 1280), BF16), ((128, 1024), BF16)],
+        [((128, 1024), BF16), ((128, 1024), BF16)],
         ids,
         qkv_weight,
         proj_weight,
-        fc1_weight,
         fc2_weight,
     )
-
-    def gather(shard, by_y):
-        far = swap(shard, Z_HIGH)
-        (send,) = call(offer_kernel, [(shard.shape, BF16)], ids, shard, far)
-        (w0,) = call(
-            merge_kernel, [((256, shard.shape[1]), BF16)], ids, shard, far, swap(send, CORE)
-        )
-        w1, w2 = swap(w0, X), swap(w0, Y)
-        return w0, w1, w2, (swap(w1, Y) if by_y else swap(w2, X))
-
-    got = lax.all_to_all(sent, "dp", 0, 0)
-    w_qkv = gather(shards[0], True)
-    here, there, slots = call(
-        pick_kernel, [(behind, BF16), (behind, BF16), ((16, 128), F32)], ids, got
+    far_a = swap(shard_a, Z_HIGH)
+    keep, send = call(
+        pack_kernel,
+        [((4, 2 * PAD, 1024), BF16)] * 2,
+        ids,
+        clip_rows,
+        out_grad,
+        params,
+        scratch=[((400, 1024), F32), ((8, 2 * PAD, 1024), BF16)],
+    )
+    *parts, far_a = tie(*to_devices(keep, send), far_a)
+    here, there, here_grad, there_grad, slots = call(
+        pick_kernel,
+        [(behind, BF16), (behind, BF16), (plain, BF16), (plain, BF16), ((16, 8, 128), F32)],
+        ids,
+        *parts,
     )
     r1, r2, r3 = swap(here, Z_LOW), swap(there, Z_HIGH), swap(there, Z_LOW | Z_HIGH)
+    far_a, shard_a, _ = tie(far_a, shard_a, here)
+    w0 = merge(shard_a, far_a, offer(shard_a, far_a))
+    w_att = (w0, swap(w0, X), swap(w0, Y), swap(w0, X | Y))
+    r1, r2, r3, shard_f = tie(r1, r2, r3, fc1_weight)
+    far_f = swap(shard_f, Z_HIGH)
     rows, normed, vec, qkv_bias, b_fc1 = call(
         norm_one_kernel,
         [
@@ -953,11 +1075,7 @@
         r3,
         scratch=[((half, 1024), F32), ((8, 1024), F32)],
     )
-    late = lax.optimization_barrier((shards[1], shards[2], out_grad, here))
-    w_mid = gather(late[0], False)
-    w_fc2 = gather(late[1], True)
-
-    wide = ((count, 1024), F32)
+
     whole_one, *qkv = call(
         qkv_kernel,
         [((count, 1024), BF16)] + [((count, 192), BF16)] * 4,
@@ -965,15 +1083,14 @@
         normed,
         swap(normed, CORE),
         qkv_bias,
-        *w_qkv,
+        *w_att,
         scratch=[wide, ((4, count, 192), BF16)],
         flops=2 * count * 1024 * 768,
     )
-
-    def trade(parts):
-        return [parts[0]] + [swap(parts[m], CHIP_MASKS[m]) for m in range(1, 4)]
-
-    qkv = trade(qkv)
+    shard_g, *qkv = tie(shard_g, *qkv)
+    far_g = swap(shard_g, Z_HIGH)
+    *qkv, f0 = tie(*trade(qkv), merge(shard_f, far_f, offer(shard_f, far_f)))
+    f1, f2 = swap(f0, X), swap(f0, Y)
     tokens = 4 * count
     *mixed, lse = call(
         attention_kernel,
@@ -983,57 +1100,56 @@
         scratch=[((tokens, 192), F32)] + [((tokens, 64), BF16)] * 3,
         flops=4 * tokens * tokens * 64,
     )
+    here_grad, there_grad, *mixed = tie(here_grad, there_grad, *mixed)
+    s1, s2, s3 = (
+        swap(here_grad, Z_LOW),
+        swap(there_grad, Z_HIGH),
+        swap(there_grad, Z_LOW | Z_HIGH),
+    )
+    *mixed, f1, f2, g0 = tie(*trade(mixed), f1, f2, merge(shard_g, far_g, offer(shard_g, far_g)))
+    w_fc1 = (f0, f1, f2, swap(f2, X))
+    g1, g2 = swap(g0, X), swap(g0, Y)
     attended, keep, send = call(
         proj_kernel,
         [((count, 256), BF16), ((half, 1024), F32), ((half, 1024), BF16)],
         ids,
-        *trade(mixed),
-        *w_mid,
+        *mixed,
+        *w_att,
         scratch=[((4, count, 64), BF16)],
         flops=2 * count * 1024 * 256,
     )
 
-    def all_z(keep, send):
-        part, send = call(
-            pair_kernel,
-            [((half, 1024), F32), ((half, 1024), BF16)],
-            ids,
-            keep,
-            swap(send, CORE),
+    def pair(keep, send):
+        return call(
+            pair_kernel, [((half, 1024), F32), ((half, 1024), BF16)], ids, keep, swap(send, CORE)
         )
-        return part, swap(send, Z_LOW)
-
-    def one_z(keep, send):
-        part, send = call(
+
+    def halve(keep, send):
+        return call(
             half_kernel, [((own, 1024), F32), ((own, 1024), BF16)], ids, keep, swap(send, CORE)
         )
-        return part, swap(send, Z_LOW)
-
+
+    part, send = pair(keep, send)
+    (grads,) = call(
+        lay_grad_kernel,
+        [((half, 1024), BF16)],
+        ids,
+        here_grad,
+        s1,
+        s2,
+        s3,
+        scratch=[((half, 1024), F32)],
+    )
     residual, normed_two = call(
         norm_two_kernel,
         [((half, 1024), F32), ((half, 1024), BF16)],
         ids,
         rows,
-        *all_z(keep, send),
+        part,
+        swap(send, Z_LOW),
         vec,
     )
-
-    (sent,) = call(
-        pack_grad_kernel, [(block, BF16)], ids, late[2], scratch=[((400, 1024), F32)]
-    )
-    got = lax.all_to_all(sent, "dp", 0, 0)
-    here, there = call(pick_grad_kernel, [((PAD, 1024), BF16)] * 2, ids, slots, got)
-    r1, r2, r3 = swap(here, Z_LOW), swap(there, Z_HIGH), swap(there, Z_LOW | Z_HIGH)
-    (grads,) = call(
-        lay_grad_kernel,
-        [((half, 1024), BF16)],
-        ids,
-        here,
-        r1,
-        r2,
-        r3,
-        scratch=[((half, 1024), F32)],
-    )
+    w_fc2 = (g0, g1, g2, swap(g1, Y))
     whole_mlp, grad_hidden = call(
         grad_hidden_kernel,
         [((count, 1024), BF16), ((count, 1024), F32)],
@@ -1054,16 +1170,34 @@
         swap(normed_two, CORE),
         grad_hidden,
         b_fc1,
-        *w_mid,
+        *w_fc1,
         scratch=[wide],
         flops=4 * count * 1024 * 1024,
     )
+    part, send = pair(keep, send)
+    late = tie(send, whole_mlp, hidden, whole_two, grad_pre)
+    grad_outs = [((2, 256, 1024), BF16), ((256, 1024), F32), ((256, 1024), F32)]
+    cost = 2 * count * 1024 * 1024
+    send_f, *rest_f = call(grads_fc1_kernel, grad_outs, ids, late[3], late[4], flops=cost)
+    send_g, *rest_g = call(grads_fc2_kernel, grad_outs, ids, late[1], late[2], flops=cost)
+    sums_f = (*rest_f, swap(send_f, X))
+    sums_g = (*rest_g, swap(send_g, Y))
+    keep_out, send_out = call(
+        fc2_kernel,
+        [((half, 1024), F32), ((half, 1024), BF16)],
+        ids,
+        late[2],
+        *w_fc2,
+        flops=cost,
+    )
+    away, keep_out, send_out = tie(swap(send, Z_LOW), keep_out, send_out)
     grad_residual, grad_branch, sums_two = call(
         norm_two_back_kernel,
         [((half, 1024), F32), ((half, 1024), BF16), ((8, 1024), F32)],
         ids,
         residual,
-        *all_z(keep, send),
+        part,
+        away,
         grads,
         vec,
     )
@@ -1074,9 +1208,21 @@
         ids,
         grad_branch,
         swap(grad_branch, CORE),
-        *w_mid,
+        *w_att,
         scratch=[wide, ((4, count, 64), BF16)],
         flops=2 * count * 1024 * 256,
+    )
+    *grad_att, keep_out, send_out = tie(*grad_att, keep_out, send_out)
+    part_out, send_out = halve(keep_out, send_out)
+    here_out, there_out = call(
+        layer_out_kernel,
+        [(plain, BF16)] * 2,
+        ids,
+        residual,
+        part_out,
+        swap(send_out, Z_LOW),
+        vec,
+        scratch=[((2 * PAD, 1024), F32)],
     )
     grad_qkv = call(
         attention_back_kernel,
@@ -1093,16 +1239,23 @@
         [((count, 768), BF16), ((half, 1024), F32), ((half, 1024), BF16), ((1, 1024), F32)],
         ids,
         *trade(grad_qkv),
-        *w_qkv,
+        *w_att,
         scratch=[((4, count, 192), BF16)],
         flops=2 * count * 1024 * 768,
+    )
+    part, send = halve(keep, send)
+    late = tie(send, whole_one, joined, whole_branch, attended)
+    grad_outs = [((2, 256, 512), BF16), ((256, 512), F32), ((256, 512), F32)]
+    send_x, here_x, there_x, send_y, here_y, there_y = call(
+        grads_att_kernel, grad_outs * 2, ids, *late[1:], flops=cost
     )
     here, there, small = call(
         norm_one_back_kernel,
         [(behind, BF16), (behind, BF16), ((8, 1024), BF16)],
         ids,
         rows,
-        *one_z(keep, send),
+        part,
+        swap(send, Z_LOW),
         grad_residual,
         vec,
         sums_two,
@@ -1110,16 +1263,16 @@
         sums_qv,
         scratch=[((2 * PAD, 1024), F32)],
     )
-    (sent,) = call(
+    keep, send = call(
         give_grad_kernel,
-        [(block, BF16)],
+        [((4, PAD, 1024), BF16)] * 2,
         ids,
         slots,
         here,
         swap(small, Z_LOW),
         swap(there, Z_HIGH),
         swap(small, Z_LOW | Z_HIGH),
-        scratch=[((8, 1024), F32), ((8, 1024), F32), ((PAD, 1024), F32)],
+        scratch=[((8, 1024), F32), ((8, 1024), F32), (plain, F32)],
     )
     input_grad, grad_gains, grad_biases, grad_last, grad_qv, grad_b_fc1 = call(
         take_grad_kernel,
@@ -1132,52 +1285,54 @@
             ((1, 128), F32),
         ],
         ids,
-        lax.all_to_all(sent, "dp", 0, 0),
+        *to_devices(keep, send),
+        scratch=[((8, PAD, 1024), F32)],
     )
 
     keep, send = call(
-        fc2_kernel,
-        [((half, 1024), F32), ((half, 1024), BF16)],
-        ids,
-        hidden,
-        *w_fc2,
-        flops=2 * count * 1024 * 1024,
-    )
-    here, there = call(
-        layer_out_kernel,
-        [((PAD, 1024), BF16)] * 2,
-        ids,
-        residual,
-        *one_z(keep, send),
-        vec,
-        scratch=[((2 * PAD, 1024), F32)],
-    )
-    (sent,) = call(
-        give_kernel, [(block, BF16)], ids, slots, here, swap(there, Z_HIGH)
+        give_kernel,
+        [((4, PAD, 1024), BF16)] * 2,
+        ids,
+        slots,
+        here_out,
+        swap(there_out, Z_HIGH),
     )
     (layer_out,) = call(
         take_kernel,
         [((count, 1024), BF16)],
         ids,
-        lax.all_to_all(sent, "dp", 0, 0),
-        scratch=[((count, 1024), F32)],
-    )
-
-    grad_fc2 = settle_grad(sum_grad(ids, whole_mlp, hidden, True), core)
-    grad_fc1 = settle_grad(sum_grad(ids, whole_two, grad_pre, False), core)
-    grad_proj = settle_grad(sum_grad(ids, whole_branch, attended, True), core)
-    grad_w = settle_grad(sum_grad(ids, whole_one, joined, False), core)
+        *to_devices(keep, send),
+        scratch=[((8, PAD, 1024), F32), wide],
+    )
+
+    grad_fc1, grad_fc2 = sum_last(
+        ids,
+        finish_mlp_kernel,
+        [((128, 1024), F32), ((1024, 128), F32)],
+        *sum_third(ids, sum_second(ids, sums_f, sums_g)),
+    )
+    grad_w, grad_proj = sum_last(
+        ids,
+        finish_att_kernel,
+        [((3, 128, 256), F32), ((256, 128), F32)],
+        *sum_third(
+            ids,
+            sum_second(
+                ids, (here_x, there_x, swap(send_x, X)), (here_y, there_y, swap(send_y, Y))
+            ),
+        ),
+    )
     return (
         layer_out,
         input_grad,
         grad_gains,
         grad_biases,
-        jnp.transpose(grad_w.reshape(128, 3, 256), (1, 0, 2)),
+        grad_w,
         grad_qv.reshape(2, 4, 8),
-        jnp.transpose(grad_proj),
+        grad_proj,
         grad_fc1,
         grad_b_fc1,
-        jnp.transpose(grad_fc2),
+        grad_fc2,
         grad_last[0],
     )
 

time: 371 us -> 315 us (0.85)
  other arithmetic: 24.4 us -> 1.4 us
  local copies, waits for them, and re-layouts: 25.3 us -> 2.38 us
  starting transfers between devices: 82.2 us -> 71.5 us
  waiting for transfers between devices: 156 us -> 166 us
  Pallas kernels: 79.1 us -> 70.9 us
    ppermute x61 -> x71, waiting for transfers between devices: 137 us -> 166 us  [swap(): return lax.ppermute(value, AXES, [(i, i ^ mask) for i in range(32)])]
    unnamed x131 -> x12, local copies, waits for them, and re-layouts: 25.1 us -> 2.29 us
    all_to_all x4 -> x0, waiting for transfers between devices: 19.5 us -> none  [the longest x2 13.3 us: on_device_spread(): got = lax.all_to_all(sent, 'dp', 0, 0)]
    all_to_all x4 -> x0, starting transfers between devices: 16.7 us -> none  [the longest x2 8.72 us: on_device_spread(): got = lax.all_to_all(sent, 'dp', 0, 0)]
    convert_element_type x12 -> x0, other arithmetic: 15 us -> none  [the longest x4 7.45 us: settle_grad(): moved = lax.ppermute(part.astype(BF16), AXES, pairs).astype(F32)]
    ppermute x61 -> x71, starting transfers between devices: 60.2 us -> 69.9 us  [swap(): return lax.ppermute(value, AXES, [(i, i ^ mask) for i in range(32)])]
    pallas_call x38 -> x48, Pallas kernels: 79.1 us -> 70.9 us  [call(): pl.pallas_call(body, out_shape=[jax.ShapeDtypeStruct(s, t) for s, t in ou...]
    select_n x4 -> x0, other arithmetic: 5.75 us -> none  [settle_grad(): part = jnp.where(core == 0, part, moved)]
  transfers between devices with their start and end apart: 69 -> 73, of which waited for: 27 -> 39; matrix products, arithmetic and copies ran while one was open for 7% -> 0% of each run, Pallas kernels for 19% -> 18%
where the time goes in v3:
time: 315 us; the launch traced here: 314 us
  waiting for transfers between devices  166 us (53%)
  starting transfers between devices  71.5 us (23%)
  Pallas kernels  70.9 us (23%)
    ppermute x71, waiting for transfers between devices, swap(): return lax.ppermute(value, AXES, [(i, i ^ mask) for i in range(32)])  166 us
    pallas_call x48, Pallas kernels, call(): pl.pallas_call(body, out_shape=[jax.ShapeDtypeStruct(s, t) for s, t in ou...  70.9 us
    ppermute x71, starting transfers between devices, swap(): return lax.ppermute(value, AXES, [(i, i ^ mask) for i in range(32)])  69.9 us
  transfers between devices with their start and end apart: 73, of which 39 were waited for; matrix products, arithmetic and copies ran while one was open for 0% of the time, Pallas kernels for 18%

profile of v3, /device:TPU:0, one launch (start us, length us, event | category | flops | bytes accessed | tf_op | source)
XLA Modules:
  0.0 314.5 jit_solution(11473357948038962736)
XLA Ops:
  6.8 2.1 collective-permute-done.got
  9.5 2.9 collective-permute-start.1
  12.5 1.5 collective-permute-start.2
  14.7 3.1 collective-permute-start.4
  17.8 11.4 %collective-permute-done.4.far = bf16[128,1024]{1,0:T(8,128)(2,1)S(1)} collective-permute-done((bf16[128,1024]{1,0:T(8,128)(2,1)S(1)}, bf16[128,1024]{1,0:T(8,128)(2,1)S(1)}, u32[]{:S(2)}, u32[]{:S(2)}) %collective-permute-start.4) | collective-permute-done | bytes 262176 | tf_op jit(solution)/shard_map/ppermute | solution.py:321
  29.2 5.4 %collective-permute-done.2.d2 = bf16[2,112,1024]{2,1,0:T(8,128)(2,1)S(1)} collective-permute-done((bf16[2,112,1024]{2,1,0:T(8,128)(2,1)S(1)}, bf16[2,112,1024]{2,1,0:T(8,128)(2,1)S(1)}, u32[]{:S(2)}, u32[]{:S(2)}) %collective-permute-start.2) | collective-permute-done | bytes 458784 | tf_op jit(solution)/shard_map/ppermute | solution.py:321
  34.6 1.5 shard_map.197
  36.8 3.7 %collective-permute-start.7 = (bf16[64,1024]{1,0:T(8,128)(2,1)S(1)}, bf16[64,1024]{1,0:T(8,128)(2,1)S(1)}, u32[]{:S(2)}, u32[]{:S(2)}) collective-permute-start(bf16[64,1024]{1,0:T(8,128)(2,1)S(1)} %get-tuple-element.195), channel_id=1, source_target_pairs={{0,3},{1,2},{2,1},{3,0},{4,7},{5,6},{6,5},{7,4},{8,11},{9,10},{10,... | collective-permute-start | bytes 393224 | tf_op jit(solution)/shard_map/ppermute | solution.py:321
  41.9 1.6 collective-permute-start.12
  46.3 5.9 %collective-permute-done.6.r2 = bf16[64,1024]{1,0:T(8,128)(2,1)S(1)} collective-permute-done((bf16[64,1024]{1,0:T(8,128)(2,1)S(1)}, bf16[64,1024]{1,0:T(8,128)(2,1)S(1)}, u32[]{:S(2)}, u32[]{:S(2)}) %collective-permute-start.6) | collective-permute-done | bytes 131104 | tf_op jit(solution)/shard_map/ppermute | solution.py:321
  53.7 14.5 %collective-permute-done.16.far = bf16[128,1024]{1,0:T(8,128)(2,1)S(1)} collective-permute-done((bf16[128,1024]{1,0:T(8,128)(2,1)S(1)}, bf16[128,1024]{1,0:T(8,128)(2,1)S(1)}, u32[]{:S(2)}, u32[]{:S(2)}) %collective-permute-start.16) | collective-permute-done | bytes 262176 | tf_op jit(solution)/shard_map/ppermute | solution.py:321
  69.0 1.6 shard_map.201
  75.8 2.7 collective-permute-done.13.a1
  78.5 3.2 %collective-permute-done.14.a2 = bf16[392,192]{1,0:T(8,128)(2,1)S(1)} collective-permute-done((bf16[392,192]{1,0:T(8,128)(2,1)S(1)}, bf16[392,192]{1,0:T(8,128)(2,1)S(1)}, u32[]{:S(2)}, u32[]{:S(2)}) %collective-permute-start.14) | collective-permute-done | bytes 150560 | tf_op jit(solution)/shard_map/ppermute | solution.py:321
  81.7 1.6 collective-permute-done.15.a3
  84.1 1.5 collective-permute-start.21
  85.6 1.9 collective-permute-done.23.far
  88.2 7.6 %shard_map.204 = (bf16[392,64]{1,0:T(8,128)(2,1)S(1)}, bf16[392,64]{1,0:T(8,128)(2,1)S(1)}, bf16[392,64]{1,0:T(8,128)(2,1)S(1)}, bf16[392,64]{1,0:T(8,128)(2,1)S(1)}, f32[7,8,224]{2,1,0:T(8,128)S(1)}) custom-call(s32[5]{0:T(128)S(1)} %stack.19.ids, bf16[392,192]{1,0:T(8,128)(2,1)S(1)} %get-tuple-element.217.a0, ...), custom_call_target="tpu_custom_call" | custom-call | flops 629407744 | bytes 852992 | tf_op jit(solution)/shard_map/pallas_call | solution.py:332
  101.1 1.6 collective-permute-done.19.a2
  102.8 1.5 collective-permute-done.20.a3
  107.9 2.0 collective-permute-start.28
  109.9 2.4 collective-permute-start.30
  113.1 6.7 %collective-permute-done.32.w1 = bf16[256,1024]{1,0:T(8,128)(2,1)S(1)} collective-permute-done((bf16[256,1024]{1,0:T(8,128)(2,1)S(1)}, bf16[256,1024]{1,0:T(8,128)(2,1)S(1)}, u32[]{:S(2)}, u32[]{:S(2)}) %collective-permute-start.32) | collective-permute-done | bytes 524320 | tf_op jit(solution)/shard_map/ppermute | solution.py:321
  121.9 1.7 collective-permute-start.29
  123.5 1.6 collective-permute-done.30.r3
  125.9 3.9 %collective-permute-done.29.r2 = bf16[56,1024]{1,0:T(8,128)(2,1)S(1)} collective-permute-done((bf16[56,1024]{1,0:T(8,128)(2,1)S(1)}, bf16[56,1024]{1,0:T(8,128)(2,1)S(1)}, u32[]{:S(2)}, u32[]{:S(2)}) %collective-permute-start.29) | collective-permute-done | bytes 114720 | tf_op jit(solution)/shard_map/ppermute | solution.py:321
  132.4 4.2 %collective-permute-done.34.w3 = bf16[256,1024]{1,0:T(8,128)(2,1)S(1)} collective-permute-done((bf16[256,1024]{1,0:T(8,128)(2,1)S(1)}, bf16[256,1024]{1,0:T(8,128)(2,1)S(1)}, u32[]{:S(2)}, u32[]{:S(2)}) %collective-permute-start.34) | collective-permute-done | bytes 524320 | tf_op jit(solution)/shard_map/ppermute | solution.py:321
  136.6 1.6 shard_map.211
  138.4 5.8 %shard_map.212 = (bf16[392,1024]{1,0:T(8,128)(2,1)S(1)}, bf16[392,1024]{1,0:T(8,128)(2,1)S(1)}, bf16[392,1024]{1,0:T(8,128)(2,1)S(1)}, f32[1,1024]{1,0:T(1,128)S...) custom-call(s32[5]{0:T(128)S(1)} %stack.19.ids, bf16[196,1024]{1,0:T(8,128)(2,1)S(1)} %get-tuple-element.241.own, ...), custom_call_target="tpu_custom_call" | custom-call | flops 1644167168 | bytes 8126464 | tf_op jit(solution)/shard_map/pallas_call | solution.py:332
  144.3 1.7 collective-permute-done.36.got
  146.8 1.8 shard_map.237
  149.5 1.8 shard_map.235
  151.3 1.5 collective-permute-start.67
  152.8 1.6 shard_map.214
  154.5 3.8 %collective-permute-done.37.got = bf16[196,1024]{1,0:T(8,128)(2,1)S(1)} collective-permute-done((bf16[196,1024]{1,0:T(8,128)(2,1)S(1)}, bf16[196,1024]{1,0:T(8,128)(2,1)S(1)}, u32[]{:S(2)}, u32[]{:S(2)}) %collective-permute-start.37) | collective-permute-done | bytes 401440 | tf_op jit(solution)/shard_map/ppermute | solution.py:321
  158.2 1.5 shard_map.215
  159.8 1.7 collective-permute-done.38.got
  163.5 1.5 collective-permute-start.47
  166.2 13.3 %collective-permute-done.46.g1 = bf16[392,64]{1,0:T(8,128)(2,1)S(1)} collective-permute-done((bf16[392,64]{1,0:T(8,128)(2,1)S(1)}, bf16[392,64]{1,0:T(8,128)(2,1)S(1)}, u32[]{:S(2)}, u32[]{:S(2)}) %collective-permute-start.46) | collective-permute-done | bytes 50208 | tf_op jit(solution)/shard_map/ppermute | solution.py:321
  179.5 1.7 collective-permute-done.48.g3
  181.2 12.0 %shard_map.222 = (bf16[392,192]{1,0:T(8,128)(2,1)S(1)}, bf16[392,192]{1,0:T(8,128)(2,1)S(1)}, bf16[392,192]{1,0:T(8,128)(2,1)S(1)}, bf16[392,192]{1,0:T(8,128)(2,1)S(1)}) custom-call(s32[5]{0:T(128)S(1)} %stack.19.ids, bf16[392,192]{1,0:T(8,128)(2,1)S(1)} %get-tuple-element.217.a0, bf16[392,192]{1,0:T(8,128)(2,1)S(1)} %collective-permute-done.13.a1, ...), custom_call_target="tpu_custom_call" | custom-call | flops 1573519360 | bytes 1455104 | tf_op jit(solution)/shard_map/pallas_call | solution.py:332
  194.1 1.5 collective-permute-start.50
  196.8 4.2 %collective-permute-done.49.g1 = bf16[392,192]{1,0:T(8,128)(2,1)S(1)} collective-permute-done((bf16[392,192]{1,0:T(8,128)(2,1)S(1)}, bf16[392,192]{1,0:T(8,128)(2,1)S(1)}, u32[]{:S(2)}, u32[]{:S(2)}) %collective-permute-start.49) | collective-permute-done | bytes 150560 | tf_op jit(solution)/shard_map/ppermute | solution.py:321
  201.0 2.9 collective-permute-done.50.g2
  203.9 1.5 shard_map.223
  209.7 1.8 shard_map.229
  211.6 1.5 collective-permute-start.61
  213.8 7.2 %collective-permute-done.70.got_y = bf16[256,1024]{1,0:T(8,128)(2,1)S(1)} collective-permute-done((bf16[256,1024]{1,0:T(8,128)(2,1)S(1)}, bf16[256,1024]{1,0:T(8,128)(2,1)S(1)}, u32[]{:S(2)}, u32[]{:S(2)}) %collective-permute-start.70) | collective-permute-done | bytes 524320 | tf_op jit(solution)/shard_map/ppermute | solution.py:321
  221.0 2.0 collective-permute-done.68.got_x
  224.8 7.1 %collective-permute-done.61.got = bf16[2,256,512]{2,1,0:T(8,128)(2,1)S(1)} collective-permute-done((bf16[2,256,512]{2,1,0:T(8,128)(2,1)S(1)}, bf16[2,256,512]{2,1,0:T(8,128)(2,1)S(1)}, u32[]{:S(2)}, u32[]{:S(2)}) %collective-permute-start.61) | collective-permute-done | bytes 524320 | tf_op jit(solution)/shard_map/ppermute | solution.py:321
  235.9 1.5 collective-permute-start.40
  238.0 16.5 %collective-permute-done.40.got = bf16[98,1024]{1,0:T(8,128)(2,1)S(1)} collective-permute-done((bf16[98,1024]{1,0:T(8,128)(2,1)S(1)}, bf16[98,1024]{1,0:T(8,128)(2,1)S(1)}, u32[]{:S(2)}, u32[]{:S(2)}) %collective-permute-start.40) | collective-permute-done | bytes 200736 | tf_op jit(solution)/shard_map/ppermute | solution.py:321
  256.7 11.5 %collective-permute-done.41.away = bf16[56,1024]{1,0:T(8,128)(2,1)S(1)} collective-permute-done((bf16[56,1024]{1,0:T(8,128)(2,1)S(1)}, bf16[56,1024]{1,0:T(8,128)(2,1)S(1)}, u32[]{:S(2)}, u32[]{:S(2)}) %collective-permute-start.41) | collective-permute-done | bytes 114720 | tf_op jit(solution)/shard_map/ppermute | solution.py:321
  270.2 2.0 collective-permute-start.56
  272.2 4.5 %collective-permute-done.56.s3 = bf16[8,1024]{1,0:T(8,128)(2,1)S(1)} collective-permute-done((bf16[8,1024]{1,0:T(8,128)(2,1)S(1)}, bf16[8,1024]{1,0:T(8,128)(2,1)S(1)}, u32[]{:S(2)}, u32[]{:S(2)}) %collective-permute-start.56) | collective-permute-done | bytes 16416 | tf_op jit(solution)/shard_map/ppermute | solution.py:321
  276.7 3.6 %collective-permute-start.54 = (bf16[8,1024]{1,0:T(8,128)(2,1)S(1)}, bf16[8,1024]{1,0:T(8,128)(2,1)S(1)}, u32[]{:S(2)}, u32[]{:S(2)}) collective-permute-start(bf16[8,1024]{1,0:T(8,128)(2,1)S(1)} %get-tuple-element.297), channel_id=1, source_target_pairs={{0,1},{1,0},{2,3},{3,2},{4,5},{5,4},{6,7},{7,6},{8,9},{9,8},{10,11... | collective-permute-start | bytes 49160 | tf_op jit(solution)/shard_map/ppermute | solution.py:321
  280.4 1.7 collective-permute-done.54.s1
  284.8 1.5 collective-permute-start.43
  289.7 3.7 %collective-permute-done.43.d1 = bf16[2,56,1024]{2,1,0:T(8,128)(2,1)S(1)} collective-permute-done((bf16[2,56,1024]{2,1,0:T(8,128)(2,1)S(1)}, bf16[2,56,1024]{2,1,0:T(8,128)(2,1)S(1)}, u32[]{:S(2)}, u32[]{:S(2)}) %collective-permute-start.43) | collective-permute-done | bytes 229408 | tf_op jit(solution)/shard_map/ppermute | solution.py:321
  294.8 3.7 %collective-permute-done.44.d2 = bf16[2,56,1024]{2,1,0:T(8,128)(2,1)S(1)} collective-permute-done((bf16[2,56,1024]{2,1,0:T(8,128)(2,1)S(1)}, bf16[2,56,1024]{2,1,0:T(8,128)(2,1)S(1)}, u32[]{:S(2)}, u32[]{:S(2)}) %collective-permute-start.44) | collective-permute-done | bytes 229408 | tf_op jit(solution)/shard_map/ppermute | solution.py:321
  300.6 1.8 shard_map.221
  303.2 6.1 %collective-permute-done.59.d2 = bf16[2,56,1024]{2,1,0:T(8,128)(2,1)S(1)} collective-permute-done((bf16[2,56,1024]{2,1,0:T(8,128)(2,1)S(1)}, bf16[2,56,1024]{2,1,0:T(8,128)(2,1)S(1)}, u32[]{:S(2)}, u32[]{:S(2)}) %collective-permute-start.59) | collective-permute-done | bytes 229408 | tf_op jit(solution)/shard_map/ppermute | solution.py:321
  309.4 2.0 shard_map.228
  312.7 1.7 shard_map.241
  (145 shorter events, 70.4 us)
Async XLA Ops:
  9.5 19.7 %collective-permute-start.1 = (bf16[2,112,1024]{2,1,0:T(8,128)(2,1)S(1)}, bf16[2,112,1024]{2,1,0:T(8,128)(2,1)S(1)}, u32[]{:S(2)}, u32[]{:S(2)}) collective-permute-start(bf16[2,112,1024]{2,1,0:T(8,128)(2,1)S(1)} %get-tuple-element.184), channel_id=1, source_target_pairs={{0,8},{1,9},{2,10},{3,11},{4,12},{5,13},{6,14},{7,15},{8,0},{9,1},... | collective-permute-start | bytes 1376264 | tf_op jit(solution)/shard_map/ppermute | solution.py:321
  12.5 22.1 %collective-permute-start.2 = (bf16[2,112,1024]{2,1,0:T(8,128)(2,1)S(1)}, bf16[2,112,1024]{2,1,0:T(8,128)(2,1)S(1)}, u32[]{:S(2)}, u32[]{:S(2)}) collective-permute-start(bf16[2,112,1024]{2,1,0:T(8,128)(2,1)S(1)} %get-tuple-element.185), channel_id=1, source_target_pairs={{0,16},{1,17},{2,18},{3,19},{4,20},{5,21},{6,22},{7,23},{8,24},{9,... | collective-permute-start | bytes 1376264 | tf_op jit(solution)/shard_map/ppermute | solution.py:321
  14.0 20.6 %collective-permute-start.3 = (bf16[2,112,1024]{2,1,0:T(8,128)(2,1)S(1)}, bf16[2,112,1024]{2,1,0:T(8,128)(2,1)S(1)}, u32[]{:S(2)}, u32[]{:S(2)}) collective-permute-start(bf16[2,112,1024]{2,1,0:T(8,128)(2,1)S(1)} %get-tuple-element.186), channel_id=1, source_target_pairs={{0,24},{1,25},{2,26},{3,27},{4,28},{5,29},{6,30},{7,31},{8,16},{9,... | collective-permute-start | bytes 1376264 | tf_op jit(solution)/shard_map/ppermute | solution.py:321
  14.7 14.5 %collective-permute-start.4 = (bf16[128,1024]{1,0:T(8,128)(2,1)S(1)}, bf16[128,1024]{1,0:T(8,128)(2,1)S(1)}, u32[]{:S(2)}, u32[]{:S(2)}) collective-permute-start(bf16[128,1024]{1,0:T(8,128)(2,1)S(1)} %get-tuple-element.206.own), channel_id=1, source_target_pairs={{0,2},{1,3},{2,0},{3,1},{4,6},{5,7},{6,4},{7,5},{8,10},{9,11},{10,... | collective-permute-start | bytes 786440 | tf_op jit(solution)/shard_map/ppermute | solution.py:321
  36.8 8.3 %collective-permute-start.7 = (bf16[64,1024]{1,0:T(8,128)(2,1)S(1)}, bf16[64,1024]{1,0:T(8,128)(2,1)S(1)}, u32[]{:S(2)}, u32[]{:S(2)}) collective-permute-start(bf16[64,1024]{1,0:T(8,128)(2,1)S(1)} %get-tuple-element.195), channel_id=1, source_target_pairs={{0,3},{1,2},{2,1},{3,0},{4,7},{5,6},{6,5},{7,4},{8,11},{9,10},{10,... | collective-permute-start | bytes 393224 | tf_op jit(solution)/shard_map/ppermute | solution.py:321
  40.5 11.7 %collective-permute-start.6 = (bf16[64,1024]{1,0:T(8,128)(2,1)S(1)}, bf16[64,1024]{1,0:T(8,128)(2,1)S(1)}, u32[]{:S(2)}, u32[]{:S(2)}) collective-permute-start(bf16[64,1024]{1,0:T(8,128)(2,1)S(1)} %get-tuple-element.195), channel_id=1, source_target_pairs={{0,2},{1,3},{2,0},{3,1},{4,6},{5,7},{6,4},{7,5},{8,10},{9,11},{10,... | collective-permute-start | bytes 393224 | tf_op jit(solution)/shard_map/ppermute | solution.py:321
  40.5 11.7 %collective-permute-start.5 = (bf16[64,1024]{1,0:T(8,128)(2,1)S(1)}, bf16[64,1024]{1,0:T(8,128)(2,1)S(1)}, u32[]{:S(2)}, u32[]{:S(2)}) collective-permute-start(bf16[64,1024]{1,0:T(8,128)(2,1)S(1)} %get-tuple-element.194.here), channel_id=1, source_target_pairs={{0,1},{1,0},{2,3},{3,2},{4,5},{5,4},{6,7},{7,6},{8,9},{9,8},{10,11... | collective-permute-start | bytes 393224 | tf_op jit(solution)/shard_map/ppermute | solution.py:321
  41.9 27.1 %collective-permute-start.12 = (bf16[256,1024]{1,0:T(8,128)(2,1)S(1)}, bf16[256,1024]{1,0:T(8,128)(2,1)S(1)}, u32[]{:S(2)}, u32[]{:S(2)}) collective-permute-start(bf16[256,1024]{1,0:T(8,128)(2,1)S(1)} %shard_map.200.w0), channel_id=1, source_target_pairs={{0,24},{1,25},{2,26},{3,27},{4,28},{5,29},{6,30},{7,31},{8,16},{9,... | collective-permute-start | bytes 1572872 | tf_op jit(solution)/shard_map/ppermute | solution.py:321
  43.4 25.6 %collective-permute-start.11 = (bf16[256,1024]{1,0:T(8,128)(2,1)S(1)}, bf16[256,1024]{1,0:T(8,128)(2,1)S(1)}, u32[]{:S(2)}, u32[]{:S(2)}) collective-permute-start(bf16[256,1024]{1,0:T(8,128)(2,1)S(1)} %shard_map.200.w0), channel_id=1, source_target_pairs={{0,16},{1,17},{2,18},{3,19},{4,20},{5,21},{6,22},{7,23},{8,24},{9,... | collective-permute-start | bytes 1572872 | tf_op jit(solution)/shard_map/ppermute | solution.py:321
  45.1 23.9 %collective-permute-start.10 = (bf16[256,1024]{1,0:T(8,128)(2,1)S(1)}, bf16[256,1024]{1,0:T(8,128)(2,1)S(1)}, u32[]{:S(2)}, u32[]{:S(2)}) collective-permute-start(bf16[256,1024]{1,0:T(8,128)(2,1)S(1)} %shard_map.200.w0), channel_id=1, source_target_pairs={{0,8},{1,9},{2,10},{3,11},{4,12},{5,13},{6,14},{7,15},{8,0},{9,1},... | collective-permute-start | bytes 1572872 | tf_op jit(solution)/shard_map/ppermute | solution.py:321
  53.1 15.9 %collective-permute-start.8 = (bf16[196,1024]{1,0:T(8,128)(2,1)S(1)}, bf16[196,1024]{1,0:T(8,128)(2,1)S(1)}, u32[]{:S(2)}, u32[]{:S(2)}) collective-permute-start(bf16[196,1024]{1,0:T(8,128)(2,1)S(1)} %get-tuple-element.203.own), channel_id=1, source_target_pairs={{0,4},{1,5},{2,6},{3,7},{4,0},{5,1},{6,2},{7,3},{8,12},{9,13},{10,... | collective-permute-start | bytes 1204232 | tf_op jit(solution)/shard_map/ppermute | solution.py:321
  53.2 15.1 %collective-permute-start.16 = (bf16[128,1024]{1,0:T(8,128)(2,1)S(1)}, bf16[128,1024]{1,0:T(8,128)(2,1)S(1)}, u32[]{:S(2)}, u32[]{:S(2)}) collective-permute-start(bf16[128,1024]{1,0:T(8,128)(2,1)S(1)} %copy-done), channel_id=1, source_target_pairs={{0,2},{1,3},{2,0},{3,1},{4,6},{5,7},{6,4},{7,5},{8,10},{9,11},{10,... | collective-permute-start | bytes 786440 | tf_op jit(solution)/shard_map/ppermute | solution.py:321
  68.9 6.3 %collective-permute-start.17 = (bf16[128,1024]{1,0:T(8,128)(2,1)S(1)}, bf16[128,1024]{1,0:T(8,128)(2,1)S(1)}, u32[]{:S(2)}, u32[]{:S(2)}) collective-permute-start(bf16[128,1024]{1,0:T(8,128)(2,1)S(1)} %shard_map.202), channel_id=1, source_target_pairs={{0,4},{1,5},{2,6},{3,7},{4,0},{5,1},{6,2},{7,3},{8,12},{9,13},{10,... | collective-permute-start | bytes 786440 | tf_op jit(solution)/shard_map/ppermute | solution.py:321
  70.6 7.9 %collective-permute-start.13 = (bf16[392,192]{1,0:T(8,128)(2,1)S(1)}, bf16[392,192]{1,0:T(8,128)(2,1)S(1)}, u32[]{:S(2)}, u32[]{:S(2)}) collective-permute-start(bf16[392,192]{1,0:T(8,128)(2,1)S(1)} %get-tuple-element.213), channel_id=1, source_target_pairs={{0,8},{1,9},{2,10},{3,11},{4,12},{5,13},{6,14},{7,15},{8,0},{9,1},... | collective-permute-start | bytes 451592 | tf_op jit(solution)/shard_map/ppermute | solution.py:321
  71.9 9.7 %collective-permute-start.14 = (bf16[392,192]{1,0:T(8,128)(2,1)S(1)}, bf16[392,192]{1,0:T(8,128)(2,1)S(1)}, u32[]{:S(2)}, u32[]{:S(2)}) collective-permute-start(bf16[392,192]{1,0:T(8,128)(2,1)S(1)} %get-tuple-element.214), channel_id=1, source_target_pairs={{0,16},{1,17},{2,18},{3,19},{4,20},{5,21},{6,22},{7,23},{8,24},{9,... | collective-permute-start | bytes 451592 | tf_op jit(solution)/shard_map/ppermute | solution.py:321
  72.8 10.5 %collective-permute-start.15 = (bf16[392,192]{1,0:T(8,128)(2,1)S(1)}, bf16[392,192]{1,0:T(8,128)(2,1)S(1)}, u32[]{:S(2)}, u32[]{:S(2)}) collective-permute-start(bf16[392,192]{1,0:T(8,128)(2,1)S(1)} %get-tuple-element.215), channel_id=1, source_target_pairs={{0,24},{1,25},{2,26},{3,27},{4,28},{5,29},{6,30},{7,31},{8,16},{9,... | collective-permute-start | bytes 451592 | tf_op jit(solution)/shard_map/ppermute | solution.py:321
  74.2 13.3 %collective-permute-start.23 = (bf16[128,1024]{1,0:T(8,128)(2,1)S(1)}, bf16[128,1024]{1,0:T(8,128)(2,1)S(1)}, u32[]{:S(2)}, u32[]{:S(2)}) collective-permute-start(bf16[128,1024]{1,0:T(8,128)(2,1)S(1)} %get-tuple-element.230.own), channel_id=1, source_target_pairs={{0,2},{1,3},{2,0},{3,1},{4,6},{5,7},{6,4},{7,5},{8,10},{9,11},{10,... | collective-permute-start | bytes 786440 | tf_op jit(solution)/shard_map/ppermute | solution.py:321
  83.3 21.0 %collective-permute-start.22 = (bf16[256,1024]{1,0:T(8,128)(2,1)S(1)}, bf16[256,1024]{1,0:T(8,128)(2,1)S(1)}, u32[]{:S(2)}, u32[]{:S(2)}) collective-permute-start(bf16[256,1024]{1,0:T(8,128)(2,1)S(1)} %shard_map.203.w0), channel_id=1, source_target_pairs={{0,16},{1,17},{2,18},{3,19},{4,20},{5,21},{6,22},{7,23},{8,24},{9,... | collective-permute-start | bytes 1572872 | tf_op jit(solution)/shard_map/ppermute | solution.py:321
  84.1 20.1 %collective-permute-start.21 = (bf16[256,1024]{1,0:T(8,128)(2,1)S(1)}, bf16[256,1024]{1,0:T(8,128)(2,1)S(1)}, u32[]{:S(2)}, u32[]{:S(2)}) collective-permute-start(bf16[256,1024]{1,0:T(8,128)(2,1)S(1)} %shard_map.203.w0), channel_id=1, source_target_pairs={{0,8},{1,9},{2,10},{3,11},{4,12},{5,13},{6,14},{7,15},{8,0},{9,1},... | collective-permute-start | bytes 1572872 | tf_op jit(solution)/shard_map/ppermute | solution.py:321
  88.1 10.0 %collective-permute-start.24 = (bf16[128,1024]{1,0:T(8,128)(2,1)S(1)}, bf16[128,1024]{1,0:T(8,128)(2,1)S(1)}, u32[]{:S(2)}, u32[]{:S(2)}) collective-permute-start(bf16[128,1024]{1,0:T(8,128)(2,1)S(1)} %shard_map.205), channel_id=1, source_target_pairs={{0,4},{1,5},{2,6},{3,7},{4,0},{5,1},{6,2},{7,3},{8,12},{9,13},{10,... | collective-permute-start | bytes 786440 | tf_op jit(solution)/shard_map/ppermute | solution.py:321
  97.2 5.6 %collective-permute-start.19 = (bf16[392,64]{1,0:T(8,128)(2,1)S(1)}, bf16[392,64]{1,0:T(8,128)(2,1)S(1)}, u32[]{:S(2)}, u32[]{:S(2)}) collective-permute-start(bf16[392,64]{1,0:T(8,128)(2,1)S(1)} %get-tuple-element.227), channel_id=1, source_target_pairs={{0,16},{1,17},{2,18},{3,19},{4,20},{5,21},{6,22},{7,23},{8,24},{9,... | collective-permute-start | bytes 150536 | tf_op jit(solution)/shard_map/ppermute | solution.py:321
  98.1 6.1 %collective-permute-start.20 = (bf16[392,64]{1,0:T(8,128)(2,1)S(1)}, bf16[392,64]{1,0:T(8,128)(2,1)S(1)}, u32[]{:S(2)}, u32[]{:S(2)}) collective-permute-start(bf16[392,64]{1,0:T(8,128)(2,1)S(1)} %get-tuple-element.228), channel_id=1, source_target_pairs={{0,24},{1,25},{2,26},{3,27},{4,28},{5,29},{6,30},{7,31},{8,16},{9,... | collective-permute-start | bytes 150536 | tf_op jit(solution)/shard_map/ppermute | solution.py:321
  105.4 14.3 %collective-permute-start.32 = (bf16[256,1024]{1,0:T(8,128)(2,1)S(1)}, bf16[256,1024]{1,0:T(8,128)(2,1)S(1)}, u32[]{:S(2)}, u32[]{:S(2)}) collective-permute-start(bf16[256,1024]{1,0:T(8,128)(2,1)S(1)} %shard_map.206.w0), channel_id=1, source_target_pairs={{0,8},{1,9},{2,10},{3,11},{4,12},{5,13},{6,14},{7,15},{8,0},{9,1},... | collective-permute-start | bytes 1572872 | tf_op jit(solution)/shard_map/ppermute | solution.py:321
  107.8 22.8 %collective-permute-start.26 = (bf16[196,1024]{1,0:T(8,128)(2,1)S(1)}, bf16[196,1024]{1,0:T(8,128)(2,1)S(1)}, u32[]{:S(2)}, u32[]{:S(2)}) collective-permute-start(bf16[196,1024]{1,0:T(8,128)(2,1)S(1)} %get-tuple-element.238), channel_id=1, source_target_pairs={{0,1},{1,0},{2,3},{3,2},{4,5},{5,4},{6,7},{7,6},{8,9},{9,8},{10,11... | collective-permute-start | bytes 1204232 | tf_op jit(solution)/shard_map/ppermute | solution.py:321
  107.9 14.0 %collective-permute-start.28 = (bf16[56,1024]{1,0:T(8,128)(2,1)S(1)}, bf16[56,1024]{1,0:T(8,128)(2,1)S(1)}, u32[]{:S(2)}, u32[]{:S(2)}) collective-permute-start(bf16[56,1024]{1,0:T(8,128)(2,1)S(1)} %get-tuple-element.242.here), channel_id=1, source_target_pairs={{0,1},{1,0},{2,3},{3,2},{4,5},{5,4},{6,7},{7,6},{8,9},{9,8},{10,11... | collective-permute-start | bytes 344072 | tf_op jit(solution)/shard_map/ppermute | solution.py:321
  109.9 15.2 %collective-permute-start.30 = (bf16[56,1024]{1,0:T(8,128)(2,1)S(1)}, bf16[56,1024]{1,0:T(8,128)(2,1)S(1)}, u32[]{:S(2)}, u32[]{:S(2)}) collective-permute-start(bf16[56,1024]{1,0:T(8,128)(2,1)S(1)} %get-tuple-element.243), channel_id=1, source_target_pairs={{0,3},{1,2},{2,1},{3,0},{4,7},{5,6},{6,5},{7,4},{8,11},{9,10},{10,... | collective-permute-start | bytes 344072 | tf_op jit(solution)/shard_map/ppermute | solution.py:321
  112.3 20.1 %collective-permute-start.33 = (bf16[256,1024]{1,0:T(8,128)(2,1)S(1)}, bf16[256,1024]{1,0:T(8,128)(2,1)S(1)}, u32[]{:S(2)}, u32[]{:S(2)}) collective-permute-start(bf16[256,1024]{1,0:T(8,128)(2,1)S(1)} %shard_map.206.w0), channel_id=1, source_target_pairs={{0,16},{1,17},{2,18},{3,19},{4,20},{5,21},{6,22},{7,23},{8,24},{9,... | collective-permute-start | bytes 1572872 | tf_op jit(solution)/shard_map/ppermute | solution.py:321
  119.8 16.9 %collective-permute-start.34 = (bf16[256,1024]{1,0:T(8,128)(2,1)S(1)}, bf16[256,1024]{1,0:T(8,128)(2,1)S(1)}, u32[]{:S(2)}, u32[]{:S(2)}) collective-permute-start(bf16[256,1024]{1,0:T(8,128)(2,1)S(1)} %collective-permute-done.32.w1), channel_id=1, source_target_pairs={{0,16},{1,17},{2,18},{3,19},{4,20},{5,21},{6,22},{7,23},{8,24},{9,... | collective-permute-start | bytes 1572872 | tf_op jit(solution)/shard_map/ppermute | solution.py:321
  121.9 8.0 %collective-permute-start.29 = (bf16[56,1024]{1,0:T(8,128)(2,1)S(1)}, bf16[56,1024]{1,0:T(8,128)(2,1)S(1)}, u32[]{:S(2)}, u32[]{:S(2)}) collective-permute-start(bf16[56,1024]{1,0:T(8,128)(2,1)S(1)} %get-tuple-element.243), channel_id=1, source_target_pairs={{0,2},{1,3},{2,0},{3,1},{4,6},{5,7},{6,4},{7,5},{8,10},{9,11},{10,... | collective-permute-start | bytes 344072 | tf_op jit(solution)/shard_map/ppermute | solution.py:321
  125.1 13.3 %collective-permute-start.35 = (bf16[256,1024]{1,0:T(8,128)(2,1)S(1)}, bf16[256,1024]{1,0:T(8,128)(2,1)S(1)}, u32[]{:S(2)}, u32[]{:S(2)}) collective-permute-start(bf16[256,1024]{1,0:T(8,128)(2,1)S(1)} %collective-permute-done.22.w2), channel_id=1, source_target_pairs={{0,8},{1,9},{2,10},{3,11},{4,12},{5,13},{6,14},{7,15},{8,0},{9,1},... | collective-permute-start | bytes 1572872 | tf_op jit(solution)/shard_map/ppermute | solution.py:321
  131.6 6.8 %collective-permute-start.27 = (bf16[196,1024]{1,0:T(8,128)(2,1)S(1)}, bf16[196,1024]{1,0:T(8,128)(2,1)S(1)}, u32[]{:S(2)}, u32[]{:S(2)}) collective-permute-start(bf16[196,1024]{1,0:T(8,128)(2,1)S(1)} %get-tuple-element.241.own), channel_id=1, source_target_pairs={{0,4},{1,5},{2,6},{3,7},{4,0},{5,1},{6,2},{7,3},{8,12},{9,13},{10,... | collective-permute-start | bytes 1204232 | tf_op jit(solution)/shard_map/ppermute | solution.py:321
  146.7 11.6 %collective-permute-start.37 = (bf16[196,1024]{1,0:T(8,128)(2,1)S(1)}, bf16[196,1024]{1,0:T(8,128)(2,1)S(1)}, u32[]{:S(2)}, u32[]{:S(2)}) collective-permute-start(bf16[196,1024]{1,0:T(8,128)(2,1)S(1)} %get-tuple-element.252), channel_id=1, source_target_pairs={{0,1},{1,0},{2,3},{3,2},{4,5},{5,4},{6,7},{7,6},{8,9},{9,8},{10,11... | collective-permute-start | bytes 1204232 | tf_op jit(solution)/shard_map/ppermute | solution.py:321
  148.6 56.9 %collective-permute-start.69 = (bf16[2,256,1024]{2,1,0:T(8,128)(2,1)S(1)}, bf16[2,256,1024]{2,1,0:T(8,128)(2,1)S(1)}, u32[]{:S(2)}, u32[]{:S(2)}) collective-permute-start(bf16[2,256,1024]{2,1,0:T(8,128)(2,1)S(1)} %get-tuple-element.342), channel_id=1, source_target_pairs={{0,16},{1,17},{2,18},{3,19},{4,20},{5,21},{6,22},{7,23},{8,24},{9,... | collective-permute-start | bytes 3145736 | tf_op jit(solution)/shard_map/ppermute | solution.py:321
  151.3 56.1 %collective-permute-start.67 = (bf16[2,256,1024]{2,1,0:T(8,128)(2,1)S(1)}, bf16[2,256,1024]{2,1,0:T(8,128)(2,1)S(1)}, u32[]{:S(2)}, u32[]{:S(2)}) collective-permute-start(bf16[2,256,1024]{2,1,0:T(8,128)(2,1)S(1)} %get-tuple-element.336), channel_id=1, source_target_pairs={{0,8},{1,9},{2,10},{3,11},{4,12},{5,13},{6,14},{7,15},{8,0},{9,1},... | collective-permute-start | bytes 3145736 | tf_op jit(solution)/shard_map/ppermute | solution.py:321
  162.6 16.9 %collective-permute-start.46 = (bf16[392,64]{1,0:T(8,128)(2,1)S(1)}, bf16[392,64]{1,0:T(8,128)(2,1)S(1)}, u32[]{:S(2)}, u32[]{:S(2)}) collective-permute-start(bf16[392,64]{1,0:T(8,128)(2,1)S(1)} %get-tuple-element.280), channel_id=1, source_target_pairs={{0,8},{1,9},{2,10},{3,11},{4,12},{5,13},{6,14},{7,15},{8,0},{9,1},... | collective-permute-start | bytes 150536 | tf_op jit(solution)/shard_map/ppermute | solution.py:321
  163.5 16.0 %collective-permute-start.47 = (bf16[392,64]{1,0:T(8,128)(2,1)S(1)}, bf16[392,64]{1,0:T(8,128)(2,1)S(1)}, u32[]{:S(2)}, u32[]{:S(2)}) collective-permute-start(bf16[392,64]{1,0:T(8,128)(2,1)S(1)} %get-tuple-element.281), channel_id=1, source_target_pairs={{0,16},{1,17},{2,18},{3,19},{4,20},{5,21},{6,22},{7,23},{8,24},{9,... | collective-permute-start | bytes 150536 | tf_op jit(solution)/shard_map/ppermute | solution.py:321
  165.0 16.2 %collective-permute-start.48 = (bf16[392,64]{1,0:T(8,128)(2,1)S(1)}, bf16[392,64]{1,0:T(8,128)(2,1)S(1)}, u32[]{:S(2)}, u32[]{:S(2)}) collective-permute-start(bf16[392,64]{1,0:T(8,128)(2,1)S(1)} %get-tuple-element.282), channel_id=1, source_target_pairs={{0,24},{1,25},{2,26},{3,27},{4,28},{5,29},{6,30},{7,31},{8,16},{9,... | collective-permute-start | bytes 150536 | tf_op jit(solution)/shard_map/ppermute | solution.py:321
  193.2 7.8 %collective-permute-start.49 = (bf16[392,192]{1,0:T(8,128)(2,1)S(1)}, bf16[392,192]{1,0:T(8,128)(2,1)S(1)}, u32[]{:S(2)}, u32[]{:S(2)}) collective-permute-start(bf16[392,192]{1,0:T(8,128)(2,1)S(1)} %get-tuple-element.285), channel_id=1, source_target_pairs={{0,8},{1,9},{2,10},{3,11},{4,12},{5,13},{6,14},{7,15},{8,0},{9,1},... | collective-permute-start | bytes 451592 | tf_op jit(solution)/shard_map/ppermute | solution.py:321
  194.1 9.8 %collective-permute-start.50 = (bf16[392,192]{1,0:T(8,128)(2,1)S(1)}, bf16[392,192]{1,0:T(8,128)(2,1)S(1)}, u32[]{:S(2)}, u32[]{:S(2)}) collective-permute-start(bf16[392,192]{1,0:T(8,128)(2,1)S(1)} %get-tuple-element.286), channel_id=1, source_target_pairs={{0,16},{1,17},{2,18},{3,19},{4,20},{5,21},{6,22},{7,23},{8,24},{9,... | collective-permute-start | bytes 451592 | tf_op jit(solution)/shard_map/ppermute | solution.py:321
  195.6 8.3 %collective-permute-start.51 = (bf16[392,192]{1,0:T(8,128)(2,1)S(1)}, bf16[392,192]{1,0:T(8,128)(2,1)S(1)}, u32[]{:S(2)}, u32[]{:S(2)}) collective-permute-start(bf16[392,192]{1,0:T(8,128)(2,1)S(1)} %get-tuple-element.287), channel_id=1, source_target_pairs={{0,24},{1,25},{2,26},{3,27},{4,28},{5,29},{6,30},{7,31},{8,16},{9,... | collective-permute-start | bytes 451592 | tf_op jit(solution)/shard_map/ppermute | solution.py:321
  206.2 14.8 %collective-permute-start.70 = (bf16[256,1024]{1,0:T(8,128)(2,1)S(1)}, bf16[256,1024]{1,0:T(8,128)(2,1)S(1)}, u32[]{:S(2)}, u32[]{:S(2)}) collective-permute-start(bf16[256,1024]{1,0:T(8,128)(2,1)S(1)} %get-tuple-element.344), channel_id=1, source_target_pairs={{0,8},{1,9},{2,10},{3,11},{4,12},{5,13},{6,14},{7,15},{8,0},{9,1},... | collective-permute-start | bytes 1572872 | tf_op jit(solution)/shard_map/ppermute | solution.py:321
  208.2 14.8 %collective-permute-start.68 = (bf16[256,1024]{1,0:T(8,128)(2,1)S(1)}, bf16[256,1024]{1,0:T(8,128)(2,1)S(1)}, u32[]{:S(2)}, u32[]{:S(2)}) collective-permute-start(bf16[256,1024]{1,0:T(8,128)(2,1)S(1)} %get-tuple-element.338), channel_id=1, source_target_pairs={{0,16},{1,17},{2,18},{3,19},{4,20},{5,21},{6,22},{7,23},{8,24},{9,... | collective-permute-start | bytes 1572872 | tf_op jit(solution)/shard_map/ppermute | solution.py:321
  211.6 20.3 %collective-permute-start.61 = (bf16[2,256,512]{2,1,0:T(8,128)(2,1)S(1)}, bf16[2,256,512]{2,1,0:T(8,128)(2,1)S(1)}, u32[]{:S(2)}, u32[]{:S(2)}) collective-permute-start(bf16[2,256,512]{2,1,0:T(8,128)(2,1)S(1)} %get-tuple-element.317), channel_id=1, source_target_pairs={{0,8},{1,9},{2,10},{3,11},{4,12},{5,13},{6,14},{7,15},{8,0},{9,1},... | collective-permute-start | bytes 1572872 | tf_op jit(solution)/shard_map/ppermute | solution.py:321
  213.1 20.8 %collective-permute-start.63 = (bf16[2,256,512]{2,1,0:T(8,128)(2,1)S(1)}, bf16[2,256,512]{2,1,0:T(8,128)(2,1)S(1)}, u32[]{:S(2)}, u32[]{:S(2)}) collective-permute-start(bf16[2,256,512]{2,1,0:T(8,128)(2,1)S(1)} %get-tuple-element.322), channel_id=1, source_target_pairs={{0,16},{1,17},{2,18},{3,19},{4,20},{5,21},{6,22},{7,23},{8,24},{9,... | collective-permute-start | bytes 1572872 | tf_op jit(solution)/shard_map/ppermute | solution.py:321
  213.8 21.4 %collective-permute-start.39 = (bf16[196,1024]{1,0:T(8,128)(2,1)S(1)}, bf16[196,1024]{1,0:T(8,128)(2,1)S(1)}, u32[]{:S(2)}, u32[]{:S(2)}) collective-permute-start(bf16[196,1024]{1,0:T(8,128)(2,1)S(1)} %get-tuple-element.269), channel_id=1, source_target_pairs={{0,4},{1,5},{2,6},{3,7},{4,0},{5,1},{6,2},{7,3},{8,12},{9,13},{10,... | collective-permute-start | bytes 1204232 | tf_op jit(solution)/shard_map/ppermute | solution.py:321
  223.8 59.2 %collective-permute-start.71 = (bf16[2,256,1024]{2,1,0:T(8,128)(2,1)S(1)}, bf16[2,256,1024]{2,1,0:T(8,128)(2,1)S(1)}, u32[]{:S(2)}, u32[]{:S(2)}) collective-permute-start(bf16[2,256,1024]{2,1,0:T(8,128)(2,1)S(1)} %get-tuple-element.346), channel_id=1, source_target_pairs={{4,6},{5,7},{6,4},{7,5},{12,14},{13,15},{14,12},{15,13},{20,22},{2... | collective-permute-start | bytes 3145736 | tf_op jit(solution)/shard_map/ppermute | solution.py:969
  232.5 22.8 %collective-permute-start.62 = (bf16[256,512]{1,0:T(8,128)(2,1)S(1)}, bf16[256,512]{1,0:T(8,128)(2,1)S(1)}, u32[]{:S(2)}, u32[]{:S(2)}) collective-permute-start(bf16[256,512]{1,0:T(8,128)(2,1)S(1)} %get-tuple-element.319), channel_id=1, source_target_pairs={{0,16},{1,17},{2,18},{3,19},{4,20},{5,21},{6,22},{7,23},{8,24},{9,... | collective-permute-start | bytes 786440 | tf_op jit(solution)/shard_map/ppermute | solution.py:321
  234.5 20.8 %collective-permute-start.64 = (bf16[256,512]{1,0:T(8,128)(2,1)S(1)}, bf16[256,512]{1,0:T(8,128)(2,1)S(1)}, u32[]{:S(2)}, u32[]{:S(2)}) collective-permute-start(bf16[256,512]{1,0:T(8,128)(2,1)S(1)} %get-tuple-element.324), channel_id=1, source_target_pairs={{0,8},{1,9},{2,10},{3,11},{4,12},{5,13},{6,14},{7,15},{8,0},{9,1},... | collective-permute-start | bytes 786440 | tf_op jit(solution)/shard_map/ppermute | solution.py:321
  235.9 18.6 %collective-permute-start.40 = (bf16[98,1024]{1,0:T(8,128)(2,1)S(1)}, bf16[98,1024]{1,0:T(8,128)(2,1)S(1)}, u32[]{:S(2)}, u32[]{:S(2)}) collective-permute-start(bf16[98,1024]{1,0:T(8,128)(2,1)S(1)} %get-tuple-element.271), channel_id=1, source_target_pairs={{0,1},{1,0},{2,3},{3,2},{4,5},{5,4},{6,7},{7,6},{8,9},{9,8},{10,11... | collective-permute-start | bytes 602120 | tf_op jit(solution)/shard_map/ppermute | solution.py:321
  237.4 31.7 %collective-permute-start.53 = (bf16[98,1024]{1,0:T(8,128)(2,1)S(1)}, bf16[98,1024]{1,0:T(8,128)(2,1)S(1)}, u32[]{:S(2)}, u32[]{:S(2)}) collective-permute-start(bf16[98,1024]{1,0:T(8,128)(2,1)S(1)} %get-tuple-element.291), channel_id=1, source_target_pairs={{0,1},{1,0},{2,3},{3,2},{4,5},{5,4},{6,7},{7,6},{8,9},{9,8},{10,11... | collective-permute-start | bytes 602120 | tf_op jit(solution)/shard_map/ppermute | solution.py:321
  255.2 13.0 %collective-permute-start.41 = (bf16[56,1024]{1,0:T(8,128)(2,1)S(1)}, bf16[56,1024]{1,0:T(8,128)(2,1)S(1)}, u32[]{:S(2)}, u32[]{:S(2)}) collective-permute-start(bf16[56,1024]{1,0:T(8,128)(2,1)S(1)} %get-tuple-element.273), channel_id=1, source_target_pairs={{0,2},{1,3},{2,0},{3,1},{4,6},{5,7},{6,4},{7,5},{8,10},{9,11},{10,... | collective-permute-start | bytes 344072 | tf_op jit(solution)/shard_map/ppermute | solution.py:321
  256.0 31.0 %collective-permute-start.65 = (bf16[2,256,512]{2,1,0:T(8,128)(2,1)S(1)}, bf16[2,256,512]{2,1,0:T(8,128)(2,1)S(1)}, u32[]{:S(2)}, u32[]{:S(2)}) collective-permute-start(bf16[2,256,512]{2,1,0:T(8,128)(2,1)S(1)} %get-tuple-element.326), channel_id=1, source_target_pairs={{4,6},{5,7},{6,4},{7,5},{12,14},{13,15},{14,12},{15,13},{20,22},{2... | collective-permute-start | bytes 1572872 | tf_op jit(solution)/shard_map/ppermute | solution.py:969
  269.0 15.2 %collective-permute-start.42 = (bf16[4,56,1024]{2,1,0:T(8,128)(2,1)S(1)}, bf16[4,56,1024]{2,1,0:T(8,128)(2,1)S(1)}, u32[]{:S(2)}, u32[]{:S(2)}) collective-permute-start(bf16[4,56,1024]{2,1,0:T(8,128)(2,1)S(1)} %get-tuple-element.275), channel_id=1, source_target_pairs={{0,4},{1,5},{2,6},{3,7},{4,0},{5,1},{6,2},{7,3},{8,12},{9,13},{10,... | collective-permute-start | bytes 1376264 | tf_op jit(solution)/shard_map/ppermute | solution.py:321
  270.2 11.9 %collective-permute-start.55 = (bf16[64,1024]{1,0:T(8,128)(2,1)S(1)}, bf16[64,1024]{1,0:T(8,128)(2,1)S(1)}, u32[]{:S(2)}, u32[]{:S(2)}) collective-permute-start(bf16[64,1024]{1,0:T(8,128)(2,1)S(1)} %get-tuple-element.298), channel_id=1, source_target_pairs={{0,2},{1,3},{2,0},{3,1},{4,6},{5,7},{6,4},{7,5},{8,10},{9,11},{10,... | collective-permute-start | bytes 393224 | tf_op jit(solution)/shard_map/ppermute | solution.py:321
  270.2 6.5 %collective-permute-start.56 = (bf16[8,1024]{1,0:T(8,128)(2,1)S(1)}, bf16[8,1024]{1,0:T(8,128)(2,1)S(1)}, u32[]{:S(2)}, u32[]{:S(2)}) collective-permute-start(bf16[8,1024]{1,0:T(8,128)(2,1)S(1)} %get-tuple-element.297), channel_id=1, source_target_pairs={{0,3},{1,2},{2,1},{3,0},{4,7},{5,6},{6,5},{7,4},{8,11},{9,10},{10,... | collective-permute-start | bytes 49160 | tf_op jit(solution)/shard_map/ppermute | solution.py:321
  282.9 6.1 %collective-permute-start.57 = (bf16[4,56,1024]{2,1,0:T(8,128)(2,1)S(1)}, bf16[4,56,1024]{2,1,0:T(8,128)(2,1)S(1)}, u32[]{:S(2)}, u32[]{:S(2)}) collective-permute-start(bf16[4,56,1024]{2,1,0:T(8,128)(2,1)S(1)} %get-tuple-element.300), channel_id=1, source_target_pairs={{0,4},{1,5},{2,6},{3,7},{4,0},{5,1},{6,2},{7,3},{8,12},{9,13},{10,... | collective-permute-start | bytes 1376264 | tf_op jit(solution)/shard_map/ppermute | solution.py:321
  283.7 29.0 %collective-permute-start.72 = (bf16[2,128,1024]{2,1,0:T(8,128)(2,1)S(1)}, bf16[2,128,1024]{2,1,0:T(8,128)(2,1)S(1)}, u32[]{:S(2)}, u32[]{:S(2)}) collective-permute-start(bf16[2,128,1024]{2,1,0:T(8,128)(2,1)S(1)} %get-tuple-element.348), channel_id=1, source_target_pairs={{0,4},{1,5},{2,6},{3,7},{4,0},{5,1},{6,2},{7,3},{8,12},{9,13},{10,... | collective-permute-start | bytes 1572872 | tf_op jit(solution)/shard_map/ppermute | solution.py:321
  284.8 8.5 %collective-permute-start.43 = (bf16[2,56,1024]{2,1,0:T(8,128)(2,1)S(1)}, bf16[2,56,1024]{2,1,0:T(8,128)(2,1)S(1)}, u32[]{:S(2)}, u32[]{:S(2)}) collective-permute-start(bf16[2,56,1024]{2,1,0:T(8,128)(2,1)S(1)} %get-tuple-element.276), channel_id=1, source_target_pairs={{0,8},{1,9},{2,10},{3,11},{4,12},{5,13},{6,14},{7,15},{8,0},{9,1},... | collective-permute-start | bytes 688136 | tf_op jit(solution)/shard_map/ppermute | solution.py:321
  286.3 12.1 %collective-permute-start.44 = (bf16[2,56,1024]{2,1,0:T(8,128)(2,1)S(1)}, bf16[2,56,1024]{2,1,0:T(8,128)(2,1)S(1)}, u32[]{:S(2)}, u32[]{:S(2)}) collective-permute-start(bf16[2,56,1024]{2,1,0:T(8,128)(2,1)S(1)} %get-tuple-element.277), channel_id=1, source_target_pairs={{0,16},{1,17},{2,18},{3,19},{4,20},{5,21},{6,22},{7,23},{8,24},{9,... | collective-permute-start | bytes 688136 | tf_op jit(solution)/shard_map/ppermute | solution.py:321
  287.1 12.2 %collective-permute-start.45 = (bf16[2,56,1024]{2,1,0:T(8,128)(2,1)S(1)}, bf16[2,56,1024]{2,1,0:T(8,128)(2,1)S(1)}, u32[]{:S(2)}, u32[]{:S(2)}) collective-permute-start(bf16[2,56,1024]{2,1,0:T(8,128)(2,1)S(1)} %get-tuple-element.278), channel_id=1, source_target_pairs={{0,24},{1,25},{2,26},{3,27},{4,28},{5,29},{6,30},{7,31},{8,16},{9,... | collective-permute-start | bytes 688136 | tf_op jit(solution)/shard_map/ppermute | solution.py:321
  289.0 22.3 %collective-permute-start.66 = (bf16[2,128,512]{2,1,0:T(8,128)(2,1)S(1)}, bf16[2,128,512]{2,1,0:T(8,128)(2,1)S(1)}, u32[]{:S(2)}, u32[]{:S(2)}) collective-permute-start(bf16[2,128,512]{2,1,0:T(8,128)(2,1)S(1)} %get-tuple-element.328), channel_id=1, source_target_pairs={{0,4},{1,5},{2,6},{3,7},{4,0},{5,1},{6,2},{7,3},{8,12},{9,13},{10,... | collective-permute-start | bytes 786440 | tf_op jit(solution)/shard_map/ppermute | solution.py:321
  293.4 9.9 %collective-permute-start.58 = (bf16[2,56,1024]{2,1,0:T(8,128)(2,1)S(1)}, bf16[2,56,1024]{2,1,0:T(8,128)(2,1)S(1)}, u32[]{:S(2)}, u32[]{:S(2)}) collective-permute-start(bf16[2,56,1024]{2,1,0:T(8,128)(2,1)S(1)} %get-tuple-element.301), channel_id=1, source_target_pairs={{0,8},{1,9},{2,10},{3,11},{4,12},{5,13},{6,14},{7,15},{8,0},{9,1},... | collective-permute-start | bytes 688136 | tf_op jit(solution)/shard_map/ppermute | solution.py:321
  298.4 10.9 %collective-permute-start.59 = (bf16[2,56,1024]{2,1,0:T(8,128)(2,1)S(1)}, bf16[2,56,1024]{2,1,0:T(8,128)(2,1)S(1)}, u32[]{:S(2)}, u32[]{:S(2)}) collective-permute-start(bf16[2,56,1024]{2,1,0:T(8,128)(2,1)S(1)} %get-tuple-element.302), channel_id=1, source_target_pairs={{0,16},{1,17},{2,18},{3,19},{4,20},{5,21},{6,22},{7,23},{8,24},{9,... | collective-permute-start | bytes 688136 | tf_op jit(solution)/shard_map/ppermute | solution.py:321
  299.3 10.1 %collective-permute-start.60 = (bf16[2,56,1024]{2,1,0:T(8,128)(2,1)S(1)}, bf16[2,56,1024]{2,1,0:T(8,128)(2,1)S(1)}, u32[]{:S(2)}, u32[]{:S(2)}) collective-permute-start(bf16[2,56,1024]{2,1,0:T(8,128)(2,1)S(1)} %get-tuple-element.303), channel_id=1, source_target_pairs={{0,24},{1,25},{2,26},{3,27},{4,28},{5,29},{6,30},{7,31},{8,16},{9,... | collective-permute-start | bytes 688136 | tf_op jit(solution)/shard_map/ppermute | solution.py:321
  (15 other events, 74.8 us)

commit v4 on v3

--- a/solution.py
+++ b/solution.py
@@ -314,6 +314,7 @@
 NN, NT, TN = ((1,), (0,)), ((1,), (1,)), ((0,), (0,))
 SHARE = 49
 PAD = 56
+SMALL = 104
 CHIP_ID, CORE_ID, D_ID, T_ID = range(4)
 
 
@@ -325,10 +326,38 @@
     return lax.dot_general(left, right, (dims, ((), ())), preferred_element_type=F32)
 
 
-def call(body, outs, scalars, *args, scratch=(), flops=0):
+TIMES = {
+    "pack": 1.2,
+    "pick": 1.5,
+    "norm_one": 1.0,
+    "qkv": 1.6,
+    "attention": 7.6,
+    "proj": 1.1,
+    "norm_two": 0.9,
+    "grad_hidden": 1.6,
+    "fc": 5.6,
+    "grads_fc1": 1.8,
+    "grads_fc2": 1.8,
+    "fc2": 1.6,
+    "norm_two_back": 1.5,
+    "grad_att": 1.1,
+    "attention_back": 12.0,
+    "qkv_back": 1.5,
+    "half_grad": 1.1,
+    "grads_att": 1.8,
+    "norm_one_back": 1.0,
+    "give": 1.3,
+    "take": 12.0,
+    "finish_mlp": 1.7,
+    "finish_att": 1.4,
+}
+
+
+def call(body, outs, scalars, *args, scratch=()):
     moved = sum(math.prod(a.shape) * a.dtype.itemsize for a in args)
     moved += sum(math.prod(s) * jnp.dtype(t).itemsize for s, t in outs)
     held = sum(math.prod(s[:-1]) * max(s[-1], 128) * jnp.dtype(t).itemsize for s, t in scratch)
+    time = TIMES.get(body.__name__.removesuffix("_kernel"), 0.7)
     return pl.pallas_call(
         body,
         out_shape=[jax.ShapeDtypeStruct(s, t) for s, t in outs],
@@ -337,7 +366,9 @@
         out_specs=[pl.BlockSpec(memory_space=pltpu.VMEM)] * len(outs),
         scratch_shapes=[pltpu.VMEM(s, t) for s, t in scratch],
         compiler_params=pltpu.CompilerParams(vmem_limit_bytes=moved + held + (4 << 20)),
-        cost_estimate=pl.CostEstimate(flops=flops, bytes_accessed=moved, transcendentals=0),
+        cost_estimate=pl.CostEstimate(
+            flops=int(time * 1.15e9), bytes_accessed=moved, transcendentals=0
+        ),
     )(scalars, *args)
 
 
@@ -512,20 +543,37 @@
 PROJ = 3
 
 
-def qkv_kernel(ids, own, got, qv_bias, w0, w1, w2, w3, whole, o0, o1, o2, o3, wide, heads):
-    weights = (w0, w1, w2, w3)
+def part_of(weights, m, j):
+    if m < 3:
+        return weights[m][:, lanes(j)]
+    return weights[3 + j // 2][:, lanes(j % 2)]
+
+
+VALUES = 400
+
+
+def fold_rows(value):
+    half = value.shape[0] // 2
+    return jnp.concatenate([value[:half], value[half:]], axis=1)
+
+
+def qkv_kernel(ids, own, got, qv_bias, w0, w1, w2, w3, w4, whole, o0, o1, o2, o3, wide, heads):
+    weights = (w0, w1, w2, w3, w4)
     join_rows(wide, own, got)
     whole[...] = wide[...].astype(BF16)
     for j in range(3):
         total = dot(whole[:, lanes(0)], w0[:, lanes(j)], NN)
         for m in range(1, 4):
-            total = total + dot(whole[:, lanes(m)], weights[m][:, lanes(j)], NN)
+            total = total + dot(whole[:, lanes(m)], part_of(weights, m, j), NN)
         for h in range(4):
             part = total[:, 64 * h : 64 * h + 64]
             if j != 1:
                 k = (j // 2) * 4 + h
                 part = part + qv_bias[k : k + 1, 0:64]
-            heads[h, :, 64 * j : 64 * j + 64] = part.astype(BF16)
+            if j < 2:
+                heads[h, 0 : part.shape[0], 64 * j : 64 * j + 64] = part.astype(BF16)
+            else:
+                heads[h, VALUES:, :] = fold_rows(part).astype(BF16)
     for m, out in enumerate((o0, o1, o2, o3)):
         out[...] = heads[ids[CHIP_ID] ^ m, :, :]
 
@@ -533,10 +581,19 @@
 STEP = 224
 
 
+def stage_qkv(stage, parts):
+    tokens = stage.shape[0] // 4
+    half = tokens // 2
+    for m, part in enumerate(parts):
+        start = tokens * m
+        stage[start : start + tokens, 0:128] = part[0:tokens, :].astype(F32)
+        stage[start : start + half, 128:192] = part[VALUES:, 0:64].astype(F32)
+        stage[start + half : start + tokens, 128:192] = part[VALUES:, 64:128].astype(F32)
+
+
 def attention_kernel(ids, a0, a1, a2, a3, o0, o1, o2, o3, lse, stage, q, k, v):
-    tokens = a0.shape[0]
-    for m, part in enumerate((a0, a1, a2, a3)):
-        stage[tokens * m : tokens * m + tokens, :] = part[...].astype(F32)
+    tokens = stage.shape[0] // 4
+    stage_qkv(stage, (a0, a1, a2, a3))
     q[...] = (stage[:, 0:64] * 0.125).astype(BF16)
     k[...] = stage[:, 64:128].astype(BF16)
     v[...] = stage[:, 128:192].astype(BF16)
@@ -555,20 +612,21 @@
 
     lax.fori_loop(0, stage.shape[0] // STEP, body, 0)
     for m, out in enumerate((o0, o1, o2, o3)):
-        out[...] = stage[tokens * m : tokens * m + tokens, 0:64].astype(BF16)
+        out[...] = fold_rows(stage[tokens * m : tokens * m + tokens, 0:64]).astype(BF16)
 
 
 def attention_back_kernel(
     ids, a0, a1, a2, a3, g0, g1, g2, g3, lse, o0, o1, o2, o3, stage, q, k, v, g, grad_k, grad_v
 ):
-    tokens = a0.shape[0]
-    for m, part in enumerate((a0, a1, a2, a3)):
-        stage[tokens * m : tokens * m + tokens, :] = part[...].astype(F32)
+    tokens = stage.shape[0] // 4
+    stage_qkv(stage, (a0, a1, a2, a3))
     q[...] = (stage[:, 0:64] * 0.125).astype(BF16)
     k[...] = stage[:, 64:128].astype(BF16)
     v[...] = stage[:, 128:192].astype(BF16)
     for m, part in enumerate((g0, g1, g2, g3)):
-        stage[tokens * m : tokens * m + tokens, 0:64] = part[...].astype(F32)
+        middle = tokens * m + tokens // 2
+        stage[tokens * m : middle, 0:64] = part[:, 0:64].astype(F32)
+        stage[middle : tokens * m + tokens, 0:64] = part[:, 64:128].astype(F32)
     g[...] = stage[:, 0:64].astype(BF16)
     keys_t = jnp.transpose(k[...])
     grad_k[...] = jnp.zeros_like(grad_k)
@@ -589,9 +647,9 @@
     lax.fori_loop(0, stage.shape[0] // STEP, body, 0)
     for m, out in enumerate((o0, o1, o2, o3)):
         rows = slice(tokens * m, tokens * m + tokens)
-        out[:, 0:64] = stage[rows, 0:64].astype(BF16)
-        out[:, 64:128] = grad_k[rows, :].astype(BF16)
-        out[:, 128:192] = grad_v[rows, :].astype(BF16)
+        out[0:tokens, 0:64] = stage[rows, 0:64].astype(BF16)
+        out[0:tokens, 64:128] = grad_k[rows, :].astype(BF16)
+        out[VALUES:, :] = fold_rows(grad_v[rows, :]).astype(BF16)
 
 
 def split_rows(total, keep, send, cols):
@@ -600,14 +658,18 @@
     send[:, cols] = total[half:].astype(BF16)
 
 
-def proj_kernel(ids, a0, a1, a2, a3, w0, w1, w2, w3, joined, keep, send, heads):
+def proj_kernel(ids, a0, a1, a2, a3, w0, w1, w2, w3, w4, joined, keep, send, heads, wide):
     for m, part in enumerate((a0, a1, a2, a3)):
         heads[m, :, :] = part[...]
+    half = keep.shape[0]
     for h in range(4):
-        joined[:, 64 * h : 64 * h + 64] = heads[h ^ ids[CHIP_ID], :, :]
+        part = heads[h ^ ids[CHIP_ID], :, :].astype(F32)
+        wide[0:half, 64 * h : 64 * h + 64] = part[:, 0:64]
+        wide[half:, 64 * h : 64 * h + 64] = part[:, 64:128]
+    joined[...] = wide[...].astype(BF16)
     for m in range(4):
-        weight = (w0, w1, w2, w3)[m]
-        split_rows(dot(joined[...], weight[:, lanes(PROJ)], NT), keep, send, lanes(m))
+        weight = part_of((w0, w1, w2, w3, w4), m, PROJ)
+        split_rows(dot(joined[...], weight, NT), keep, send, lanes(m))
 
 
 def pair_kernel(ids, keep, got, part, send):
@@ -622,6 +684,28 @@
     low = is_zero(z_low(ids))
     part[...] = pick(low, total[:own], total[own:])
     send[...] = pick(low, total[own:], total[:own]).astype(BF16)
+
+
+def half_grad_kernel(ids, keep, got, rows, sums_two, sums_fc1, sums_qv, part, send, small):
+    own = part.shape[0]
+    total = keep[...] + got[...].astype(F32)
+    low = is_zero(z_low(ids))
+    part[...] = pick(low, total[:own], total[own:])
+    scaled, _ = norm_parts(rows[...].astype(F32))
+    send[0:own, :] = pick(low, total[own:], total[:own]).astype(BF16)
+    sums = jnp.concatenate(
+        [
+            jnp.sum(total * scaled, axis=0, keepdims=True),
+            sums_two[0:1, :],
+            jnp.sum(total, axis=0, keepdims=True),
+            sums_two[1:4, :],
+            sums_qv[...],
+            sums_fc1[...],
+        ],
+        axis=0,
+    )
+    small[...] = sums
+    send[SMALL : SMALL + 8, :] = sums.astype(BF16)
 
 
 def norm_two_kernel(ids, rows, part, got, vec, residual, normed):
@@ -701,36 +785,43 @@
     sums[4:8, :] = jnp.zeros((4, sums.shape[1]), F32)
 
 
-def grad_att_kernel(ids, own, got, w0, w1, w2, w3, whole, o0, o1, o2, o3, wide, heads):
+def grad_att_kernel(ids, own, got, w0, w1, w2, w3, w4, whole, o0, o1, o2, o3, wide, heads):
     join_rows(wide, own, got)
     whole[...] = wide[...].astype(BF16)
-    weights = (w0, w1, w2, w3)
+    weights = (w0, w1, w2, w3, w4)
     total = dot(whole[:, lanes(0)], w0[:, lanes(PROJ)], NN)
     for m in range(1, 4):
-        total = total + dot(whole[:, lanes(m)], weights[m][:, lanes(PROJ)], NN)
+        total = total + dot(whole[:, lanes(m)], part_of(weights, m, PROJ), NN)
     for h in range(4):
-        heads[h, :, :] = total[:, 64 * h : 64 * h + 64].astype(BF16)
+        heads[h, :, :] = fold_rows(total[:, 64 * h : 64 * h + 64]).astype(BF16)
     for m, out in enumerate((o0, o1, o2, o3)):
         out[...] = heads[ids[CHIP_ID] ^ m, :, :]
 
 
-def qkv_back_kernel(ids, g0, g1, g2, g3, w0, w1, w2, w3, joined, keep, send, sums, heads):
+def qkv_back_kernel(ids, g0, g1, g2, g3, w0, w1, w2, w3, w4, joined, keep, send, sums, heads, wide):
     for m, part in enumerate((g0, g1, g2, g3)):
         heads[m, :, :] = part[...]
+    half, tokens = keep.shape[0], joined.shape[0]
     for h in range(4):
         part = heads[h ^ ids[CHIP_ID], :, :]
-        for j in range(3):
-            piece = part[:, 64 * j : 64 * j + 64]
-            joined[:, 256 * j + 64 * h : 256 * j + 64 * h + 64] = piece
-            if j != 1:
-                k = (j // 2) * 4 + h
-                total = jnp.sum(piece.astype(F32), axis=0, keepdims=True)
-                sums[0:1, 128 * k : 128 * k + 128] = jnp.concatenate(
-                    [total, jnp.zeros((1, 64), F32)], axis=1
-                )
+        for j in range(2):
+            joined[:, 256 * j + 64 * h : 256 * j + 64 * h + 64] = part[
+                0:tokens, 64 * j : 64 * j + 64
+            ]
+        values = part[VALUES:, :].astype(F32)
+        wide[0:half, 64 * h : 64 * h + 64] = values[:, 0:64]
+        wide[half:, 64 * h : 64 * h + 64] = values[:, 64:128]
+        for k, value in ((h, part[0:tokens, 0:64]), (4 + h, wide[:, 64 * h : 64 * h + 64])):
+            total = jnp.sum(value.astype(F32), axis=0, keepdims=True)
+            sums[0:1, 128 * k : 128 * k + 128] = jnp.concatenate(
+                [total, jnp.zeros((1, 64), F32)], axis=1
+            )
+    joined[:, 512:768] = wide[...].astype(BF16)
     for m in range(4):
-        weight = (w0, w1, w2, w3)[m]
-        total = dot(joined[...], weight[:, 0:768], NT)
+        weights = (w0, w1, w2, w3, w4)
+        total = dot(joined[:, lanes(0)], part_of(weights, m, 0), NT)
+        for j in (1, 2):
+            total = total + dot(joined[:, lanes(j)], part_of(weights, m, j), NT)
         split_rows(total, keep, send, lanes(m))
 
 
@@ -750,26 +841,16 @@
 
 
 def norm_one_back_kernel(
-    ids, rows, part, got, grad_residual, vec, sums_two, sums_fc1, sums_qv, here, there, small_out, wide
+    ids, rows, part, got, grad_residual, vec, small, here, there, wide
 ):
     scaled, inverse = norm_parts(own_half(ids, rows))
-    total = part[...] + got[...].astype(F32)
+    total = part[...] + got[0 : 2 * SHARE, :].astype(F32)
     result = own_half(ids, grad_residual) + norm_back(total, scaled, inverse, vec[0:1, :])
     to_owners(ids, result, wide, here, there)
-    small = jnp.concatenate(
-        [
-            jnp.sum(total * scaled, axis=0, keepdims=True),
-            sums_two[0:1, :],
-            jnp.sum(total, axis=0, keepdims=True),
-            sums_two[1:4, :],
-            sums_qv[...],
-            sums_fc1[...],
-        ],
-        axis=0,
-    )
-    small_out[...] = small.astype(BF16)
-    here[PAD : PAD + 8, :] = small.astype(BF16)
-    there[PAD : PAD + 8, :] = small.astype(BF16)
+    far = jnp.where(row_ids((8, 1024)) < 6, got[SMALL : SMALL + 8, :].astype(F32), 0.0)
+    sums = (small[...] + far).astype(BF16)
+    here[PAD : PAD + 8, :] = sums
+    there[PAD : PAD + 8, :] = sums
 
 
 def layer_out_kernel(ids, residual, part, got, vec, here, there, wide):
@@ -787,20 +868,20 @@
     return jnp.where(slots[d, 0:1, 0:1] > 0.5, left, value)
 
 
-def give_kernel(ids, slots, here, away, keep, send):
-    left = here[0:PAD, :].astype(F32)
-    right = away[0:PAD, :].astype(F32)
+def give_out_kernel(ids, slots, here, away, keep, send):
+    left = here[...].astype(F32)
+    right = away[...].astype(F32)
     for out, flip in ((keep, 0), (send, 1)):
         for m, d in enumerate(far_chips(ids, flip)):
             out[m, :, :] = for_slot(slots, d, left, right).astype(BF16)
 
 
-def give_grad_kernel(ids, slots, here, s1, away, s3, keep, send, rel, flat, tail):
+def give_kernel(ids, slots, here, away, keep, send, rel, flat, tail):
     left = here[0:PAD, :].astype(F32)
     right = away[0:PAD, :].astype(F32)
     own = here[PAD : PAD + 8, :].astype(F32)
     far = away[PAD : PAD + 8, :].astype(F32)
-    rel[...] = own + far + s1[...].astype(F32) + s3[...].astype(F32)
+    rel[...] = own + far
     home = pick(is_zero(ids[CORE_ID]), own, far)
     for m in range(4):
         flat[:, chip_lanes(ids, m)] = rel[:, lanes(m)]
@@ -826,14 +907,12 @@
         out[SHARE * j : SHARE * j + SHARE, :] = stage[j, 0:SHARE, :]
 
 
-def take_kernel(ids, keep, got, d1, d2, d3, out, stage, wide):
+def take_out_kernel(ids, keep, got, d1, d2, d3, out, stage, wide):
     settle_rows(arrived(ids, keep, got, d1, d2, d3), stage, wide)
-    out[...] = wide[...].astype(out.dtype)
-
-
-def take_grad_kernel(
-    ids, keep, got, d1, d2, d3, out, gains, biases, last, qv, b_fc1, stage
-):
+    out[...] = wide[...].astype(BF16)
+
+
+def take_kernel(ids, keep, got, d1, d2, d3, out, gains, biases, last, qv, b_fc1, stage):
     parts = arrived(ids, keep, got, d1, d2, d3)
     settle_rows(parts, stage, out)
     total = jnp.zeros((8, 384), F32)
@@ -844,8 +923,8 @@
     biases[...] = rows[3:7, 0:32]
     last[...] = rows[6:7, 0:32]
     b_fc1[...] = total[7:8, 0:128]
-    parts = jnp.concatenate([total[1:8, 128:256], total[1:2, 256:384]], axis=0)
-    qv[...] = pltpu.roll(parts, (128 - 8 * ids[D_ID]) & 127, 1)[:, 0:8]
+    pieces = jnp.concatenate([total[1:8, 128:256], total[1:2, 256:384]], axis=0)
+    qv[...] = pltpu.roll(pieces, (128 - 8 * ids[D_ID]) & 127, 1)[:, 0:8]
 
 
 def shards_kernel(ids, qkv, proj, fc2, first, second):
@@ -915,37 +994,48 @@
     whole[...] = here[...] + got[0, :, :].astype(F32)
 
 
-def gather_kernel(ids, whole_x, got_x, whole_y, got_y, part, send):
-    for k, (whole, got) in enumerate(((whole_x, got_x), (whole_y, got_y))):
-        total = whole[...] + got[...].astype(F32)
-        part[k, :, :] = total
-        send[k, :, :] = total.astype(BF16)
-
-
-def divide_kernel(ids, part, moved, keep, send):
+def gather_kernel(ids, whole_x, got_x, whole_y, got_y, keep, send):
+    n = whole_x.shape[1]
+    for core in range(2):
+
+        @pl.when(ids[CORE_ID] == core)
+        def _():
+            own = slice(128 * core, 128 * core + 128)
+            other = slice(128 - 128 * core, 256 - 128 * core)
+            for cols, whole, got in (
+                (slice(0, n), whole_x, got_x),
+                (slice(n, 2 * n), whole_y, got_y),
+            ):
+                for out, rows in ((keep, own), (send, other)):
+                    total = whole[rows, :] + got[rows, :].astype(F32)
+                    out[:, cols] = total.astype(BF16)
+
+
+def away_kernel(ids, keep, got, out):
     @pl.when(ids[CORE_ID] == 0)
     def _():
-        keep[...] = part[:, 0:128, :]
-        send[...] = part[:, 128:256, :].astype(BF16)
+        out[...] = got[...]
 
     @pl.when(ids[CORE_ID] != 0)
     def _():
-        keep[...] = moved[:, 128:256, :].astype(F32)
-        send[...] = moved[:, 0:128, :]
-
-
-def finish_mlp_kernel(ids, keep, got, fc1, fc2):
-    fc1[...] = keep[0, :, :] + got[0, :, :].astype(F32)
-    fc2[...] = jnp.transpose(keep[1, :, :] + got[1, :, :].astype(F32))
-
-
-def finish_att_kernel(ids, keep, got, qkv, proj):
-    first = keep[0, :, :] + got[0, :, :].astype(F32)
-    second = keep[1, :, :] + got[1, :, :].astype(F32)
-    qkv[0, :, :] = first[:, 0:256]
-    qkv[1, :, :] = first[:, 256:512]
-    qkv[2, :, :] = second[:, 0:256]
-    proj[...] = jnp.transpose(second[:, 256:512])
+        out[...] = keep[...]
+
+
+def whole_sum(ids, keep, got, moved, cols):
+    core = is_zero(ids[CORE_ID])
+    own = pick(core, keep[:, cols].astype(F32), got[:, cols].astype(F32))
+    return own + moved[:, cols].astype(F32)
+
+
+def finish_mlp_kernel(ids, keep, got, moved, fc1, fc2):
+    fc1[...] = whole_sum(ids, keep, got, moved, slice(0, 1024))
+    fc2[...] = jnp.transpose(whole_sum(ids, keep, got, moved, slice(1024, 2048)))
+
+
+def finish_att_kernel(ids, keep, got, moved, qkv, proj):
+    for j in range(3):
+        qkv[j, :, :] = whole_sum(ids, keep, got, moved, lanes(j))
+    proj[...] = jnp.transpose(whole_sum(ids, keep, got, moved, lanes(PROJ)))
 
 
 def tie(*values):
@@ -957,24 +1047,19 @@
     outs = [((256, n), BF16), ((256, n), F32)]
     other_x, whole_x = call(fold_kernel, outs, ids, *first)
     other_y, whole_y = call(fold_kernel, outs, ids, *second)
+    return whole_x, other_x, whole_y, other_y
+
+
+def send_second(whole_x, other_x, whole_y, other_y):
     return whole_x, swap(other_x, Y), whole_y, swap(other_y, X)
 
 
 def sum_third(ids, parts):
-    n = parts[0].shape[1]
-    part, send = call(
-        gather_kernel, [((2, 256, n), F32), ((2, 256, n), BF16)], ids, *parts
-    )
-    pairs = [(i, i ^ Z_HIGH) for i in range(32) if i & CORE]
-    return part, lax.ppermute(send, AXES, pairs)
-
-
-def sum_last(ids, body, outs, part, moved):
-    n = part.shape[2]
-    keep, send = call(
-        divide_kernel, [((2, 128, n), F32), ((2, 128, n), BF16)], ids, part, moved
-    )
-    return call(body, outs, ids, keep, swap(send, CORE))
+    n = 2 * parts[0].shape[1]
+    keep, send = call(gather_kernel, [((128, n), BF16)] * 2, ids, *parts)
+    got = swap(send, CORE)
+    (away,) = call(away_kernel, [((128, n), BF16)], ids, keep, got)
+    return keep, got, away
 
 
 def on_device_spread(
@@ -997,13 +1082,16 @@
     half, own = count // 2, count // 4
     behind = (PAD + 8, 1024)
     plain = (PAD, 1024)
+    packed = (VALUES + half, 128)
     wide = ((count, 1024), F32)
 
-    def to_devices(keep, send):
+    def to_chips(keep, send):
         got = swap(send, CORE)
         shape = (2, *keep.shape[1:])
-        outs = call(pair_up_kernel, [(shape, BF16)] * 3, ids, keep, got)
-        return keep, got, *(swap(outs[m], CHIP_MASKS[m + 1]) for m in range(3))
+        return got, *call(pair_up_kernel, [(shape, BF16)] * 3, ids, keep, got)
+
+    def over_chips(pairs):
+        return [swap(pairs[m], CHIP_MASKS[m + 1]) for m in range(3)]
 
     def offer(shard, far):
         (send,) = call(offer_kernel, [(shard.shape, BF16)], ids, shard, far)
@@ -1037,16 +1125,21 @@
         fc2_weight,
     )
     far_a = swap(shard_a, Z_HIGH)
+    own_rows, _ = tie(clip_rows, shard_a)
     keep, send = call(
         pack_kernel,
         [((4, 2 * PAD, 1024), BF16)] * 2,
         ids,
-        clip_rows,
+        own_rows,
         out_grad,
         params,
         scratch=[((400, 1024), F32), ((8, 2 * PAD, 1024), BF16)],
     )
-    *parts, far_a = tie(*to_devices(keep, send), far_a)
+    w0 = merge(shard_a, far_a, offer(shard_a, far_a))
+    shard_f, _ = tie(fc1_weight, far_a)
+    far_f = swap(shard_f, Z_HIGH)
+    got, *pairs = to_chips(keep, send)
+    *parts, w0 = tie(keep, got, *over_chips(pairs), w0)
     here, there, here_grad, there_grad, slots = call(
         pick_kernel,
         [(behind, BF16), (behind, BF16), (plain, BF16), (plain, BF16), ((16, 8, 128), F32)],
@@ -1054,11 +1147,10 @@
         *parts,
     )
     r1, r2, r3 = swap(here, Z_LOW), swap(there, Z_HIGH), swap(there, Z_LOW | Z_HIGH)
-    far_a, shard_a, _ = tie(far_a, shard_a, here)
-    w0 = merge(shard_a, far_a, offer(shard_a, far_a))
-    w_att = (w0, swap(w0, X), swap(w0, Y), swap(w0, X | Y))
-    r1, r2, r3, shard_f = tie(r1, r2, r3, fc1_weight)
-    far_f = swap(shard_f, Z_HIGH)
+    w1, w2 = swap(w0, X), swap(w0, Y)
+    w_att = (w0, w1, w2, swap(w2[:, :512], X), swap(w1[:, 512:], Y))
+    r1, r2, r3, far_f, shard_f = tie(r1, r2, r3, far_f, shard_f)
+    f0 = merge(shard_f, far_f, offer(shard_f, far_f))
     rows, normed, vec, qkv_bias, b_fc1 = call(
         norm_one_kernel,
         [
@@ -1078,45 +1170,39 @@
 
     whole_one, *qkv = call(
         qkv_kernel,
-        [((count, 1024), BF16)] + [((count, 192), BF16)] * 4,
+        [((count, 1024), BF16)] + [(packed, BF16)] * 4,
         ids,
         normed,
         swap(normed, CORE),
         qkv_bias,
         *w_att,
-        scratch=[wide, ((4, count, 192), BF16)],
-        flops=2 * count * 1024 * 768,
+        scratch=[wide, ((4, *packed), BF16)],
     )
     shard_g, *qkv = tie(shard_g, *qkv)
     far_g = swap(shard_g, Z_HIGH)
-    *qkv, f0 = tie(*trade(qkv), merge(shard_f, far_f, offer(shard_f, far_f)))
+    *qkv, f0, here_grad, there_grad = tie(*trade(qkv), f0, here_grad, there_grad)
     f1, f2 = swap(f0, X), swap(f0, Y)
+    s1, s2 = swap(here_grad, Z_LOW), swap(there_grad, Z_HIGH)
     tokens = 4 * count
     *mixed, lse = call(
         attention_kernel,
-        [((count, 64), BF16)] * 4 + [((tokens // STEP, 8, STEP), F32)],
+        [((half, 128), BF16)] * 4 + [((tokens // STEP, 8, STEP), F32)],
         ids,
         *qkv,
         scratch=[((tokens, 192), F32)] + [((tokens, 64), BF16)] * 3,
-        flops=4 * tokens * tokens * 64,
-    )
-    here_grad, there_grad, *mixed = tie(here_grad, there_grad, *mixed)
-    s1, s2, s3 = (
-        swap(here_grad, Z_LOW),
-        swap(there_grad, Z_HIGH),
-        swap(there_grad, Z_LOW | Z_HIGH),
-    )
-    *mixed, f1, f2, g0 = tie(*trade(mixed), f1, f2, merge(shard_g, far_g, offer(shard_g, far_g)))
-    w_fc1 = (f0, f1, f2, swap(f2, X))
+    )
+    shard_g, far_g, *mixed = tie(shard_g, far_g, *mixed)
+    g0 = merge(shard_g, far_g, offer(shard_g, far_g))
+    *mixed, f1, f2, s1, s2 = tie(*trade(mixed), f1, f2, s1, s2)
     g1, g2 = swap(g0, X), swap(g0, Y)
+    f3, g3, s3 = swap(f2, X), swap(g1, Y), swap(s2, Z_LOW)
     attended, keep, send = call(
         proj_kernel,
         [((count, 256), BF16), ((half, 1024), F32), ((half, 1024), BF16)],
         ids,
         *mixed,
         *w_att,
-        scratch=[((4, count, 64), BF16)],
-        flops=2 * count * 1024 * 256,
+        scratch=[((4, half, 128), BF16), ((count, 256), F32)],
     )
 
     def pair(keep, send):
@@ -1130,6 +1216,8 @@
         )
 
     part, send = pair(keep, send)
+    away, s3 = tie(swap(send, Z_LOW), s3)
+    w_fc1, w_fc2 = (f0, f1, f2, f3), (g0, g1, g2, g3)
     (grads,) = call(
         lay_grad_kernel,
         [((half, 1024), BF16)],
@@ -1146,10 +1234,9 @@
         ids,
         rows,
         part,
-        swap(send, Z_LOW),
+        away,
         vec,
     )
-    w_fc2 = (g0, g1, g2, swap(g1, Y))
     whole_mlp, grad_hidden = call(
         grad_hidden_kernel,
         [((count, 1024), BF16), ((count, 1024), F32)],
@@ -1158,7 +1245,6 @@
         swap(grads, CORE),
         *w_fc2,
         scratch=[wide],
-        flops=2 * count * 1024 * 1024,
     )
 
     whole_two, hidden, grad_pre, sums_fc1, keep, send = call(
@@ -1172,14 +1258,13 @@
         b_fc1,
         *w_fc1,
         scratch=[wide],
-        flops=4 * count * 1024 * 1024,
     )
     part, send = pair(keep, send)
     late = tie(send, whole_mlp, hidden, whole_two, grad_pre)
     grad_outs = [((2, 256, 1024), BF16), ((256, 1024), F32), ((256, 1024), F32)]
     cost = 2 * count * 1024 * 1024
-    send_f, *rest_f = call(grads_fc1_kernel, grad_outs, ids, late[3], late[4], flops=cost)
-    send_g, *rest_g = call(grads_fc2_kernel, grad_outs, ids, late[1], late[2], flops=cost)
+    send_f, *rest_f = call(grads_fc1_kernel, grad_outs, ids, late[3], late[4])
+    send_g, *rest_g = call(grads_fc2_kernel, grad_outs, ids, late[1], late[2])
     sums_f = (*rest_f, swap(send_f, X))
     sums_g = (*rest_g, swap(send_g, Y))
     keep_out, send_out = call(
@@ -1188,9 +1273,10 @@
         ids,
         late[2],
         *w_fc2,
-        flops=cost,
     )
     away, keep_out, send_out = tie(swap(send, Z_LOW), keep_out, send_out)
+    part_out, send_out = halve(keep_out, send_out)
+    away_out = swap(send_out, Z_LOW)
     grad_residual, grad_branch, sums_two = call(
         norm_two_back_kernel,
         [((half, 1024), F32), ((half, 1024), BF16), ((8, 1024), F32)],
@@ -1204,78 +1290,107 @@
 
     whole_branch, *grad_att = call(
         grad_att_kernel,
-        [((count, 1024), BF16)] + [((count, 64), BF16)] * 4,
+        [((count, 1024), BF16)] + [((half, 128), BF16)] * 4,
         ids,
         grad_branch,
         swap(grad_branch, CORE),
         *w_att,
-        scratch=[wide, ((4, count, 64), BF16)],
-        flops=2 * count * 1024 * 256,
-    )
-    *grad_att, keep_out, send_out = tie(*grad_att, keep_out, send_out)
-    part_out, send_out = halve(keep_out, send_out)
+        scratch=[wide, ((4, half, 128), BF16)],
+    )
+    *grad_att, part_out, away_out = tie(*grad_att, part_out, away_out)
     here_out, there_out = call(
         layer_out_kernel,
         [(plain, BF16)] * 2,
         ids,
         residual,
         part_out,
-        swap(send_out, Z_LOW),
+        away_out,
         vec,
         scratch=[((2 * PAD, 1024), F32)],
     )
+    sums_mlp = sum_second(ids, sums_f, sums_g)
+    *grad_att, whole_x, other_x, whole_y, other_y, here_out, there_out = tie(
+        *trade(grad_att), *sums_mlp, here_out, there_out
+    )
+    sums_mlp = send_second(whole_x, other_x, whole_y, other_y)
+    away_out = swap(there_out, Z_HIGH)
     grad_qkv = call(
         attention_back_kernel,
-        [((count, 192), BF16)] * 4,
+        [(packed, BF16)] * 4,
         ids,
         *qkv,
-        *trade(grad_att),
+        *grad_att,
         lse,
         scratch=[((tokens, 192), F32)] + [((tokens, 64), BF16)] * 4 + [((tokens, 64), F32)] * 2,
-        flops=10 * tokens * tokens * 64,
-    )
+    )
+    *grad_qkv, away_out, whole_x, got_x, whole_y, got_y = tie(*grad_qkv, away_out, *sums_mlp)
+    *sums_mlp, moved_mlp = sum_third(ids, (whole_x, got_x, whole_y, got_y))
+    keep_out, send_out = call(
+        give_out_kernel, [((4, PAD, 1024), BF16)] * 2, ids, slots, here_out, away_out
+    )
+    got_out, *pairs_out = to_chips(keep_out, send_out)
+    *grad_qkv, moved_mlp, got_out, p1, p2, p3 = tie(
+        *trade(grad_qkv), moved_mlp, got_out, *pairs_out
+    )
+    moved_mlp = swap(moved_mlp, Z_HIGH)
+    parts_out = over_chips((p1, p2, p3))
     joined, keep, send, sums_qv = call(
         qkv_back_kernel,
         [((count, 768), BF16), ((half, 1024), F32), ((half, 1024), BF16), ((1, 1024), F32)],
         ids,
-        *trade(grad_qkv),
+        *grad_qkv,
         *w_att,
-        scratch=[((4, count, 192), BF16)],
-        flops=2 * count * 1024 * 768,
-    )
-    part, send = halve(keep, send)
+        scratch=[((4, *packed), BF16), ((count, 256), F32)],
+    )
+    part, send, small = call(
+        half_grad_kernel,
+        [((own, 1024), F32), ((SMALL + 8, 1024), BF16), ((8, 1024), F32)],
+        ids,
+        keep,
+        swap(send, CORE),
+        rows,
+        sums_two,
+        sums_fc1,
+        sums_qv,
+    )
     late = tie(send, whole_one, joined, whole_branch, attended)
     grad_outs = [((2, 256, 512), BF16), ((256, 512), F32), ((256, 512), F32)]
     send_x, here_x, there_x, send_y, here_y, there_y = call(
-        grads_att_kernel, grad_outs * 2, ids, *late[1:], flops=cost
-    )
-    here, there, small = call(
+        grads_att_kernel, grad_outs * 2, ids, *late[1:]
+    )
+    away, send_x, send_y, *parts_out = tie(swap(send, Z_LOW), send_x, send_y, *parts_out)
+    parts_out = keep_out, got_out, *parts_out
+    got_x, got_y = swap(send_x, X), swap(send_y, Y)
+    here, there = call(
         norm_one_back_kernel,
-        [(behind, BF16), (behind, BF16), ((8, 1024), BF16)],
+        [(behind, BF16)] * 2,
         ids,
         rows,
         part,
-        swap(send, Z_LOW),
+        away,
         grad_residual,
         vec,
-        sums_two,
-        sums_fc1,
-        sums_qv,
+        small,
         scratch=[((2 * PAD, 1024), F32)],
     )
+    away, got_x, got_y, moved_mlp = tie(swap(there, Z_HIGH), got_x, got_y, moved_mlp)
+    sums_att = sum_second(ids, (here_x, there_x, got_x), (here_y, there_y, got_y))
     keep, send = call(
-        give_grad_kernel,
+        give_kernel,
         [((4, PAD, 1024), BF16)] * 2,
         ids,
         slots,
         here,
-        swap(small, Z_LOW),
-        swap(there, Z_HIGH),
-        swap(small, Z_LOW | Z_HIGH),
+        away,
         scratch=[((8, 1024), F32), ((8, 1024), F32), (plain, F32)],
     )
+    got, *pairs = to_chips(keep, send)
+    *pairs, whole_x, other_x, whole_y, other_y = tie(*pairs, *sums_att)
+    parts = keep, got, *over_chips(pairs)
+    *sums_att, moved_att = sum_third(ids, send_second(whole_x, other_x, whole_y, other_y))
+    moved_att = swap(moved_att, Z_HIGH)
     input_grad, grad_gains, grad_biases, grad_last, grad_qv, grad_b_fc1 = call(
-        take_grad_kernel,
+        take_kernel,
         [
             ((count, 1024), F32),
             ((2, 32), F32),
@@ -1285,42 +1400,30 @@
             ((1, 128), F32),
         ],
         ids,
-        *to_devices(keep, send),
+        *parts,
         scratch=[((8, PAD, 1024), F32)],
     )
-
-    keep, send = call(
-        give_kernel,
-        [((4, PAD, 1024), BF16)] * 2,
-        ids,
-        slots,
-        here_out,
-        swap(there_out, Z_HIGH),
-    )
     (layer_out,) = call(
-        take_kernel,
+        take_out_kernel,
         [((count, 1024), BF16)],
         ids,
-        *to_devices(keep, send),
+        *parts_out,
         scratch=[((8, PAD, 1024), F32), wide],
     )
-
-    grad_fc1, grad_fc2 = sum_last(
-        ids,
+    grad_fc1, grad_fc2 = call(
         finish_mlp_kernel,
         [((128, 1024), F32), ((1024, 128), F32)],
-        *sum_third(ids, sum_second(ids, sums_f, sums_g)),
-    )
-    grad_w, grad_proj = sum_last(
-        ids,
+        ids,
+        *sums_mlp,
+        moved_mlp,
+    )
+    moved_att, _ = tie(moved_att, input_grad)
+    grad_w, grad_proj = call(
         finish_att_kernel,
         [((3, 128, 256), F32), ((256, 128), F32)],
-        *sum_third(
-            ids,
-            sum_second(
-                ids, (here_x, there_x, swap(send_x, X)), (here_y, there_y, swap(send_y, Y))
-            ),
-        ),
+        ids,
+        *sums_att,
+        moved_att,
     )
     return (
         layer_out,

time: 315 us -> 271 us (0.86)
  waiting for transfers between devices: 166 us -> 129 us
  starting transfers between devices: 71.5 us -> 65.6 us
    ppermute x71 -> x72, waiting for transfers between devices: 166 us -> 129 us  [swap(): return lax.ppermute(value, AXES, [(i, i ^ mask) for i in range(32)])]
    ppermute x71 -> x72, starting transfers between devices: 69.9 us -> 65.6 us  [swap(): return lax.ppermute(value, AXES, [(i, i ^ mask) for i in range(32)])]
  transfers between devices with their start and end apart: 73 -> 72, of which waited for: 39 -> 36; matrix products, arithmetic and copies ran while one was open for 0% -> 0% of each run, Pallas kernels for 18% -> 21%
where the time goes in v4:
time: 271 us; the launch traced here: 270 us
  waiting for transfers between devices  129 us (48%)
  Pallas kernels  71.2 us (26%)
  starting transfers between devices  65.6 us (24%)
  local copies, waits for them, and re-layouts  2.87 us (1%)
    ppermute x72, waiting for transfers between devices, swap(): return lax.ppermute(value, AXES, [(i, i ^ mask) for i in range(32)])  129 us
    pallas_call x48, Pallas kernels, call(): pl.pallas_call(body, out_shape=[jax.ShapeDtypeStruct(s, t) for s, t in ou...  71.2 us
    ppermute x72, starting transfers between devices, swap(): return lax.ppermute(value, AXES, [(i, i ^ mask) for i in range(32)])  65.6 us
  transfers between devices with their start and end apart: 72, of which 36 were waited for; matrix products, arithmetic and copies ran while one was open for 0% of the time, Pallas kernels for 21%

profile of v4, /device:TPU:0, one launch (start us, length us, event | category | flops | bytes accessed | tf_op | source)
XLA Modules:
  0.0 270.4 jit_solution(2683295439382047649)
XLA Ops:
  6.8 3.7 %collective-permute-start.4 = (bf16[128,1024]{1,0:T(8,128)(2,1)S(1)}, bf16[128,1024]{1,0:T(8,128)(2,1)S(1)}, u32[]{:S(2)}, u32[]{:S(2)}) collective-permute-start(bf16[128,1024]{1,0:T(8,128)(2,1)S(1)} %get-tuple-element.230.own), channel_id=1, source_target_pairs={{0,2},{1,3},{2,0},{3,1},{4,6},{5,7},{6,4},{7,5},{8,10},{9,11},{10,... | collective-permute-start | bytes 786440 | tf_op jit(solution)/shard_map/ppermute | solution.py:322
  11.1 1.6 collective-permute-start.1
  12.6 1.5 collective-permute-start.2
  14.6 8.3 %collective-permute-done.4.far = bf16[128,1024]{1,0:T(8,128)(2,1)S(1)} collective-permute-done((bf16[128,1024]{1,0:T(8,128)(2,1)S(1)}, bf16[128,1024]{1,0:T(8,128)(2,1)S(1)}, u32[]{:S(2)}, u32[]{:S(2)}) %collective-permute-start.4) | collective-permute-done | bytes 262176 | tf_op jit(solution)/shard_map/ppermute | solution.py:322
  23.7 1.4 collective-permute-done.5.got
  25.7 9.1 %collective-permute-done.2.d2 = bf16[2,112,1024]{2,1,0:T(8,128)(2,1)S(1)} collective-permute-done((bf16[2,112,1024]{2,1,0:T(8,128)(2,1)S(1)}, bf16[2,112,1024]{2,1,0:T(8,128)(2,1)S(1)}, u32[]{:S(2)}, u32[]{:S(2)}) %collective-permute-start.2) | collective-permute-done | bytes 458784 | tf_op jit(solution)/shard_map/ppermute | solution.py:322
  34.8 1.5 collective-permute-start.12
  36.8 1.6 shard_map.199
  38.4 1.6 collective-permute-start.6
  40.0 2.2 collective-permute-start.8
  42.4 2.7 %collective-permute-done.6.r1 = bf16[64,1024]{1,0:T(8,128)(2,1)S(1)} collective-permute-done((bf16[64,1024]{1,0:T(8,128)(2,1)S(1)}, bf16[64,1024]{1,0:T(8,128)(2,1)S(1)}, u32[]{:S(2)}, u32[]{:S(2)}) %collective-permute-start.6) | collective-permute-done | bytes 131104 | tf_op jit(solution)/shard_map/ppermute | solution.py:322
  45.1 3.3 %collective-permute-done.8.r3 = bf16[64,1024]{1,0:T(8,128)(2,1)S(1)} collective-permute-done((bf16[64,1024]{1,0:T(8,128)(2,1)S(1)}, bf16[64,1024]{1,0:T(8,128)(2,1)S(1)}, u32[]{:S(2)}, u32[]{:S(2)}) %collective-permute-start.8) | collective-permute-done | bytes 131104 | tf_op jit(solution)/shard_map/ppermute | solution.py:322
  48.4 4.3 %collective-permute-done.7.r2 = bf16[64,1024]{1,0:T(8,128)(2,1)S(1)} collective-permute-done((bf16[64,1024]{1,0:T(8,128)(2,1)S(1)}, bf16[64,1024]{1,0:T(8,128)(2,1)S(1)}, u32[]{:S(2)}, u32[]{:S(2)}) %collective-permute-start.7) | collective-permute-done | bytes 131104 | tf_op jit(solution)/shard_map/ppermute | solution.py:322
  53.8 1.5 collective-permute-start.13
  56.7 5.9 %collective-permute-done.13.w3 = bf16[256,512]{1,0:T(8,128)(2,1)S(1)} collective-permute-done((bf16[256,512]{1,0:T(8,128)(2,1)S(1)}, bf16[256,512]{1,0:T(8,128)(2,1)S(1)}, u32[]{:S(2)}, u32[]{:S(2)}) %collective-permute-start.13) | collective-permute-done | bytes 262176 | tf_op jit(solution)/shard_map/ppermute | solution.py:322
  63.8 1.6 shard_map.201
  66.0 1.5 collective-permute-start.17
  67.5 1.4 collective-permute-start.18
  69.9 2.4 collective-permute-done.16.a1
  72.3 2.2 collective-permute-done.17.a2
  76.9 2.9 %collective-permute-start.25 = (bf16[56,1024]{1,0:T(8,128)(2,1)S(1)}, bf16[56,1024]{1,0:T(8,128)(2,1)S(1)}, u32[]{:S(2)}, u32[]{:S(2)}) collective-permute-start(bf16[56,1024]{1,0:T(8,128)(2,1)S(1)} %get-tuple-element.280.here), channel_id=1, source_target_pairs={{0,1},{1,0},{2,3},{3,2},{4,5},{5,4},{6,7},{7,6},{8,9},{9,8},{10,11... | collective-permute-start | bytes 344072 | tf_op jit(solution)/shard_map/ppermute | solution.py:322
  79.8 7.7 %shard_map.204 = (bf16[196,128]{1,0:T(8,128)(2,1)S(1)}, bf16[196,128]{1,0:T(8,128)(2,1)S(1)}, bf16[196,128]{1,0:T(8,128)(2,1)S(1)}, bf16[196,128]{1,0:T(8,128)(2,1)S(1)}, f32[7,8,224]{2,1,0:T(8,128)S(1)}) custom-call(s32[5]{0:T(128)S(1)} %stack.19.ids, bf16[596,128]{1,0:T(8,128)(2,1)S(1)} %get-tuple-element.267.a0, ...), custom_call_target="tpu_custom_call" | custom-call | flops 8739999744 | bytes 861184 | tf_op jit(solution)/shard_map/pallas_call | solution.py:361
  87.5 1.3 collective-permute-start.20
  89.6 1.5 collective-permute-start.22
  91.8 1.3 collective-permute-done.21.a2
  93.1 1.5 collective-permute-done.22.a3
  96.3 1.3 collective-permute-start.33
  98.3 2.0 collective-permute-start.29
  101.4 9.3 %collective-permute-done.33.w1 = bf16[256,1024]{1,0:T(8,128)(2,1)S(1)} collective-permute-done((bf16[256,1024]{1,0:T(8,128)(2,1)S(1)}, bf16[256,1024]{1,0:T(8,128)(2,1)S(1)}, u32[]{:S(2)}, u32[]{:S(2)}) %collective-permute-start.33) | collective-permute-done | bytes 524320 | tf_op jit(solution)/shard_map/ppermute | solution.py:322
  115.4 9.7 %collective-permute-done.35.w3 = bf16[256,1024]{1,0:T(8,128)(2,1)S(1)} collective-permute-done((bf16[256,1024]{1,0:T(8,128)(2,1)S(1)}, bf16[256,1024]{1,0:T(8,128)(2,1)S(1)}, u32[]{:S(2)}, u32[]{:S(2)}) %collective-permute-start.35) | collective-permute-done | bytes 524320 | tf_op jit(solution)/shard_map/ppermute | solution.py:322
  125.1 1.6 shard_map.211
  127.5 5.8 %shard_map.212 = (bf16[392,1024]{1,0:T(8,128)(2,1)S(1)}, bf16[392,1024]{1,0:T(8,128)(2,1)S(1)}, bf16[392,1024]{1,0:T(8,128)(2,1)S(1)}, f32[1,1024]{1,0:T(1,128)S...) custom-call(s32[5]{0:T(128)S(1)} %stack.19.ids, bf16[196,1024]{1,0:T(8,128)(2,1)S(1)} %get-tuple-element.294.own, ...), custom_call_target="tpu_custom_call" | custom-call | flops 6440000000 | bytes 8126464 | tf_op jit(solution)/shard_map/pallas_call | solution.py:361
  133.4 1.7 collective-permute-done.37.got
  136.1 1.8 shard_map.220
  139.0 1.8 shard_map.218
  142.0 1.6 shard_map.214
  143.5 3.8 %collective-permute-done.38.got = bf16[196,1024]{1,0:T(8,128)(2,1)S(1)} collective-permute-done((bf16[196,1024]{1,0:T(8,128)(2,1)S(1)}, bf16[196,1024]{1,0:T(8,128)(2,1)S(1)}, u32[]{:S(2)}, u32[]{:S(2)}) %collective-permute-start.38) | collective-permute-done | bytes 401440 | tf_op jit(solution)/shard_map/ppermute | solution.py:322
  147.3 1.5 shard_map.215
  151.8 5.6 %collective-permute-done.41.got = bf16[98,1024]{1,0:T(8,128)(2,1)S(1)} collective-permute-done((bf16[98,1024]{1,0:T(8,128)(2,1)S(1)}, bf16[98,1024]{1,0:T(8,128)(2,1)S(1)}, u32[]{:S(2)}, u32[]{:S(2)}) %collective-permute-start.41) | collective-permute-done | bytes 200736 | tf_op jit(solution)/shard_map/ppermute | solution.py:322
  159.4 1.4 collective-permute-start.44
  161.6 1.8 collective-permute-done.46.got
  164.2 2.5 collective-permute-done.45.got
  168.2 1.4 collective-permute-start.47
  171.7 12.1 %shard_map.223 = (bf16[596,128]{1,0:T(8,128)(2,1)S(1)}, bf16[596,128]{1,0:T(8,128)(2,1)S(1)}, bf16[596,128]{1,0:T(8,128)(2,1)S(1)}, bf16[596,128]{1,0:T(8,128)(2,1)S(1)}) custom-call(s32[5]{0:T(128)S(1)} %stack.19.ids, bf16[596,128]{1,0:T(8,128)(2,1)S(1)} %get-tuple-element.267.a0, bf16[596,128]{1,0:T(8,128)(2,1)S(1)} %collective-permute-done.16.a1, ...), custom_call_target="tpu_custom_call" | custom-call | flops 13799999488 | bytes 1471488 | tf_op jit(solution)/shard_map/pallas_call | solution.py:361
  188.0 1.5 collective-permute-start.52
  191.0 1.9 collective-permute-done.50.g1
  192.9 3.1 %collective-permute-done.51.g2 = bf16[596,128]{1,0:T(8,128)(2,1)S(1)} collective-permute-done((bf16[596,128]{1,0:T(8,128)(2,1)S(1)}, bf16[596,128]{1,0:T(8,128)(2,1)S(1)}, u32[]{:S(2)}, u32[]{:S(2)}) %collective-permute-start.51) | collective-permute-done | bytes 152608 | tf_op jit(solution)/shard_map/ppermute | solution.py:322
  196.0 1.6 shard_map.228
  199.7 1.5 collective-permute-start.59
  202.7 2.9 %collective-permute-start.63 = (bf16[128,2048]{1,0:T(8,128)(2,1)S(1)}, bf16[128,2048]{1,0:T(8,128)(2,1)S(1)}, u32[]{:S(2)}, u32[]{:S(2)}) collective-permute-start(bf16[128,2048]{1,0:T(8,128)(2,1)S(1)} %shard_map.226), channel_id=1, source_target_pairs={{0,2},{1,3},{2,0},{3,1},{4,6},{5,7},{6,4},{7,5},{8,10},{9,11},{10,... | collective-permute-start | bytes 1572872 | tf_op jit(solution)/shard_map/ppermute | solution.py:322
  205.6 1.8 shard_map.230
  207.5 3.9 %collective-permute-done.58.d2 = bf16[2,56,1024]{2,1,0:T(8,128)(2,1)S(1)} collective-permute-done((bf16[2,56,1024]{2,1,0:T(8,128)(2,1)S(1)}, bf16[2,56,1024]{2,1,0:T(8,128)(2,1)S(1)}, u32[]{:S(2)}, u32[]{:S(2)}) %collective-permute-start.58) | collective-permute-done | bytes 229408 | tf_op jit(solution)/shard_map/ppermute | solution.py:322
  211.4 2.8 %collective-permute-done.56.got = bf16[112,1024]{1,0:T(8,128)(2,1)S(1)} collective-permute-done((bf16[112,1024]{1,0:T(8,128)(2,1)S(1)}, bf16[112,1024]{1,0:T(8,128)(2,1)S(1)}, u32[]{:S(2)}, u32[]{:S(2)}) %collective-permute-start.56) | collective-permute-done | bytes 229408 | tf_op jit(solution)/shard_map/ppermute | solution.py:322
  217.4 15.1 %collective-permute-done.63.moved = bf16[128,2048]{1,0:T(8,128)(2,1)S(1)} collective-permute-done((bf16[128,2048]{1,0:T(8,128)(2,1)S(1)}, bf16[128,2048]{1,0:T(8,128)(2,1)S(1)}, u32[]{:S(2)}, u32[]{:S(2)}) %collective-permute-start.63) | collective-permute-done | bytes 524320 | tf_op jit(solution)/shard_map/ppermute | solution.py:322
  232.5 1.4 collective-permute-done.60.away
  239.3 6.4 %collective-permute-done.68.got_x = bf16[256,512]{1,0:T(8,128)(2,1)S(1)} collective-permute-done((bf16[256,512]{1,0:T(8,128)(2,1)S(1)}, bf16[256,512]{1,0:T(8,128)(2,1)S(1)}, u32[]{:S(2)}, u32[]{:S(2)}) %collective-permute-start.68) | collective-permute-done | bytes 262176 | tf_op jit(solution)/shard_map/ppermute | solution.py:322
  247.1 1.8 shard_map.231
  250.9 1.4 collective-permute-start.67
  252.3 1.8 shard_map.241
  254.8 2.5 collective-permute-done.65.d1
  257.3 5.2 %collective-permute-done.66.d2 = bf16[2,56,1024]{2,1,0:T(8,128)(2,1)S(1)} collective-permute-done((bf16[2,56,1024]{2,1,0:T(8,128)(2,1)S(1)}, bf16[2,56,1024]{2,1,0:T(8,128)(2,1)S(1)}, u32[]{:S(2)}, u32[]{:S(2)}) %collective-permute-start.66) | collective-permute-done | bytes 229408 | tf_op jit(solution)/shard_map/ppermute | solution.py:322
  262.5 2.0 shard_map.237
  264.5 4.5 %collective-permute-done.71.moved = bf16[128,1024]{1,0:T(8,128)(2,1)S(1)} collective-permute-done((bf16[128,1024]{1,0:T(8,128)(2,1)S(1)}, bf16[128,1024]{1,0:T(8,128)(2,1)S(1)}, u32[]{:S(2)}, u32[]{:S(2)}) %collective-permute-start.71) | collective-permute-done | bytes 262176 | tf_op jit(solution)/shard_map/ppermute | solution.py:322
  268.9 1.4 shard_map.240
  (153 shorter events, 61.7 us)
Async XLA Ops:
  6.2 4.2 %collective-permute-start = (bf16[4,112,1024]{2,1,0:T(8,128)(2,1)S(1)}, bf16[4,112,1024]{2,1,0:T(8,128)(2,1)S(1)}, u32[]{:S(2)}, u32[]{:S(2)}) collective-permute-start(bf16[4,112,1024]{2,1,0:T(8,128)(2,1)S(1)} %get-tuple-element.233), channel_id=1, source_target_pairs={{0,4},{1,5},{2,6},{3,7},{4,0},{5,1},{6,2},{7,3},{8,12},{9,13},{10,... | collective-permute-start | bytes 2752520 | tf_op jit(solution)/shard_map/ppermute | solution.py:322
  6.8 16.2 %collective-permute-start.4 = (bf16[128,1024]{1,0:T(8,128)(2,1)S(1)}, bf16[128,1024]{1,0:T(8,128)(2,1)S(1)}, u32[]{:S(2)}, u32[]{:S(2)}) collective-permute-start(bf16[128,1024]{1,0:T(8,128)(2,1)S(1)} %get-tuple-element.230.own), channel_id=1, source_target_pairs={{0,2},{1,3},{2,0},{3,1},{4,6},{5,7},{6,4},{7,5},{8,10},{9,11},{10,... | collective-permute-start | bytes 786440 | tf_op jit(solution)/shard_map/ppermute | solution.py:322
  11.1 14.6 %collective-permute-start.1 = (bf16[2,112,1024]{2,1,0:T(8,128)(2,1)S(1)}, bf16[2,112,1024]{2,1,0:T(8,128)(2,1)S(1)}, u32[]{:S(2)}, u32[]{:S(2)}) collective-permute-start(bf16[2,112,1024]{2,1,0:T(8,128)(2,1)S(1)} %get-tuple-element.234), channel_id=1, source_target_pairs={{0,8},{1,9},{2,10},{3,11},{4,12},{5,13},{6,14},{7,15},{8,0},{9,1},... | collective-permute-start | bytes 1376264 | tf_op jit(solution)/shard_map/ppermute | solution.py:322
  12.6 22.1 %collective-permute-start.2 = (bf16[2,112,1024]{2,1,0:T(8,128)(2,1)S(1)}, bf16[2,112,1024]{2,1,0:T(8,128)(2,1)S(1)}, u32[]{:S(2)}, u32[]{:S(2)}) collective-permute-start(bf16[2,112,1024]{2,1,0:T(8,128)(2,1)S(1)} %get-tuple-element.235), channel_id=1, source_target_pairs={{0,16},{1,17},{2,18},{3,19},{4,20},{5,21},{6,22},{7,23},{8,24},{9,... | collective-permute-start | bytes 1376264 | tf_op jit(solution)/shard_map/ppermute | solution.py:322
  14.2 20.6 %collective-permute-start.3 = (bf16[2,112,1024]{2,1,0:T(8,128)(2,1)S(1)}, bf16[2,112,1024]{2,1,0:T(8,128)(2,1)S(1)}, u32[]{:S(2)}, u32[]{:S(2)}) collective-permute-start(bf16[2,112,1024]{2,1,0:T(8,128)(2,1)S(1)} %get-tuple-element.236), channel_id=1, source_target_pairs={{0,24},{1,25},{2,26},{3,27},{4,28},{5,29},{6,30},{7,31},{8,16},{9,... | collective-permute-start | bytes 1376264 | tf_op jit(solution)/shard_map/ppermute | solution.py:322
  23.6 18.7 %collective-permute-start.9 = (bf16[128,1024]{1,0:T(8,128)(2,1)S(1)}, bf16[128,1024]{1,0:T(8,128)(2,1)S(1)}, u32[]{:S(2)}, u32[]{:S(2)}) collective-permute-start(bf16[128,1024]{1,0:T(8,128)(2,1)S(1)} %copy-done.3), channel_id=1, source_target_pairs={{0,2},{1,3},{2,0},{3,1},{4,6},{5,7},{6,4},{7,5},{8,10},{9,11},{10,... | collective-permute-start | bytes 786440 | tf_op jit(solution)/shard_map/ppermute | solution.py:322
  34.8 19.0 %collective-permute-start.12 = (bf16[256,1024]{1,0:T(8,128)(2,1)S(1)}, bf16[256,1024]{1,0:T(8,128)(2,1)S(1)}, u32[]{:S(2)}, u32[]{:S(2)}) collective-permute-start(bf16[256,1024]{1,0:T(8,128)(2,1)S(1)} %shard_map.198.w0), channel_id=1, source_target_pairs={{0,16},{1,17},{2,18},{3,19},{4,20},{5,21},{6,22},{7,23},{8,24},{9,... | collective-permute-start | bytes 1572872 | tf_op jit(solution)/shard_map/ppermute | solution.py:322
  36.3 19.0 %collective-permute-start.11 = (bf16[256,1024]{1,0:T(8,128)(2,1)S(1)}, bf16[256,1024]{1,0:T(8,128)(2,1)S(1)}, u32[]{:S(2)}, u32[]{:S(2)}) collective-permute-start(bf16[256,1024]{1,0:T(8,128)(2,1)S(1)} %shard_map.198.w0), channel_id=1, source_target_pairs={{0,8},{1,9},{2,10},{3,11},{4,12},{5,13},{6,14},{7,15},{8,0},{9,1},... | collective-permute-start | bytes 1572872 | tf_op jit(solution)/shard_map/ppermute | solution.py:322
  38.4 6.7 %collective-permute-start.6 = (bf16[64,1024]{1,0:T(8,128)(2,1)S(1)}, bf16[64,1024]{1,0:T(8,128)(2,1)S(1)}, u32[]{:S(2)}, u32[]{:S(2)}) collective-permute-start(bf16[64,1024]{1,0:T(8,128)(2,1)S(1)} %get-tuple-element.243.here), channel_id=1, source_target_pairs={{0,1},{1,0},{2,3},{3,2},{4,5},{5,4},{6,7},{7,6},{8,9},{9,8},{10,11... | collective-permute-start | bytes 393224 | tf_op jit(solution)/shard_map/ppermute | solution.py:322
  40.0 8.4 %collective-permute-start.8 = (bf16[64,1024]{1,0:T(8,128)(2,1)S(1)}, bf16[64,1024]{1,0:T(8,128)(2,1)S(1)}, u32[]{:S(2)}, u32[]{:S(2)}) collective-permute-start(bf16[64,1024]{1,0:T(8,128)(2,1)S(1)} %get-tuple-element.244), channel_id=1, source_target_pairs={{0,3},{1,2},{2,1},{3,0},{4,7},{5,6},{6,5},{7,4},{8,11},{9,10},{10,... | collective-permute-start | bytes 393224 | tf_op jit(solution)/shard_map/ppermute | solution.py:322
  42.3 10.4 %collective-permute-start.7 = (bf16[64,1024]{1,0:T(8,128)(2,1)S(1)}, bf16[64,1024]{1,0:T(8,128)(2,1)S(1)}, u32[]{:S(2)}, u32[]{:S(2)}) collective-permute-start(bf16[64,1024]{1,0:T(8,128)(2,1)S(1)} %get-tuple-element.244), channel_id=1, source_target_pairs={{0,2},{1,3},{2,0},{3,1},{4,6},{5,7},{6,4},{7,5},{8,10},{9,11},{10,... | collective-permute-start | bytes 393224 | tf_op jit(solution)/shard_map/ppermute | solution.py:322
  53.8 8.8 %collective-permute-start.13 = (bf16[256,512]{1,0:T(8,128)(2,1)S(1)}, bf16[256,512]{1,0:T(8,128)(2,1)S(1)}, u32[]{:S(2)}, u32[]{:S(2)}) collective-permute-start(bf16[256,512]{1,0:T(8,128)(2,1)S(1)} %slice.8), channel_id=1, source_target_pairs={{0,8},{1,9},{2,10},{3,11},{4,12},{5,13},{6,14},{7,15},{8,0},{9,1},... | collective-permute-start | bytes 786440 | tf_op jit(solution)/shard_map/ppermute | solution.py:322
  55.3 8.5 %collective-permute-start.14 = (bf16[256,512]{1,0:T(8,128)(2,1)S(1)}, bf16[256,512]{1,0:T(8,128)(2,1)S(1)}, u32[]{:S(2)}, u32[]{:S(2)}) collective-permute-start(bf16[256,512]{1,0:T(8,128)(2,1)S(1)} %slice.9), channel_id=1, source_target_pairs={{0,16},{1,17},{2,18},{3,19},{4,20},{5,21},{6,22},{7,23},{8,24},{9,... | collective-permute-start | bytes 786440 | tf_op jit(solution)/shard_map/ppermute | solution.py:322
  56.6 12.3 %collective-permute-start.19 = (bf16[128,1024]{1,0:T(8,128)(2,1)S(1)}, bf16[128,1024]{1,0:T(8,128)(2,1)S(1)}, u32[]{:S(2)}, u32[]{:S(2)}) collective-permute-start(bf16[128,1024]{1,0:T(8,128)(2,1)S(1)} %shard_map.202), channel_id=1, source_target_pairs={{0,4},{1,5},{2,6},{3,7},{4,0},{5,1},{6,2},{7,3},{8,12},{9,13},{10,... | collective-permute-start | bytes 786440 | tf_op jit(solution)/shard_map/ppermute | solution.py:322
  65.4 7.0 %collective-permute-start.16 = (bf16[596,128]{1,0:T(8,128)(2,1)S(1)}, bf16[596,128]{1,0:T(8,128)(2,1)S(1)}, u32[]{:S(2)}, u32[]{:S(2)}) collective-permute-start(bf16[596,128]{1,0:T(8,128)(2,1)S(1)} %get-tuple-element.260), channel_id=1, source_target_pairs={{0,8},{1,9},{2,10},{3,11},{4,12},{5,13},{6,14},{7,15},{8,0},{9,1},... | collective-permute-start | bytes 457736 | tf_op jit(solution)/shard_map/ppermute | solution.py:322
  66.0 8.5 %collective-permute-start.17 = (bf16[596,128]{1,0:T(8,128)(2,1)S(1)}, bf16[596,128]{1,0:T(8,128)(2,1)S(1)}, u32[]{:S(2)}, u32[]{:S(2)}) collective-permute-start(bf16[596,128]{1,0:T(8,128)(2,1)S(1)} %get-tuple-element.261), channel_id=1, source_target_pairs={{0,16},{1,17},{2,18},{3,19},{4,20},{5,21},{6,22},{7,23},{8,24},{9,... | collective-permute-start | bytes 457736 | tf_op jit(solution)/shard_map/ppermute | solution.py:322
  67.5 7.0 %collective-permute-start.18 = (bf16[596,128]{1,0:T(8,128)(2,1)S(1)}, bf16[596,128]{1,0:T(8,128)(2,1)S(1)}, u32[]{:S(2)}, u32[]{:S(2)}) collective-permute-start(bf16[596,128]{1,0:T(8,128)(2,1)S(1)} %get-tuple-element.262), channel_id=1, source_target_pairs={{0,24},{1,25},{2,26},{3,27},{4,28},{5,29},{6,30},{7,31},{8,16},{9,... | collective-permute-start | bytes 457736 | tf_op jit(solution)/shard_map/ppermute | solution.py:322
  69.5 18.0 %collective-permute-start.15 = (bf16[128,1024]{1,0:T(8,128)(2,1)S(1)}, bf16[128,1024]{1,0:T(8,128)(2,1)S(1)}, u32[]{:S(2)}, u32[]{:S(2)}) collective-permute-start(bf16[128,1024]{1,0:T(8,128)(2,1)S(1)} %get-tuple-element.297.own), channel_id=1, source_target_pairs={{0,2},{1,3},{2,0},{3,1},{4,6},{5,7},{6,4},{7,5},{8,10},{9,11},{10,... | collective-permute-start | bytes 786440 | tf_op jit(solution)/shard_map/ppermute | solution.py:322
  74.5 20.1 %collective-permute-start.24 = (bf16[256,1024]{1,0:T(8,128)(2,1)S(1)}, bf16[256,1024]{1,0:T(8,128)(2,1)S(1)}, u32[]{:S(2)}, u32[]{:S(2)}) collective-permute-start(bf16[256,1024]{1,0:T(8,128)(2,1)S(1)} %shard_map.203.w0), channel_id=1, source_target_pairs={{0,16},{1,17},{2,18},{3,19},{4,20},{5,21},{6,22},{7,23},{8,24},{9,... | collective-permute-start | bytes 1572872 | tf_op jit(solution)/shard_map/ppermute | solution.py:322
  75.8 18.8 %collective-permute-start.23 = (bf16[256,1024]{1,0:T(8,128)(2,1)S(1)}, bf16[256,1024]{1,0:T(8,128)(2,1)S(1)}, u32[]{:S(2)}, u32[]{:S(2)}) collective-permute-start(bf16[256,1024]{1,0:T(8,128)(2,1)S(1)} %shard_map.203.w0), channel_id=1, source_target_pairs={{0,8},{1,9},{2,10},{3,11},{4,12},{5,13},{6,14},{7,15},{8,0},{9,1},... | collective-permute-start | bytes 1572872 | tf_op jit(solution)/shard_map/ppermute | solution.py:322
  76.6 12.2 %collective-permute-start.26 = (bf16[56,1024]{1,0:T(8,128)(2,1)S(1)}, bf16[56,1024]{1,0:T(8,128)(2,1)S(1)}, u32[]{:S(2)}, u32[]{:S(2)}) collective-permute-start(bf16[56,1024]{1,0:T(8,128)(2,1)S(1)} %get-tuple-element.281), channel_id=1, source_target_pairs={{0,2},{1,3},{2,0},{3,1},{4,6},{5,7},{6,4},{7,5},{8,10},{9,11},{10,... | collective-permute-start | bytes 344072 | tf_op jit(solution)/shard_map/ppermute | solution.py:322
  76.9 12.7 %collective-permute-start.25 = (bf16[56,1024]{1,0:T(8,128)(2,1)S(1)}, bf16[56,1024]{1,0:T(8,128)(2,1)S(1)}, u32[]{:S(2)}, u32[]{:S(2)}) collective-permute-start(bf16[56,1024]{1,0:T(8,128)(2,1)S(1)} %get-tuple-element.280.here), channel_id=1, source_target_pairs={{0,1},{1,0},{2,3},{3,2},{4,5},{5,4},{6,7},{7,6},{8,9},{9,8},{10,11... | collective-permute-start | bytes 344072 | tf_op jit(solution)/shard_map/ppermute | solution.py:322
  87.5 4.3 %collective-permute-start.20 = (bf16[196,128]{1,0:T(8,128)(2,1)S(1)}, bf16[196,128]{1,0:T(8,128)(2,1)S(1)}, u32[]{:S(2)}, u32[]{:S(2)}) collective-permute-start(bf16[196,128]{1,0:T(8,128)(2,1)S(1)} %get-tuple-element.276), channel_id=1, source_target_pairs={{0,8},{1,9},{2,10},{3,11},{4,12},{5,13},{6,14},{7,15},{8,0},{9,1},... | collective-permute-start | bytes 150536 | tf_op jit(solution)/shard_map/ppermute | solution.py:322
  88.8 4.3 %collective-permute-start.21 = (bf16[196,128]{1,0:T(8,128)(2,1)S(1)}, bf16[196,128]{1,0:T(8,128)(2,1)S(1)}, u32[]{:S(2)}, u32[]{:S(2)}) collective-permute-start(bf16[196,128]{1,0:T(8,128)(2,1)S(1)} %get-tuple-element.277), channel_id=1, source_target_pairs={{0,16},{1,17},{2,18},{3,19},{4,20},{5,21},{6,22},{7,23},{8,24},{9,... | collective-permute-start | bytes 150536 | tf_op jit(solution)/shard_map/ppermute | solution.py:322
  89.6 5.0 %collective-permute-start.22 = (bf16[196,128]{1,0:T(8,128)(2,1)S(1)}, bf16[196,128]{1,0:T(8,128)(2,1)S(1)}, u32[]{:S(2)}, u32[]{:S(2)}) collective-permute-start(bf16[196,128]{1,0:T(8,128)(2,1)S(1)} %get-tuple-element.278), channel_id=1, source_target_pairs={{0,24},{1,25},{2,26},{3,27},{4,28},{5,29},{6,30},{7,31},{8,16},{9,... | collective-permute-start | bytes 150536 | tf_op jit(solution)/shard_map/ppermute | solution.py:322
  91.8 3.9 %collective-permute-start.32 = (bf16[128,1024]{1,0:T(8,128)(2,1)S(1)}, bf16[128,1024]{1,0:T(8,128)(2,1)S(1)}, u32[]{:S(2)}, u32[]{:S(2)}) collective-permute-start(bf16[128,1024]{1,0:T(8,128)(2,1)S(1)} %shard_map.209), channel_id=1, source_target_pairs={{0,4},{1,5},{2,6},{3,7},{4,0},{5,1},{6,2},{7,3},{8,12},{9,13},{10,... | collective-permute-start | bytes 786440 | tf_op jit(solution)/shard_map/ppermute | solution.py:322
  96.3 14.4 %collective-permute-start.33 = (bf16[256,1024]{1,0:T(8,128)(2,1)S(1)}, bf16[256,1024]{1,0:T(8,128)(2,1)S(1)}, u32[]{:S(2)}, u32[]{:S(2)}) collective-permute-start(bf16[256,1024]{1,0:T(8,128)(2,1)S(1)} %shard_map.210.w0), channel_id=1, source_target_pairs={{0,8},{1,9},{2,10},{3,11},{4,12},{5,13},{6,14},{7,15},{8,0},{9,1},... | collective-permute-start | bytes 1572872 | tf_op jit(solution)/shard_map/ppermute | solution.py:322
  98.2 14.1 %collective-permute-start.28 = (bf16[196,1024]{1,0:T(8,128)(2,1)S(1)}, bf16[196,1024]{1,0:T(8,128)(2,1)S(1)}, u32[]{:S(2)}, u32[]{:S(2)}) collective-permute-start(bf16[196,1024]{1,0:T(8,128)(2,1)S(1)} %get-tuple-element.289), channel_id=1, source_target_pairs={{0,1},{1,0},{2,3},{3,2},{4,5},{5,4},{6,7},{7,6},{8,9},{9,8},{10,11... | collective-permute-start | bytes 1204232 | tf_op jit(solution)/shard_map/ppermute | solution.py:322
  98.3 14.0 %collective-permute-start.29 = (bf16[56,1024]{1,0:T(8,128)(2,1)S(1)}, bf16[56,1024]{1,0:T(8,128)(2,1)S(1)}, u32[]{:S(2)}, u32[]{:S(2)}) collective-permute-start(bf16[56,1024]{1,0:T(8,128)(2,1)S(1)} %collective-permute-done.26.r2), channel_id=1, source_target_pairs={{0,1},{1,0},{2,3},{3,2},{4,5},{5,4},{6,7},{7,6},{8,9},{9,8},{10,11... | collective-permute-start | bytes 344072 | tf_op jit(solution)/shard_map/ppermute | solution.py:322
  100.3 15.0 %collective-permute-start.34 = (bf16[256,1024]{1,0:T(8,128)(2,1)S(1)}, bf16[256,1024]{1,0:T(8,128)(2,1)S(1)}, u32[]{:S(2)}, u32[]{:S(2)}) collective-permute-start(bf16[256,1024]{1,0:T(8,128)(2,1)S(1)} %shard_map.210.w0), channel_id=1, source_target_pairs={{0,16},{1,17},{2,18},{3,19},{4,20},{5,21},{6,22},{7,23},{8,24},{9,... | collective-permute-start | bytes 1572872 | tf_op jit(solution)/shard_map/ppermute | solution.py:322
  110.7 14.4 %collective-permute-start.35 = (bf16[256,1024]{1,0:T(8,128)(2,1)S(1)}, bf16[256,1024]{1,0:T(8,128)(2,1)S(1)}, u32[]{:S(2)}, u32[]{:S(2)}) collective-permute-start(bf16[256,1024]{1,0:T(8,128)(2,1)S(1)} %collective-permute-done.33.w1), channel_id=1, source_target_pairs={{0,16},{1,17},{2,18},{3,19},{4,20},{5,21},{6,22},{7,23},{8,24},{9,... | collective-permute-start | bytes 1572872 | tf_op jit(solution)/shard_map/ppermute | solution.py:322
  113.1 12.0 %collective-permute-start.31 = (bf16[196,1024]{1,0:T(8,128)(2,1)S(1)}, bf16[196,1024]{1,0:T(8,128)(2,1)S(1)}, u32[]{:S(2)}, u32[]{:S(2)}) collective-permute-start(bf16[196,1024]{1,0:T(8,128)(2,1)S(1)} %shard_map.208.own.grads), channel_id=1, source_target_pairs={{0,4},{1,5},{2,6},{3,7},{4,0},{5,1},{6,2},{7,3},{8,12},{9,13},{10,... | collective-permute-start | bytes 1204232 | tf_op jit(solution)/shard_map/ppermute | solution.py:322
  113.2 14.3 %collective-permute-start.36 = (bf16[256,1024]{1,0:T(8,128)(2,1)S(1)}, bf16[256,1024]{1,0:T(8,128)(2,1)S(1)}, u32[]{:S(2)}, u32[]{:S(2)}) collective-permute-start(bf16[256,1024]{1,0:T(8,128)(2,1)S(1)} %collective-permute-done.24.w2), channel_id=1, source_target_pairs={{0,8},{1,9},{2,10},{3,11},{4,12},{5,13},{6,14},{7,15},{8,0},{9,1},... | collective-permute-start | bytes 1572872 | tf_op jit(solution)/shard_map/ppermute | solution.py:322
  115.1 12.4 %collective-permute-start.30 = (bf16[196,1024]{1,0:T(8,128)(2,1)S(1)}, bf16[196,1024]{1,0:T(8,128)(2,1)S(1)}, u32[]{:S(2)}, u32[]{:S(2)}) collective-permute-start(bf16[196,1024]{1,0:T(8,128)(2,1)S(1)} %get-tuple-element.294.own), channel_id=1, source_target_pairs={{0,4},{1,5},{2,6},{3,7},{4,0},{5,1},{6,2},{7,3},{8,12},{9,13},{10,... | collective-permute-start | bytes 1204232 | tf_op jit(solution)/shard_map/ppermute | solution.py:322
  135.7 11.6 %collective-permute-start.38 = (bf16[196,1024]{1,0:T(8,128)(2,1)S(1)}, bf16[196,1024]{1,0:T(8,128)(2,1)S(1)}, u32[]{:S(2)}, u32[]{:S(2)}) collective-permute-start(bf16[196,1024]{1,0:T(8,128)(2,1)S(1)} %get-tuple-element.306), channel_id=1, source_target_pairs={{0,1},{1,0},{2,3},{3,2},{4,5},{5,4},{6,7},{7,6},{8,9},{9,8},{10,11... | collective-permute-start | bytes 1204232 | tf_op jit(solution)/shard_map/ppermute | solution.py:322
  137.9 25.5 %collective-permute-start.46 = (bf16[2,256,1024]{2,1,0:T(8,128)(2,1)S(1)}, bf16[2,256,1024]{2,1,0:T(8,128)(2,1)S(1)}, u32[]{:S(2)}, u32[]{:S(2)}) collective-permute-start(bf16[2,256,1024]{2,1,0:T(8,128)(2,1)S(1)} %get-tuple-element.338), channel_id=1, source_target_pairs={{0,16},{1,17},{2,18},{3,19},{4,20},{5,21},{6,22},{7,23},{8,24},{9,... | collective-permute-start | bytes 3145736 | tf_op jit(solution)/shard_map/ppermute | solution.py:322
  140.8 25.8 %collective-permute-start.45 = (bf16[2,256,1024]{2,1,0:T(8,128)(2,1)S(1)}, bf16[2,256,1024]{2,1,0:T(8,128)(2,1)S(1)}, u32[]{:S(2)}, u32[]{:S(2)}) collective-permute-start(bf16[2,256,1024]{2,1,0:T(8,128)(2,1)S(1)} %get-tuple-element.332), channel_id=1, source_target_pairs={{0,8},{1,9},{2,10},{3,11},{4,12},{5,13},{6,14},{7,15},{8,0},{9,1},... | collective-permute-start | bytes 3145736 | tf_op jit(solution)/shard_map/ppermute | solution.py:322
  150.1 7.2 %collective-permute-start.41 = (bf16[98,1024]{1,0:T(8,128)(2,1)S(1)}, bf16[98,1024]{1,0:T(8,128)(2,1)S(1)}, u32[]{:S(2)}, u32[]{:S(2)}) collective-permute-start(bf16[98,1024]{1,0:T(8,128)(2,1)S(1)} %get-tuple-element.323), channel_id=1, source_target_pairs={{0,1},{1,0},{2,3},{3,2},{4,5},{5,4},{6,7},{7,6},{8,9},{9,8},{10,11... | collective-permute-start | bytes 602120 | tf_op jit(solution)/shard_map/ppermute | solution.py:322
  157.4 10.0 %collective-permute-start.42 = (bf16[196,128]{1,0:T(8,128)(2,1)S(1)}, bf16[196,128]{1,0:T(8,128)(2,1)S(1)}, u32[]{:S(2)}, u32[]{:S(2)}) collective-permute-start(bf16[196,128]{1,0:T(8,128)(2,1)S(1)} %get-tuple-element.325), channel_id=1, source_target_pairs={{0,8},{1,9},{2,10},{3,11},{4,12},{5,13},{6,14},{7,15},{8,0},{9,1},... | collective-permute-start | bytes 150536 | tf_op jit(solution)/shard_map/ppermute | solution.py:322
  158.4 9.0 %collective-permute-start.43 = (bf16[196,128]{1,0:T(8,128)(2,1)S(1)}, bf16[196,128]{1,0:T(8,128)(2,1)S(1)}, u32[]{:S(2)}, u32[]{:S(2)}) collective-permute-start(bf16[196,128]{1,0:T(8,128)(2,1)S(1)} %get-tuple-element.326), channel_id=1, source_target_pairs={{0,16},{1,17},{2,18},{3,19},{4,20},{5,21},{6,22},{7,23},{8,24},{9,... | collective-permute-start | bytes 150536 | tf_op jit(solution)/shard_map/ppermute | solution.py:322
  159.4 8.8 %collective-permute-start.44 = (bf16[196,128]{1,0:T(8,128)(2,1)S(1)}, bf16[196,128]{1,0:T(8,128)(2,1)S(1)}, u32[]{:S(2)}, u32[]{:S(2)}) collective-permute-start(bf16[196,128]{1,0:T(8,128)(2,1)S(1)} %get-tuple-element.327), channel_id=1, source_target_pairs={{0,24},{1,25},{2,26},{3,27},{4,28},{5,29},{6,30},{7,31},{8,16},{9,... | collective-permute-start | bytes 150536 | tf_op jit(solution)/shard_map/ppermute | solution.py:322
  168.2 15.6 %collective-permute-start.47 = (bf16[56,1024]{1,0:T(8,128)(2,1)S(1)}, bf16[56,1024]{1,0:T(8,128)(2,1)S(1)}, u32[]{:S(2)}, u32[]{:S(2)}) collective-permute-start(bf16[56,1024]{1,0:T(8,128)(2,1)S(1)} %get-tuple-element.355), channel_id=1, source_target_pairs={{0,2},{1,3},{2,0},{3,1},{4,6},{5,7},{6,4},{7,5},{8,10},{9,11},{10,... | collective-permute-start | bytes 344072 | tf_op jit(solution)/shard_map/ppermute | solution.py:322
  169.7 14.2 %collective-permute-start.48 = (bf16[256,1024]{1,0:T(8,128)(2,1)S(1)}, bf16[256,1024]{1,0:T(8,128)(2,1)S(1)}, u32[]{:S(2)}, u32[]{:S(2)}) collective-permute-start(bf16[256,1024]{1,0:T(8,128)(2,1)S(1)} %get-tuple-element.357), channel_id=1, source_target_pairs={{0,16},{1,17},{2,18},{3,19},{4,20},{5,21},{6,22},{7,23},{8,24},{9,... | collective-permute-start | bytes 1572872 | tf_op jit(solution)/shard_map/ppermute | solution.py:322
  170.7 13.2 %collective-permute-start.49 = (bf16[256,1024]{1,0:T(8,128)(2,1)S(1)}, bf16[256,1024]{1,0:T(8,128)(2,1)S(1)}, u32[]{:S(2)}, u32[]{:S(2)}) collective-permute-start(bf16[256,1024]{1,0:T(8,128)(2,1)S(1)} %get-tuple-element.359), channel_id=1, source_target_pairs={{0,8},{1,9},{2,10},{3,11},{4,12},{5,13},{6,14},{7,15},{8,0},{9,1},... | collective-permute-start | bytes 1572872 | tf_op jit(solution)/shard_map/ppermute | solution.py:322
  184.6 4.9 %collective-permute-start.54 = (bf16[4,56,1024]{2,1,0:T(8,128)(2,1)S(1)}, bf16[4,56,1024]{2,1,0:T(8,128)(2,1)S(1)}, u32[]{:S(2)}, u32[]{:S(2)}) collective-permute-start(bf16[4,56,1024]{2,1,0:T(8,128)(2,1)S(1)} %get-tuple-element.372), channel_id=1, source_target_pairs={{0,4},{1,5},{2,6},{3,7},{4,0},{5,1},{6,2},{7,3},{8,12},{9,13},{10,... | collective-permute-start | bytes 1376264 | tf_op jit(solution)/shard_map/ppermute | solution.py:322
  185.5 4.6 %collective-permute-start.53 = (bf16[128,2048]{1,0:T(8,128)(2,1)S(1)}, bf16[128,2048]{1,0:T(8,128)(2,1)S(1)}, u32[]{:S(2)}, u32[]{:S(2)}) collective-permute-start(bf16[128,2048]{1,0:T(8,128)(2,1)S(1)} %get-tuple-element.371), channel_id=1, source_target_pairs={{0,4},{1,5},{2,6},{3,7},{4,0},{5,1},{6,2},{7,3},{8,12},{9,13},{10,... | collective-permute-start | bytes 1572872 | tf_op jit(solution)/shard_map/ppermute | solution.py:322
  186.1 6.8 %collective-permute-start.50 = (bf16[596,128]{1,0:T(8,128)(2,1)S(1)}, bf16[596,128]{1,0:T(8,128)(2,1)S(1)}, u32[]{:S(2)}, u32[]{:S(2)}) collective-permute-start(bf16[596,128]{1,0:T(8,128)(2,1)S(1)} %get-tuple-element.363), channel_id=1, source_target_pairs={{0,8},{1,9},{2,10},{3,11},{4,12},{5,13},{6,14},{7,15},{8,0},{9,1},... | collective-permute-start | bytes 457736 | tf_op jit(solution)/shard_map/ppermute | solution.py:322
  187.0 9.0 %collective-permute-start.51 = (bf16[596,128]{1,0:T(8,128)(2,1)S(1)}, bf16[596,128]{1,0:T(8,128)(2,1)S(1)}, u32[]{:S(2)}, u32[]{:S(2)}) collective-permute-start(bf16[596,128]{1,0:T(8,128)(2,1)S(1)} %get-tuple-element.364), channel_id=1, source_target_pairs={{0,16},{1,17},{2,18},{3,19},{4,20},{5,21},{6,22},{7,23},{8,24},{9,... | collective-permute-start | bytes 457736 | tf_op jit(solution)/shard_map/ppermute | solution.py:322
  188.0 8.0 %collective-permute-start.52 = (bf16[596,128]{1,0:T(8,128)(2,1)S(1)}, bf16[596,128]{1,0:T(8,128)(2,1)S(1)}, u32[]{:S(2)}, u32[]{:S(2)}) collective-permute-start(bf16[596,128]{1,0:T(8,128)(2,1)S(1)} %get-tuple-element.365), channel_id=1, source_target_pairs={{0,24},{1,25},{2,26},{3,27},{4,28},{5,29},{6,30},{7,31},{8,16},{9,... | collective-permute-start | bytes 457736 | tf_op jit(solution)/shard_map/ppermute | solution.py:322
  197.7 9.8 %collective-permute-start.57 = (bf16[2,56,1024]{2,1,0:T(8,128)(2,1)S(1)}, bf16[2,56,1024]{2,1,0:T(8,128)(2,1)S(1)}, u32[]{:S(2)}, u32[]{:S(2)}) collective-permute-start(bf16[2,56,1024]{2,1,0:T(8,128)(2,1)S(1)} %get-tuple-element.397), channel_id=1, source_target_pairs={{0,8},{1,9},{2,10},{3,11},{4,12},{5,13},{6,14},{7,15},{8,0},{9,1},... | collective-permute-start | bytes 688136 | tf_op jit(solution)/shard_map/ppermute | solution.py:322
  198.8 12.6 %collective-permute-start.58 = (bf16[2,56,1024]{2,1,0:T(8,128)(2,1)S(1)}, bf16[2,56,1024]{2,1,0:T(8,128)(2,1)S(1)}, u32[]{:S(2)}, u32[]{:S(2)}) collective-permute-start(bf16[2,56,1024]{2,1,0:T(8,128)(2,1)S(1)} %get-tuple-element.398), channel_id=1, source_target_pairs={{0,16},{1,17},{2,18},{3,19},{4,20},{5,21},{6,22},{7,23},{8,24},{9,... | collective-permute-start | bytes 688136 | tf_op jit(solution)/shard_map/ppermute | solution.py:322
  199.7 11.6 %collective-permute-start.59 = (bf16[2,56,1024]{2,1,0:T(8,128)(2,1)S(1)}, bf16[2,56,1024]{2,1,0:T(8,128)(2,1)S(1)}, u32[]{:S(2)}, u32[]{:S(2)}) collective-permute-start(bf16[2,56,1024]{2,1,0:T(8,128)(2,1)S(1)} %get-tuple-element.399), channel_id=1, source_target_pairs={{0,24},{1,25},{2,26},{3,27},{4,28},{5,29},{6,30},{7,31},{8,16},{9,... | collective-permute-start | bytes 688136 | tf_op jit(solution)/shard_map/ppermute | solution.py:322
  202.3 11.9 %collective-permute-start.56 = (bf16[112,1024]{1,0:T(8,128)(2,1)S(1)}, bf16[112,1024]{1,0:T(8,128)(2,1)S(1)}, u32[]{:S(2)}, u32[]{:S(2)}) collective-permute-start(bf16[112,1024]{1,0:T(8,128)(2,1)S(1)} %get-tuple-element.386), channel_id=1, source_target_pairs={{0,1},{1,0},{2,3},{3,2},{4,5},{5,4},{6,7},{7,6},{8,9},{9,8},{10,11... | collective-permute-start | bytes 688136 | tf_op jit(solution)/shard_map/ppermute | solution.py:322
  202.7 29.8 %collective-permute-start.63 = (bf16[128,2048]{1,0:T(8,128)(2,1)S(1)}, bf16[128,2048]{1,0:T(8,128)(2,1)S(1)}, u32[]{:S(2)}, u32[]{:S(2)}) collective-permute-start(bf16[128,2048]{1,0:T(8,128)(2,1)S(1)} %shard_map.226), channel_id=1, source_target_pairs={{0,2},{1,3},{2,0},{3,1},{4,6},{5,7},{6,4},{7,5},{8,10},{9,11},{10,... | collective-permute-start | bytes 1572872 | tf_op jit(solution)/shard_map/ppermute | solution.py:322
  214.2 19.7 %collective-permute-start.61 = (bf16[2,256,512]{2,1,0:T(8,128)(2,1)S(1)}, bf16[2,256,512]{2,1,0:T(8,128)(2,1)S(1)}, u32[]{:S(2)}, u32[]{:S(2)}) collective-permute-start(bf16[2,256,512]{2,1,0:T(8,128)(2,1)S(1)} %get-tuple-element.409), channel_id=1, source_target_pairs={{0,8},{1,9},{2,10},{3,11},{4,12},{5,13},{6,14},{7,15},{8,0},{9,1},... | collective-permute-start | bytes 1572872 | tf_op jit(solution)/shard_map/ppermute | solution.py:322
  215.3 18.7 %collective-permute-start.62 = (bf16[2,256,512]{2,1,0:T(8,128)(2,1)S(1)}, bf16[2,256,512]{2,1,0:T(8,128)(2,1)S(1)}, u32[]{:S(2)}, u32[]{:S(2)}) collective-permute-start(bf16[2,256,512]{2,1,0:T(8,128)(2,1)S(1)} %get-tuple-element.410), channel_id=1, source_target_pairs={{0,16},{1,17},{2,18},{3,19},{4,20},{5,21},{6,22},{7,23},{8,24},{9,... | collective-permute-start | bytes 1572872 | tf_op jit(solution)/shard_map/ppermute | solution.py:322
  217.3 16.7 %collective-permute-start.60 = (bf16[64,1024]{1,0:T(8,128)(2,1)S(1)}, bf16[64,1024]{1,0:T(8,128)(2,1)S(1)}, u32[]{:S(2)}, u32[]{:S(2)}) collective-permute-start(bf16[64,1024]{1,0:T(8,128)(2,1)S(1)} %get-tuple-element.408), channel_id=1, source_target_pairs={{0,2},{1,3},{2,0},{3,1},{4,6},{5,7},{6,4},{7,5},{8,10},{9,11},{10,... | collective-permute-start | bytes 393224 | tf_op jit(solution)/shard_map/ppermute | solution.py:322
  237.2 8.4 %collective-permute-start.68 = (bf16[256,512]{1,0:T(8,128)(2,1)S(1)}, bf16[256,512]{1,0:T(8,128)(2,1)S(1)}, u32[]{:S(2)}, u32[]{:S(2)}) collective-permute-start(bf16[256,512]{1,0:T(8,128)(2,1)S(1)} %get-tuple-element.435), channel_id=1, source_target_pairs={{0,16},{1,17},{2,18},{3,19},{4,20},{5,21},{6,22},{7,23},{8,24},{9,... | collective-permute-start | bytes 786440 | tf_op jit(solution)/shard_map/ppermute | solution.py:322
  238.3 8.1 %collective-permute-start.69 = (bf16[256,512]{1,0:T(8,128)(2,1)S(1)}, bf16[256,512]{1,0:T(8,128)(2,1)S(1)}, u32[]{:S(2)}, u32[]{:S(2)}) collective-permute-start(bf16[256,512]{1,0:T(8,128)(2,1)S(1)} %get-tuple-element.437), channel_id=1, source_target_pairs={{0,8},{1,9},{2,10},{3,11},{4,12},{5,13},{6,14},{7,15},{8,0},{9,1},... | collective-permute-start | bytes 786440 | tf_op jit(solution)/shard_map/ppermute | solution.py:322
  247.0 7.1 %collective-permute-start.70 = (bf16[128,1024]{1,0:T(8,128)(2,1)S(1)}, bf16[128,1024]{1,0:T(8,128)(2,1)S(1)}, u32[]{:S(2)}, u32[]{:S(2)}) collective-permute-start(bf16[128,1024]{1,0:T(8,128)(2,1)S(1)} %get-tuple-element.439), channel_id=1, source_target_pairs={{0,4},{1,5},{2,6},{3,7},{4,0},{5,1},{6,2},{7,3},{8,12},{9,13},{10,... | collective-permute-start | bytes 786440 | tf_op jit(solution)/shard_map/ppermute | solution.py:322
  248.9 8.4 %collective-permute-start.65 = (bf16[2,56,1024]{2,1,0:T(8,128)(2,1)S(1)}, bf16[2,56,1024]{2,1,0:T(8,128)(2,1)S(1)}, u32[]{:S(2)}, u32[]{:S(2)}) collective-permute-start(bf16[2,56,1024]{2,1,0:T(8,128)(2,1)S(1)} %get-tuple-element.428), channel_id=1, source_target_pairs={{0,8},{1,9},{2,10},{3,11},{4,12},{5,13},{6,14},{7,15},{8,0},{9,1},... | collective-permute-start | bytes 688136 | tf_op jit(solution)/shard_map/ppermute | solution.py:322
  249.8 12.6 %collective-permute-start.66 = (bf16[2,56,1024]{2,1,0:T(8,128)(2,1)S(1)}, bf16[2,56,1024]{2,1,0:T(8,128)(2,1)S(1)}, u32[]{:S(2)}, u32[]{:S(2)}) collective-permute-start(bf16[2,56,1024]{2,1,0:T(8,128)(2,1)S(1)} %get-tuple-element.429), channel_id=1, source_target_pairs={{0,16},{1,17},{2,18},{3,19},{4,20},{5,21},{6,22},{7,23},{8,24},{9,... | collective-permute-start | bytes 688136 | tf_op jit(solution)/shard_map/ppermute | solution.py:322
  250.9 11.6 %collective-permute-start.67 = (bf16[2,56,1024]{2,1,0:T(8,128)(2,1)S(1)}, bf16[2,56,1024]{2,1,0:T(8,128)(2,1)S(1)}, u32[]{:S(2)}, u32[]{:S(2)}) collective-permute-start(bf16[2,56,1024]{2,1,0:T(8,128)(2,1)S(1)} %get-tuple-element.430), channel_id=1, source_target_pairs={{0,24},{1,25},{2,26},{3,27},{4,28},{5,29},{6,30},{7,31},{8,16},{9,... | collective-permute-start | bytes 688136 | tf_op jit(solution)/shard_map/ppermute | solution.py:322
  254.7 14.2 %collective-permute-start.71 = (bf16[128,1024]{1,0:T(8,128)(2,1)S(1)}, bf16[128,1024]{1,0:T(8,128)(2,1)S(1)}, u32[]{:S(2)}, u32[]{:S(2)}) collective-permute-start(bf16[128,1024]{1,0:T(8,128)(2,1)S(1)} %shard_map.239), channel_id=1, source_target_pairs={{0,2},{1,3},{2,0},{3,1},{4,6},{5,7},{6,4},{7,5},{8,10},{9,11},{10,... | collective-permute-start | bytes 786440 | tf_op jit(solution)/shard_map/ppermute | solution.py:322
  (18 other events, 44.7 us)

commit v5 on v4

--- a/solution.py
+++ b/solution.py
@@ -347,10 +347,13 @@
     "grads_att": 1.8,
     "norm_one_back": 1.0,
     "give": 1.3,
-    "take": 12.0,
+    "take": 2.0,
     "finish_mlp": 1.7,
     "finish_att": 1.4,
 }
+
+
+SPACE = {"attention_kernel": 16, "attention_back_kernel": 12}
 
 
 def call(body, outs, scalars, *args, scratch=()):
@@ -365,7 +368,7 @@
         + [pl.BlockSpec(memory_space=pltpu.VMEM)] * len(args),
         out_specs=[pl.BlockSpec(memory_space=pltpu.VMEM)] * len(outs),
         scratch_shapes=[pltpu.VMEM(s, t) for s, t in scratch],
-        compiler_params=pltpu.CompilerParams(vmem_limit_bytes=moved + held + (4 << 20)),
+        compiler_params=pltpu.CompilerParams(vmem_limit_bytes=moved + held + (SPACE.get(body.__name__, 4) << 20)),
         cost_estimate=pl.CostEstimate(
             flops=int(time * 1.15e9), bytes_accessed=moved, transcendentals=0
         ),
@@ -578,7 +581,7 @@
         out[...] = heads[ids[CHIP_ID] ^ m, :, :]
 
 
-STEP = 224
+STEP, BACK_STEP = 392, 112
 
 
 def stage_qkv(stage, parts):
@@ -591,60 +594,63 @@
         stage[start + half : start + tokens, 128:192] = part[VALUES:, 64:128].astype(F32)
 
 
-def attention_kernel(ids, a0, a1, a2, a3, o0, o1, o2, o3, lse, stage, q, k, v):
+def attention_kernel(ids, a0, a1, a2, a3, o0, o1, o2, o3, back, stage, q, k, v):
     tokens = stage.shape[0] // 4
     stage_qkv(stage, (a0, a1, a2, a3))
     q[...] = (stage[:, 0:64] * 0.125).astype(BF16)
     k[...] = stage[:, 64:128].astype(BF16)
-    v[...] = stage[:, 128:192].astype(BF16)
-
-    def body(i, carry):
-        rows = pl.ds(pl.multiple_of(i * STEP, 32), STEP)
+    v[:, 0:64] = stage[:, 128:192].astype(BF16)
+    v[:, 64:128] = jnp.ones((v.shape[0], 64), BF16)
+    for i in range(stage.shape[0] // STEP):
+        rows = slice(i * STEP, i * STEP + STEP)
         scores = dot(q[rows, :], k[...], NT)
         top = jnp.max(scores, axis=1, keepdims=True)
-        weights = jnp.exp(scores - top)
-        total = jnp.sum(weights, axis=1, keepdims=True)
-        mixed = dot(weights.astype(BF16), v[...], NN)
-        stage[rows, 0:64] = mixed / total
-        spread = jnp.broadcast_to(top + jnp.log(total), (STEP, 128))
-        lse[i, :, :] = jnp.transpose(spread)[0:8, :]
-        return carry
-
-    lax.fori_loop(0, stage.shape[0] // STEP, body, 0)
+        mixed = dot(jnp.exp(scores - top).astype(BF16), v[...], NN)
+        total = mixed[:, 64:128]
+        back[rows, 0:64] = mixed[:, 0:64] / total
+        back[rows, 64:128] = top + jnp.log(total)
     for m, out in enumerate((o0, o1, o2, o3)):
-        out[...] = fold_rows(stage[tokens * m : tokens * m + tokens, 0:64]).astype(BF16)
+        out[...] = fold_rows(back[tokens * m : tokens * m + tokens, 0:64]).astype(BF16)
+
+
+def with_shift(value, shift):
+    high = shift.astype(BF16).astype(F32)
+    middle = (shift - high).astype(BF16).astype(F32)
+    low = shift - high - middle
+    lane = lax.broadcasted_iota(jnp.int32, (value.shape[0], 64), 1)
+    extra = jnp.where(lane == 0, -high, jnp.where(lane == 1, -middle, jnp.where(lane == 2, -low, 0.0)))
+    return jnp.concatenate([value, extra], axis=1).astype(BF16)
+
+
+def with_ones(value):
+    lane = lax.broadcasted_iota(jnp.int32, (value.shape[0], 64), 1)
+    return jnp.concatenate([value, jnp.where(lane < 3, 1.0, 0.0)], axis=1).astype(BF16)
 
 
 def attention_back_kernel(
-    ids, a0, a1, a2, a3, g0, g1, g2, g3, lse, o0, o1, o2, o3, stage, q, k, v, g, grad_k, grad_v
+    ids, a0, a1, a2, a3, g0, g1, g2, g3, back, o0, o1, o2, o3, stage, q, k, v, g, grad_k, grad_v
 ):
     tokens = stage.shape[0] // 4
     stage_qkv(stage, (a0, a1, a2, a3))
-    q[...] = (stage[:, 0:64] * 0.125).astype(BF16)
-    k[...] = stage[:, 64:128].astype(BF16)
-    v[...] = stage[:, 128:192].astype(BF16)
+    q[...] = with_shift(stage[:, 0:64] * 0.125, back[:, 64:65])
+    k[...] = with_ones(stage[:, 64:128])
+    v[...] = with_ones(stage[:, 128:192])
     for m, part in enumerate((g0, g1, g2, g3)):
         middle = tokens * m + tokens // 2
         stage[tokens * m : middle, 0:64] = part[:, 0:64].astype(F32)
         stage[middle : tokens * m + tokens, 0:64] = part[:, 64:128].astype(F32)
-    g[...] = stage[:, 0:64].astype(BF16)
-    keys_t = jnp.transpose(k[...])
-    grad_k[...] = jnp.zeros_like(grad_k)
-    grad_v[...] = jnp.zeros_like(grad_v)
-
-    def body(i, carry):
-        rows = pl.ds(pl.multiple_of(i * STEP, 32), STEP)
-        queries, grad = q[rows, :], g[rows, :]
-        probs = jnp.exp(dot(k[...], queries, NT) - lse[i, 0:1, :])
-        grad_probs = dot(v[...], grad, NT)
-        row_dot = jnp.sum(probs * grad_probs, axis=0, keepdims=True)
-        grad_scores = (probs * (grad_probs - row_dot)).astype(BF16)
-        grad_v[...] += dot(probs.astype(BF16), grad, NN)
-        grad_k[...] += dot(grad_scores, queries, NN)
+    grads = stage[:, 0:64]
+    g[...] = with_shift(grads, jnp.sum(grads * back[:, 0:64], axis=1, keepdims=True))
+    keys_t = jnp.transpose(k[:, 0:64])
+    for i in range(stage.shape[0] // BACK_STEP):
+        rows = slice(i * BACK_STEP, i * BACK_STEP + BACK_STEP)
+        probs = jnp.exp(dot(k[...], q[rows, :], NT))
+        grad_scores = (probs * dot(v[...], g[rows, :], NT)).astype(BF16)
+        part_v = dot(probs.astype(BF16), g[rows, 0:64], NN)
+        part_k = dot(grad_scores, q[rows, 0:64], NN)
+        grad_v[...] = part_v if i == 0 else grad_v[...] + part_v
+        grad_k[...] = part_k if i == 0 else grad_k[...] + part_k
         stage[rows, 0:64] = jnp.transpose(dot(keys_t, grad_scores, NN)) * 0.125
-        return carry
-
-    lax.fori_loop(0, stage.shape[0] // STEP, body, 0)
     for m, out in enumerate((o0, o1, o2, o3)):
         rows = slice(tokens * m, tokens * m + tokens)
         out[0:tokens, 0:64] = stage[rows, 0:64].astype(BF16)
@@ -1184,12 +1190,12 @@
     f1, f2 = swap(f0, X), swap(f0, Y)
     s1, s2 = swap(here_grad, Z_LOW), swap(there_grad, Z_HIGH)
     tokens = 4 * count
-    *mixed, lse = call(
+    *mixed, back = call(
         attention_kernel,
-        [((half, 128), BF16)] * 4 + [((tokens // STEP, 8, STEP), F32)],
+        [((half, 128), BF16)] * 4 + [((tokens, 128), F32)],
         ids,
         *qkv,
-        scratch=[((tokens, 192), F32)] + [((tokens, 64), BF16)] * 3,
+        scratch=[((tokens, 192), F32)] + [((tokens, 64), BF16)] * 2 + [((tokens, 128), BF16)],
     )
     shard_g, far_g, *mixed = tie(shard_g, far_g, *mixed)
     g0 = merge(shard_g, far_g, offer(shard_g, far_g))
@@ -1320,19 +1326,17 @@
         ids,
         *qkv,
         *grad_att,
-        lse,
-        scratch=[((tokens, 192), F32)] + [((tokens, 64), BF16)] * 4 + [((tokens, 64), F32)] * 2,
+        back,
+        scratch=[((tokens, 192), F32)] + [((tokens, 128), BF16)] * 4 + [((tokens, 64), F32)] * 2,
     )
     *grad_qkv, away_out, whole_x, got_x, whole_y, got_y = tie(*grad_qkv, away_out, *sums_mlp)
     *sums_mlp, moved_mlp = sum_third(ids, (whole_x, got_x, whole_y, got_y))
+    moved_mlp = swap(moved_mlp, Z_HIGH)
     keep_out, send_out = call(
         give_out_kernel, [((4, PAD, 1024), BF16)] * 2, ids, slots, here_out, away_out
     )
     got_out, *pairs_out = to_chips(keep_out, send_out)
-    *grad_qkv, moved_mlp, got_out, p1, p2, p3 = tie(
-        *trade(grad_qkv), moved_mlp, got_out, *pairs_out
-    )
-    moved_mlp = swap(moved_mlp, Z_HIGH)
+    *grad_qkv, got_out, p1, p2, p3 = tie(*trade(grad_qkv), got_out, *pairs_out)
     parts_out = over_chips((p1, p2, p3))
     joined, keep, send, sums_qv = call(
         qkv_back_kernel,
@@ -1385,7 +1389,7 @@
         scratch=[((8, 1024), F32), ((8, 1024), F32), (plain, F32)],
     )
     got, *pairs = to_chips(keep, send)
-    *pairs, whole_x, other_x, whole_y, other_y = tie(*pairs, *sums_att)
+    whole_x, other_x, whole_y, other_y = sums_att
     parts = keep, got, *over_chips(pairs)
     *sums_att, moved_att = sum_third(ids, send_second(whole_x, other_x, whole_y, other_y))
     moved_att = swap(moved_att, Z_HIGH)

time: 271 us -> 263 us (0.970)
  Pallas kernels: 71.2 us -> 64.8 us
    pallas_call x48, Pallas kernels: 71.2 us -> 64.8 us  [call(): pl.pallas_call(body, out_shape=[jax.ShapeDtypeStruct(s, t) for s, t in ou...]
  transfers between devices with their start and end apart: 72 -> 72, of which waited for: 36 -> 38; matrix products, arithmetic and copies ran while one was open for 0% -> 0% of each run, Pallas kernels for 21% -> 20%
where the time goes in v5:
time: 263 us
  waiting for transfers between devices  129 us (49%)
  Pallas kernels  64.8 us (25%)
  starting transfers between devices  64.4 us (24%)
  local copies, waits for them, and re-layouts  2.87 us (1%)
    ppermute x72, waiting for transfers between devices, swap(): return lax.ppermute(value, AXES, [(i, i ^ mask) for i in range(32)])  129 us
    pallas_call x48, Pallas kernels, call(): pl.pallas_call(body, out_shape=[jax.ShapeDtypeStruct(s, t) for s, t in ou...  64.8 us
    ppermute x72, starting transfers between devices, swap(): return lax.ppermute(value, AXES, [(i, i ^ mask) for i in range(32)])  64.4 us
  transfers between devices with their start and end apart: 72, of which 38 were waited for; matrix products, arithmetic and copies ran while one was open for 0% of the time, Pallas kernels for 20%

profile of v5, /device:TPU:0, one launch (start us, length us, event | category | flops | bytes accessed | tf_op | source)
XLA Modules:
  0.0 262.8 jit_solution(6726315164361258872)
XLA Ops:
  6.8 3.7 %collective-permute-start.4 = (bf16[128,1024]{1,0:T(8,128)(2,1)S(1)}, bf16[128,1024]{1,0:T(8,128)(2,1)S(1)}, u32[]{:S(2)}, u32[]{:S(2)}) collective-permute-start(bf16[128,1024]{1,0:T(8,128)(2,1)S(1)} %get-tuple-element.222.own), channel_id=1, source_target_pairs={{0,2},{1,3},{2,0},{3,1},{4,6},{5,7},{6,4},{7,5},{8,10},{9,11},{10,... | collective-permute-start | bytes 786440 | tf_op jit(solution)/shard_map/ppermute | solution.py:322
  11.1 1.6 collective-permute-start.1
  12.6 1.5 collective-permute-start.2
  14.6 8.3 %collective-permute-done.4.far = bf16[128,1024]{1,0:T(8,128)(2,1)S(1)} collective-permute-done((bf16[128,1024]{1,0:T(8,128)(2,1)S(1)}, bf16[128,1024]{1,0:T(8,128)(2,1)S(1)}, u32[]{:S(2)}, u32[]{:S(2)}) %collective-permute-start.4) | collective-permute-done | bytes 262176 | tf_op jit(solution)/shard_map/ppermute | solution.py:322
  23.7 1.4 collective-permute-done.5.got
  25.7 9.1 %collective-permute-done.2.d2 = bf16[2,112,1024]{2,1,0:T(8,128)(2,1)S(1)} collective-permute-done((bf16[2,112,1024]{2,1,0:T(8,128)(2,1)S(1)}, bf16[2,112,1024]{2,1,0:T(8,128)(2,1)S(1)}, u32[]{:S(2)}, u32[]{:S(2)}) %collective-permute-start.2) | collective-permute-done | bytes 458784 | tf_op jit(solution)/shard_map/ppermute | solution.py:322
  34.8 1.5 collective-permute-start.12
  36.8 1.6 shard_map.199
  38.4 1.6 collective-permute-start.6
  40.0 2.2 collective-permute-start.8
  42.4 2.7 %collective-permute-done.6.r1 = bf16[64,1024]{1,0:T(8,128)(2,1)S(1)} collective-permute-done((bf16[64,1024]{1,0:T(8,128)(2,1)S(1)}, bf16[64,1024]{1,0:T(8,128)(2,1)S(1)}, u32[]{:S(2)}, u32[]{:S(2)}) %collective-permute-start.6) | collective-permute-done | bytes 131104 | tf_op jit(solution)/shard_map/ppermute | solution.py:322
  45.1 3.3 %collective-permute-done.8.r3 = bf16[64,1024]{1,0:T(8,128)(2,1)S(1)} collective-permute-done((bf16[64,1024]{1,0:T(8,128)(2,1)S(1)}, bf16[64,1024]{1,0:T(8,128)(2,1)S(1)}, u32[]{:S(2)}, u32[]{:S(2)}) %collective-permute-start.8) | collective-permute-done | bytes 131104 | tf_op jit(solution)/shard_map/ppermute | solution.py:322
  48.4 4.3 %collective-permute-done.7.r2 = bf16[64,1024]{1,0:T(8,128)(2,1)S(1)} collective-permute-done((bf16[64,1024]{1,0:T(8,128)(2,1)S(1)}, bf16[64,1024]{1,0:T(8,128)(2,1)S(1)}, u32[]{:S(2)}, u32[]{:S(2)}) %collective-permute-start.7) | collective-permute-done | bytes 131104 | tf_op jit(solution)/shard_map/ppermute | solution.py:322
  53.8 1.5 collective-permute-start.13
  56.7 5.9 %collective-permute-done.13.w3 = bf16[256,512]{1,0:T(8,128)(2,1)S(1)} collective-permute-done((bf16[256,512]{1,0:T(8,128)(2,1)S(1)}, bf16[256,512]{1,0:T(8,128)(2,1)S(1)}, u32[]{:S(2)}, u32[]{:S(2)}) %collective-permute-start.13) | collective-permute-done | bytes 262176 | tf_op jit(solution)/shard_map/ppermute | solution.py:322
  63.8 1.6 shard_map.201
  66.0 1.5 collective-permute-start.17
  67.5 1.4 collective-permute-start.18
  69.9 2.4 collective-permute-done.16.a1
  72.3 2.2 collective-permute-done.17.a2
  76.9 2.9 %collective-permute-start.25 = (bf16[56,1024]{1,0:T(8,128)(2,1)S(1)}, bf16[56,1024]{1,0:T(8,128)(2,1)S(1)}, u32[]{:S(2)}, u32[]{:S(2)}) collective-permute-start(bf16[56,1024]{1,0:T(8,128)(2,1)S(1)} %get-tuple-element.272.here), channel_id=1, source_target_pairs={{0,1},{1,0},{2,3},{3,2},{4,5},{5,4},{6,7},{7,6},{8,9},{9,8},{10,11... | collective-permute-start | bytes 344072 | tf_op jit(solution)/shard_map/ppermute | solution.py:322
  79.8 5.1 %shard_map.204 = (bf16[196,128]{1,0:T(8,128)(2,1)S(1)}, bf16[196,128]{1,0:T(8,128)(2,1)S(1)}, bf16[196,128]{1,0:T(8,128)(2,1)S(1)}, bf16[196,128]{1,0:T(8,128)(2,1)S(1)}, f32[1568,128]{1,0:T(8,128)S(1)}) custom-call(s32[5]{0:T(128)S(1)} %stack.19.ids, bf16[596,128]{1,0:T(8,128)(2,1)S(1)} %get-tuple-element.259.a0, ...), custom_call_target="tpu_custom_call" | custom-call | flops 8739999744 | bytes 1613824 | tf_op jit(solution)/shard_map/pallas_call | solution.py:364
  86.2 1.7 collective-permute-done.26.r2
  88.5 1.4 collective-permute-start.22
  90.6 1.9 collective-permute-done.21.a2
  95.4 1.5 collective-permute-start.33
  97.7 2.0 collective-permute-start.29
  100.5 9.3 %collective-permute-done.33.w1 = bf16[256,1024]{1,0:T(8,128)(2,1)S(1)} collective-permute-done((bf16[256,1024]{1,0:T(8,128)(2,1)S(1)}, bf16[256,1024]{1,0:T(8,128)(2,1)S(1)}, u32[]{:S(2)}, u32[]{:S(2)}) %collective-permute-start.33) | collective-permute-done | bytes 524320 | tf_op jit(solution)/shard_map/ppermute | solution.py:322
  109.8 1.4 collective-permute-start.35
  114.6 9.8 %collective-permute-done.35.w3 = bf16[256,1024]{1,0:T(8,128)(2,1)S(1)} collective-permute-done((bf16[256,1024]{1,0:T(8,128)(2,1)S(1)}, bf16[256,1024]{1,0:T(8,128)(2,1)S(1)}, u32[]{:S(2)}, u32[]{:S(2)}) %collective-permute-start.35) | collective-permute-done | bytes 524320 | tf_op jit(solution)/shard_map/ppermute | solution.py:322
  124.4 1.6 shard_map.211
  126.8 5.6 %shard_map.212 = (bf16[392,1024]{1,0:T(8,128)(2,1)S(1)}, bf16[392,1024]{1,0:T(8,128)(2,1)S(1)}, bf16[392,1024]{1,0:T(8,128)(2,1)S(1)}, f32[1,1024]{1,0:T(1,128)S...) custom-call(s32[5]{0:T(128)S(1)} %stack.19.ids, bf16[196,1024]{1,0:T(8,128)(2,1)S(1)} %get-tuple-element.286.own, ...), custom_call_target="tpu_custom_call" | custom-call | flops 6440000000 | bytes 8126464 | tf_op jit(solution)/shard_map/pallas_call | solution.py:364
  132.5 1.7 collective-permute-done.37.got
  135.3 1.8 shard_map.220
  137.9 1.8 shard_map.218
  141.1 1.6 shard_map.214
  142.7 3.8 %collective-permute-done.38.got = bf16[196,1024]{1,0:T(8,128)(2,1)S(1)} collective-permute-done((bf16[196,1024]{1,0:T(8,128)(2,1)S(1)}, bf16[196,1024]{1,0:T(8,128)(2,1)S(1)}, u32[]{:S(2)}, u32[]{:S(2)}) %collective-permute-start.38) | collective-permute-done | bytes 401440 | tf_op jit(solution)/shard_map/ppermute | solution.py:322
  146.5 1.5 shard_map.215
  151.0 5.6 %collective-permute-done.41.got = bf16[98,1024]{1,0:T(8,128)(2,1)S(1)} collective-permute-done((bf16[98,1024]{1,0:T(8,128)(2,1)S(1)}, bf16[98,1024]{1,0:T(8,128)(2,1)S(1)}, u32[]{:S(2)}, u32[]{:S(2)}) %collective-permute-start.41) | collective-permute-done | bytes 200736 | tf_op jit(solution)/shard_map/ppermute | solution.py:322
  158.5 1.5 collective-permute-start.44
  160.8 1.9 collective-permute-done.46.got
  163.4 2.2 collective-permute-done.45.got
  167.4 1.5 collective-permute-start.47
  170.9 8.6 %shard_map.223 = (bf16[596,128]{1,0:T(8,128)(2,1)S(1)}, bf16[596,128]{1,0:T(8,128)(2,1)S(1)}, bf16[596,128]{1,0:T(8,128)(2,1)S(1)}, bf16[596,128]{1,0:T(8,128)(2,1)S(1)}) custom-call(s32[5]{0:T(128)S(1)} %stack.19.ids, bf16[596,128]{1,0:T(8,128)(2,1)S(1)} %get-tuple-element.259.a0, bf16[596,128]{1,0:T(8,128)(2,1)S(1)} %collective-permute-done.16.a1, ...), custom_call_target="tpu_custom_call" | custom-call | flops 13799999488 | bytes 2224128 | tf_op jit(solution)/shard_map/pallas_call | solution.py:364
  184.3 1.4 collective-permute-start.52
  187.1 1.9 collective-permute-done.50.g1
  189.0 3.8 %collective-permute-done.51.g2 = bf16[596,128]{1,0:T(8,128)(2,1)S(1)} collective-permute-done((bf16[596,128]{1,0:T(8,128)(2,1)S(1)}, bf16[596,128]{1,0:T(8,128)(2,1)S(1)}, u32[]{:S(2)}, u32[]{:S(2)}) %collective-permute-start.51) | collective-permute-done | bytes 152608 | tf_op jit(solution)/shard_map/ppermute | solution.py:322
  192.8 1.6 shard_map.226
  196.6 1.4 collective-permute-start.58
  200.3 2.7 %collective-permute-start.63 = (bf16[128,2048]{1,0:T(8,128)(2,1)S(1)}, bf16[128,2048]{1,0:T(8,128)(2,1)S(1)}, u32[]{:S(2)}, u32[]{:S(2)}) collective-permute-start(bf16[128,2048]{1,0:T(8,128)(2,1)S(1)} %shard_map.232), channel_id=1, source_target_pairs={{0,2},{1,3},{2,0},{3,1},{4,6},{5,7},{6,4},{7,5},{8,10},{9,11},{10,... | collective-permute-start | bytes 1572872 | tf_op jit(solution)/shard_map/ppermute | solution.py:322
  203.0 1.9 shard_map.228
  204.9 3.1 %collective-permute-done.57.d2 = bf16[2,56,1024]{2,1,0:T(8,128)(2,1)S(1)} collective-permute-done((bf16[2,56,1024]{2,1,0:T(8,128)(2,1)S(1)}, bf16[2,56,1024]{2,1,0:T(8,128)(2,1)S(1)}, u32[]{:S(2)}, u32[]{:S(2)}) %collective-permute-start.57) | collective-permute-done | bytes 229408 | tf_op jit(solution)/shard_map/ppermute | solution.py:322
  207.9 2.5 collective-permute-done.55.got
  213.5 16.4 %collective-permute-done.63.moved = bf16[128,2048]{1,0:T(8,128)(2,1)S(1)} collective-permute-done((bf16[128,2048]{1,0:T(8,128)(2,1)S(1)}, bf16[128,2048]{1,0:T(8,128)(2,1)S(1)}, u32[]{:S(2)}, u32[]{:S(2)}) %collective-permute-start.63) | collective-permute-done | bytes 524320 | tf_op jit(solution)/shard_map/ppermute | solution.py:322
  229.9 1.4 collective-permute-done.59.away
  235.7 3.0 %collective-permute-done.68.got_x = bf16[256,512]{1,0:T(8,128)(2,1)S(1)} collective-permute-done((bf16[256,512]{1,0:T(8,128)(2,1)S(1)}, bf16[256,512]{1,0:T(8,128)(2,1)S(1)}, u32[]{:S(2)}, u32[]{:S(2)}) %collective-permute-start.68) | collective-permute-done | bytes 262176 | tf_op jit(solution)/shard_map/ppermute | solution.py:322
  240.7 1.8 shard_map.229
  245.1 1.5 collective-permute-start.67
  247.2 1.8 shard_map.241
  249.0 2.5 collective-permute-done.65.d1
  251.5 5.5 %collective-permute-done.66.d2 = bf16[2,56,1024]{2,1,0:T(8,128)(2,1)S(1)} collective-permute-done((bf16[2,56,1024]{2,1,0:T(8,128)(2,1)S(1)}, bf16[2,56,1024]{2,1,0:T(8,128)(2,1)S(1)}, u32[]{:S(2)}, u32[]{:S(2)}) %collective-permute-start.66) | collective-permute-done | bytes 229408 | tf_op jit(solution)/shard_map/ppermute | solution.py:322
  256.9 2.0 shard_map.235
  258.9 2.4 collective-permute-done.71.moved
  261.4 1.4 shard_map.240
  (153 shorter events, 63.9 us)
Async XLA Ops:
  6.2 4.2 %collective-permute-start = (bf16[4,112,1024]{2,1,0:T(8,128)(2,1)S(1)}, bf16[4,112,1024]{2,1,0:T(8,128)(2,1)S(1)}, u32[]{:S(2)}, u32[]{:S(2)}) collective-permute-start(bf16[4,112,1024]{2,1,0:T(8,128)(2,1)S(1)} %get-tuple-element.225), channel_id=1, source_target_pairs={{0,4},{1,5},{2,6},{3,7},{4,0},{5,1},{6,2},{7,3},{8,12},{9,13},{10,... | collective-permute-start | bytes 2752520 | tf_op jit(solution)/shard_map/ppermute | solution.py:322
  6.8 16.2 %collective-permute-start.4 = (bf16[128,1024]{1,0:T(8,128)(2,1)S(1)}, bf16[128,1024]{1,0:T(8,128)(2,1)S(1)}, u32[]{:S(2)}, u32[]{:S(2)}) collective-permute-start(bf16[128,1024]{1,0:T(8,128)(2,1)S(1)} %get-tuple-element.222.own), channel_id=1, source_target_pairs={{0,2},{1,3},{2,0},{3,1},{4,6},{5,7},{6,4},{7,5},{8,10},{9,11},{10,... | collective-permute-start | bytes 786440 | tf_op jit(solution)/shard_map/ppermute | solution.py:322
  11.1 14.6 %collective-permute-start.1 = (bf16[2,112,1024]{2,1,0:T(8,128)(2,1)S(1)}, bf16[2,112,1024]{2,1,0:T(8,128)(2,1)S(1)}, u32[]{:S(2)}, u32[]{:S(2)}) collective-permute-start(bf16[2,112,1024]{2,1,0:T(8,128)(2,1)S(1)} %get-tuple-element.226), channel_id=1, source_target_pairs={{0,8},{1,9},{2,10},{3,11},{4,12},{5,13},{6,14},{7,15},{8,0},{9,1},... | collective-permute-start | bytes 1376264 | tf_op jit(solution)/shard_map/ppermute | solution.py:322
  12.6 22.1 %collective-permute-start.2 = (bf16[2,112,1024]{2,1,0:T(8,128)(2,1)S(1)}, bf16[2,112,1024]{2,1,0:T(8,128)(2,1)S(1)}, u32[]{:S(2)}, u32[]{:S(2)}) collective-permute-start(bf16[2,112,1024]{2,1,0:T(8,128)(2,1)S(1)} %get-tuple-element.227), channel_id=1, source_target_pairs={{0,16},{1,17},{2,18},{3,19},{4,20},{5,21},{6,22},{7,23},{8,24},{9,... | collective-permute-start | bytes 1376264 | tf_op jit(solution)/shard_map/ppermute | solution.py:322
  14.2 20.6 %collective-permute-start.3 = (bf16[2,112,1024]{2,1,0:T(8,128)(2,1)S(1)}, bf16[2,112,1024]{2,1,0:T(8,128)(2,1)S(1)}, u32[]{:S(2)}, u32[]{:S(2)}) collective-permute-start(bf16[2,112,1024]{2,1,0:T(8,128)(2,1)S(1)} %get-tuple-element.228), channel_id=1, source_target_pairs={{0,24},{1,25},{2,26},{3,27},{4,28},{5,29},{6,30},{7,31},{8,16},{9,... | collective-permute-start | bytes 1376264 | tf_op jit(solution)/shard_map/ppermute | solution.py:322
  23.6 18.7 %collective-permute-start.9 = (bf16[128,1024]{1,0:T(8,128)(2,1)S(1)}, bf16[128,1024]{1,0:T(8,128)(2,1)S(1)}, u32[]{:S(2)}, u32[]{:S(2)}) collective-permute-start(bf16[128,1024]{1,0:T(8,128)(2,1)S(1)} %copy-done.3), channel_id=1, source_target_pairs={{0,2},{1,3},{2,0},{3,1},{4,6},{5,7},{6,4},{7,5},{8,10},{9,11},{10,... | collective-permute-start | bytes 786440 | tf_op jit(solution)/shard_map/ppermute | solution.py:322
  34.8 19.0 %collective-permute-start.12 = (bf16[256,1024]{1,0:T(8,128)(2,1)S(1)}, bf16[256,1024]{1,0:T(8,128)(2,1)S(1)}, u32[]{:S(2)}, u32[]{:S(2)}) collective-permute-start(bf16[256,1024]{1,0:T(8,128)(2,1)S(1)} %shard_map.198.w0), channel_id=1, source_target_pairs={{0,16},{1,17},{2,18},{3,19},{4,20},{5,21},{6,22},{7,23},{8,24},{9,... | collective-permute-start | bytes 1572872 | tf_op jit(solution)/shard_map/ppermute | solution.py:322
  36.3 19.0 %collective-permute-start.11 = (bf16[256,1024]{1,0:T(8,128)(2,1)S(1)}, bf16[256,1024]{1,0:T(8,128)(2,1)S(1)}, u32[]{:S(2)}, u32[]{:S(2)}) collective-permute-start(bf16[256,1024]{1,0:T(8,128)(2,1)S(1)} %shard_map.198.w0), channel_id=1, source_target_pairs={{0,8},{1,9},{2,10},{3,11},{4,12},{5,13},{6,14},{7,15},{8,0},{9,1},... | collective-permute-start | bytes 1572872 | tf_op jit(solution)/shard_map/ppermute | solution.py:322
  38.4 6.7 %collective-permute-start.6 = (bf16[64,1024]{1,0:T(8,128)(2,1)S(1)}, bf16[64,1024]{1,0:T(8,128)(2,1)S(1)}, u32[]{:S(2)}, u32[]{:S(2)}) collective-permute-start(bf16[64,1024]{1,0:T(8,128)(2,1)S(1)} %get-tuple-element.235.here), channel_id=1, source_target_pairs={{0,1},{1,0},{2,3},{3,2},{4,5},{5,4},{6,7},{7,6},{8,9},{9,8},{10,11... | collective-permute-start | bytes 393224 | tf_op jit(solution)/shard_map/ppermute | solution.py:322
  40.0 8.4 %collective-permute-start.8 = (bf16[64,1024]{1,0:T(8,128)(2,1)S(1)}, bf16[64,1024]{1,0:T(8,128)(2,1)S(1)}, u32[]{:S(2)}, u32[]{:S(2)}) collective-permute-start(bf16[64,1024]{1,0:T(8,128)(2,1)S(1)} %get-tuple-element.236), channel_id=1, source_target_pairs={{0,3},{1,2},{2,1},{3,0},{4,7},{5,6},{6,5},{7,4},{8,11},{9,10},{10,... | collective-permute-start | bytes 393224 | tf_op jit(solution)/shard_map/ppermute | solution.py:322
  42.3 10.4 %collective-permute-start.7 = (bf16[64,1024]{1,0:T(8,128)(2,1)S(1)}, bf16[64,1024]{1,0:T(8,128)(2,1)S(1)}, u32[]{:S(2)}, u32[]{:S(2)}) collective-permute-start(bf16[64,1024]{1,0:T(8,128)(2,1)S(1)} %get-tuple-element.236), channel_id=1, source_target_pairs={{0,2},{1,3},{2,0},{3,1},{4,6},{5,7},{6,4},{7,5},{8,10},{9,11},{10,... | collective-permute-start | bytes 393224 | tf_op jit(solution)/shard_map/ppermute | solution.py:322
  53.8 8.8 %collective-permute-start.13 = (bf16[256,512]{1,0:T(8,128)(2,1)S(1)}, bf16[256,512]{1,0:T(8,128)(2,1)S(1)}, u32[]{:S(2)}, u32[]{:S(2)}) collective-permute-start(bf16[256,512]{1,0:T(8,128)(2,1)S(1)} %slice.8), channel_id=1, source_target_pairs={{0,8},{1,9},{2,10},{3,11},{4,12},{5,13},{6,14},{7,15},{8,0},{9,1},... | collective-permute-start | bytes 786440 | tf_op jit(solution)/shard_map/ppermute | solution.py:322
  55.3 8.5 %collective-permute-start.14 = (bf16[256,512]{1,0:T(8,128)(2,1)S(1)}, bf16[256,512]{1,0:T(8,128)(2,1)S(1)}, u32[]{:S(2)}, u32[]{:S(2)}) collective-permute-start(bf16[256,512]{1,0:T(8,128)(2,1)S(1)} %slice.9), channel_id=1, source_target_pairs={{0,16},{1,17},{2,18},{3,19},{4,20},{5,21},{6,22},{7,23},{8,24},{9,... | collective-permute-start | bytes 786440 | tf_op jit(solution)/shard_map/ppermute | solution.py:322
  56.6 12.3 %collective-permute-start.19 = (bf16[128,1024]{1,0:T(8,128)(2,1)S(1)}, bf16[128,1024]{1,0:T(8,128)(2,1)S(1)}, u32[]{:S(2)}, u32[]{:S(2)}) collective-permute-start(bf16[128,1024]{1,0:T(8,128)(2,1)S(1)} %shard_map.202), channel_id=1, source_target_pairs={{0,4},{1,5},{2,6},{3,7},{4,0},{5,1},{6,2},{7,3},{8,12},{9,13},{10,... | collective-permute-start | bytes 786440 | tf_op jit(solution)/shard_map/ppermute | solution.py:322
  65.3 7.0 %collective-permute-start.16 = (bf16[596,128]{1,0:T(8,128)(2,1)S(1)}, bf16[596,128]{1,0:T(8,128)(2,1)S(1)}, u32[]{:S(2)}, u32[]{:S(2)}) collective-permute-start(bf16[596,128]{1,0:T(8,128)(2,1)S(1)} %get-tuple-element.252), channel_id=1, source_target_pairs={{0,8},{1,9},{2,10},{3,11},{4,12},{5,13},{6,14},{7,15},{8,0},{9,1},... | collective-permute-start | bytes 457736 | tf_op jit(solution)/shard_map/ppermute | solution.py:322
  66.0 8.5 %collective-permute-start.17 = (bf16[596,128]{1,0:T(8,128)(2,1)S(1)}, bf16[596,128]{1,0:T(8,128)(2,1)S(1)}, u32[]{:S(2)}, u32[]{:S(2)}) collective-permute-start(bf16[596,128]{1,0:T(8,128)(2,1)S(1)} %get-tuple-element.253), channel_id=1, source_target_pairs={{0,16},{1,17},{2,18},{3,19},{4,20},{5,21},{6,22},{7,23},{8,24},{9,... | collective-permute-start | bytes 457736 | tf_op jit(solution)/shard_map/ppermute | solution.py:322
  67.5 7.0 %collective-permute-start.18 = (bf16[596,128]{1,0:T(8,128)(2,1)S(1)}, bf16[596,128]{1,0:T(8,128)(2,1)S(1)}, u32[]{:S(2)}, u32[]{:S(2)}) collective-permute-start(bf16[596,128]{1,0:T(8,128)(2,1)S(1)} %get-tuple-element.254), channel_id=1, source_target_pairs={{0,24},{1,25},{2,26},{3,27},{4,28},{5,29},{6,30},{7,31},{8,16},{9,... | collective-permute-start | bytes 457736 | tf_op jit(solution)/shard_map/ppermute | solution.py:322
  69.5 16.0 %collective-permute-start.15 = (bf16[128,1024]{1,0:T(8,128)(2,1)S(1)}, bf16[128,1024]{1,0:T(8,128)(2,1)S(1)}, u32[]{:S(2)}, u32[]{:S(2)}) collective-permute-start(bf16[128,1024]{1,0:T(8,128)(2,1)S(1)} %get-tuple-element.289.own), channel_id=1, source_target_pairs={{0,2},{1,3},{2,0},{3,1},{4,6},{5,7},{6,4},{7,5},{8,10},{9,11},{10,... | collective-permute-start | bytes 786440 | tf_op jit(solution)/shard_map/ppermute | solution.py:322
  74.5 19.0 %collective-permute-start.24 = (bf16[256,1024]{1,0:T(8,128)(2,1)S(1)}, bf16[256,1024]{1,0:T(8,128)(2,1)S(1)}, u32[]{:S(2)}, u32[]{:S(2)}) collective-permute-start(bf16[256,1024]{1,0:T(8,128)(2,1)S(1)} %shard_map.203.w0), channel_id=1, source_target_pairs={{0,16},{1,17},{2,18},{3,19},{4,20},{5,21},{6,22},{7,23},{8,24},{9,... | collective-permute-start | bytes 1572872 | tf_op jit(solution)/shard_map/ppermute | solution.py:322
  75.8 17.8 %collective-permute-start.23 = (bf16[256,1024]{1,0:T(8,128)(2,1)S(1)}, bf16[256,1024]{1,0:T(8,128)(2,1)S(1)}, u32[]{:S(2)}, u32[]{:S(2)}) collective-permute-start(bf16[256,1024]{1,0:T(8,128)(2,1)S(1)} %shard_map.203.w0), channel_id=1, source_target_pairs={{0,8},{1,9},{2,10},{3,11},{4,12},{5,13},{6,14},{7,15},{8,0},{9,1},... | collective-permute-start | bytes 1572872 | tf_op jit(solution)/shard_map/ppermute | solution.py:322
  76.6 11.3 %collective-permute-start.26 = (bf16[56,1024]{1,0:T(8,128)(2,1)S(1)}, bf16[56,1024]{1,0:T(8,128)(2,1)S(1)}, u32[]{:S(2)}, u32[]{:S(2)}) collective-permute-start(bf16[56,1024]{1,0:T(8,128)(2,1)S(1)} %get-tuple-element.273), channel_id=1, source_target_pairs={{0,2},{1,3},{2,0},{3,1},{4,6},{5,7},{6,4},{7,5},{8,10},{9,11},{10,... | collective-permute-start | bytes 344072 | tf_op jit(solution)/shard_map/ppermute | solution.py:322
  76.9 11.6 %collective-permute-start.25 = (bf16[56,1024]{1,0:T(8,128)(2,1)S(1)}, bf16[56,1024]{1,0:T(8,128)(2,1)S(1)}, u32[]{:S(2)}, u32[]{:S(2)}) collective-permute-start(bf16[56,1024]{1,0:T(8,128)(2,1)S(1)} %get-tuple-element.272.here), channel_id=1, source_target_pairs={{0,1},{1,0},{2,3},{3,2},{4,5},{5,4},{6,7},{7,6},{8,9},{9,8},{10,11... | collective-permute-start | bytes 344072 | tf_op jit(solution)/shard_map/ppermute | solution.py:322
  85.5 5.0 %collective-permute-start.20 = (bf16[196,128]{1,0:T(8,128)(2,1)S(1)}, bf16[196,128]{1,0:T(8,128)(2,1)S(1)}, u32[]{:S(2)}, u32[]{:S(2)}) collective-permute-start(bf16[196,128]{1,0:T(8,128)(2,1)S(1)} %get-tuple-element.268), channel_id=1, source_target_pairs={{0,8},{1,9},{2,10},{3,11},{4,12},{5,13},{6,14},{7,15},{8,0},{9,1},... | collective-permute-start | bytes 150536 | tf_op jit(solution)/shard_map/ppermute | solution.py:322
  87.9 4.7 %collective-permute-start.21 = (bf16[196,128]{1,0:T(8,128)(2,1)S(1)}, bf16[196,128]{1,0:T(8,128)(2,1)S(1)}, u32[]{:S(2)}, u32[]{:S(2)}) collective-permute-start(bf16[196,128]{1,0:T(8,128)(2,1)S(1)} %get-tuple-element.269), channel_id=1, source_target_pairs={{0,16},{1,17},{2,18},{3,19},{4,20},{5,21},{6,22},{7,23},{8,24},{9,... | collective-permute-start | bytes 150536 | tf_op jit(solution)/shard_map/ppermute | solution.py:322
  88.5 5.0 %collective-permute-start.22 = (bf16[196,128]{1,0:T(8,128)(2,1)S(1)}, bf16[196,128]{1,0:T(8,128)(2,1)S(1)}, u32[]{:S(2)}, u32[]{:S(2)}) collective-permute-start(bf16[196,128]{1,0:T(8,128)(2,1)S(1)} %get-tuple-element.270), channel_id=1, source_target_pairs={{0,24},{1,25},{2,26},{3,27},{4,28},{5,29},{6,30},{7,31},{8,16},{9,... | collective-permute-start | bytes 150536 | tf_op jit(solution)/shard_map/ppermute | solution.py:322
  95.4 14.4 %collective-permute-start.33 = (bf16[256,1024]{1,0:T(8,128)(2,1)S(1)}, bf16[256,1024]{1,0:T(8,128)(2,1)S(1)}, u32[]{:S(2)}, u32[]{:S(2)}) collective-permute-start(bf16[256,1024]{1,0:T(8,128)(2,1)S(1)} %shard_map.210.w0), channel_id=1, source_target_pairs={{0,8},{1,9},{2,10},{3,11},{4,12},{5,13},{6,14},{7,15},{8,0},{9,1},... | collective-permute-start | bytes 1572872 | tf_op jit(solution)/shard_map/ppermute | solution.py:322
  97.6 14.1 %collective-permute-start.28 = (bf16[196,1024]{1,0:T(8,128)(2,1)S(1)}, bf16[196,1024]{1,0:T(8,128)(2,1)S(1)}, u32[]{:S(2)}, u32[]{:S(2)}) collective-permute-start(bf16[196,1024]{1,0:T(8,128)(2,1)S(1)} %get-tuple-element.281), channel_id=1, source_target_pairs={{0,1},{1,0},{2,3},{3,2},{4,5},{5,4},{6,7},{7,6},{8,9},{9,8},{10,11... | collective-permute-start | bytes 1204232 | tf_op jit(solution)/shard_map/ppermute | solution.py:322
  97.7 14.0 %collective-permute-start.29 = (bf16[56,1024]{1,0:T(8,128)(2,1)S(1)}, bf16[56,1024]{1,0:T(8,128)(2,1)S(1)}, u32[]{:S(2)}, u32[]{:S(2)}) collective-permute-start(bf16[56,1024]{1,0:T(8,128)(2,1)S(1)} %collective-permute-done.26.r2), channel_id=1, source_target_pairs={{0,1},{1,0},{2,3},{3,2},{4,5},{5,4},{6,7},{7,6},{8,9},{9,8},{10,11... | collective-permute-start | bytes 344072 | tf_op jit(solution)/shard_map/ppermute | solution.py:322
  99.7 14.9 %collective-permute-start.34 = (bf16[256,1024]{1,0:T(8,128)(2,1)S(1)}, bf16[256,1024]{1,0:T(8,128)(2,1)S(1)}, u32[]{:S(2)}, u32[]{:S(2)}) collective-permute-start(bf16[256,1024]{1,0:T(8,128)(2,1)S(1)} %shard_map.210.w0), channel_id=1, source_target_pairs={{0,16},{1,17},{2,18},{3,19},{4,20},{5,21},{6,22},{7,23},{8,24},{9,... | collective-permute-start | bytes 1572872 | tf_op jit(solution)/shard_map/ppermute | solution.py:322
  109.8 14.6 %collective-permute-start.35 = (bf16[256,1024]{1,0:T(8,128)(2,1)S(1)}, bf16[256,1024]{1,0:T(8,128)(2,1)S(1)}, u32[]{:S(2)}, u32[]{:S(2)}) collective-permute-start(bf16[256,1024]{1,0:T(8,128)(2,1)S(1)} %collective-permute-done.33.w1), channel_id=1, source_target_pairs={{0,16},{1,17},{2,18},{3,19},{4,20},{5,21},{6,22},{7,23},{8,24},{9,... | collective-permute-start | bytes 1572872 | tf_op jit(solution)/shard_map/ppermute | solution.py:322
  112.4 12.0 %collective-permute-start.31 = (bf16[196,1024]{1,0:T(8,128)(2,1)S(1)}, bf16[196,1024]{1,0:T(8,128)(2,1)S(1)}, u32[]{:S(2)}, u32[]{:S(2)}) collective-permute-start(bf16[196,1024]{1,0:T(8,128)(2,1)S(1)} %shard_map.208.own.grads), channel_id=1, source_target_pairs={{0,4},{1,5},{2,6},{3,7},{4,0},{5,1},{6,2},{7,3},{8,12},{9,13},{10,... | collective-permute-start | bytes 1204232 | tf_op jit(solution)/shard_map/ppermute | solution.py:322
  112.5 14.3 %collective-permute-start.36 = (bf16[256,1024]{1,0:T(8,128)(2,1)S(1)}, bf16[256,1024]{1,0:T(8,128)(2,1)S(1)}, u32[]{:S(2)}, u32[]{:S(2)}) collective-permute-start(bf16[256,1024]{1,0:T(8,128)(2,1)S(1)} %collective-permute-done.24.w2), channel_id=1, source_target_pairs={{0,8},{1,9},{2,10},{3,11},{4,12},{5,13},{6,14},{7,15},{8,0},{9,1},... | collective-permute-start | bytes 1572872 | tf_op jit(solution)/shard_map/ppermute | solution.py:322
  114.3 12.5 %collective-permute-start.30 = (bf16[196,1024]{1,0:T(8,128)(2,1)S(1)}, bf16[196,1024]{1,0:T(8,128)(2,1)S(1)}, u32[]{:S(2)}, u32[]{:S(2)}) collective-permute-start(bf16[196,1024]{1,0:T(8,128)(2,1)S(1)} %get-tuple-element.286.own), channel_id=1, source_target_pairs={{0,4},{1,5},{2,6},{3,7},{4,0},{5,1},{6,2},{7,3},{8,12},{9,13},{10,... | collective-permute-start | bytes 1204232 | tf_op jit(solution)/shard_map/ppermute | solution.py:322
  134.9 11.6 %collective-permute-start.38 = (bf16[196,1024]{1,0:T(8,128)(2,1)S(1)}, bf16[196,1024]{1,0:T(8,128)(2,1)S(1)}, u32[]{:S(2)}, u32[]{:S(2)}) collective-permute-start(bf16[196,1024]{1,0:T(8,128)(2,1)S(1)} %get-tuple-element.298), channel_id=1, source_target_pairs={{0,1},{1,0},{2,3},{3,2},{4,5},{5,4},{6,7},{7,6},{8,9},{9,8},{10,11... | collective-permute-start | bytes 1204232 | tf_op jit(solution)/shard_map/ppermute | solution.py:322
  137.1 25.5 %collective-permute-start.46 = (bf16[2,256,1024]{2,1,0:T(8,128)(2,1)S(1)}, bf16[2,256,1024]{2,1,0:T(8,128)(2,1)S(1)}, u32[]{:S(2)}, u32[]{:S(2)}) collective-permute-start(bf16[2,256,1024]{2,1,0:T(8,128)(2,1)S(1)} %get-tuple-element.330), channel_id=1, source_target_pairs={{0,16},{1,17},{2,18},{3,19},{4,20},{5,21},{6,22},{7,23},{8,24},{9,... | collective-permute-start | bytes 3145736 | tf_op jit(solution)/shard_map/ppermute | solution.py:322
  139.8 25.8 %collective-permute-start.45 = (bf16[2,256,1024]{2,1,0:T(8,128)(2,1)S(1)}, bf16[2,256,1024]{2,1,0:T(8,128)(2,1)S(1)}, u32[]{:S(2)}, u32[]{:S(2)}) collective-permute-start(bf16[2,256,1024]{2,1,0:T(8,128)(2,1)S(1)} %get-tuple-element.324), channel_id=1, source_target_pairs={{0,8},{1,9},{2,10},{3,11},{4,12},{5,13},{6,14},{7,15},{8,0},{9,1},... | collective-permute-start | bytes 3145736 | tf_op jit(solution)/shard_map/ppermute | solution.py:322
  149.3 7.2 %collective-permute-start.41 = (bf16[98,1024]{1,0:T(8,128)(2,1)S(1)}, bf16[98,1024]{1,0:T(8,128)(2,1)S(1)}, u32[]{:S(2)}, u32[]{:S(2)}) collective-permute-start(bf16[98,1024]{1,0:T(8,128)(2,1)S(1)} %get-tuple-element.315), channel_id=1, source_target_pairs={{0,1},{1,0},{2,3},{3,2},{4,5},{5,4},{6,7},{7,6},{8,9},{9,8},{10,11... | collective-permute-start | bytes 602120 | tf_op jit(solution)/shard_map/ppermute | solution.py:322
  156.5 9.8 %collective-permute-start.42 = (bf16[196,128]{1,0:T(8,128)(2,1)S(1)}, bf16[196,128]{1,0:T(8,128)(2,1)S(1)}, u32[]{:S(2)}, u32[]{:S(2)}) collective-permute-start(bf16[196,128]{1,0:T(8,128)(2,1)S(1)} %get-tuple-element.317), channel_id=1, source_target_pairs={{0,8},{1,9},{2,10},{3,11},{4,12},{5,13},{6,14},{7,15},{8,0},{9,1},... | collective-permute-start | bytes 150536 | tf_op jit(solution)/shard_map/ppermute | solution.py:322
  157.4 9.0 %collective-permute-start.43 = (bf16[196,128]{1,0:T(8,128)(2,1)S(1)}, bf16[196,128]{1,0:T(8,128)(2,1)S(1)}, u32[]{:S(2)}, u32[]{:S(2)}) collective-permute-start(bf16[196,128]{1,0:T(8,128)(2,1)S(1)} %get-tuple-element.318), channel_id=1, source_target_pairs={{0,16},{1,17},{2,18},{3,19},{4,20},{5,21},{6,22},{7,23},{8,24},{9,... | collective-permute-start | bytes 150536 | tf_op jit(solution)/shard_map/ppermute | solution.py:322
  158.5 8.8 %collective-permute-start.44 = (bf16[196,128]{1,0:T(8,128)(2,1)S(1)}, bf16[196,128]{1,0:T(8,128)(2,1)S(1)}, u32[]{:S(2)}, u32[]{:S(2)}) collective-permute-start(bf16[196,128]{1,0:T(8,128)(2,1)S(1)} %get-tuple-element.319), channel_id=1, source_target_pairs={{0,24},{1,25},{2,26},{3,27},{4,28},{5,29},{6,30},{7,31},{8,16},{9,... | collective-permute-start | bytes 150536 | tf_op jit(solution)/shard_map/ppermute | solution.py:322
  167.4 12.1 %collective-permute-start.47 = (bf16[56,1024]{1,0:T(8,128)(2,1)S(1)}, bf16[56,1024]{1,0:T(8,128)(2,1)S(1)}, u32[]{:S(2)}, u32[]{:S(2)}) collective-permute-start(bf16[56,1024]{1,0:T(8,128)(2,1)S(1)} %get-tuple-element.347), channel_id=1, source_target_pairs={{0,2},{1,3},{2,0},{3,1},{4,6},{5,7},{6,4},{7,5},{8,10},{9,11},{10,... | collective-permute-start | bytes 344072 | tf_op jit(solution)/shard_map/ppermute | solution.py:322
  168.9 11.9 %collective-permute-start.48 = (bf16[256,1024]{1,0:T(8,128)(2,1)S(1)}, bf16[256,1024]{1,0:T(8,128)(2,1)S(1)}, u32[]{:S(2)}, u32[]{:S(2)}) collective-permute-start(bf16[256,1024]{1,0:T(8,128)(2,1)S(1)} %get-tuple-element.349), channel_id=1, source_target_pairs={{0,16},{1,17},{2,18},{3,19},{4,20},{5,21},{6,22},{7,23},{8,24},{9,... | collective-permute-start | bytes 1572872 | tf_op jit(solution)/shard_map/ppermute | solution.py:322
  169.7 11.6 %collective-permute-start.49 = (bf16[256,1024]{1,0:T(8,128)(2,1)S(1)}, bf16[256,1024]{1,0:T(8,128)(2,1)S(1)}, u32[]{:S(2)}, u32[]{:S(2)}) collective-permute-start(bf16[256,1024]{1,0:T(8,128)(2,1)S(1)} %get-tuple-element.351), channel_id=1, source_target_pairs={{0,8},{1,9},{2,10},{3,11},{4,12},{5,13},{6,14},{7,15},{8,0},{9,1},... | collective-permute-start | bytes 1572872 | tf_op jit(solution)/shard_map/ppermute | solution.py:322
  182.1 4.4 %collective-permute-start.53 = (bf16[4,56,1024]{2,1,0:T(8,128)(2,1)S(1)}, bf16[4,56,1024]{2,1,0:T(8,128)(2,1)S(1)}, u32[]{:S(2)}, u32[]{:S(2)}) collective-permute-start(bf16[4,56,1024]{2,1,0:T(8,128)(2,1)S(1)} %get-tuple-element.358), channel_id=1, source_target_pairs={{0,4},{1,5},{2,6},{3,7},{4,0},{5,1},{6,2},{7,3},{8,12},{9,13},{10,... | collective-permute-start | bytes 1376264 | tf_op jit(solution)/shard_map/ppermute | solution.py:322
  182.2 6.8 %collective-permute-start.50 = (bf16[596,128]{1,0:T(8,128)(2,1)S(1)}, bf16[596,128]{1,0:T(8,128)(2,1)S(1)}, u32[]{:S(2)}, u32[]{:S(2)}) collective-permute-start(bf16[596,128]{1,0:T(8,128)(2,1)S(1)} %get-tuple-element.355), channel_id=1, source_target_pairs={{0,8},{1,9},{2,10},{3,11},{4,12},{5,13},{6,14},{7,15},{8,0},{9,1},... | collective-permute-start | bytes 457736 | tf_op jit(solution)/shard_map/ppermute | solution.py:322
  183.5 9.3 %collective-permute-start.51 = (bf16[596,128]{1,0:T(8,128)(2,1)S(1)}, bf16[596,128]{1,0:T(8,128)(2,1)S(1)}, u32[]{:S(2)}, u32[]{:S(2)}) collective-permute-start(bf16[596,128]{1,0:T(8,128)(2,1)S(1)} %get-tuple-element.356), channel_id=1, source_target_pairs={{0,16},{1,17},{2,18},{3,19},{4,20},{5,21},{6,22},{7,23},{8,24},{9,... | collective-permute-start | bytes 457736 | tf_op jit(solution)/shard_map/ppermute | solution.py:322
  184.3 8.5 %collective-permute-start.52 = (bf16[596,128]{1,0:T(8,128)(2,1)S(1)}, bf16[596,128]{1,0:T(8,128)(2,1)S(1)}, u32[]{:S(2)}, u32[]{:S(2)}) collective-permute-start(bf16[596,128]{1,0:T(8,128)(2,1)S(1)} %get-tuple-element.357), channel_id=1, source_target_pairs={{0,24},{1,25},{2,26},{3,27},{4,28},{5,29},{6,30},{7,31},{8,16},{9,... | collective-permute-start | bytes 457736 | tf_op jit(solution)/shard_map/ppermute | solution.py:322
  186.5 13.2 %collective-permute-start.62 = (bf16[128,2048]{1,0:T(8,128)(2,1)S(1)}, bf16[128,2048]{1,0:T(8,128)(2,1)S(1)}, u32[]{:S(2)}, u32[]{:S(2)}) collective-permute-start(bf16[128,2048]{1,0:T(8,128)(2,1)S(1)} %get-tuple-element.402), channel_id=1, source_target_pairs={{0,4},{1,5},{2,6},{3,7},{4,0},{5,1},{6,2},{7,3},{8,12},{9,13},{10,... | collective-permute-start | bytes 1572872 | tf_op jit(solution)/shard_map/ppermute | solution.py:322
  194.4 10.4 %collective-permute-start.56 = (bf16[2,56,1024]{2,1,0:T(8,128)(2,1)S(1)}, bf16[2,56,1024]{2,1,0:T(8,128)(2,1)S(1)}, u32[]{:S(2)}, u32[]{:S(2)}) collective-permute-start(bf16[2,56,1024]{2,1,0:T(8,128)(2,1)S(1)} %get-tuple-element.383), channel_id=1, source_target_pairs={{0,8},{1,9},{2,10},{3,11},{4,12},{5,13},{6,14},{7,15},{8,0},{9,1},... | collective-permute-start | bytes 688136 | tf_op jit(solution)/shard_map/ppermute | solution.py:322
  195.3 12.6 %collective-permute-start.57 = (bf16[2,56,1024]{2,1,0:T(8,128)(2,1)S(1)}, bf16[2,56,1024]{2,1,0:T(8,128)(2,1)S(1)}, u32[]{:S(2)}, u32[]{:S(2)}) collective-permute-start(bf16[2,56,1024]{2,1,0:T(8,128)(2,1)S(1)} %get-tuple-element.384), channel_id=1, source_target_pairs={{0,16},{1,17},{2,18},{3,19},{4,20},{5,21},{6,22},{7,23},{8,24},{9,... | collective-permute-start | bytes 688136 | tf_op jit(solution)/shard_map/ppermute | solution.py:322
  196.6 11.4 %collective-permute-start.58 = (bf16[2,56,1024]{2,1,0:T(8,128)(2,1)S(1)}, bf16[2,56,1024]{2,1,0:T(8,128)(2,1)S(1)}, u32[]{:S(2)}, u32[]{:S(2)}) collective-permute-start(bf16[2,56,1024]{2,1,0:T(8,128)(2,1)S(1)} %get-tuple-element.385), channel_id=1, source_target_pairs={{0,24},{1,25},{2,26},{3,27},{4,28},{5,29},{6,30},{7,31},{8,16},{9,... | collective-permute-start | bytes 688136 | tf_op jit(solution)/shard_map/ppermute | solution.py:322
  199.1 11.3 %collective-permute-start.55 = (bf16[112,1024]{1,0:T(8,128)(2,1)S(1)}, bf16[112,1024]{1,0:T(8,128)(2,1)S(1)}, u32[]{:S(2)}, u32[]{:S(2)}) collective-permute-start(bf16[112,1024]{1,0:T(8,128)(2,1)S(1)} %get-tuple-element.372), channel_id=1, source_target_pairs={{0,1},{1,0},{2,3},{3,2},{4,5},{5,4},{6,7},{7,6},{8,9},{9,8},{10,11... | collective-permute-start | bytes 688136 | tf_op jit(solution)/shard_map/ppermute | solution.py:322
  200.3 29.6 %collective-permute-start.63 = (bf16[128,2048]{1,0:T(8,128)(2,1)S(1)}, bf16[128,2048]{1,0:T(8,128)(2,1)S(1)}, u32[]{:S(2)}, u32[]{:S(2)}) collective-permute-start(bf16[128,2048]{1,0:T(8,128)(2,1)S(1)} %shard_map.232), channel_id=1, source_target_pairs={{0,2},{1,3},{2,0},{3,1},{4,6},{5,7},{6,4},{7,5},{8,10},{9,11},{10,... | collective-permute-start | bytes 1572872 | tf_op jit(solution)/shard_map/ppermute | solution.py:322
  210.4 20.9 %collective-permute-start.60 = (bf16[2,256,512]{2,1,0:T(8,128)(2,1)S(1)}, bf16[2,256,512]{2,1,0:T(8,128)(2,1)S(1)}, u32[]{:S(2)}, u32[]{:S(2)}) collective-permute-start(bf16[2,256,512]{2,1,0:T(8,128)(2,1)S(1)} %get-tuple-element.395), channel_id=1, source_target_pairs={{0,8},{1,9},{2,10},{3,11},{4,12},{5,13},{6,14},{7,15},{8,0},{9,1},... | collective-permute-start | bytes 1572872 | tf_op jit(solution)/shard_map/ppermute | solution.py:322
  211.2 20.1 %collective-permute-start.61 = (bf16[2,256,512]{2,1,0:T(8,128)(2,1)S(1)}, bf16[2,256,512]{2,1,0:T(8,128)(2,1)S(1)}, u32[]{:S(2)}, u32[]{:S(2)}) collective-permute-start(bf16[2,256,512]{2,1,0:T(8,128)(2,1)S(1)} %get-tuple-element.396), channel_id=1, source_target_pairs={{0,16},{1,17},{2,18},{3,19},{4,20},{5,21},{6,22},{7,23},{8,24},{9,... | collective-permute-start | bytes 1572872 | tf_op jit(solution)/shard_map/ppermute | solution.py:322
  213.4 17.9 %collective-permute-start.59 = (bf16[64,1024]{1,0:T(8,128)(2,1)S(1)}, bf16[64,1024]{1,0:T(8,128)(2,1)S(1)}, u32[]{:S(2)}, u32[]{:S(2)}) collective-permute-start(bf16[64,1024]{1,0:T(8,128)(2,1)S(1)} %get-tuple-element.394), channel_id=1, source_target_pairs={{0,2},{1,3},{2,0},{3,1},{4,6},{5,7},{6,4},{7,5},{8,10},{9,11},{10,... | collective-permute-start | bytes 393224 | tf_op jit(solution)/shard_map/ppermute | solution.py:322
  231.9 6.7 %collective-permute-start.68 = (bf16[256,512]{1,0:T(8,128)(2,1)S(1)}, bf16[256,512]{1,0:T(8,128)(2,1)S(1)}, u32[]{:S(2)}, u32[]{:S(2)}) collective-permute-start(bf16[256,512]{1,0:T(8,128)(2,1)S(1)} %get-tuple-element.416), channel_id=1, source_target_pairs={{0,16},{1,17},{2,18},{3,19},{4,20},{5,21},{6,22},{7,23},{8,24},{9,... | collective-permute-start | bytes 786440 | tf_op jit(solution)/shard_map/ppermute | solution.py:322
  233.5 6.4 %collective-permute-start.69 = (bf16[256,512]{1,0:T(8,128)(2,1)S(1)}, bf16[256,512]{1,0:T(8,128)(2,1)S(1)}, u32[]{:S(2)}, u32[]{:S(2)}) collective-permute-start(bf16[256,512]{1,0:T(8,128)(2,1)S(1)} %get-tuple-element.421), channel_id=1, source_target_pairs={{0,8},{1,9},{2,10},{3,11},{4,12},{5,13},{6,14},{7,15},{8,0},{9,1},... | collective-permute-start | bytes 786440 | tf_op jit(solution)/shard_map/ppermute | solution.py:322
  235.6 6.8 %collective-permute-start.64 = (bf16[4,56,1024]{2,1,0:T(8,128)(2,1)S(1)}, bf16[4,56,1024]{2,1,0:T(8,128)(2,1)S(1)}, u32[]{:S(2)}, u32[]{:S(2)}) collective-permute-start(bf16[4,56,1024]{2,1,0:T(8,128)(2,1)S(1)} %get-tuple-element.405), channel_id=1, source_target_pairs={{0,4},{1,5},{2,6},{3,7},{4,0},{5,1},{6,2},{7,3},{8,12},{9,13},{10,... | collective-permute-start | bytes 1376264 | tf_op jit(solution)/shard_map/ppermute | solution.py:322
  240.6 6.0 %collective-permute-start.70 = (bf16[128,1024]{1,0:T(8,128)(2,1)S(1)}, bf16[128,1024]{1,0:T(8,128)(2,1)S(1)}, u32[]{:S(2)}, u32[]{:S(2)}) collective-permute-start(bf16[128,1024]{1,0:T(8,128)(2,1)S(1)} %get-tuple-element.423), channel_id=1, source_target_pairs={{0,4},{1,5},{2,6},{3,7},{4,0},{5,1},{6,2},{7,3},{8,12},{9,13},{10,... | collective-permute-start | bytes 786440 | tf_op jit(solution)/shard_map/ppermute | solution.py:322
  243.0 8.5 %collective-permute-start.65 = (bf16[2,56,1024]{2,1,0:T(8,128)(2,1)S(1)}, bf16[2,56,1024]{2,1,0:T(8,128)(2,1)S(1)}, u32[]{:S(2)}, u32[]{:S(2)}) collective-permute-start(bf16[2,56,1024]{2,1,0:T(8,128)(2,1)S(1)} %get-tuple-element.406), channel_id=1, source_target_pairs={{0,8},{1,9},{2,10},{3,11},{4,12},{5,13},{6,14},{7,15},{8,0},{9,1},... | collective-permute-start | bytes 688136 | tf_op jit(solution)/shard_map/ppermute | solution.py:322
  244.3 12.6 %collective-permute-start.66 = (bf16[2,56,1024]{2,1,0:T(8,128)(2,1)S(1)}, bf16[2,56,1024]{2,1,0:T(8,128)(2,1)S(1)}, u32[]{:S(2)}, u32[]{:S(2)}) collective-permute-start(bf16[2,56,1024]{2,1,0:T(8,128)(2,1)S(1)} %get-tuple-element.407), channel_id=1, source_target_pairs={{0,16},{1,17},{2,18},{3,19},{4,20},{5,21},{6,22},{7,23},{8,24},{9,... | collective-permute-start | bytes 688136 | tf_op jit(solution)/shard_map/ppermute | solution.py:322
  245.1 11.8 %collective-permute-start.67 = (bf16[2,56,1024]{2,1,0:T(8,128)(2,1)S(1)}, bf16[2,56,1024]{2,1,0:T(8,128)(2,1)S(1)}, u32[]{:S(2)}, u32[]{:S(2)}) collective-permute-start(bf16[2,56,1024]{2,1,0:T(8,128)(2,1)S(1)} %get-tuple-element.408), channel_id=1, source_target_pairs={{0,24},{1,25},{2,26},{3,27},{4,28},{5,29},{6,30},{7,31},{8,16},{9,... | collective-permute-start | bytes 688136 | tf_op jit(solution)/shard_map/ppermute | solution.py:322
  247.2 14.2 %collective-permute-start.71 = (bf16[128,1024]{1,0:T(8,128)(2,1)S(1)}, bf16[128,1024]{1,0:T(8,128)(2,1)S(1)}, u32[]{:S(2)}, u32[]{:S(2)}) collective-permute-start(bf16[128,1024]{1,0:T(8,128)(2,1)S(1)} %shard_map.239), channel_id=1, source_target_pairs={{0,2},{1,3},{2,0},{3,1},{4,6},{5,7},{6,4},{7,5},{8,10},{9,11},{10,... | collective-permute-start | bytes 786440 | tf_op jit(solution)/shard_map/ppermute | solution.py:322
  (18 other events, 47.4 us)

commit v6 on v5

--- a/solution.py
+++ b/solution.py
@@ -334,8 +334,8 @@
     "attention": 7.6,
     "proj": 1.1,
     "norm_two": 0.9,
-    "grad_hidden": 1.6,
-    "fc": 5.6,
+    "mlp_start": 1.0,
+    "fc": 5.0,
     "grads_fc1": 1.8,
     "grads_fc2": 1.8,
     "fc2": 1.6,
@@ -721,33 +721,42 @@
     normed[...] = (scaled * vec[1:2, :] + vec[3:4, :]).astype(BF16)
 
 
-def grad_hidden_kernel(ids, own, got, w0, w1, w2, w3, whole, out, wide):
+def mlp_start_kernel(
+    ids, own, got, own_grad, got_grad, b_fc1, f0, f1, f2, g0, g1, g2, whole, whole_grad, pre, back, wide
+):
     join_rows(wide, own, got)
     whole[...] = wide[...].astype(BF16)
-    for c in range(4):
-        total = dot(whole[:, lanes(0)], w0[:, lanes(c)], NN)
-        for m, weight in enumerate((w1, w2, w3)):
-            total = total + dot(whole[:, lanes(m + 1)], weight[:, lanes(c)], NN)
-        out[:, lanes(c)] = total
+    join_rows(wide, own_grad, got_grad)
+    whole_grad[...] = wide[...].astype(BF16)
+
+    def body(c, carry):
+        cols = pl.ds(pl.multiple_of(c * 256, 256), 256)
+        total = b_fc1[:, cols] + dot(whole[:, lanes(0)], f0[:, cols], NN)
+        grad = dot(whole_grad[:, lanes(0)], g0[:, cols], NN)
+        for m, (f, g) in ((1, (f1, g1)), (2, (f2, g2))):
+            total = total + dot(whole[:, lanes(m)], f[:, cols], NN)
+            grad = grad + dot(whole_grad[:, lanes(m)], g[:, cols], NN)
+        pre[:, cols] = total
+        back[:, cols] = grad
+        return carry
+
+    lax.fori_loop(0, 4, body, 0)
 
 
 def fc_kernel(
-    ids, own, got, grad_hidden, b_fc1, w0, w1, w2, w3, whole, hidden, grad_pre, sums, keep, send, wide
+    ids, whole, whole_grad, start, back, w0, w1, w2, w3, g3, hidden, grad_pre, sums, keep, send, wide
 ):
     weights = (w0, w1, w2, w3)
-    join_rows(wide, own, got)
-    whole[...] = wide[...].astype(BF16)
     wide[...] = jnp.zeros_like(wide)
 
     def body(c, carry):
         cols = pl.ds(pl.multiple_of(c * 256, 256), 256)
-        pre = b_fc1[:, cols] + dot(whole[:, lanes(0)], w0[:, cols], NN)
-        for m in range(1, 4):
-            pre = pre + dot(whole[:, lanes(m)], weights[m][:, cols], NN)
+        pre = start[:, cols] + dot(whole[:, lanes(3)], w3[:, cols], NN)
+        grad_hidden = back[:, cols] + dot(whole_grad[:, lanes(3)], g3[:, cols], NN)
         half_erf = 0.5 * (1.0 + lax.erf(pre * root_half))
         hidden[:, cols] = (pre * half_erf).astype(BF16)
         slope = half_erf + pre * jnp.exp(-0.5 * pre * pre) * inv_root_tau
-        grad = (grad_hidden[:, cols] * slope).astype(BF16)
+        grad = (grad_hidden * slope).astype(BF16)
         grad_pre[:, cols] = grad
         sums[:, cols] = jnp.sum(grad.astype(F32), axis=0, keepdims=True)
         for m in range(4):
@@ -1131,7 +1140,7 @@
         fc2_weight,
     )
     far_a = swap(shard_a, Z_HIGH)
-    own_rows, _ = tie(clip_rows, shard_a)
+    own_rows = clip_rows
     keep, send = call(
         pack_kernel,
         [((4, 2 * PAD, 1024), BF16)] * 2,
@@ -1243,26 +1252,31 @@
         away,
         vec,
     )
-    whole_mlp, grad_hidden = call(
-        grad_hidden_kernel,
-        [((count, 1024), BF16), ((count, 1024), F32)],
-        ids,
+    whole_two, whole_mlp, start, grad_hidden = call(
+        mlp_start_kernel,
+        [((count, 1024), BF16)] * 2 + [((count, 1024), F32)] * 2,
+        ids,
+        normed_two,
+        swap(normed_two, CORE),
         grads,
         swap(grads, CORE),
-        *w_fc2,
+        b_fc1,
+        *w_fc1[:3],
+        *w_fc2[:3],
         scratch=[wide],
     )
 
-    whole_two, hidden, grad_pre, sums_fc1, keep, send = call(
+    hidden, grad_pre, sums_fc1, keep, send = call(
         fc_kernel,
-        [((count, 1024), BF16)] * 3
+        [((count, 1024), BF16)] * 2
         + [((1, 1024), F32), ((half, 1024), F32), ((half, 1024), BF16)],
         ids,
-        normed_two,
-        swap(normed_two, CORE),
+        whole_two,
+        whole_mlp,
+        start,
         grad_hidden,
-        b_fc1,
         *w_fc1,
+        w_fc2[3],
         scratch=[wide],
     )
     part, send = pair(keep, send)

time: 263 us -> 261 us (level)
  waiting for transfers between devices: 129 us -> 126 us
  transfers between devices with their start and end apart: 72 -> 72, of which waited for: 38 -> 40; matrix products, arithmetic and copies ran while one was open for 0% -> 0% of each run, Pallas kernels for 20% -> 21%
where the time goes in v6:
time: 261 us; the launch traced here: 260 us
  waiting for transfers between devices  126 us (48%)
  starting transfers between devices  64.4 us (25%)
  Pallas kernels  64.1 us (25%)
    ppermute x72, waiting for transfers between devices, swap(): return lax.ppermute(value, AXES, [(i, i ^ mask) for i in range(32)])  126 us
    ppermute x72, starting transfers between devices, swap(): return lax.ppermute(value, AXES, [(i, i ^ mask) for i in range(32)])  64.4 us
    pallas_call x48, Pallas kernels, call(): pl.pallas_call(body, out_shape=[jax.ShapeDtypeStruct(s, t) for s, t in ou...  64.1 us
  transfers between devices with their start and end apart: 72, of which 40 were waited for; matrix products, arithmetic and copies ran while one was open for 0% of the time, Pallas kernels for 21%

profile of v6, /device:TPU:0, one launch (start us, length us, event | category | flops | bytes accessed | tf_op | source)
XLA Modules:
  0.0 260.4 jit_solution(5395344143310071582)
XLA Ops:
  7.5 3.7 %collective-permute-start.4 = (bf16[128,1024]{1,0:T(8,128)(2,1)S(1)}, bf16[128,1024]{1,0:T(8,128)(2,1)S(1)}, u32[]{:S(2)}, u32[]{:S(2)}) collective-permute-start(bf16[128,1024]{1,0:T(8,128)(2,1)S(1)} %get-tuple-element.227.own), channel_id=1, source_target_pairs={{0,2},{1,3},{2,0},{3,1},{4,6},{5,7},{6,4},{7,5},{8,10},{9,11},{10,... | collective-permute-start | bytes 786440 | tf_op jit(solution)/shard_map/ppermute | solution.py:322
  11.8 1.6 collective-permute-start.1
  13.4 1.5 collective-permute-start.2
  15.4 8.4 %collective-permute-done.4.far = bf16[128,1024]{1,0:T(8,128)(2,1)S(1)} collective-permute-done((bf16[128,1024]{1,0:T(8,128)(2,1)S(1)}, bf16[128,1024]{1,0:T(8,128)(2,1)S(1)}, u32[]{:S(2)}, u32[]{:S(2)}) %collective-permute-start.4) | collective-permute-done | bytes 262176 | tf_op jit(solution)/shard_map/ppermute | solution.py:322
  26.5 9.0 %collective-permute-done.2.d2 = bf16[2,112,1024]{2,1,0:T(8,128)(2,1)S(1)} collective-permute-done((bf16[2,112,1024]{2,1,0:T(8,128)(2,1)S(1)}, bf16[2,112,1024]{2,1,0:T(8,128)(2,1)S(1)}, u32[]{:S(2)}, u32[]{:S(2)}) %collective-permute-start.2) | collective-permute-done | bytes 458784 | tf_op jit(solution)/shard_map/ppermute | solution.py:322
  35.6 1.5 collective-permute-start.12
  37.6 1.6 shard_map.199
  39.2 1.6 collective-permute-start.6
  40.8 1.5 collective-permute-start.8
  42.7 3.7 %collective-permute-done.6.r1 = bf16[64,1024]{1,0:T(8,128)(2,1)S(1)} collective-permute-done((bf16[64,1024]{1,0:T(8,128)(2,1)S(1)}, bf16[64,1024]{1,0:T(8,128)(2,1)S(1)}, u32[]{:S(2)}, u32[]{:S(2)}) %collective-permute-start.6) | collective-permute-done | bytes 131104 | tf_op jit(solution)/shard_map/ppermute | solution.py:322
  46.4 2.7 %collective-permute-done.8.r3 = bf16[64,1024]{1,0:T(8,128)(2,1)S(1)} collective-permute-done((bf16[64,1024]{1,0:T(8,128)(2,1)S(1)}, bf16[64,1024]{1,0:T(8,128)(2,1)S(1)}, u32[]{:S(2)}, u32[]{:S(2)}) %collective-permute-start.8) | collective-permute-done | bytes 131104 | tf_op jit(solution)/shard_map/ppermute | solution.py:322
  49.1 4.2 %collective-permute-done.7.r2 = bf16[64,1024]{1,0:T(8,128)(2,1)S(1)} collective-permute-done((bf16[64,1024]{1,0:T(8,128)(2,1)S(1)}, bf16[64,1024]{1,0:T(8,128)(2,1)S(1)}, u32[]{:S(2)}, u32[]{:S(2)}) %collective-permute-start.7) | collective-permute-done | bytes 131104 | tf_op jit(solution)/shard_map/ppermute | solution.py:322
  54.4 1.5 collective-permute-start.13
  57.3 5.9 %collective-permute-done.13.w3 = bf16[256,512]{1,0:T(8,128)(2,1)S(1)} collective-permute-done((bf16[256,512]{1,0:T(8,128)(2,1)S(1)}, bf16[256,512]{1,0:T(8,128)(2,1)S(1)}, u32[]{:S(2)}, u32[]{:S(2)}) %collective-permute-start.13) | collective-permute-done | bytes 262176 | tf_op jit(solution)/shard_map/ppermute | solution.py:322
  64.4 1.5 shard_map.201
  66.6 1.5 collective-permute-start.17
  70.2 2.7 %collective-permute-done.16.a1 = bf16[596,128]{1,0:T(8,128)(2,1)S(1)} collective-permute-done((bf16[596,128]{1,0:T(8,128)(2,1)S(1)}, bf16[596,128]{1,0:T(8,128)(2,1)S(1)}, u32[]{:S(2)}, u32[]{:S(2)}) %collective-permute-start.16) | collective-permute-done | bytes 152608 | tf_op jit(solution)/shard_map/ppermute | solution.py:322
  72.9 2.2 collective-permute-done.17.a2
  77.2 2.6 %collective-permute-start.25 = (bf16[56,1024]{1,0:T(8,128)(2,1)S(1)}, bf16[56,1024]{1,0:T(8,128)(2,1)S(1)}, u32[]{:S(2)}, u32[]{:S(2)}) collective-permute-start(bf16[56,1024]{1,0:T(8,128)(2,1)S(1)} %get-tuple-element.271.here), channel_id=1, source_target_pairs={{0,1},{1,0},{2,3},{3,2},{4,5},{5,4},{6,7},{7,6},{8,9},{9,8},{10,11... | collective-permute-start | bytes 344072 | tf_op jit(solution)/shard_map/ppermute | solution.py:322
  79.8 5.1 %shard_map.204 = (bf16[196,128]{1,0:T(8,128)(2,1)S(1)}, bf16[196,128]{1,0:T(8,128)(2,1)S(1)}, bf16[196,128]{1,0:T(8,128)(2,1)S(1)}, bf16[196,128]{1,0:T(8,128)(2,1)S(1)}, f32[1568,128]{1,0:T(8,128)S(1)}) custom-call(s32[5]{0:T(128)S(1)} %stack.19.ids, bf16[596,128]{1,0:T(8,128)(2,1)S(1)} %get-tuple-element.258.a0, ...), custom_call_target="tpu_custom_call" | custom-call | flops 8739999744 | bytes 1613824 | tf_op jit(solution)/shard_map/pallas_call | solution.py:364
  86.2 1.7 collective-permute-done.26.r2
  90.0 2.6 collective-permute-done.21.a2
  97.7 1.5 collective-permute-start.33
  100.0 2.0 collective-permute-start.29
  104.0 8.6 %collective-permute-done.33.g1.w1 = bf16[256,1024]{1,0:T(8,128)(2,1)S(1)} collective-permute-done((bf16[256,1024]{1,0:T(8,128)(2,1)S(1)}, bf16[256,1024]{1,0:T(8,128)(2,1)S(1)}, u32[]{:S(2)}, u32[]{:S(2)}) %collective-permute-start.33) | collective-permute-done | bytes 524320 | tf_op jit(solution)/shard_map/ppermute | solution.py:322
  117.7 3.0 %shard_map.211 = (bf16[392,1024]{1,0:T(8,128)(2,1)S(1)}, bf16[392,1024]{1,0:T(8,128)(2,1)S(1)}, f32[392,1024]{1,0:T(8,128)S(1)}, f32[392,1024]{1,0:T(8,128)S(1)}) custom-call(s32[5]{0:T(128)S(1)} %stack.19.ids, bf16[196,1024]{1,0:T(8,128)(2,1)S(1)} %get-tuple-element.285.own, bf16[196,1024]{1,0:T(8,128)(2,1)S(1)} %collective-permute-done.30.got, ...), custom_call_target="tpu_custom_call" | custom-call | flops 1150000000 | bytes 9572352 | tf_op jit(solution)/shard_map/pallas_call | solution.py:364
  120.6 2.6 %collective-permute-done.35.w3 = bf16[256,1024]{1,0:T(8,128)(2,1)S(1)} collective-permute-done((bf16[256,1024]{1,0:T(8,128)(2,1)S(1)}, bf16[256,1024]{1,0:T(8,128)(2,1)S(1)}, u32[]{:S(2)}, u32[]{:S(2)}) %collective-permute-start.35) | collective-permute-done | bytes 524320 | tf_op jit(solution)/shard_map/ppermute | solution.py:322
  123.3 3.4 %collective-permute-done.36.g3.w3 = bf16[256,1024]{1,0:T(8,128)(2,1)S(1)} collective-permute-done((bf16[256,1024]{1,0:T(8,128)(2,1)S(1)}, bf16[256,1024]{1,0:T(8,128)(2,1)S(1)}, u32[]{:S(2)}, u32[]{:S(2)}) %collective-permute-start.36) | collective-permute-done | bytes 524320 | tf_op jit(solution)/shard_map/ppermute | solution.py:322
  126.6 3.6 %shard_map.212 = (bf16[392,1024]{1,0:T(8,128)(2,1)S(1)}, bf16[392,1024]{1,0:T(8,128)(2,1)S(1)}, f32[1,1024]{1,0:T(1,128)S(1)}, f32[196,1024]{1,0:T(8,128)S(1)}, bf16[196,1024]{1,0:T(8,128)(2,1)S(1)}) custom-call(s32[5]{0:T(128)S(1)} %stack.19.ids, bf16[392,1024]{1,0:T(8,128)(2,1)S(1)} %get-tuple-element.320.whole.left, ...), custom_call_target="tpu_custom_call" | custom-call | flops 5750000128 | bytes 10252288 | tf_op jit(solution)/shard_map/pallas_call | solution.py:364
  130.3 1.7 collective-permute-done.37.got
  133.1 1.8 shard_map.220
  135.5 1.8 shard_map.218
  137.4 1.5 collective-permute-start.45
  138.9 1.6 shard_map.214
  140.5 3.8 %collective-permute-done.38.got = bf16[196,1024]{1,0:T(8,128)(2,1)S(1)} collective-permute-done((bf16[196,1024]{1,0:T(8,128)(2,1)S(1)}, bf16[196,1024]{1,0:T(8,128)(2,1)S(1)}, u32[]{:S(2)}, u32[]{:S(2)}) %collective-permute-start.38) | collective-permute-done | bytes 401440 | tf_op jit(solution)/shard_map/ppermute | solution.py:322
  144.2 1.5 shard_map.215
  148.7 5.6 %collective-permute-done.41.got = bf16[98,1024]{1,0:T(8,128)(2,1)S(1)} collective-permute-done((bf16[98,1024]{1,0:T(8,128)(2,1)S(1)}, bf16[98,1024]{1,0:T(8,128)(2,1)S(1)}, u32[]{:S(2)}, u32[]{:S(2)}) %collective-permute-start.41) | collective-permute-done | bytes 200736 | tf_op jit(solution)/shard_map/ppermute | solution.py:322
  156.3 1.5 collective-permute-start.44
  158.5 1.9 collective-permute-done.46.got
  161.2 2.0 collective-permute-done.45.got
  165.2 2.0 collective-permute-start.47
  169.2 8.6 %shard_map.223 = (bf16[596,128]{1,0:T(8,128)(2,1)S(1)}, bf16[596,128]{1,0:T(8,128)(2,1)S(1)}, bf16[596,128]{1,0:T(8,128)(2,1)S(1)}, bf16[596,128]{1,0:T(8,128)(2,1)S(1)}) custom-call(s32[5]{0:T(128)S(1)} %stack.19.ids, bf16[596,128]{1,0:T(8,128)(2,1)S(1)} %get-tuple-element.258.a0, bf16[596,128]{1,0:T(8,128)(2,1)S(1)} %collective-permute-done.16.a1, ...), custom_call_target="tpu_custom_call" | custom-call | flops 13799999488 | bytes 2224128 | tf_op jit(solution)/shard_map/pallas_call | solution.py:364
  180.2 1.5 collective-permute-start.50
  185.2 1.9 collective-permute-done.50.g1
  187.1 4.0 %collective-permute-done.51.g2 = bf16[596,128]{1,0:T(8,128)(2,1)S(1)} collective-permute-done((bf16[596,128]{1,0:T(8,128)(2,1)S(1)}, bf16[596,128]{1,0:T(8,128)(2,1)S(1)}, u32[]{:S(2)}, u32[]{:S(2)}) %collective-permute-start.51) | collective-permute-done | bytes 152608 | tf_op jit(solution)/shard_map/ppermute | solution.py:322
  191.1 1.6 shard_map.226
  193.4 1.5 collective-permute-start.57
  198.4 2.3 collective-permute-start.63
  200.7 1.8 shard_map.228
  202.6 3.3 %collective-permute-done.57.d2 = bf16[2,56,1024]{2,1,0:T(8,128)(2,1)S(1)} collective-permute-done((bf16[2,56,1024]{2,1,0:T(8,128)(2,1)S(1)}, bf16[2,56,1024]{2,1,0:T(8,128)(2,1)S(1)}, u32[]{:S(2)}, u32[]{:S(2)}) %collective-permute-start.57) | collective-permute-done | bytes 229408 | tf_op jit(solution)/shard_map/ppermute | solution.py:322
  206.0 2.3 collective-permute-done.55.got
  208.9 1.5 collective-permute-start.61
  211.4 16.6 %collective-permute-done.63.moved = bf16[128,2048]{1,0:T(8,128)(2,1)S(1)} collective-permute-done((bf16[128,2048]{1,0:T(8,128)(2,1)S(1)}, bf16[128,2048]{1,0:T(8,128)(2,1)S(1)}, u32[]{:S(2)}, u32[]{:S(2)}) %collective-permute-start.63) | collective-permute-done | bytes 524320 | tf_op jit(solution)/shard_map/ppermute | solution.py:322
  231.4 1.6 collective-permute-start.69
  233.9 2.9 %collective-permute-done.68.got_x = bf16[256,512]{1,0:T(8,128)(2,1)S(1)} collective-permute-done((bf16[256,512]{1,0:T(8,128)(2,1)S(1)}, bf16[256,512]{1,0:T(8,128)(2,1)S(1)}, u32[]{:S(2)}, u32[]{:S(2)}) %collective-permute-start.68) | collective-permute-done | bytes 262176 | tf_op jit(solution)/shard_map/ppermute | solution.py:322
  238.6 1.8 shard_map.229
  240.9 1.6 collective-permute-start.65
  243.0 1.5 collective-permute-start.67
  245.1 1.8 shard_map.241
  246.9 2.5 collective-permute-done.65.d1
  249.4 5.8 %collective-permute-done.66.d2 = bf16[2,56,1024]{2,1,0:T(8,128)(2,1)S(1)} collective-permute-done((bf16[2,56,1024]{2,1,0:T(8,128)(2,1)S(1)}, bf16[2,56,1024]{2,1,0:T(8,128)(2,1)S(1)}, u32[]{:S(2)}, u32[]{:S(2)}) %collective-permute-start.66) | collective-permute-done | bytes 229408 | tf_op jit(solution)/shard_map/ppermute | solution.py:322
  255.1 2.0 shard_map.235
  257.1 1.8 collective-permute-done.71.moved
  258.9 1.4 shard_map.240
  (145 shorter events, 67.1 us)
Async XLA Ops:
  6.3 4.9 %collective-permute-start = (bf16[4,112,1024]{2,1,0:T(8,128)(2,1)S(1)}, bf16[4,112,1024]{2,1,0:T(8,128)(2,1)S(1)}, u32[]{:S(2)}, u32[]{:S(2)}) collective-permute-start(bf16[4,112,1024]{2,1,0:T(8,128)(2,1)S(1)} %get-tuple-element.223), channel_id=1, source_target_pairs={{0,4},{1,5},{2,6},{3,7},{4,0},{5,1},{6,2},{7,3},{8,12},{9,13},{10,... | collective-permute-start | bytes 2752520 | tf_op jit(solution)/shard_map/ppermute | solution.py:322
  7.5 16.2 %collective-permute-start.4 = (bf16[128,1024]{1,0:T(8,128)(2,1)S(1)}, bf16[128,1024]{1,0:T(8,128)(2,1)S(1)}, u32[]{:S(2)}, u32[]{:S(2)}) collective-permute-start(bf16[128,1024]{1,0:T(8,128)(2,1)S(1)} %get-tuple-element.227.own), channel_id=1, source_target_pairs={{0,2},{1,3},{2,0},{3,1},{4,6},{5,7},{6,4},{7,5},{8,10},{9,11},{10,... | collective-permute-start | bytes 786440 | tf_op jit(solution)/shard_map/ppermute | solution.py:322
  11.8 14.7 %collective-permute-start.1 = (bf16[2,112,1024]{2,1,0:T(8,128)(2,1)S(1)}, bf16[2,112,1024]{2,1,0:T(8,128)(2,1)S(1)}, u32[]{:S(2)}, u32[]{:S(2)}) collective-permute-start(bf16[2,112,1024]{2,1,0:T(8,128)(2,1)S(1)} %get-tuple-element.224), channel_id=1, source_target_pairs={{0,8},{1,9},{2,10},{3,11},{4,12},{5,13},{6,14},{7,15},{8,0},{9,1},... | collective-permute-start | bytes 1376264 | tf_op jit(solution)/shard_map/ppermute | solution.py:322
  13.4 22.2 %collective-permute-start.2 = (bf16[2,112,1024]{2,1,0:T(8,128)(2,1)S(1)}, bf16[2,112,1024]{2,1,0:T(8,128)(2,1)S(1)}, u32[]{:S(2)}, u32[]{:S(2)}) collective-permute-start(bf16[2,112,1024]{2,1,0:T(8,128)(2,1)S(1)} %get-tuple-element.225), channel_id=1, source_target_pairs={{0,16},{1,17},{2,18},{3,19},{4,20},{5,21},{6,22},{7,23},{8,24},{9,... | collective-permute-start | bytes 1376264 | tf_op jit(solution)/shard_map/ppermute | solution.py:322
  14.9 20.7 %collective-permute-start.3 = (bf16[2,112,1024]{2,1,0:T(8,128)(2,1)S(1)}, bf16[2,112,1024]{2,1,0:T(8,128)(2,1)S(1)}, u32[]{:S(2)}, u32[]{:S(2)}) collective-permute-start(bf16[2,112,1024]{2,1,0:T(8,128)(2,1)S(1)} %get-tuple-element.226), channel_id=1, source_target_pairs={{0,24},{1,25},{2,26},{3,27},{4,28},{5,29},{6,30},{7,31},{8,16},{9,... | collective-permute-start | bytes 1376264 | tf_op jit(solution)/shard_map/ppermute | solution.py:322
  24.4 17.9 %collective-permute-start.9 = (bf16[128,1024]{1,0:T(8,128)(2,1)S(1)}, bf16[128,1024]{1,0:T(8,128)(2,1)S(1)}, u32[]{:S(2)}, u32[]{:S(2)}) collective-permute-start(bf16[128,1024]{1,0:T(8,128)(2,1)S(1)} %copy-done.3), channel_id=1, source_target_pairs={{0,2},{1,3},{2,0},{3,1},{4,6},{5,7},{6,4},{7,5},{8,10},{9,11},{10,... | collective-permute-start | bytes 786440 | tf_op jit(solution)/shard_map/ppermute | solution.py:322
  35.6 18.8 %collective-permute-start.12 = (bf16[256,1024]{1,0:T(8,128)(2,1)S(1)}, bf16[256,1024]{1,0:T(8,128)(2,1)S(1)}, u32[]{:S(2)}, u32[]{:S(2)}) collective-permute-start(bf16[256,1024]{1,0:T(8,128)(2,1)S(1)} %shard_map.198.w0), channel_id=1, source_target_pairs={{0,16},{1,17},{2,18},{3,19},{4,20},{5,21},{6,22},{7,23},{8,24},{9,... | collective-permute-start | bytes 1572872 | tf_op jit(solution)/shard_map/ppermute | solution.py:322
  37.1 18.8 %collective-permute-start.11 = (bf16[256,1024]{1,0:T(8,128)(2,1)S(1)}, bf16[256,1024]{1,0:T(8,128)(2,1)S(1)}, u32[]{:S(2)}, u32[]{:S(2)}) collective-permute-start(bf16[256,1024]{1,0:T(8,128)(2,1)S(1)} %shard_map.198.w0), channel_id=1, source_target_pairs={{0,8},{1,9},{2,10},{3,11},{4,12},{5,13},{6,14},{7,15},{8,0},{9,1},... | collective-permute-start | bytes 1572872 | tf_op jit(solution)/shard_map/ppermute | solution.py:322
  39.2 7.2 %collective-permute-start.6 = (bf16[64,1024]{1,0:T(8,128)(2,1)S(1)}, bf16[64,1024]{1,0:T(8,128)(2,1)S(1)}, u32[]{:S(2)}, u32[]{:S(2)}) collective-permute-start(bf16[64,1024]{1,0:T(8,128)(2,1)S(1)} %get-tuple-element.234.here), channel_id=1, source_target_pairs={{0,1},{1,0},{2,3},{3,2},{4,5},{5,4},{6,7},{7,6},{8,9},{9,8},{10,11... | collective-permute-start | bytes 393224 | tf_op jit(solution)/shard_map/ppermute | solution.py:322
  40.8 8.3 %collective-permute-start.8 = (bf16[64,1024]{1,0:T(8,128)(2,1)S(1)}, bf16[64,1024]{1,0:T(8,128)(2,1)S(1)}, u32[]{:S(2)}, u32[]{:S(2)}) collective-permute-start(bf16[64,1024]{1,0:T(8,128)(2,1)S(1)} %get-tuple-element.235), channel_id=1, source_target_pairs={{0,3},{1,2},{2,1},{3,0},{4,7},{5,6},{6,5},{7,4},{8,11},{9,10},{10,... | collective-permute-start | bytes 393224 | tf_op jit(solution)/shard_map/ppermute | solution.py:322
  42.3 11.0 %collective-permute-start.7 = (bf16[64,1024]{1,0:T(8,128)(2,1)S(1)}, bf16[64,1024]{1,0:T(8,128)(2,1)S(1)}, u32[]{:S(2)}, u32[]{:S(2)}) collective-permute-start(bf16[64,1024]{1,0:T(8,128)(2,1)S(1)} %get-tuple-element.235), channel_id=1, source_target_pairs={{0,2},{1,3},{2,0},{3,1},{4,6},{5,7},{6,4},{7,5},{8,10},{9,11},{10,... | collective-permute-start | bytes 393224 | tf_op jit(solution)/shard_map/ppermute | solution.py:322
  54.4 8.8 %collective-permute-start.13 = (bf16[256,512]{1,0:T(8,128)(2,1)S(1)}, bf16[256,512]{1,0:T(8,128)(2,1)S(1)}, u32[]{:S(2)}, u32[]{:S(2)}) collective-permute-start(bf16[256,512]{1,0:T(8,128)(2,1)S(1)} %slice.8), channel_id=1, source_target_pairs={{0,8},{1,9},{2,10},{3,11},{4,12},{5,13},{6,14},{7,15},{8,0},{9,1},... | collective-permute-start | bytes 786440 | tf_op jit(solution)/shard_map/ppermute | solution.py:322
  55.9 8.5 %collective-permute-start.14 = (bf16[256,512]{1,0:T(8,128)(2,1)S(1)}, bf16[256,512]{1,0:T(8,128)(2,1)S(1)}, u32[]{:S(2)}, u32[]{:S(2)}) collective-permute-start(bf16[256,512]{1,0:T(8,128)(2,1)S(1)} %slice.9), channel_id=1, source_target_pairs={{0,16},{1,17},{2,18},{3,19},{4,20},{5,21},{6,22},{7,23},{8,24},{9,... | collective-permute-start | bytes 786440 | tf_op jit(solution)/shard_map/ppermute | solution.py:322
  57.2 12.3 %collective-permute-start.19 = (bf16[128,1024]{1,0:T(8,128)(2,1)S(1)}, bf16[128,1024]{1,0:T(8,128)(2,1)S(1)}, u32[]{:S(2)}, u32[]{:S(2)}) collective-permute-start(bf16[128,1024]{1,0:T(8,128)(2,1)S(1)} %shard_map.202), channel_id=1, source_target_pairs={{0,4},{1,5},{2,6},{3,7},{4,0},{5,1},{6,2},{7,3},{8,12},{9,13},{10,... | collective-permute-start | bytes 786440 | tf_op jit(solution)/shard_map/ppermute | solution.py:322
  66.0 7.0 %collective-permute-start.16 = (bf16[596,128]{1,0:T(8,128)(2,1)S(1)}, bf16[596,128]{1,0:T(8,128)(2,1)S(1)}, u32[]{:S(2)}, u32[]{:S(2)}) collective-permute-start(bf16[596,128]{1,0:T(8,128)(2,1)S(1)} %get-tuple-element.251), channel_id=1, source_target_pairs={{0,8},{1,9},{2,10},{3,11},{4,12},{5,13},{6,14},{7,15},{8,0},{9,1},... | collective-permute-start | bytes 457736 | tf_op jit(solution)/shard_map/ppermute | solution.py:322
  66.6 8.5 %collective-permute-start.17 = (bf16[596,128]{1,0:T(8,128)(2,1)S(1)}, bf16[596,128]{1,0:T(8,128)(2,1)S(1)}, u32[]{:S(2)}, u32[]{:S(2)}) collective-permute-start(bf16[596,128]{1,0:T(8,128)(2,1)S(1)} %get-tuple-element.252), channel_id=1, source_target_pairs={{0,16},{1,17},{2,18},{3,19},{4,20},{5,21},{6,22},{7,23},{8,24},{9,... | collective-permute-start | bytes 457736 | tf_op jit(solution)/shard_map/ppermute | solution.py:322
  68.2 7.0 %collective-permute-start.18 = (bf16[596,128]{1,0:T(8,128)(2,1)S(1)}, bf16[596,128]{1,0:T(8,128)(2,1)S(1)}, u32[]{:S(2)}, u32[]{:S(2)}) collective-permute-start(bf16[596,128]{1,0:T(8,128)(2,1)S(1)} %get-tuple-element.253), channel_id=1, source_target_pairs={{0,24},{1,25},{2,26},{3,27},{4,28},{5,29},{6,30},{7,31},{8,16},{9,... | collective-permute-start | bytes 457736 | tf_op jit(solution)/shard_map/ppermute | solution.py:322
  70.1 15.5 %collective-permute-start.15 = (bf16[128,1024]{1,0:T(8,128)(2,1)S(1)}, bf16[128,1024]{1,0:T(8,128)(2,1)S(1)}, u32[]{:S(2)}, u32[]{:S(2)}) collective-permute-start(bf16[128,1024]{1,0:T(8,128)(2,1)S(1)} %get-tuple-element.291.own), channel_id=1, source_target_pairs={{0,2},{1,3},{2,0},{3,1},{4,6},{5,7},{6,4},{7,5},{8,10},{9,11},{10,... | collective-permute-start | bytes 786440 | tf_op jit(solution)/shard_map/ppermute | solution.py:322
  75.1 18.5 %collective-permute-start.24 = (bf16[256,1024]{1,0:T(8,128)(2,1)S(1)}, bf16[256,1024]{1,0:T(8,128)(2,1)S(1)}, u32[]{:S(2)}, u32[]{:S(2)}) collective-permute-start(bf16[256,1024]{1,0:T(8,128)(2,1)S(1)} %shard_map.203.f0.w0), channel_id=1, source_target_pairs={{0,16},{1,17},{2,18},{3,19},{4,20},{5,21},{6,22},{7,23},{8,24},{9,... | collective-permute-start | bytes 1572872 | tf_op jit(solution)/shard_map/ppermute | solution.py:322
  76.4 17.1 %collective-permute-start.23 = (bf16[256,1024]{1,0:T(8,128)(2,1)S(1)}, bf16[256,1024]{1,0:T(8,128)(2,1)S(1)}, u32[]{:S(2)}, u32[]{:S(2)}) collective-permute-start(bf16[256,1024]{1,0:T(8,128)(2,1)S(1)} %shard_map.203.f0.w0), channel_id=1, source_target_pairs={{0,8},{1,9},{2,10},{3,11},{4,12},{5,13},{6,14},{7,15},{8,0},{9,1},... | collective-permute-start | bytes 1572872 | tf_op jit(solution)/shard_map/ppermute | solution.py:322
  77.2 10.8 %collective-permute-start.26 = (bf16[56,1024]{1,0:T(8,128)(2,1)S(1)}, bf16[56,1024]{1,0:T(8,128)(2,1)S(1)}, u32[]{:S(2)}, u32[]{:S(2)}) collective-permute-start(bf16[56,1024]{1,0:T(8,128)(2,1)S(1)} %get-tuple-element.272), channel_id=1, source_target_pairs={{0,2},{1,3},{2,0},{3,1},{4,6},{5,7},{6,4},{7,5},{8,10},{9,11},{10,... | collective-permute-start | bytes 344072 | tf_op jit(solution)/shard_map/ppermute | solution.py:322
  77.2 11.4 %collective-permute-start.25 = (bf16[56,1024]{1,0:T(8,128)(2,1)S(1)}, bf16[56,1024]{1,0:T(8,128)(2,1)S(1)}, u32[]{:S(2)}, u32[]{:S(2)}) collective-permute-start(bf16[56,1024]{1,0:T(8,128)(2,1)S(1)} %get-tuple-element.271.here), channel_id=1, source_target_pairs={{0,1},{1,0},{2,3},{3,2},{4,5},{5,4},{6,7},{7,6},{8,9},{9,8},{10,11... | collective-permute-start | bytes 344072 | tf_op jit(solution)/shard_map/ppermute | solution.py:322
  85.6 4.4 %collective-permute-start.20 = (bf16[196,128]{1,0:T(8,128)(2,1)S(1)}, bf16[196,128]{1,0:T(8,128)(2,1)S(1)}, u32[]{:S(2)}, u32[]{:S(2)}) collective-permute-start(bf16[196,128]{1,0:T(8,128)(2,1)S(1)} %get-tuple-element.267), channel_id=1, source_target_pairs={{0,8},{1,9},{2,10},{3,11},{4,12},{5,13},{6,14},{7,15},{8,0},{9,1},... | collective-permute-start | bytes 150536 | tf_op jit(solution)/shard_map/ppermute | solution.py:322
  87.9 4.7 %collective-permute-start.21 = (bf16[196,128]{1,0:T(8,128)(2,1)S(1)}, bf16[196,128]{1,0:T(8,128)(2,1)S(1)}, u32[]{:S(2)}, u32[]{:S(2)}) collective-permute-start(bf16[196,128]{1,0:T(8,128)(2,1)S(1)} %get-tuple-element.268), channel_id=1, source_target_pairs={{0,16},{1,17},{2,18},{3,19},{4,20},{5,21},{6,22},{7,23},{8,24},{9,... | collective-permute-start | bytes 150536 | tf_op jit(solution)/shard_map/ppermute | solution.py:322
  88.6 5.0 %collective-permute-start.22 = (bf16[196,128]{1,0:T(8,128)(2,1)S(1)}, bf16[196,128]{1,0:T(8,128)(2,1)S(1)}, u32[]{:S(2)}, u32[]{:S(2)}) collective-permute-start(bf16[196,128]{1,0:T(8,128)(2,1)S(1)} %get-tuple-element.269), channel_id=1, source_target_pairs={{0,24},{1,25},{2,26},{3,27},{4,28},{5,29},{6,30},{7,31},{8,16},{9,... | collective-permute-start | bytes 150536 | tf_op jit(solution)/shard_map/ppermute | solution.py:322
  94.6 4.7 %collective-permute-start.27 = (bf16[196,1024]{1,0:T(8,128)(2,1)S(1)}, bf16[196,1024]{1,0:T(8,128)(2,1)S(1)}, u32[]{:S(2)}, u32[]{:S(2)}) collective-permute-start(bf16[196,1024]{1,0:T(8,128)(2,1)S(1)} %get-tuple-element.278), channel_id=1, source_target_pairs={{0,4},{1,5},{2,6},{3,7},{4,0},{5,1},{6,2},{7,3},{8,12},{9,13},{10,... | collective-permute-start | bytes 1204232 | tf_op jit(solution)/shard_map/ppermute | solution.py:322
  97.7 14.8 %collective-permute-start.33 = (bf16[256,1024]{1,0:T(8,128)(2,1)S(1)}, bf16[256,1024]{1,0:T(8,128)(2,1)S(1)}, u32[]{:S(2)}, u32[]{:S(2)}) collective-permute-start(bf16[256,1024]{1,0:T(8,128)(2,1)S(1)} %shard_map.210.g0.w0), channel_id=1, source_target_pairs={{0,8},{1,9},{2,10},{3,11},{4,12},{5,13},{6,14},{7,15},{8,0},{9,1},... | collective-permute-start | bytes 1572872 | tf_op jit(solution)/shard_map/ppermute | solution.py:322
  99.9 14.1 %collective-permute-start.28 = (bf16[196,1024]{1,0:T(8,128)(2,1)S(1)}, bf16[196,1024]{1,0:T(8,128)(2,1)S(1)}, u32[]{:S(2)}, u32[]{:S(2)}) collective-permute-start(bf16[196,1024]{1,0:T(8,128)(2,1)S(1)} %get-tuple-element.280), channel_id=1, source_target_pairs={{0,1},{1,0},{2,3},{3,2},{4,5},{5,4},{6,7},{7,6},{8,9},{9,8},{10,11... | collective-permute-start | bytes 1204232 | tf_op jit(solution)/shard_map/ppermute | solution.py:322
  100.0 14.0 %collective-permute-start.29 = (bf16[56,1024]{1,0:T(8,128)(2,1)S(1)}, bf16[56,1024]{1,0:T(8,128)(2,1)S(1)}, u32[]{:S(2)}, u32[]{:S(2)}) collective-permute-start(bf16[56,1024]{1,0:T(8,128)(2,1)S(1)} %collective-permute-done.26.r2), channel_id=1, source_target_pairs={{0,1},{1,0},{2,3},{3,2},{4,5},{5,4},{6,7},{7,6},{8,9},{9,8},{10,11... | collective-permute-start | bytes 344072 | tf_op jit(solution)/shard_map/ppermute | solution.py:322
  102.0 14.5 %collective-permute-start.34 = (bf16[256,1024]{1,0:T(8,128)(2,1)S(1)}, bf16[256,1024]{1,0:T(8,128)(2,1)S(1)}, u32[]{:S(2)}, u32[]{:S(2)}) collective-permute-start(bf16[256,1024]{1,0:T(8,128)(2,1)S(1)} %shard_map.210.g0.w0), channel_id=1, source_target_pairs={{0,16},{1,17},{2,18},{3,19},{4,20},{5,21},{6,22},{7,23},{8,24},{9,... | collective-permute-start | bytes 1572872 | tf_op jit(solution)/shard_map/ppermute | solution.py:322
  102.6 20.7 %collective-permute-start.35 = (bf16[256,1024]{1,0:T(8,128)(2,1)S(1)}, bf16[256,1024]{1,0:T(8,128)(2,1)S(1)}, u32[]{:S(2)}, u32[]{:S(2)}) collective-permute-start(bf16[256,1024]{1,0:T(8,128)(2,1)S(1)} %collective-permute-done.24.f2.w2), channel_id=1, source_target_pairs={{0,8},{1,9},{2,10},{3,11},{4,12},{5,13},{6,14},{7,15},{8,0},{9,1},... | collective-permute-start | bytes 1572872 | tf_op jit(solution)/shard_map/ppermute | solution.py:322
  112.6 14.0 %collective-permute-start.36 = (bf16[256,1024]{1,0:T(8,128)(2,1)S(1)}, bf16[256,1024]{1,0:T(8,128)(2,1)S(1)}, u32[]{:S(2)}, u32[]{:S(2)}) collective-permute-start(bf16[256,1024]{1,0:T(8,128)(2,1)S(1)} %collective-permute-done.33.g1.w1), channel_id=1, source_target_pairs={{0,16},{1,17},{2,18},{3,19},{4,20},{5,21},{6,22},{7,23},{8,24},{9,... | collective-permute-start | bytes 1572872 | tf_op jit(solution)/shard_map/ppermute | solution.py:322
  132.7 11.6 %collective-permute-start.38 = (bf16[196,1024]{1,0:T(8,128)(2,1)S(1)}, bf16[196,1024]{1,0:T(8,128)(2,1)S(1)}, u32[]{:S(2)}, u32[]{:S(2)}) collective-permute-start(bf16[196,1024]{1,0:T(8,128)(2,1)S(1)} %get-tuple-element.300), channel_id=1, source_target_pairs={{0,1},{1,0},{2,3},{3,2},{4,5},{5,4},{6,7},{7,6},{8,9},{9,8},{10,11... | collective-permute-start | bytes 1204232 | tf_op jit(solution)/shard_map/ppermute | solution.py:322
  134.9 25.5 %collective-permute-start.46 = (bf16[2,256,1024]{2,1,0:T(8,128)(2,1)S(1)}, bf16[2,256,1024]{2,1,0:T(8,128)(2,1)S(1)}, u32[]{:S(2)}, u32[]{:S(2)}) collective-permute-start(bf16[2,256,1024]{2,1,0:T(8,128)(2,1)S(1)} %get-tuple-element.330), channel_id=1, source_target_pairs={{0,16},{1,17},{2,18},{3,19},{4,20},{5,21},{6,22},{7,23},{8,24},{9,... | collective-permute-start | bytes 3145736 | tf_op jit(solution)/shard_map/ppermute | solution.py:322
  137.4 25.8 %collective-permute-start.45 = (bf16[2,256,1024]{2,1,0:T(8,128)(2,1)S(1)}, bf16[2,256,1024]{2,1,0:T(8,128)(2,1)S(1)}, u32[]{:S(2)}, u32[]{:S(2)}) collective-permute-start(bf16[2,256,1024]{2,1,0:T(8,128)(2,1)S(1)} %get-tuple-element.324), channel_id=1, source_target_pairs={{0,8},{1,9},{2,10},{3,11},{4,12},{5,13},{6,14},{7,15},{8,0},{9,1},... | collective-permute-start | bytes 3145736 | tf_op jit(solution)/shard_map/ppermute | solution.py:322
  147.1 7.2 %collective-permute-start.41 = (bf16[98,1024]{1,0:T(8,128)(2,1)S(1)}, bf16[98,1024]{1,0:T(8,128)(2,1)S(1)}, u32[]{:S(2)}, u32[]{:S(2)}) collective-permute-start(bf16[98,1024]{1,0:T(8,128)(2,1)S(1)} %get-tuple-element.315), channel_id=1, source_target_pairs={{0,1},{1,0},{2,3},{3,2},{4,5},{5,4},{6,7},{7,6},{8,9},{9,8},{10,11... | collective-permute-start | bytes 602120 | tf_op jit(solution)/shard_map/ppermute | solution.py:322
  154.3 9.6 %collective-permute-start.42 = (bf16[196,128]{1,0:T(8,128)(2,1)S(1)}, bf16[196,128]{1,0:T(8,128)(2,1)S(1)}, u32[]{:S(2)}, u32[]{:S(2)}) collective-permute-start(bf16[196,128]{1,0:T(8,128)(2,1)S(1)} %get-tuple-element.317), channel_id=1, source_target_pairs={{0,8},{1,9},{2,10},{3,11},{4,12},{5,13},{6,14},{7,15},{8,0},{9,1},... | collective-permute-start | bytes 150536 | tf_op jit(solution)/shard_map/ppermute | solution.py:322
  154.9 9.0 %collective-permute-start.43 = (bf16[196,128]{1,0:T(8,128)(2,1)S(1)}, bf16[196,128]{1,0:T(8,128)(2,1)S(1)}, u32[]{:S(2)}, u32[]{:S(2)}) collective-permute-start(bf16[196,128]{1,0:T(8,128)(2,1)S(1)} %get-tuple-element.318), channel_id=1, source_target_pairs={{0,16},{1,17},{2,18},{3,19},{4,20},{5,21},{6,22},{7,23},{8,24},{9,... | collective-permute-start | bytes 150536 | tf_op jit(solution)/shard_map/ppermute | solution.py:322
  156.3 8.9 %collective-permute-start.44 = (bf16[196,128]{1,0:T(8,128)(2,1)S(1)}, bf16[196,128]{1,0:T(8,128)(2,1)S(1)}, u32[]{:S(2)}, u32[]{:S(2)}) collective-permute-start(bf16[196,128]{1,0:T(8,128)(2,1)S(1)} %get-tuple-element.319), channel_id=1, source_target_pairs={{0,24},{1,25},{2,26},{3,27},{4,28},{5,29},{6,30},{7,31},{8,16},{9,... | collective-permute-start | bytes 150536 | tf_op jit(solution)/shard_map/ppermute | solution.py:322
  165.2 12.6 %collective-permute-start.47 = (bf16[56,1024]{1,0:T(8,128)(2,1)S(1)}, bf16[56,1024]{1,0:T(8,128)(2,1)S(1)}, u32[]{:S(2)}, u32[]{:S(2)}) collective-permute-start(bf16[56,1024]{1,0:T(8,128)(2,1)S(1)} %get-tuple-element.347), channel_id=1, source_target_pairs={{0,2},{1,3},{2,0},{3,1},{4,6},{5,7},{6,4},{7,5},{8,10},{9,11},{10,... | collective-permute-start | bytes 344072 | tf_op jit(solution)/shard_map/ppermute | solution.py:322
  167.2 11.9 %collective-permute-start.48 = (bf16[256,1024]{1,0:T(8,128)(2,1)S(1)}, bf16[256,1024]{1,0:T(8,128)(2,1)S(1)}, u32[]{:S(2)}, u32[]{:S(2)}) collective-permute-start(bf16[256,1024]{1,0:T(8,128)(2,1)S(1)} %get-tuple-element.349), channel_id=1, source_target_pairs={{0,16},{1,17},{2,18},{3,19},{4,20},{5,21},{6,22},{7,23},{8,24},{9,... | collective-permute-start | bytes 1572872 | tf_op jit(solution)/shard_map/ppermute | solution.py:322
  167.7 11.6 %collective-permute-start.49 = (bf16[256,1024]{1,0:T(8,128)(2,1)S(1)}, bf16[256,1024]{1,0:T(8,128)(2,1)S(1)}, u32[]{:S(2)}, u32[]{:S(2)}) collective-permute-start(bf16[256,1024]{1,0:T(8,128)(2,1)S(1)} %get-tuple-element.351), channel_id=1, source_target_pairs={{0,8},{1,9},{2,10},{3,11},{4,12},{5,13},{6,14},{7,15},{8,0},{9,1},... | collective-permute-start | bytes 1572872 | tf_op jit(solution)/shard_map/ppermute | solution.py:322
  180.1 4.4 %collective-permute-start.53 = (bf16[4,56,1024]{2,1,0:T(8,128)(2,1)S(1)}, bf16[4,56,1024]{2,1,0:T(8,128)(2,1)S(1)}, u32[]{:S(2)}, u32[]{:S(2)}) collective-permute-start(bf16[4,56,1024]{2,1,0:T(8,128)(2,1)S(1)} %get-tuple-element.358), channel_id=1, source_target_pairs={{0,4},{1,5},{2,6},{3,7},{4,0},{5,1},{6,2},{7,3},{8,12},{9,13},{10,... | collective-permute-start | bytes 1376264 | tf_op jit(solution)/shard_map/ppermute | solution.py:322
  180.2 6.8 %collective-permute-start.50 = (bf16[596,128]{1,0:T(8,128)(2,1)S(1)}, bf16[596,128]{1,0:T(8,128)(2,1)S(1)}, u32[]{:S(2)}, u32[]{:S(2)}) collective-permute-start(bf16[596,128]{1,0:T(8,128)(2,1)S(1)} %get-tuple-element.355), channel_id=1, source_target_pairs={{0,8},{1,9},{2,10},{3,11},{4,12},{5,13},{6,14},{7,15},{8,0},{9,1},... | collective-permute-start | bytes 457736 | tf_op jit(solution)/shard_map/ppermute | solution.py:322
  181.7 9.3 %collective-permute-start.51 = (bf16[596,128]{1,0:T(8,128)(2,1)S(1)}, bf16[596,128]{1,0:T(8,128)(2,1)S(1)}, u32[]{:S(2)}, u32[]{:S(2)}) collective-permute-start(bf16[596,128]{1,0:T(8,128)(2,1)S(1)} %get-tuple-element.356), channel_id=1, source_target_pairs={{0,16},{1,17},{2,18},{3,19},{4,20},{5,21},{6,22},{7,23},{8,24},{9,... | collective-permute-start | bytes 457736 | tf_op jit(solution)/shard_map/ppermute | solution.py:322
  182.3 8.7 %collective-permute-start.52 = (bf16[596,128]{1,0:T(8,128)(2,1)S(1)}, bf16[596,128]{1,0:T(8,128)(2,1)S(1)}, u32[]{:S(2)}, u32[]{:S(2)}) collective-permute-start(bf16[596,128]{1,0:T(8,128)(2,1)S(1)} %get-tuple-element.357), channel_id=1, source_target_pairs={{0,24},{1,25},{2,26},{3,27},{4,28},{5,29},{6,30},{7,31},{8,16},{9,... | collective-permute-start | bytes 457736 | tf_op jit(solution)/shard_map/ppermute | solution.py:322
  184.5 13.3 %collective-permute-start.62 = (bf16[128,2048]{1,0:T(8,128)(2,1)S(1)}, bf16[128,2048]{1,0:T(8,128)(2,1)S(1)}, u32[]{:S(2)}, u32[]{:S(2)}) collective-permute-start(bf16[128,2048]{1,0:T(8,128)(2,1)S(1)} %get-tuple-element.402), channel_id=1, source_target_pairs={{0,4},{1,5},{2,6},{3,7},{4,0},{5,1},{6,2},{7,3},{8,12},{9,13},{10,... | collective-permute-start | bytes 1572872 | tf_op jit(solution)/shard_map/ppermute | solution.py:322
  192.6 3.6 %collective-permute-start.54 = (bf16[196,1024]{1,0:T(8,128)(2,1)S(1)}, bf16[196,1024]{1,0:T(8,128)(2,1)S(1)}, u32[]{:S(2)}, u32[]{:S(2)}) collective-permute-start(bf16[196,1024]{1,0:T(8,128)(2,1)S(1)} %get-tuple-element.368), channel_id=1, source_target_pairs={{0,4},{1,5},{2,6},{3,7},{4,0},{5,1},{6,2},{7,3},{8,12},{9,13},{10,... | collective-permute-start | bytes 1204232 | tf_op jit(solution)/shard_map/ppermute | solution.py:322
  192.7 9.9 %collective-permute-start.56 = (bf16[2,56,1024]{2,1,0:T(8,128)(2,1)S(1)}, bf16[2,56,1024]{2,1,0:T(8,128)(2,1)S(1)}, u32[]{:S(2)}, u32[]{:S(2)}) collective-permute-start(bf16[2,56,1024]{2,1,0:T(8,128)(2,1)S(1)} %get-tuple-element.383), channel_id=1, source_target_pairs={{0,8},{1,9},{2,10},{3,11},{4,12},{5,13},{6,14},{7,15},{8,0},{9,1},... | collective-permute-start | bytes 688136 | tf_op jit(solution)/shard_map/ppermute | solution.py:322
  193.4 12.6 %collective-permute-start.57 = (bf16[2,56,1024]{2,1,0:T(8,128)(2,1)S(1)}, bf16[2,56,1024]{2,1,0:T(8,128)(2,1)S(1)}, u32[]{:S(2)}, u32[]{:S(2)}) collective-permute-start(bf16[2,56,1024]{2,1,0:T(8,128)(2,1)S(1)} %get-tuple-element.384), channel_id=1, source_target_pairs={{0,16},{1,17},{2,18},{3,19},{4,20},{5,21},{6,22},{7,23},{8,24},{9,... | collective-permute-start | bytes 688136 | tf_op jit(solution)/shard_map/ppermute | solution.py:322
  194.9 11.0 %collective-permute-start.58 = (bf16[2,56,1024]{2,1,0:T(8,128)(2,1)S(1)}, bf16[2,56,1024]{2,1,0:T(8,128)(2,1)S(1)}, u32[]{:S(2)}, u32[]{:S(2)}) collective-permute-start(bf16[2,56,1024]{2,1,0:T(8,128)(2,1)S(1)} %get-tuple-element.385), channel_id=1, source_target_pairs={{0,24},{1,25},{2,26},{3,27},{4,28},{5,29},{6,30},{7,31},{8,16},{9,... | collective-permute-start | bytes 688136 | tf_op jit(solution)/shard_map/ppermute | solution.py:322
  197.4 10.9 %collective-permute-start.55 = (bf16[112,1024]{1,0:T(8,128)(2,1)S(1)}, bf16[112,1024]{1,0:T(8,128)(2,1)S(1)}, u32[]{:S(2)}, u32[]{:S(2)}) collective-permute-start(bf16[112,1024]{1,0:T(8,128)(2,1)S(1)} %get-tuple-element.372), channel_id=1, source_target_pairs={{0,1},{1,0},{2,3},{3,2},{4,5},{5,4},{6,7},{7,6},{8,9},{9,8},{10,11... | collective-permute-start | bytes 688136 | tf_op jit(solution)/shard_map/ppermute | solution.py:322
  198.4 29.6 %collective-permute-start.63 = (bf16[128,2048]{1,0:T(8,128)(2,1)S(1)}, bf16[128,2048]{1,0:T(8,128)(2,1)S(1)}, u32[]{:S(2)}, u32[]{:S(2)}) collective-permute-start(bf16[128,2048]{1,0:T(8,128)(2,1)S(1)} %shard_map.232), channel_id=1, source_target_pairs={{0,2},{1,3},{2,0},{3,1},{4,6},{5,7},{6,4},{7,5},{8,10},{9,11},{10,... | collective-permute-start | bytes 1572872 | tf_op jit(solution)/shard_map/ppermute | solution.py:322
  208.3 21.2 %collective-permute-start.60 = (bf16[2,256,512]{2,1,0:T(8,128)(2,1)S(1)}, bf16[2,256,512]{2,1,0:T(8,128)(2,1)S(1)}, u32[]{:S(2)}, u32[]{:S(2)}) collective-permute-start(bf16[2,256,512]{2,1,0:T(8,128)(2,1)S(1)} %get-tuple-element.395), channel_id=1, source_target_pairs={{0,8},{1,9},{2,10},{3,11},{4,12},{5,13},{6,14},{7,15},{8,0},{9,1},... | collective-permute-start | bytes 1572872 | tf_op jit(solution)/shard_map/ppermute | solution.py:322
  208.9 20.6 %collective-permute-start.61 = (bf16[2,256,512]{2,1,0:T(8,128)(2,1)S(1)}, bf16[2,256,512]{2,1,0:T(8,128)(2,1)S(1)}, u32[]{:S(2)}, u32[]{:S(2)}) collective-permute-start(bf16[2,256,512]{2,1,0:T(8,128)(2,1)S(1)} %get-tuple-element.396), channel_id=1, source_target_pairs={{0,16},{1,17},{2,18},{3,19},{4,20},{5,21},{6,22},{7,23},{8,24},{9,... | collective-permute-start | bytes 1572872 | tf_op jit(solution)/shard_map/ppermute | solution.py:322
  211.4 18.1 %collective-permute-start.59 = (bf16[64,1024]{1,0:T(8,128)(2,1)S(1)}, bf16[64,1024]{1,0:T(8,128)(2,1)S(1)}, u32[]{:S(2)}, u32[]{:S(2)}) collective-permute-start(bf16[64,1024]{1,0:T(8,128)(2,1)S(1)} %get-tuple-element.394), channel_id=1, source_target_pairs={{0,2},{1,3},{2,0},{3,1},{4,6},{5,7},{6,4},{7,5},{8,10},{9,11},{10,... | collective-permute-start | bytes 393224 | tf_op jit(solution)/shard_map/ppermute | solution.py:322
  230.1 6.7 %collective-permute-start.68 = (bf16[256,512]{1,0:T(8,128)(2,1)S(1)}, bf16[256,512]{1,0:T(8,128)(2,1)S(1)}, u32[]{:S(2)}, u32[]{:S(2)}) collective-permute-start(bf16[256,512]{1,0:T(8,128)(2,1)S(1)} %get-tuple-element.416), channel_id=1, source_target_pairs={{0,16},{1,17},{2,18},{3,19},{4,20},{5,21},{6,22},{7,23},{8,24},{9,... | collective-permute-start | bytes 786440 | tf_op jit(solution)/shard_map/ppermute | solution.py:322
  231.4 6.4 %collective-permute-start.69 = (bf16[256,512]{1,0:T(8,128)(2,1)S(1)}, bf16[256,512]{1,0:T(8,128)(2,1)S(1)}, u32[]{:S(2)}, u32[]{:S(2)}) collective-permute-start(bf16[256,512]{1,0:T(8,128)(2,1)S(1)} %get-tuple-element.421), channel_id=1, source_target_pairs={{0,8},{1,9},{2,10},{3,11},{4,12},{5,13},{6,14},{7,15},{8,0},{9,1},... | collective-permute-start | bytes 786440 | tf_op jit(solution)/shard_map/ppermute | solution.py:322
  233.8 6.5 %collective-permute-start.64 = (bf16[4,56,1024]{2,1,0:T(8,128)(2,1)S(1)}, bf16[4,56,1024]{2,1,0:T(8,128)(2,1)S(1)}, u32[]{:S(2)}, u32[]{:S(2)}) collective-permute-start(bf16[4,56,1024]{2,1,0:T(8,128)(2,1)S(1)} %get-tuple-element.405), channel_id=1, source_target_pairs={{0,4},{1,5},{2,6},{3,7},{4,0},{5,1},{6,2},{7,3},{8,12},{9,13},{10,... | collective-permute-start | bytes 1376264 | tf_op jit(solution)/shard_map/ppermute | solution.py:322
  238.5 6.0 %collective-permute-start.70 = (bf16[128,1024]{1,0:T(8,128)(2,1)S(1)}, bf16[128,1024]{1,0:T(8,128)(2,1)S(1)}, u32[]{:S(2)}, u32[]{:S(2)}) collective-permute-start(bf16[128,1024]{1,0:T(8,128)(2,1)S(1)} %get-tuple-element.423), channel_id=1, source_target_pairs={{0,4},{1,5},{2,6},{3,7},{4,0},{5,1},{6,2},{7,3},{8,12},{9,13},{10,... | collective-permute-start | bytes 786440 | tf_op jit(solution)/shard_map/ppermute | solution.py:322
  240.9 8.5 %collective-permute-start.65 = (bf16[2,56,1024]{2,1,0:T(8,128)(2,1)S(1)}, bf16[2,56,1024]{2,1,0:T(8,128)(2,1)S(1)}, u32[]{:S(2)}, u32[]{:S(2)}) collective-permute-start(bf16[2,56,1024]{2,1,0:T(8,128)(2,1)S(1)} %get-tuple-element.406), channel_id=1, source_target_pairs={{0,8},{1,9},{2,10},{3,11},{4,12},{5,13},{6,14},{7,15},{8,0},{9,1},... | collective-permute-start | bytes 688136 | tf_op jit(solution)/shard_map/ppermute | solution.py:322
  242.5 12.6 %collective-permute-start.66 = (bf16[2,56,1024]{2,1,0:T(8,128)(2,1)S(1)}, bf16[2,56,1024]{2,1,0:T(8,128)(2,1)S(1)}, u32[]{:S(2)}, u32[]{:S(2)}) collective-permute-start(bf16[2,56,1024]{2,1,0:T(8,128)(2,1)S(1)} %get-tuple-element.407), channel_id=1, source_target_pairs={{0,16},{1,17},{2,18},{3,19},{4,20},{5,21},{6,22},{7,23},{8,24},{9,... | collective-permute-start | bytes 688136 | tf_op jit(solution)/shard_map/ppermute | solution.py:322
  243.0 12.2 %collective-permute-start.67 = (bf16[2,56,1024]{2,1,0:T(8,128)(2,1)S(1)}, bf16[2,56,1024]{2,1,0:T(8,128)(2,1)S(1)}, u32[]{:S(2)}, u32[]{:S(2)}) collective-permute-start(bf16[2,56,1024]{2,1,0:T(8,128)(2,1)S(1)} %get-tuple-element.408), channel_id=1, source_target_pairs={{0,24},{1,25},{2,26},{3,27},{4,28},{5,29},{6,30},{7,31},{8,16},{9,... | collective-permute-start | bytes 688136 | tf_op jit(solution)/shard_map/ppermute | solution.py:322
  245.0 13.9 %collective-permute-start.71 = (bf16[128,1024]{1,0:T(8,128)(2,1)S(1)}, bf16[128,1024]{1,0:T(8,128)(2,1)S(1)}, u32[]{:S(2)}, u32[]{:S(2)}) collective-permute-start(bf16[128,1024]{1,0:T(8,128)(2,1)S(1)} %shard_map.239), channel_id=1, source_target_pairs={{0,2},{1,3},{2,0},{3,1},{4,6},{5,7},{6,4},{7,5},{8,10},{9,11},{10,... | collective-permute-start | bytes 786440 | tf_op jit(solution)/shard_map/ppermute | solution.py:322
  (14 other events, 36.0 us)

commit v7 on v6

--- a/solution.py
+++ b/solution.py
@@ -330,7 +330,8 @@
     "pack": 1.2,
     "pick": 1.5,
     "norm_one": 1.0,
-    "qkv": 1.6,
+    "qkv": 0.8,
+    "qkv_start": 1.4,
     "attention": 7.6,
     "proj": 1.1,
     "norm_two": 0.9,
@@ -560,14 +561,20 @@
     return jnp.concatenate([value[:half], value[half:]], axis=1)
 
 
-def qkv_kernel(ids, own, got, qv_bias, w0, w1, w2, w3, w4, whole, o0, o1, o2, o3, wide, heads):
-    weights = (w0, w1, w2, w3, w4)
+def qkv_start_kernel(ids, own, got, w0, w1, w2, whole, start, wide):
     join_rows(wide, own, got)
     whole[...] = wide[...].astype(BF16)
     for j in range(3):
         total = dot(whole[:, lanes(0)], w0[:, lanes(j)], NN)
-        for m in range(1, 4):
-            total = total + dot(whole[:, lanes(m)], part_of(weights, m, j), NN)
+        for m, weight in ((1, w1), (2, w2)):
+            total = total + dot(whole[:, lanes(m)], weight[:, lanes(j)], NN)
+        start[:, lanes(j)] = total
+
+
+def qkv_kernel(ids, whole, start, qv_bias, w3, w4, o0, o1, o2, o3, heads):
+    for j in range(3):
+        weight = (w3, w4)[j // 2][:, lanes(j % 2)]
+        total = start[:, lanes(j)] + dot(whole[:, lanes(3)], weight, NN)
         for h in range(4):
             part = total[:, 64 * h : 64 * h + 64]
             if j != 1:
@@ -1183,16 +1190,26 @@
         scratch=[((half, 1024), F32), ((8, 1024), F32)],
     )
 
-    whole_one, *qkv = call(
-        qkv_kernel,
-        [((count, 1024), BF16)] + [(packed, BF16)] * 4,
+    whole_one, start = call(
+        qkv_start_kernel,
+        [((count, 1024), BF16), ((count, 768), F32)],
         ids,
         normed,
         swap(normed, CORE),
+        *w_att[:3],
+        scratch=[wide],
+    )
+    qkv = call(
+        qkv_kernel,
+        [(packed, BF16)] * 4,
+        ids,
+        whole_one,
+        start,
         qkv_bias,
-        *w_att,
-        scratch=[wide, ((4, *packed), BF16)],
-    )
+        *w_att[3:],
+        scratch=[((4, *packed), BF16)],
+    )
+
     shard_g, *qkv = tie(shard_g, *qkv)
     far_g = swap(shard_g, Z_HIGH)
     *qkv, f0, here_grad, there_grad = tie(*trade(qkv), f0, here_grad, there_grad)

time: 261 us -> 258 us (0.989)
  waiting for transfers between devices: 126 us -> 122 us
    ppermute x72, waiting for transfers between devices: 126 us -> 122 us  [swap(): return lax.ppermute(value, AXES, [(i, i ^ mask) for i in range(32)])]
    pallas_call x48 -> x49, Pallas kernels: 64.1 us -> 65 us  [call(): pl.pallas_call(body, out_shape=[jax.ShapeDtypeStruct(s, t) for s, t in ou...]
  transfers between devices with their start and end apart: 72 -> 72, of which waited for: 40 -> 41; matrix products, arithmetic and copies ran while one was open for 0% -> 0% of each run, Pallas kernels for 21% -> 22%
where the time goes in v7:
time: 258 us
  waiting for transfers between devices  122 us (47%)
  starting transfers between devices  65.1 us (25%)
  Pallas kernels  65 us (25%)
    ppermute x72, waiting for transfers between devices, swap(): return lax.ppermute(value, AXES, [(i, i ^ mask) for i in range(32)])  122 us
    ppermute x72, starting transfers between devices, swap(): return lax.ppermute(value, AXES, [(i, i ^ mask) for i in range(32)])  65.1 us
    pallas_call x49, Pallas kernels, call(): pl.pallas_call(body, out_shape=[jax.ShapeDtypeStruct(s, t) for s, t in ou...  65 us
  transfers between devices with their start and end apart: 72, of which 41 were waited for; matrix products, arithmetic and copies ran while one was open for 0% of the time, Pallas kernels for 22%

profile of v7, /device:TPU:0, one launch (start us, length us, event | category | flops | bytes accessed | tf_op | source)
XLA Modules:
  0.0 258.0 jit_solution(10552594320315352331)
XLA Ops:
  7.5 3.7 %collective-permute-start.4 = (bf16[128,1024]{1,0:T(8,128)(2,1)S(1)}, bf16[128,1024]{1,0:T(8,128)(2,1)S(1)}, u32[]{:S(2)}, u32[]{:S(2)}) collective-permute-start(bf16[128,1024]{1,0:T(8,128)(2,1)S(1)} %get-tuple-element.228.own), channel_id=1, source_target_pairs={{0,2},{1,3},{2,0},{3,1},{4,6},{5,7},{6,4},{7,5},{8,10},{9,11},{10,... | collective-permute-start | bytes 786440 | tf_op jit(solution)/shard_map/ppermute | solution.py:322
  11.8 1.6 collective-permute-start.1
  13.4 1.5 collective-permute-start.2
  15.4 8.4 %collective-permute-done.4.far = bf16[128,1024]{1,0:T(8,128)(2,1)S(1)} collective-permute-done((bf16[128,1024]{1,0:T(8,128)(2,1)S(1)}, bf16[128,1024]{1,0:T(8,128)(2,1)S(1)}, u32[]{:S(2)}, u32[]{:S(2)}) %collective-permute-start.4) | collective-permute-done | bytes 262176 | tf_op jit(solution)/shard_map/ppermute | solution.py:322
  24.5 1.4 collective-permute-done.5.got
  26.5 9.0 %collective-permute-done.2.d2 = bf16[2,112,1024]{2,1,0:T(8,128)(2,1)S(1)} collective-permute-done((bf16[2,112,1024]{2,1,0:T(8,128)(2,1)S(1)}, bf16[2,112,1024]{2,1,0:T(8,128)(2,1)S(1)}, u32[]{:S(2)}, u32[]{:S(2)}) %collective-permute-start.2) | collective-permute-done | bytes 458784 | tf_op jit(solution)/shard_map/ppermute | solution.py:322
  35.6 1.6 shard_map.199
  37.1 1.6 collective-permute-start.6
  38.8 1.5 collective-permute-start.8
  40.7 1.5 collective-permute-start.12
  43.4 3.9 %collective-permute-done.8.r3 = bf16[64,1024]{1,0:T(8,128)(2,1)S(1)} collective-permute-done((bf16[64,1024]{1,0:T(8,128)(2,1)S(1)}, bf16[64,1024]{1,0:T(8,128)(2,1)S(1)}, u32[]{:S(2)}, u32[]{:S(2)}) %collective-permute-start.8) | collective-permute-done | bytes 131104 | tf_op jit(solution)/shard_map/ppermute | solution.py:322
  47.3 4.7 %collective-permute-done.7.r2 = bf16[64,1024]{1,0:T(8,128)(2,1)S(1)} collective-permute-done((bf16[64,1024]{1,0:T(8,128)(2,1)S(1)}, bf16[64,1024]{1,0:T(8,128)(2,1)S(1)}, u32[]{:S(2)}, u32[]{:S(2)}) %collective-permute-start.7) | collective-permute-done | bytes 131104 | tf_op jit(solution)/shard_map/ppermute | solution.py:322
  53.0 1.4 collective-permute-start.13
  57.2 4.6 %collective-permute-done.13.w3 = bf16[256,512]{1,0:T(8,128)(2,1)S(1)} collective-permute-done((bf16[256,512]{1,0:T(8,128)(2,1)S(1)}, bf16[256,512]{1,0:T(8,128)(2,1)S(1)}, u32[]{:S(2)}, u32[]{:S(2)}) %collective-permute-start.13) | collective-permute-done | bytes 262176 | tf_op jit(solution)/shard_map/ppermute | solution.py:322
  64.8 1.5 collective-permute-start.17
  68.7 2.4 collective-permute-done.16.a1
  71.0 2.3 collective-permute-done.17.a2
  75.4 2.4 collective-permute-start.25
  77.8 5.1 %shard_map.205 = (bf16[196,128]{1,0:T(8,128)(2,1)S(1)}, bf16[196,128]{1,0:T(8,128)(2,1)S(1)}, bf16[196,128]{1,0:T(8,128)(2,1)S(1)}, bf16[196,128]{1,0:T(8,128)(2,1)S(1)}, f32[1568,128]{1,0:T(8,128)S(1)}) custom-call(s32[5]{0:T(128)S(1)} %stack.19.ids, bf16[596,128]{1,0:T(8,128)(2,1)S(1)} %get-tuple-element.261.a0, ...), custom_call_target="tpu_custom_call" | custom-call | flops 8739999744 | bytes 1613824 | tf_op jit(solution)/shard_map/pallas_call | solution.py:365
  86.2 1.5 collective-permute-start.22
  87.9 1.9 collective-permute-done.21.a2
  89.8 1.4 collective-permute-done.22.a3
  95.4 1.4 collective-permute-start.33
  97.5 2.0 collective-permute-start.29
  100.3 1.4 collective-permute-start.35
  101.7 8.5 %collective-permute-done.33.g1.w1 = bf16[256,1024]{1,0:T(8,128)(2,1)S(1)} collective-permute-done((bf16[256,1024]{1,0:T(8,128)(2,1)S(1)}, bf16[256,1024]{1,0:T(8,128)(2,1)S(1)}, u32[]{:S(2)}, u32[]{:S(2)}) %collective-permute-start.33) | collective-permute-done | bytes 524320 | tf_op jit(solution)/shard_map/ppermute | solution.py:322
  110.2 1.4 collective-permute-start.36
  115.3 3.0 %shard_map.212 = (bf16[392,1024]{1,0:T(8,128)(2,1)S(1)}, bf16[392,1024]{1,0:T(8,128)(2,1)S(1)}, f32[392,1024]{1,0:T(8,128)S(1)}, f32[392,1024]{1,0:T(8,128)S(1)}) custom-call(s32[5]{0:T(128)S(1)} %stack.19.ids, bf16[196,1024]{1,0:T(8,128)(2,1)S(1)} %get-tuple-element.288.own, bf16[196,1024]{1,0:T(8,128)(2,1)S(1)} %collective-permute-done.30.got, ...), custom_call_target="tpu_custom_call" | custom-call | flops 1150000000 | bytes 9572352 | tf_op jit(solution)/shard_map/pallas_call | solution.py:365
  118.3 2.6 %collective-permute-done.35.w3 = bf16[256,1024]{1,0:T(8,128)(2,1)S(1)} collective-permute-done((bf16[256,1024]{1,0:T(8,128)(2,1)S(1)}, bf16[256,1024]{1,0:T(8,128)(2,1)S(1)}, u32[]{:S(2)}, u32[]{:S(2)}) %collective-permute-start.35) | collective-permute-done | bytes 524320 | tf_op jit(solution)/shard_map/ppermute | solution.py:322
  120.9 3.2 %collective-permute-done.36.g3.w3 = bf16[256,1024]{1,0:T(8,128)(2,1)S(1)} collective-permute-done((bf16[256,1024]{1,0:T(8,128)(2,1)S(1)}, bf16[256,1024]{1,0:T(8,128)(2,1)S(1)}, u32[]{:S(2)}, u32[]{:S(2)}) %collective-permute-start.36) | collective-permute-done | bytes 524320 | tf_op jit(solution)/shard_map/ppermute | solution.py:322
  124.1 3.6 %shard_map.213 = (bf16[392,1024]{1,0:T(8,128)(2,1)S(1)}, bf16[392,1024]{1,0:T(8,128)(2,1)S(1)}, f32[1,1024]{1,0:T(1,128)S(1)}, f32[196,1024]{1,0:T(8,128)S(1)}, bf16[196,1024]{1,0:T(8,128)(2,1)S(1)}) custom-call(s32[5]{0:T(128)S(1)} %stack.19.ids, bf16[392,1024]{1,0:T(8,128)(2,1)S(1)} %get-tuple-element.323.whole.left, ...), custom_call_target="tpu_custom_call" | custom-call | flops 5750000128 | bytes 10252288 | tf_op jit(solution)/shard_map/pallas_call | solution.py:365
  127.7 1.7 collective-permute-done.37.got
  130.5 1.8 shard_map.221
  133.2 1.8 shard_map.219
  135.1 1.5 collective-permute-start.45
  136.5 1.6 shard_map.215
  138.1 3.6 %collective-permute-done.38.got = bf16[196,1024]{1,0:T(8,128)(2,1)S(1)} collective-permute-done((bf16[196,1024]{1,0:T(8,128)(2,1)S(1)}, bf16[196,1024]{1,0:T(8,128)(2,1)S(1)}, u32[]{:S(2)}, u32[]{:S(2)}) %collective-permute-start.38) | collective-permute-done | bytes 401440 | tf_op jit(solution)/shard_map/ppermute | solution.py:322
  141.7 1.5 shard_map.216
  146.2 5.6 %collective-permute-done.41.got = bf16[98,1024]{1,0:T(8,128)(2,1)S(1)} collective-permute-done((bf16[98,1024]{1,0:T(8,128)(2,1)S(1)}, bf16[98,1024]{1,0:T(8,128)(2,1)S(1)}, u32[]{:S(2)}, u32[]{:S(2)}) %collective-permute-start.41) | collective-permute-done | bytes 200736 | tf_op jit(solution)/shard_map/ppermute | solution.py:322
  152.5 1.4 collective-permute-start.43
  156.0 1.9 collective-permute-done.46.got
  158.6 2.2 collective-permute-done.45.got
  162.7 2.7 %collective-permute-start.47 = (bf16[56,1024]{1,0:T(8,128)(2,1)S(1)}, bf16[56,1024]{1,0:T(8,128)(2,1)S(1)}, u32[]{:S(2)}, u32[]{:S(2)}) collective-permute-start(bf16[56,1024]{1,0:T(8,128)(2,1)S(1)} %get-tuple-element.350), channel_id=1, source_target_pairs={{0,2},{1,3},{2,0},{3,1},{4,6},{5,7},{6,4},{7,5},{8,10},{9,11},{10,... | collective-permute-start | bytes 344072 | tf_op jit(solution)/shard_map/ppermute | solution.py:322
  167.2 8.6 %shard_map.224 = (bf16[596,128]{1,0:T(8,128)(2,1)S(1)}, bf16[596,128]{1,0:T(8,128)(2,1)S(1)}, bf16[596,128]{1,0:T(8,128)(2,1)S(1)}, bf16[596,128]{1,0:T(8,128)(2,1)S(1)}) custom-call(s32[5]{0:T(128)S(1)} %stack.19.ids, bf16[596,128]{1,0:T(8,128)(2,1)S(1)} %get-tuple-element.261.a0, bf16[596,128]{1,0:T(8,128)(2,1)S(1)} %collective-permute-done.16.a1, ...), custom_call_target="tpu_custom_call" | custom-call | flops 13799999488 | bytes 2224128 | tf_op jit(solution)/shard_map/pallas_call | solution.py:365
  175.8 1.4 collective-permute-done.48.got_x
  180.5 1.7 collective-permute-start.52
  183.6 1.9 collective-permute-done.50.g1
  185.5 3.7 %collective-permute-done.51.g2 = bf16[596,128]{1,0:T(8,128)(2,1)S(1)} collective-permute-done((bf16[596,128]{1,0:T(8,128)(2,1)S(1)}, bf16[596,128]{1,0:T(8,128)(2,1)S(1)}, u32[]{:S(2)}, u32[]{:S(2)}) %collective-permute-start.51) | collective-permute-done | bytes 152608 | tf_op jit(solution)/shard_map/ppermute | solution.py:322
  189.2 1.6 shard_map.227
  196.5 1.9 collective-permute-start.63
  198.4 1.8 shard_map.229
  200.2 4.1 %collective-permute-done.57.d2 = bf16[2,56,1024]{2,1,0:T(8,128)(2,1)S(1)} collective-permute-done((bf16[2,56,1024]{2,1,0:T(8,128)(2,1)S(1)}, bf16[2,56,1024]{2,1,0:T(8,128)(2,1)S(1)}, u32[]{:S(2)}, u32[]{:S(2)}) %collective-permute-start.57) | collective-permute-done | bytes 229408 | tf_op jit(solution)/shard_map/ppermute | solution.py:322
  204.4 1.6 collective-permute-done.55.got
  209.4 16.7 %collective-permute-done.63.moved = bf16[128,2048]{1,0:T(8,128)(2,1)S(1)} collective-permute-done((bf16[128,2048]{1,0:T(8,128)(2,1)S(1)}, bf16[128,2048]{1,0:T(8,128)(2,1)S(1)}, u32[]{:S(2)}, u32[]{:S(2)}) %collective-permute-start.63) | collective-permute-done | bytes 524320 | tf_op jit(solution)/shard_map/ppermute | solution.py:322
  226.1 1.4 collective-permute-done.59.away
  229.6 1.5 collective-permute-start.69
  232.0 2.9 %collective-permute-done.68.got_x = bf16[256,512]{1,0:T(8,128)(2,1)S(1)} collective-permute-done((bf16[256,512]{1,0:T(8,128)(2,1)S(1)}, bf16[256,512]{1,0:T(8,128)(2,1)S(1)}, u32[]{:S(2)}, u32[]{:S(2)}) %collective-permute-start.68) | collective-permute-done | bytes 262176 | tf_op jit(solution)/shard_map/ppermute | solution.py:322
  236.8 1.8 shard_map.230
  239.1 1.5 collective-permute-start.65
  243.3 1.8 shard_map.242
  245.1 2.5 collective-permute-done.65.d1
  247.6 5.7 %collective-permute-done.66.d2 = bf16[2,56,1024]{2,1,0:T(8,128)(2,1)S(1)} collective-permute-done((bf16[2,56,1024]{2,1,0:T(8,128)(2,1)S(1)}, bf16[2,56,1024]{2,1,0:T(8,128)(2,1)S(1)}, u32[]{:S(2)}, u32[]{:S(2)}) %collective-permute-start.66) | collective-permute-done | bytes 229408 | tf_op jit(solution)/shard_map/ppermute | solution.py:322
  253.3 2.0 shard_map.236
  256.6 1.4 shard_map.241
  (146 shorter events, 69.6 us)
Async XLA Ops:
  6.3 4.9 %collective-permute-start = (bf16[4,112,1024]{2,1,0:T(8,128)(2,1)S(1)}, bf16[4,112,1024]{2,1,0:T(8,128)(2,1)S(1)}, u32[]{:S(2)}, u32[]{:S(2)}) collective-permute-start(bf16[4,112,1024]{2,1,0:T(8,128)(2,1)S(1)} %get-tuple-element.224), channel_id=1, source_target_pairs={{0,4},{1,5},{2,6},{3,7},{4,0},{5,1},{6,2},{7,3},{8,12},{9,13},{10,... | collective-permute-start | bytes 2752520 | tf_op jit(solution)/shard_map/ppermute | solution.py:322
  7.5 16.2 %collective-permute-start.4 = (bf16[128,1024]{1,0:T(8,128)(2,1)S(1)}, bf16[128,1024]{1,0:T(8,128)(2,1)S(1)}, u32[]{:S(2)}, u32[]{:S(2)}) collective-permute-start(bf16[128,1024]{1,0:T(8,128)(2,1)S(1)} %get-tuple-element.228.own), channel_id=1, source_target_pairs={{0,2},{1,3},{2,0},{3,1},{4,6},{5,7},{6,4},{7,5},{8,10},{9,11},{10,... | collective-permute-start | bytes 786440 | tf_op jit(solution)/shard_map/ppermute | solution.py:322
  11.8 14.7 %collective-permute-start.1 = (bf16[2,112,1024]{2,1,0:T(8,128)(2,1)S(1)}, bf16[2,112,1024]{2,1,0:T(8,128)(2,1)S(1)}, u32[]{:S(2)}, u32[]{:S(2)}) collective-permute-start(bf16[2,112,1024]{2,1,0:T(8,128)(2,1)S(1)} %get-tuple-element.225), channel_id=1, source_target_pairs={{0,8},{1,9},{2,10},{3,11},{4,12},{5,13},{6,14},{7,15},{8,0},{9,1},... | collective-permute-start | bytes 1376264 | tf_op jit(solution)/shard_map/ppermute | solution.py:322
  13.4 22.2 %collective-permute-start.2 = (bf16[2,112,1024]{2,1,0:T(8,128)(2,1)S(1)}, bf16[2,112,1024]{2,1,0:T(8,128)(2,1)S(1)}, u32[]{:S(2)}, u32[]{:S(2)}) collective-permute-start(bf16[2,112,1024]{2,1,0:T(8,128)(2,1)S(1)} %get-tuple-element.226), channel_id=1, source_target_pairs={{0,16},{1,17},{2,18},{3,19},{4,20},{5,21},{6,22},{7,23},{8,24},{9,... | collective-permute-start | bytes 1376264 | tf_op jit(solution)/shard_map/ppermute | solution.py:322
  14.9 20.7 %collective-permute-start.3 = (bf16[2,112,1024]{2,1,0:T(8,128)(2,1)S(1)}, bf16[2,112,1024]{2,1,0:T(8,128)(2,1)S(1)}, u32[]{:S(2)}, u32[]{:S(2)}) collective-permute-start(bf16[2,112,1024]{2,1,0:T(8,128)(2,1)S(1)} %get-tuple-element.227), channel_id=1, source_target_pairs={{0,24},{1,25},{2,26},{3,27},{4,28},{5,29},{6,30},{7,31},{8,16},{9,... | collective-permute-start | bytes 1376264 | tf_op jit(solution)/shard_map/ppermute | solution.py:322
  24.4 17.8 %collective-permute-start.9 = (bf16[128,1024]{1,0:T(8,128)(2,1)S(1)}, bf16[128,1024]{1,0:T(8,128)(2,1)S(1)}, u32[]{:S(2)}, u32[]{:S(2)}) collective-permute-start(bf16[128,1024]{1,0:T(8,128)(2,1)S(1)} %copy-done.3), channel_id=1, source_target_pairs={{0,2},{1,3},{2,0},{3,1},{4,6},{5,7},{6,4},{7,5},{8,10},{9,11},{10,... | collective-permute-start | bytes 786440 | tf_op jit(solution)/shard_map/ppermute | solution.py:322
  37.1 6.3 %collective-permute-start.6 = (bf16[64,1024]{1,0:T(8,128)(2,1)S(1)}, bf16[64,1024]{1,0:T(8,128)(2,1)S(1)}, u32[]{:S(2)}, u32[]{:S(2)}) collective-permute-start(bf16[64,1024]{1,0:T(8,128)(2,1)S(1)} %get-tuple-element.235.here), channel_id=1, source_target_pairs={{0,1},{1,0},{2,3},{3,2},{4,5},{5,4},{6,7},{7,6},{8,9},{9,8},{10,11... | collective-permute-start | bytes 393224 | tf_op jit(solution)/shard_map/ppermute | solution.py:322
  38.8 8.5 %collective-permute-start.8 = (bf16[64,1024]{1,0:T(8,128)(2,1)S(1)}, bf16[64,1024]{1,0:T(8,128)(2,1)S(1)}, u32[]{:S(2)}, u32[]{:S(2)}) collective-permute-start(bf16[64,1024]{1,0:T(8,128)(2,1)S(1)} %get-tuple-element.236), channel_id=1, source_target_pairs={{0,3},{1,2},{2,1},{3,0},{4,7},{5,6},{6,5},{7,4},{8,11},{9,10},{10,... | collective-permute-start | bytes 393224 | tf_op jit(solution)/shard_map/ppermute | solution.py:322
  40.3 11.7 %collective-permute-start.7 = (bf16[64,1024]{1,0:T(8,128)(2,1)S(1)}, bf16[64,1024]{1,0:T(8,128)(2,1)S(1)}, u32[]{:S(2)}, u32[]{:S(2)}) collective-permute-start(bf16[64,1024]{1,0:T(8,128)(2,1)S(1)} %get-tuple-element.236), channel_id=1, source_target_pairs={{0,2},{1,3},{2,0},{3,1},{4,6},{5,7},{6,4},{7,5},{8,10},{9,11},{10,... | collective-permute-start | bytes 393224 | tf_op jit(solution)/shard_map/ppermute | solution.py:322
  40.7 12.3 %collective-permute-start.12 = (bf16[256,1024]{1,0:T(8,128)(2,1)S(1)}, bf16[256,1024]{1,0:T(8,128)(2,1)S(1)}, u32[]{:S(2)}, u32[]{:S(2)}) collective-permute-start(bf16[256,1024]{1,0:T(8,128)(2,1)S(1)} %shard_map.198.w0), channel_id=1, source_target_pairs={{0,16},{1,17},{2,18},{3,19},{4,20},{5,21},{6,22},{7,23},{8,24},{9,... | collective-permute-start | bytes 1572872 | tf_op jit(solution)/shard_map/ppermute | solution.py:322
  42.2 12.2 %collective-permute-start.11 = (bf16[256,1024]{1,0:T(8,128)(2,1)S(1)}, bf16[256,1024]{1,0:T(8,128)(2,1)S(1)}, u32[]{:S(2)}, u32[]{:S(2)}) collective-permute-start(bf16[256,1024]{1,0:T(8,128)(2,1)S(1)} %shard_map.198.w0), channel_id=1, source_target_pairs={{0,8},{1,9},{2,10},{3,11},{4,12},{5,13},{6,14},{7,15},{8,0},{9,1},... | collective-permute-start | bytes 1572872 | tf_op jit(solution)/shard_map/ppermute | solution.py:322
  53.0 8.8 %collective-permute-start.13 = (bf16[256,512]{1,0:T(8,128)(2,1)S(1)}, bf16[256,512]{1,0:T(8,128)(2,1)S(1)}, u32[]{:S(2)}, u32[]{:S(2)}) collective-permute-start(bf16[256,512]{1,0:T(8,128)(2,1)S(1)} %slice.8), channel_id=1, source_target_pairs={{0,8},{1,9},{2,10},{3,11},{4,12},{5,13},{6,14},{7,15},{8,0},{9,1},... | collective-permute-start | bytes 786440 | tf_op jit(solution)/shard_map/ppermute | solution.py:322
  54.5 8.5 %collective-permute-start.14 = (bf16[256,512]{1,0:T(8,128)(2,1)S(1)}, bf16[256,512]{1,0:T(8,128)(2,1)S(1)}, u32[]{:S(2)}, u32[]{:S(2)}) collective-permute-start(bf16[256,512]{1,0:T(8,128)(2,1)S(1)} %slice.9), channel_id=1, source_target_pairs={{0,16},{1,17},{2,18},{3,19},{4,20},{5,21},{6,22},{7,23},{8,24},{9,... | collective-permute-start | bytes 786440 | tf_op jit(solution)/shard_map/ppermute | solution.py:322
  55.8 11.8 %collective-permute-start.19 = (bf16[128,1024]{1,0:T(8,128)(2,1)S(1)}, bf16[128,1024]{1,0:T(8,128)(2,1)S(1)}, u32[]{:S(2)}, u32[]{:S(2)}) collective-permute-start(bf16[128,1024]{1,0:T(8,128)(2,1)S(1)} %shard_map.203), channel_id=1, source_target_pairs={{0,4},{1,5},{2,6},{3,7},{4,0},{5,1},{6,2},{7,3},{8,12},{9,13},{10,... | collective-permute-start | bytes 786440 | tf_op jit(solution)/shard_map/ppermute | solution.py:322
  64.1 7.0 %collective-permute-start.16 = (bf16[596,128]{1,0:T(8,128)(2,1)S(1)}, bf16[596,128]{1,0:T(8,128)(2,1)S(1)}, u32[]{:S(2)}, u32[]{:S(2)}) collective-permute-start(bf16[596,128]{1,0:T(8,128)(2,1)S(1)} %get-tuple-element.254), channel_id=1, source_target_pairs={{0,8},{1,9},{2,10},{3,11},{4,12},{5,13},{6,14},{7,15},{8,0},{9,1},... | collective-permute-start | bytes 457736 | tf_op jit(solution)/shard_map/ppermute | solution.py:322
  64.8 8.5 %collective-permute-start.17 = (bf16[596,128]{1,0:T(8,128)(2,1)S(1)}, bf16[596,128]{1,0:T(8,128)(2,1)S(1)}, u32[]{:S(2)}, u32[]{:S(2)}) collective-permute-start(bf16[596,128]{1,0:T(8,128)(2,1)S(1)} %get-tuple-element.255), channel_id=1, source_target_pairs={{0,16},{1,17},{2,18},{3,19},{4,20},{5,21},{6,22},{7,23},{8,24},{9,... | collective-permute-start | bytes 457736 | tf_op jit(solution)/shard_map/ppermute | solution.py:322
  66.3 7.0 %collective-permute-start.18 = (bf16[596,128]{1,0:T(8,128)(2,1)S(1)}, bf16[596,128]{1,0:T(8,128)(2,1)S(1)}, u32[]{:S(2)}, u32[]{:S(2)}) collective-permute-start(bf16[596,128]{1,0:T(8,128)(2,1)S(1)} %get-tuple-element.256), channel_id=1, source_target_pairs={{0,24},{1,25},{2,26},{3,27},{4,28},{5,29},{6,30},{7,31},{8,16},{9,... | collective-permute-start | bytes 457736 | tf_op jit(solution)/shard_map/ppermute | solution.py:322
  68.2 15.6 %collective-permute-start.15 = (bf16[128,1024]{1,0:T(8,128)(2,1)S(1)}, bf16[128,1024]{1,0:T(8,128)(2,1)S(1)}, u32[]{:S(2)}, u32[]{:S(2)}) collective-permute-start(bf16[128,1024]{1,0:T(8,128)(2,1)S(1)} %get-tuple-element.294.own), channel_id=1, source_target_pairs={{0,2},{1,3},{2,0},{3,1},{4,6},{5,7},{6,4},{7,5},{8,10},{9,11},{10,... | collective-permute-start | bytes 786440 | tf_op jit(solution)/shard_map/ppermute | solution.py:322
  73.3 17.9 %collective-permute-start.24 = (bf16[256,1024]{1,0:T(8,128)(2,1)S(1)}, bf16[256,1024]{1,0:T(8,128)(2,1)S(1)}, u32[]{:S(2)}, u32[]{:S(2)}) collective-permute-start(bf16[256,1024]{1,0:T(8,128)(2,1)S(1)} %shard_map.204.f0.w0), channel_id=1, source_target_pairs={{0,16},{1,17},{2,18},{3,19},{4,20},{5,21},{6,22},{7,23},{8,24},{9,... | collective-permute-start | bytes 1572872 | tf_op jit(solution)/shard_map/ppermute | solution.py:322
  74.6 16.6 %collective-permute-start.23 = (bf16[256,1024]{1,0:T(8,128)(2,1)S(1)}, bf16[256,1024]{1,0:T(8,128)(2,1)S(1)}, u32[]{:S(2)}, u32[]{:S(2)}) collective-permute-start(bf16[256,1024]{1,0:T(8,128)(2,1)S(1)} %shard_map.204.f0.w0), channel_id=1, source_target_pairs={{0,8},{1,9},{2,10},{3,11},{4,12},{5,13},{6,14},{7,15},{8,0},{9,1},... | collective-permute-start | bytes 1572872 | tf_op jit(solution)/shard_map/ppermute | solution.py:322
  75.4 10.2 %collective-permute-start.26 = (bf16[56,1024]{1,0:T(8,128)(2,1)S(1)}, bf16[56,1024]{1,0:T(8,128)(2,1)S(1)}, u32[]{:S(2)}, u32[]{:S(2)}) collective-permute-start(bf16[56,1024]{1,0:T(8,128)(2,1)S(1)} %get-tuple-element.275), channel_id=1, source_target_pairs={{0,2},{1,3},{2,0},{3,1},{4,6},{5,7},{6,4},{7,5},{8,10},{9,11},{10,... | collective-permute-start | bytes 344072 | tf_op jit(solution)/shard_map/ppermute | solution.py:322
  75.4 10.8 %collective-permute-start.25 = (bf16[56,1024]{1,0:T(8,128)(2,1)S(1)}, bf16[56,1024]{1,0:T(8,128)(2,1)S(1)}, u32[]{:S(2)}, u32[]{:S(2)}) collective-permute-start(bf16[56,1024]{1,0:T(8,128)(2,1)S(1)} %get-tuple-element.274.here), channel_id=1, source_target_pairs={{0,1},{1,0},{2,3},{3,2},{4,5},{5,4},{6,7},{7,6},{8,9},{9,8},{10,11... | collective-permute-start | bytes 344072 | tf_op jit(solution)/shard_map/ppermute | solution.py:322
  83.8 4.1 %collective-permute-start.20 = (bf16[196,128]{1,0:T(8,128)(2,1)S(1)}, bf16[196,128]{1,0:T(8,128)(2,1)S(1)}, u32[]{:S(2)}, u32[]{:S(2)}) collective-permute-start(bf16[196,128]{1,0:T(8,128)(2,1)S(1)} %get-tuple-element.270), channel_id=1, source_target_pairs={{0,8},{1,9},{2,10},{3,11},{4,12},{5,13},{6,14},{7,15},{8,0},{9,1},... | collective-permute-start | bytes 150536 | tf_op jit(solution)/shard_map/ppermute | solution.py:322
  85.6 4.2 %collective-permute-start.21 = (bf16[196,128]{1,0:T(8,128)(2,1)S(1)}, bf16[196,128]{1,0:T(8,128)(2,1)S(1)}, u32[]{:S(2)}, u32[]{:S(2)}) collective-permute-start(bf16[196,128]{1,0:T(8,128)(2,1)S(1)} %get-tuple-element.271), channel_id=1, source_target_pairs={{0,16},{1,17},{2,18},{3,19},{4,20},{5,21},{6,22},{7,23},{8,24},{9,... | collective-permute-start | bytes 150536 | tf_op jit(solution)/shard_map/ppermute | solution.py:322
  86.2 5.0 %collective-permute-start.22 = (bf16[196,128]{1,0:T(8,128)(2,1)S(1)}, bf16[196,128]{1,0:T(8,128)(2,1)S(1)}, u32[]{:S(2)}, u32[]{:S(2)}) collective-permute-start(bf16[196,128]{1,0:T(8,128)(2,1)S(1)} %get-tuple-element.272), channel_id=1, source_target_pairs={{0,24},{1,25},{2,26},{3,27},{4,28},{5,29},{6,30},{7,31},{8,16},{9,... | collective-permute-start | bytes 150536 | tf_op jit(solution)/shard_map/ppermute | solution.py:322
  92.2 4.5 %collective-permute-start.27 = (bf16[196,1024]{1,0:T(8,128)(2,1)S(1)}, bf16[196,1024]{1,0:T(8,128)(2,1)S(1)}, u32[]{:S(2)}, u32[]{:S(2)}) collective-permute-start(bf16[196,1024]{1,0:T(8,128)(2,1)S(1)} %get-tuple-element.281), channel_id=1, source_target_pairs={{0,4},{1,5},{2,6},{3,7},{4,0},{5,1},{6,2},{7,3},{8,12},{9,13},{10,... | collective-permute-start | bytes 1204232 | tf_op jit(solution)/shard_map/ppermute | solution.py:322
  95.4 14.8 %collective-permute-start.33 = (bf16[256,1024]{1,0:T(8,128)(2,1)S(1)}, bf16[256,1024]{1,0:T(8,128)(2,1)S(1)}, u32[]{:S(2)}, u32[]{:S(2)}) collective-permute-start(bf16[256,1024]{1,0:T(8,128)(2,1)S(1)} %shard_map.211.g0.w0), channel_id=1, source_target_pairs={{0,8},{1,9},{2,10},{3,11},{4,12},{5,13},{6,14},{7,15},{8,0},{9,1},... | collective-permute-start | bytes 1572872 | tf_op jit(solution)/shard_map/ppermute | solution.py:322
  97.4 14.2 %collective-permute-start.28 = (bf16[196,1024]{1,0:T(8,128)(2,1)S(1)}, bf16[196,1024]{1,0:T(8,128)(2,1)S(1)}, u32[]{:S(2)}, u32[]{:S(2)}) collective-permute-start(bf16[196,1024]{1,0:T(8,128)(2,1)S(1)} %get-tuple-element.283), channel_id=1, source_target_pairs={{0,1},{1,0},{2,3},{3,2},{4,5},{5,4},{6,7},{7,6},{8,9},{9,8},{10,11... | collective-permute-start | bytes 1204232 | tf_op jit(solution)/shard_map/ppermute | solution.py:322
  97.5 14.1 %collective-permute-start.29 = (bf16[56,1024]{1,0:T(8,128)(2,1)S(1)}, bf16[56,1024]{1,0:T(8,128)(2,1)S(1)}, u32[]{:S(2)}, u32[]{:S(2)}) collective-permute-start(bf16[56,1024]{1,0:T(8,128)(2,1)S(1)} %collective-permute-done.26.r2), channel_id=1, source_target_pairs={{0,1},{1,0},{2,3},{3,2},{4,5},{5,4},{6,7},{7,6},{8,9},{9,8},{10,11... | collective-permute-start | bytes 344072 | tf_op jit(solution)/shard_map/ppermute | solution.py:322
  99.5 14.4 %collective-permute-start.34 = (bf16[256,1024]{1,0:T(8,128)(2,1)S(1)}, bf16[256,1024]{1,0:T(8,128)(2,1)S(1)}, u32[]{:S(2)}, u32[]{:S(2)}) collective-permute-start(bf16[256,1024]{1,0:T(8,128)(2,1)S(1)} %shard_map.211.g0.w0), channel_id=1, source_target_pairs={{0,16},{1,17},{2,18},{3,19},{4,20},{5,21},{6,22},{7,23},{8,24},{9,... | collective-permute-start | bytes 1572872 | tf_op jit(solution)/shard_map/ppermute | solution.py:322
  100.3 20.6 %collective-permute-start.35 = (bf16[256,1024]{1,0:T(8,128)(2,1)S(1)}, bf16[256,1024]{1,0:T(8,128)(2,1)S(1)}, u32[]{:S(2)}, u32[]{:S(2)}) collective-permute-start(bf16[256,1024]{1,0:T(8,128)(2,1)S(1)} %collective-permute-done.24.f2.w2), channel_id=1, source_target_pairs={{0,8},{1,9},{2,10},{3,11},{4,12},{5,13},{6,14},{7,15},{8,0},{9,1},... | collective-permute-start | bytes 1572872 | tf_op jit(solution)/shard_map/ppermute | solution.py:322
  110.2 13.9 %collective-permute-start.36 = (bf16[256,1024]{1,0:T(8,128)(2,1)S(1)}, bf16[256,1024]{1,0:T(8,128)(2,1)S(1)}, u32[]{:S(2)}, u32[]{:S(2)}) collective-permute-start(bf16[256,1024]{1,0:T(8,128)(2,1)S(1)} %collective-permute-done.33.g1.w1), channel_id=1, source_target_pairs={{0,16},{1,17},{2,18},{3,19},{4,20},{5,21},{6,22},{7,23},{8,24},{9,... | collective-permute-start | bytes 1572872 | tf_op jit(solution)/shard_map/ppermute | solution.py:322
  130.1 11.6 %collective-permute-start.38 = (bf16[196,1024]{1,0:T(8,128)(2,1)S(1)}, bf16[196,1024]{1,0:T(8,128)(2,1)S(1)}, u32[]{:S(2)}, u32[]{:S(2)}) collective-permute-start(bf16[196,1024]{1,0:T(8,128)(2,1)S(1)} %get-tuple-element.303), channel_id=1, source_target_pairs={{0,1},{1,0},{2,3},{3,2},{4,5},{5,4},{6,7},{7,6},{8,9},{9,8},{10,11... | collective-permute-start | bytes 1204232 | tf_op jit(solution)/shard_map/ppermute | solution.py:322
  132.4 25.5 %collective-permute-start.46 = (bf16[2,256,1024]{2,1,0:T(8,128)(2,1)S(1)}, bf16[2,256,1024]{2,1,0:T(8,128)(2,1)S(1)}, u32[]{:S(2)}, u32[]{:S(2)}) collective-permute-start(bf16[2,256,1024]{2,1,0:T(8,128)(2,1)S(1)} %get-tuple-element.333), channel_id=1, source_target_pairs={{0,16},{1,17},{2,18},{3,19},{4,20},{5,21},{6,22},{7,23},{8,24},{9,... | collective-permute-start | bytes 3145736 | tf_op jit(solution)/shard_map/ppermute | solution.py:322
  135.1 25.8 %collective-permute-start.45 = (bf16[2,256,1024]{2,1,0:T(8,128)(2,1)S(1)}, bf16[2,256,1024]{2,1,0:T(8,128)(2,1)S(1)}, u32[]{:S(2)}, u32[]{:S(2)}) collective-permute-start(bf16[2,256,1024]{2,1,0:T(8,128)(2,1)S(1)} %get-tuple-element.327), channel_id=1, source_target_pairs={{0,8},{1,9},{2,10},{3,11},{4,12},{5,13},{6,14},{7,15},{8,0},{9,1},... | collective-permute-start | bytes 3145736 | tf_op jit(solution)/shard_map/ppermute | solution.py:322
  144.5 7.2 %collective-permute-start.41 = (bf16[98,1024]{1,0:T(8,128)(2,1)S(1)}, bf16[98,1024]{1,0:T(8,128)(2,1)S(1)}, u32[]{:S(2)}, u32[]{:S(2)}) collective-permute-start(bf16[98,1024]{1,0:T(8,128)(2,1)S(1)} %get-tuple-element.318), channel_id=1, source_target_pairs={{0,1},{1,0},{2,3},{3,2},{4,5},{5,4},{6,7},{7,6},{8,9},{9,8},{10,11... | collective-permute-start | bytes 602120 | tf_op jit(solution)/shard_map/ppermute | solution.py:322
  151.8 9.8 %collective-permute-start.42 = (bf16[196,128]{1,0:T(8,128)(2,1)S(1)}, bf16[196,128]{1,0:T(8,128)(2,1)S(1)}, u32[]{:S(2)}, u32[]{:S(2)}) collective-permute-start(bf16[196,128]{1,0:T(8,128)(2,1)S(1)} %get-tuple-element.320), channel_id=1, source_target_pairs={{0,8},{1,9},{2,10},{3,11},{4,12},{5,13},{6,14},{7,15},{8,0},{9,1},... | collective-permute-start | bytes 150536 | tf_op jit(solution)/shard_map/ppermute | solution.py:322
  152.5 9.1 %collective-permute-start.43 = (bf16[196,128]{1,0:T(8,128)(2,1)S(1)}, bf16[196,128]{1,0:T(8,128)(2,1)S(1)}, u32[]{:S(2)}, u32[]{:S(2)}) collective-permute-start(bf16[196,128]{1,0:T(8,128)(2,1)S(1)} %get-tuple-element.321), channel_id=1, source_target_pairs={{0,16},{1,17},{2,18},{3,19},{4,20},{5,21},{6,22},{7,23},{8,24},{9,... | collective-permute-start | bytes 150536 | tf_op jit(solution)/shard_map/ppermute | solution.py:322
  153.9 8.7 %collective-permute-start.44 = (bf16[196,128]{1,0:T(8,128)(2,1)S(1)}, bf16[196,128]{1,0:T(8,128)(2,1)S(1)}, u32[]{:S(2)}, u32[]{:S(2)}) collective-permute-start(bf16[196,128]{1,0:T(8,128)(2,1)S(1)} %get-tuple-element.322), channel_id=1, source_target_pairs={{0,24},{1,25},{2,26},{3,27},{4,28},{5,29},{6,30},{7,31},{8,16},{9,... | collective-permute-start | bytes 150536 | tf_op jit(solution)/shard_map/ppermute | solution.py:322
  162.7 13.2 %collective-permute-start.47 = (bf16[56,1024]{1,0:T(8,128)(2,1)S(1)}, bf16[56,1024]{1,0:T(8,128)(2,1)S(1)}, u32[]{:S(2)}, u32[]{:S(2)}) collective-permute-start(bf16[56,1024]{1,0:T(8,128)(2,1)S(1)} %get-tuple-element.350), channel_id=1, source_target_pairs={{0,2},{1,3},{2,0},{3,1},{4,6},{5,7},{6,4},{7,5},{8,10},{9,11},{10,... | collective-permute-start | bytes 344072 | tf_op jit(solution)/shard_map/ppermute | solution.py:322
  165.3 11.9 %collective-permute-start.48 = (bf16[256,1024]{1,0:T(8,128)(2,1)S(1)}, bf16[256,1024]{1,0:T(8,128)(2,1)S(1)}, u32[]{:S(2)}, u32[]{:S(2)}) collective-permute-start(bf16[256,1024]{1,0:T(8,128)(2,1)S(1)} %get-tuple-element.352), channel_id=1, source_target_pairs={{0,16},{1,17},{2,18},{3,19},{4,20},{5,21},{6,22},{7,23},{8,24},{9,... | collective-permute-start | bytes 1572872 | tf_op jit(solution)/shard_map/ppermute | solution.py:322
  166.1 11.6 %collective-permute-start.49 = (bf16[256,1024]{1,0:T(8,128)(2,1)S(1)}, bf16[256,1024]{1,0:T(8,128)(2,1)S(1)}, u32[]{:S(2)}, u32[]{:S(2)}) collective-permute-start(bf16[256,1024]{1,0:T(8,128)(2,1)S(1)} %get-tuple-element.354), channel_id=1, source_target_pairs={{0,8},{1,9},{2,10},{3,11},{4,12},{5,13},{6,14},{7,15},{8,0},{9,1},... | collective-permute-start | bytes 1572872 | tf_op jit(solution)/shard_map/ppermute | solution.py:322
  178.5 4.4 %collective-permute-start.53 = (bf16[4,56,1024]{2,1,0:T(8,128)(2,1)S(1)}, bf16[4,56,1024]{2,1,0:T(8,128)(2,1)S(1)}, u32[]{:S(2)}, u32[]{:S(2)}) collective-permute-start(bf16[4,56,1024]{2,1,0:T(8,128)(2,1)S(1)} %get-tuple-element.361), channel_id=1, source_target_pairs={{0,4},{1,5},{2,6},{3,7},{4,0},{5,1},{6,2},{7,3},{8,12},{9,13},{10,... | collective-permute-start | bytes 1376264 | tf_op jit(solution)/shard_map/ppermute | solution.py:322
  178.6 6.8 %collective-permute-start.50 = (bf16[596,128]{1,0:T(8,128)(2,1)S(1)}, bf16[596,128]{1,0:T(8,128)(2,1)S(1)}, u32[]{:S(2)}, u32[]{:S(2)}) collective-permute-start(bf16[596,128]{1,0:T(8,128)(2,1)S(1)} %get-tuple-element.358), channel_id=1, source_target_pairs={{0,8},{1,9},{2,10},{3,11},{4,12},{5,13},{6,14},{7,15},{8,0},{9,1},... | collective-permute-start | bytes 457736 | tf_op jit(solution)/shard_map/ppermute | solution.py:322
  179.8 9.3 %collective-permute-start.51 = (bf16[596,128]{1,0:T(8,128)(2,1)S(1)}, bf16[596,128]{1,0:T(8,128)(2,1)S(1)}, u32[]{:S(2)}, u32[]{:S(2)}) collective-permute-start(bf16[596,128]{1,0:T(8,128)(2,1)S(1)} %get-tuple-element.359), channel_id=1, source_target_pairs={{0,16},{1,17},{2,18},{3,19},{4,20},{5,21},{6,22},{7,23},{8,24},{9,... | collective-permute-start | bytes 457736 | tf_op jit(solution)/shard_map/ppermute | solution.py:322
  180.5 8.6 %collective-permute-start.52 = (bf16[596,128]{1,0:T(8,128)(2,1)S(1)}, bf16[596,128]{1,0:T(8,128)(2,1)S(1)}, u32[]{:S(2)}, u32[]{:S(2)}) collective-permute-start(bf16[596,128]{1,0:T(8,128)(2,1)S(1)} %get-tuple-element.360), channel_id=1, source_target_pairs={{0,24},{1,25},{2,26},{3,27},{4,28},{5,29},{6,30},{7,31},{8,16},{9,... | collective-permute-start | bytes 457736 | tf_op jit(solution)/shard_map/ppermute | solution.py:322
  182.9 13.0 %collective-permute-start.62 = (bf16[128,2048]{1,0:T(8,128)(2,1)S(1)}, bf16[128,2048]{1,0:T(8,128)(2,1)S(1)}, u32[]{:S(2)}, u32[]{:S(2)}) collective-permute-start(bf16[128,2048]{1,0:T(8,128)(2,1)S(1)} %get-tuple-element.404), channel_id=1, source_target_pairs={{0,4},{1,5},{2,6},{3,7},{4,0},{5,1},{6,2},{7,3},{8,12},{9,13},{10,... | collective-permute-start | bytes 1572872 | tf_op jit(solution)/shard_map/ppermute | solution.py:322
  190.7 3.6 %collective-permute-start.54 = (bf16[196,1024]{1,0:T(8,128)(2,1)S(1)}, bf16[196,1024]{1,0:T(8,128)(2,1)S(1)}, u32[]{:S(2)}, u32[]{:S(2)}) collective-permute-start(bf16[196,1024]{1,0:T(8,128)(2,1)S(1)} %get-tuple-element.371), channel_id=1, source_target_pairs={{0,4},{1,5},{2,6},{3,7},{4,0},{5,1},{6,2},{7,3},{8,12},{9,13},{10,... | collective-permute-start | bytes 1204232 | tf_op jit(solution)/shard_map/ppermute | solution.py:322
  190.8 9.4 %collective-permute-start.56 = (bf16[2,56,1024]{2,1,0:T(8,128)(2,1)S(1)}, bf16[2,56,1024]{2,1,0:T(8,128)(2,1)S(1)}, u32[]{:S(2)}, u32[]{:S(2)}) collective-permute-start(bf16[2,56,1024]{2,1,0:T(8,128)(2,1)S(1)} %get-tuple-element.385), channel_id=1, source_target_pairs={{0,8},{1,9},{2,10},{3,11},{4,12},{5,13},{6,14},{7,15},{8,0},{9,1},... | collective-permute-start | bytes 688136 | tf_op jit(solution)/shard_map/ppermute | solution.py:322
  191.8 12.6 %collective-permute-start.57 = (bf16[2,56,1024]{2,1,0:T(8,128)(2,1)S(1)}, bf16[2,56,1024]{2,1,0:T(8,128)(2,1)S(1)}, u32[]{:S(2)}, u32[]{:S(2)}) collective-permute-start(bf16[2,56,1024]{2,1,0:T(8,128)(2,1)S(1)} %get-tuple-element.386), channel_id=1, source_target_pairs={{0,16},{1,17},{2,18},{3,19},{4,20},{5,21},{6,22},{7,23},{8,24},{9,... | collective-permute-start | bytes 688136 | tf_op jit(solution)/shard_map/ppermute | solution.py:322
  193.0 11.3 %collective-permute-start.58 = (bf16[2,56,1024]{2,1,0:T(8,128)(2,1)S(1)}, bf16[2,56,1024]{2,1,0:T(8,128)(2,1)S(1)}, u32[]{:S(2)}, u32[]{:S(2)}) collective-permute-start(bf16[2,56,1024]{2,1,0:T(8,128)(2,1)S(1)} %get-tuple-element.387), channel_id=1, source_target_pairs={{0,24},{1,25},{2,26},{3,27},{4,28},{5,29},{6,30},{7,31},{8,16},{9,... | collective-permute-start | bytes 688136 | tf_op jit(solution)/shard_map/ppermute | solution.py:322
  195.5 10.5 %collective-permute-start.55 = (bf16[112,1024]{1,0:T(8,128)(2,1)S(1)}, bf16[112,1024]{1,0:T(8,128)(2,1)S(1)}, u32[]{:S(2)}, u32[]{:S(2)}) collective-permute-start(bf16[112,1024]{1,0:T(8,128)(2,1)S(1)} %get-tuple-element.375), channel_id=1, source_target_pairs={{0,1},{1,0},{2,3},{3,2},{4,5},{5,4},{6,7},{7,6},{8,9},{9,8},{10,11... | collective-permute-start | bytes 688136 | tf_op jit(solution)/shard_map/ppermute | solution.py:322
  196.5 29.6 %collective-permute-start.63 = (bf16[128,2048]{1,0:T(8,128)(2,1)S(1)}, bf16[128,2048]{1,0:T(8,128)(2,1)S(1)}, u32[]{:S(2)}, u32[]{:S(2)}) collective-permute-start(bf16[128,2048]{1,0:T(8,128)(2,1)S(1)} %shard_map.233), channel_id=1, source_target_pairs={{0,2},{1,3},{2,0},{3,1},{4,6},{5,7},{6,4},{7,5},{8,10},{9,11},{10,... | collective-permute-start | bytes 1572872 | tf_op jit(solution)/shard_map/ppermute | solution.py:322
  205.9 21.6 %collective-permute-start.60 = (bf16[2,256,512]{2,1,0:T(8,128)(2,1)S(1)}, bf16[2,256,512]{2,1,0:T(8,128)(2,1)S(1)}, u32[]{:S(2)}, u32[]{:S(2)}) collective-permute-start(bf16[2,256,512]{2,1,0:T(8,128)(2,1)S(1)} %get-tuple-element.397), channel_id=1, source_target_pairs={{0,8},{1,9},{2,10},{3,11},{4,12},{5,13},{6,14},{7,15},{8,0},{9,1},... | collective-permute-start | bytes 1572872 | tf_op jit(solution)/shard_map/ppermute | solution.py:322
  206.6 20.9 %collective-permute-start.61 = (bf16[2,256,512]{2,1,0:T(8,128)(2,1)S(1)}, bf16[2,256,512]{2,1,0:T(8,128)(2,1)S(1)}, u32[]{:S(2)}, u32[]{:S(2)}) collective-permute-start(bf16[2,256,512]{2,1,0:T(8,128)(2,1)S(1)} %get-tuple-element.398), channel_id=1, source_target_pairs={{0,16},{1,17},{2,18},{3,19},{4,20},{5,21},{6,22},{7,23},{8,24},{9,... | collective-permute-start | bytes 1572872 | tf_op jit(solution)/shard_map/ppermute | solution.py:322
  208.9 18.6 %collective-permute-start.59 = (bf16[64,1024]{1,0:T(8,128)(2,1)S(1)}, bf16[64,1024]{1,0:T(8,128)(2,1)S(1)}, u32[]{:S(2)}, u32[]{:S(2)}) collective-permute-start(bf16[64,1024]{1,0:T(8,128)(2,1)S(1)} %get-tuple-element.396), channel_id=1, source_target_pairs={{0,2},{1,3},{2,0},{3,1},{4,6},{5,7},{6,4},{7,5},{8,10},{9,11},{10,... | collective-permute-start | bytes 393224 | tf_op jit(solution)/shard_map/ppermute | solution.py:322
  228.2 6.7 %collective-permute-start.68 = (bf16[256,512]{1,0:T(8,128)(2,1)S(1)}, bf16[256,512]{1,0:T(8,128)(2,1)S(1)}, u32[]{:S(2)}, u32[]{:S(2)}) collective-permute-start(bf16[256,512]{1,0:T(8,128)(2,1)S(1)} %get-tuple-element.418), channel_id=1, source_target_pairs={{0,16},{1,17},{2,18},{3,19},{4,20},{5,21},{6,22},{7,23},{8,24},{9,... | collective-permute-start | bytes 786440 | tf_op jit(solution)/shard_map/ppermute | solution.py:322
  229.6 6.4 %collective-permute-start.69 = (bf16[256,512]{1,0:T(8,128)(2,1)S(1)}, bf16[256,512]{1,0:T(8,128)(2,1)S(1)}, u32[]{:S(2)}, u32[]{:S(2)}) collective-permute-start(bf16[256,512]{1,0:T(8,128)(2,1)S(1)} %get-tuple-element.423), channel_id=1, source_target_pairs={{0,8},{1,9},{2,10},{3,11},{4,12},{5,13},{6,14},{7,15},{8,0},{9,1},... | collective-permute-start | bytes 786440 | tf_op jit(solution)/shard_map/ppermute | solution.py:322
  231.9 6.6 %collective-permute-start.64 = (bf16[4,56,1024]{2,1,0:T(8,128)(2,1)S(1)}, bf16[4,56,1024]{2,1,0:T(8,128)(2,1)S(1)}, u32[]{:S(2)}, u32[]{:S(2)}) collective-permute-start(bf16[4,56,1024]{2,1,0:T(8,128)(2,1)S(1)} %get-tuple-element.407), channel_id=1, source_target_pairs={{0,4},{1,5},{2,6},{3,7},{4,0},{5,1},{6,2},{7,3},{8,12},{9,13},{10,... | collective-permute-start | bytes 1376264 | tf_op jit(solution)/shard_map/ppermute | solution.py:322
  236.7 6.0 %collective-permute-start.70 = (bf16[128,1024]{1,0:T(8,128)(2,1)S(1)}, bf16[128,1024]{1,0:T(8,128)(2,1)S(1)}, u32[]{:S(2)}, u32[]{:S(2)}) collective-permute-start(bf16[128,1024]{1,0:T(8,128)(2,1)S(1)} %get-tuple-element.425), channel_id=1, source_target_pairs={{0,4},{1,5},{2,6},{3,7},{4,0},{5,1},{6,2},{7,3},{8,12},{9,13},{10,... | collective-permute-start | bytes 786440 | tf_op jit(solution)/shard_map/ppermute | solution.py:322
  239.1 8.5 %collective-permute-start.65 = (bf16[2,56,1024]{2,1,0:T(8,128)(2,1)S(1)}, bf16[2,56,1024]{2,1,0:T(8,128)(2,1)S(1)}, u32[]{:S(2)}, u32[]{:S(2)}) collective-permute-start(bf16[2,56,1024]{2,1,0:T(8,128)(2,1)S(1)} %get-tuple-element.408), channel_id=1, source_target_pairs={{0,8},{1,9},{2,10},{3,11},{4,12},{5,13},{6,14},{7,15},{8,0},{9,1},... | collective-permute-start | bytes 688136 | tf_op jit(solution)/shard_map/ppermute | solution.py:322
  240.7 12.6 %collective-permute-start.66 = (bf16[2,56,1024]{2,1,0:T(8,128)(2,1)S(1)}, bf16[2,56,1024]{2,1,0:T(8,128)(2,1)S(1)}, u32[]{:S(2)}, u32[]{:S(2)}) collective-permute-start(bf16[2,56,1024]{2,1,0:T(8,128)(2,1)S(1)} %get-tuple-element.409), channel_id=1, source_target_pairs={{0,16},{1,17},{2,18},{3,19},{4,20},{5,21},{6,22},{7,23},{8,24},{9,... | collective-permute-start | bytes 688136 | tf_op jit(solution)/shard_map/ppermute | solution.py:322
  241.4 11.9 %collective-permute-start.67 = (bf16[2,56,1024]{2,1,0:T(8,128)(2,1)S(1)}, bf16[2,56,1024]{2,1,0:T(8,128)(2,1)S(1)}, u32[]{:S(2)}, u32[]{:S(2)}) collective-permute-start(bf16[2,56,1024]{2,1,0:T(8,128)(2,1)S(1)} %get-tuple-element.410), channel_id=1, source_target_pairs={{0,24},{1,25},{2,26},{3,27},{4,28},{5,29},{6,30},{7,31},{8,16},{9,... | collective-permute-start | bytes 688136 | tf_op jit(solution)/shard_map/ppermute | solution.py:322
  243.2 13.3 %collective-permute-start.71 = (bf16[128,1024]{1,0:T(8,128)(2,1)S(1)}, bf16[128,1024]{1,0:T(8,128)(2,1)S(1)}, u32[]{:S(2)}, u32[]{:S(2)}) collective-permute-start(bf16[128,1024]{1,0:T(8,128)(2,1)S(1)} %shard_map.240), channel_id=1, source_target_pairs={{0,2},{1,3},{2,0},{3,1},{4,6},{5,7},{6,4},{7,5},{8,10},{9,11},{10,... | collective-permute-start | bytes 786440 | tf_op jit(solution)/shard_map/ppermute | solution.py:322
  (14 other events, 35.9 us)
